TPU v7x, 32 devices: a whole 2x2x4 slice. The times are simulated.
32 devices in a mesh: wide: 8 (over z, y), narrow: 4 (over x, core).
Axes of the slice: x: 2, y: 2, z: 4, core: 2. Of those that a mesh axis runs over, the one named last changes fastest.
Arguments:
- tokens: bfloat16 [32768, 768], P(('wide', 'narrow')), may hold values from -6 to 6
- bucket: int32 [256], P(('wide', 'narrow')), may hold values from 0 to 7, as said below
- lengths: int32 [832], P(('wide', 'narrow')), may hold values from 5 to 128, as said below
- pairing: int32 [32, 26], P(('wide', 'narrow')), may hold values from 0 to 25, as said below
- targets: float32 [416], P(('wide', 'narrow')), may hold values from 0 to 1
- w_qkv: bfloat16 [768, 2304], replicated, may hold values from -0.21875 to 0.21875
- bias_q: bfloat16 [768], replicated, may hold values from -3 to 3
- bias_v: bfloat16 [768], replicated, may hold values from -3 to 3
- w_out: bfloat16 [768, 768], replicated, may hold values from -0.4375 to 0.4375
- bias_out: bfloat16 [768], replicated, may hold values from -3 to 3
- gain_attn: bfloat16 [768], replicated, may hold values from 0.5 to 1.5
- shift_attn: bfloat16 [768], replicated, may hold values from -1.1953125 to 1.1953125
- w_up: bfloat16 [768, 3072], replicated, may hold values from -0.21875 to 0.21875
- bias_up: bfloat16 [3072], replicated, may hold values from -3 to 3
- w_down: bfloat16 [3072, 768], replicated, may hold values from -0.109375 to 0.109375
- bias_down: bfloat16 [768], replicated, may hold values from -3 to 3
- gain_ffn: bfloat16 [768], replicated, may hold values from 0.5 to 1.5
- shift_ffn: bfloat16 [768], replicated, may hold values from -1.1953125 to 1.1953125
Outputs:
- encoded: bfloat16 [32768, 768], P(('wide', 'narrow'))
- grad_tokens: bfloat16 [32768, 768], P(('wide', 'narrow'))
- grad_w_qkv: float32 [768, 2304], P('wide')
- grad_bias_q: float32 [768], P('wide')
- grad_bias_v: float32 [768], P('wide')
- grad_w_out: float32 [768, 768], P('wide')
- grad_bias_out: float32 [768], P('wide')
- grad_gain_attn: float32 [768], P('wide')
- grad_shift_attn: float32 [768], P('wide')
- grad_w_up: float32 [768, 3072], P('wide')
- grad_bias_up: float32 [3072], P('wide')
- grad_w_down: float32 [3072, 768], P('wide')
- grad_bias_down: float32 [768], P('wide')
- grad_gain_ffn: float32 [768], P('wide')
- grad_shift_ffn: float32 [768], P('wide')
Inputs may be any that keep to these rules, and one draw needn't show every extreme that they name: `bucket`: A device's 8 batches go to different wide indices, one batch of each class c, to a wide index of c * 1 to (c + 1) * 1 - 1; in every group each wide index takes exactly 8 batches. A batch of class c holds max(1, 12 div 2^c) sentences of together at most 128 tokens; a device's lengths list its batches' sentences batch after batch; every device has a sentence of exactly 128 tokens. `pairing`: each row is a permutation of 0 to 25; entries 2p and 2p + 1 name pair p.
All inputs are finite; a program needn't handle non-finite values.
Results may differ from a plain program's by a relative error of at most 0.012.
Values may be sent and summed in bfloat16 or wider, within the bound.
No kernel may reach another device: no remote copies, remote signals or barrier semaphores. Data moves between devices by JAX's collectives and lax.ppermute only.
A program may use at most 192 MiB of HBM per device.

v0:
```python
from functools import partial

import jax
import jax.numpy as jnp
from jax import lax
from jax.sharding import PartitionSpec as P

HEADS = 12
HDIM = 64
KTOP = 12


EXACT = lax.Precision.HIGHEST
NORM_EPS = 1e-12
COS_EPS = 1e-06
MASKED = -1000000000.0
LOSS_SCALE = 1024.0


def contract_rows(left, right):
    return lax.dot_general(
        left, right, (((0,), (0,)), ((), ())), preferred_element_type=jnp.float32
    )


def times_transpose(left, right):
    return lax.dot_general(
        left, right, (((1,), (1,)), ((), ())), preferred_element_type=jnp.float32
    )


def norm_forward(values, gain, shift):
    center = values - jnp.mean(values, axis=-1, keepdims=True)
    spread = lax.rsqrt(jnp.mean(center * center, axis=-1, keepdims=True) + NORM_EPS)
    normed = center * spread
    return (normed * gain + shift, normed, spread)


def norm_backward(grad_out, normed, spread, gain):
    scaled = grad_out * gain
    grad_in = spread * (
        scaled
        - jnp.mean(scaled, axis=-1, keepdims=True)
        - normed * jnp.mean(scaled * normed, axis=-1, keepdims=True)
    )
    return (grad_in, jnp.sum(grad_out * normed, axis=0), jnp.sum(grad_out, axis=0))


def class_counts(batches):
    return jnp.array([max(1, KTOP // 2**number) for number in range(batches)], dtype=jnp.int32)


def source_layout(bucket_row, lengths_row, group_size, span):
    batches = bucket_row.shape[0]
    batch_ids = jnp.arange(batches, dtype=jnp.int32)
    classes = bucket_row // group_size
    choose = (classes[:, None] == batch_ids[None, :]).astype(jnp.int32)
    counts = jnp.sum(choose * class_counts(batches)[None, :], axis=1)
    starts = jnp.cumsum(counts) - counts
    sentence = jnp.arange(lengths_row.shape[0], dtype=jnp.int32)
    batch_of = jnp.sum((sentence[:, None] >= starts[None, :]).astype(jnp.int32), axis=1) - 1
    owner = (batch_of[:, None] == batch_ids[None, :]).astype(jnp.int32)
    within = sentence - jnp.sum(owner * starts[None, :], axis=1)
    earlier = jnp.sum(
        lengths_row[:, None] * (batch_of[:, None] < batch_ids[None, :]).astype(jnp.int32), axis=0
    )
    finish = jnp.cumsum(lengths_row) - jnp.sum(owner * earlier[None, :], axis=1)
    position = jnp.arange(span, dtype=jnp.int32)
    before = (owner.T[:, None, :] > 0) & (finish[None, None, :] <= position[None, :, None])
    passed = jnp.sum(before.astype(jnp.int32), axis=2)
    row_tags = jnp.where(passed < counts[:, None], passed + 1, 0)
    return (row_tags, batch_of, within)


def allowed_pairs(row_tags):
    span = row_tags.shape[1]
    same = (row_tags[:, :, None] == row_tags[:, None, :]) & (row_tags[:, :, None] > 0)
    return same | jnp.eye(span, dtype=jnp.bool_)[None]


def pack_rows(item, wide_count, narrow_count):
    blocks = item.reshape(wide_count, -1)
    extent = blocks.shape[1]
    padded_len = (extent + narrow_count - 1) // narrow_count * narrow_count
    blocks = jnp.pad(blocks, ((0, 0), (0, padded_len - extent)))
    return blocks.reshape(-1)


def unpack_rows(whole, item, wide_count):
    extent = item.size // wide_count
    return whole[:extent].reshape((item.shape[0] // wide_count,) + item.shape[1:])


def body(
    tokens,
    bucket,
    lengths,
    pairing,
    targets,
    w_qkv,
    bias_q,
    bias_v,
    w_out,
    bias_out,
    gain_attn,
    shift_attn,
    w_up,
    bias_up,
    w_down,
    bias_down,
    gain_ffn,
    shift_ffn,
):
    wide_count = lax.axis_size("wide")
    narrow_count = lax.axis_size("narrow")
    batches = bucket.shape[0]
    span = tokens.shape[0] // batches
    width = w_out.shape[0]
    rows_count = batches * span
    source_tags, batch_of, within = source_layout(bucket, lengths, wide_count // batches, span)
    send_rows = (
        jnp.zeros((wide_count, span, width), jnp.bfloat16)
        .at[bucket]
        .set(tokens.reshape(batches, span, width))
    )
    send_tags = jnp.zeros((wide_count, span), jnp.int32).at[bucket].set(source_tags)
    got_rows, got_tags = (
        lax.all_to_all(send_rows, "wide", split_axis=0, concat_axis=0, tiled=True),
        lax.all_to_all(send_tags, "wide", split_axis=0, concat_axis=0, tiled=True),
    )
    filled = (got_tags[:, 0] > 0).astype(jnp.int32)
    place = jnp.where(filled > 0, jnp.cumsum(filled) - filled, batches)
    chosen = (
        jnp.zeros((batches,), jnp.int32)
        .at[place]
        .set(jnp.arange(wide_count, dtype=jnp.int32), mode="drop")
    )
    arrived = got_rows[chosen].reshape(rows_count, width)
    row_tags = got_tags[chosen]
    allowed = allowed_pairs(row_tags)
    mixed = jnp.dot(arrived, w_qkv, preferred_element_type=jnp.float32)
    queries = (
        ((mixed[:, :width] + bias_q) * 0.125)
        .astype(jnp.bfloat16)
        .reshape(batches, span, HEADS, HDIM)
    )
    keys_all = mixed[:, width : 2 * width].astype(jnp.bfloat16).reshape(batches, span, HEADS, HDIM)
    values_all = (
        (mixed[:, 2 * width :] + bias_v).astype(jnp.bfloat16).reshape(batches, span, HEADS, HDIM)
    )

    def scores():
        product = jnp.einsum(
            "bqhd,bkhd->bhqk", queries, keys_all, preferred_element_type=jnp.float32
        )
        return jnp.where(allowed[:, None], product, MASKED)

    logits = scores()
    peak = jnp.max(logits, axis=-1, keepdims=True)
    raised = jnp.exp(logits - peak)
    row_total = jnp.sum(raised, axis=-1, keepdims=True)
    log_total = peak + jnp.log(row_total)
    probs_low = (raised / row_total).astype(jnp.bfloat16)
    attended = jnp.einsum(
        "bhqk,bkhd->bqhd", probs_low, values_all, preferred_element_type=jnp.float32
    )
    attended = attended.reshape(rows_count, width).astype(jnp.bfloat16)
    branch = jnp.dot(attended, w_out, preferred_element_type=jnp.float32) + bias_out
    hidden, normed_attn, spread_attn = norm_forward(
        arrived.astype(jnp.float32) + branch, gain_attn, shift_attn
    )
    hidden_low = hidden.astype(jnp.bfloat16)
    inner = jnp.dot(hidden_low, w_up, preferred_element_type=jnp.float32) + bias_up
    activated, gelu_back = jax.vjp(partial(jax.nn.gelu, approximate=False), inner)
    activated_low = activated.astype(jnp.bfloat16)
    second = jnp.dot(activated_low, w_down, preferred_element_type=jnp.float32) + bias_down
    normed_out, normed_ffn, spread_ffn = norm_forward(hidden + second, gain_ffn, shift_ffn)
    valid = (row_tags > 0).reshape(rows_count, 1).astype(jnp.float32)
    encoded = (normed_out * valid).astype(jnp.bfloat16)
    member = (
        row_tags[:, None, :] == jnp.arange(1, KTOP + 1, dtype=jnp.int32)[None, :, None]
    ).astype(jnp.float32)
    pooling = member / jnp.maximum(jnp.sum(member, axis=2, keepdims=True), 1.0)
    pooled = jnp.einsum(
        "bjl,bld->bjd", pooling, normed_out.reshape(batches, span, width), precision=EXACT
    )
    back_rows = jnp.zeros((wide_count, KTOP, width), jnp.float32).at[chosen].set(pooled)
    home_rows = lax.all_to_all(
        back_rows.astype(jnp.bfloat16), "wide", split_axis=0, concat_axis=0, tiled=True
    ).astype(back_rows.dtype)
    sent_index = bucket[batch_of] * KTOP + within
    home = home_rows.reshape(wide_count * KTOP, width)[sent_index]
    pair_ids = pairing[0]
    first_ids = pair_ids[0::2]
    partner_ids = pair_ids[1::2]
    first = home[first_ids]
    partner = home[partner_ids]
    cross = jnp.sum(first * partner, axis=-1)
    scale_first = lax.rsqrt(jnp.sum(first * first, axis=-1) + COS_EPS)
    scale_partner = lax.rsqrt(jnp.sum(partner * partner, axis=-1) + COS_EPS)
    cosine = cross * scale_first * scale_partner
    factor = 2.0 * LOSS_SCALE * (cosine - targets)
    both_scales = (factor * scale_first * scale_partner)[:, None]
    grad_first = (
        both_scales * partner - (factor * cosine * scale_first * scale_first)[:, None] * first
    )
    grad_partner = (
        both_scales * first - (factor * cosine * scale_partner * scale_partner)[:, None] * partner
    )
    grad_home = (
        jnp.zeros(home.shape, jnp.float32)
        .at[first_ids]
        .add(grad_first)
        .at[partner_ids]
        .add(grad_partner)
    )
    grad_back = jnp.zeros((wide_count * KTOP, width), jnp.float32).at[sent_index].set(grad_home)
    grad_slots = lax.all_to_all(
        grad_back.reshape(wide_count, KTOP, width).astype(jnp.bfloat16),
        "wide",
        split_axis=0,
        concat_axis=0,
        tiled=True,
    ).astype(jnp.float32)
    grad_pooled = grad_slots[chosen]
    grad_normed = jnp.einsum("bjl,bjd->bld", pooling, grad_pooled, precision=EXACT).reshape(
        rows_count, width
    )
    grad_resid_ffn, grad_gain_ffn, grad_shift_ffn = norm_backward(
        grad_normed, normed_ffn, spread_ffn, gain_ffn
    )
    grad_second_low = grad_resid_ffn.astype(jnp.bfloat16)
    grad_bias_down = jnp.sum(grad_second_low.astype(jnp.float32), axis=0)
    grad_w_down = contract_rows(activated_low, grad_second_low)
    grad_active = times_transpose(grad_second_low, w_down)
    grad_inner_low = gelu_back(grad_active)[0].astype(jnp.bfloat16)
    grad_bias_up = jnp.sum(grad_inner_low.astype(jnp.float32), axis=0)
    grad_w_up = contract_rows(hidden_low, grad_inner_low)
    grad_hidden = times_transpose(grad_inner_low, w_up) + grad_resid_ffn
    grad_resid_attn, grad_gain_attn, grad_shift_attn = norm_backward(
        grad_hidden, normed_attn, spread_attn, gain_attn
    )
    grad_branch_low = grad_resid_attn.astype(jnp.bfloat16)
    grad_bias_out = jnp.sum(grad_branch_low.astype(jnp.float32), axis=0)
    grad_w_out = contract_rows(attended, grad_branch_low)
    grad_attended = (
        times_transpose(grad_branch_low, w_out)
        .astype(jnp.bfloat16)
        .reshape(batches, span, HEADS, HDIM)
    )
    logits = scores()
    probs = jnp.exp(logits - log_total)
    probs_again = probs.astype(jnp.bfloat16)
    grad_probs = jnp.einsum(
        "bqhd,bkhd->bhqk", grad_attended, values_all, preferred_element_type=jnp.float32
    )
    balance = jnp.sum(probs * grad_probs, axis=-1, keepdims=True)
    grad_logits = (probs * (grad_probs - balance)).astype(jnp.bfloat16)
    grad_queries = jnp.einsum(
        "bhqk,bkhd->bqhd", grad_logits, keys_all, preferred_element_type=jnp.float32
    )
    grad_keys = jnp.einsum(
        "bhqk,bqhd->bkhd", grad_logits, queries, preferred_element_type=jnp.float32
    )
    grad_values = jnp.einsum(
        "bhqk,bqhd->bkhd", probs_again, grad_attended, preferred_element_type=jnp.float32
    )
    grad_queries_low = grad_queries.reshape(rows_count, width).astype(jnp.bfloat16)
    grad_values_low = grad_values.reshape(rows_count, width).astype(jnp.bfloat16)
    grad_mixed = jnp.concatenate(
        [
            grad_queries_low * jnp.bfloat16(0.125),
            grad_keys.reshape(rows_count, width).astype(jnp.bfloat16),
            grad_values_low,
        ],
        axis=1,
    )
    grad_bias_q = jnp.sum(grad_queries_low.astype(jnp.float32) * 0.125, axis=0)
    grad_bias_v = jnp.sum(grad_values_low.astype(jnp.float32), axis=0)
    grad_w_qkv = contract_rows(arrived, grad_mixed)
    grad_arrived = (times_transpose(grad_mixed, w_qkv) + grad_resid_attn).astype(jnp.bfloat16)
    grad_send = (
        jnp.zeros((wide_count, span, width), jnp.bfloat16)
        .at[chosen]
        .set(grad_arrived.reshape(batches, span, width))
    )
    returned = lax.all_to_all(grad_send, "wide", split_axis=0, concat_axis=0, tiled=True)
    grad_tokens = returned[bucket].reshape(rows_count, width)
    grads = (
        grad_w_qkv,
        grad_bias_q,
        grad_bias_v,
        grad_w_out,
        grad_bias_out,
        grad_gain_attn,
        grad_shift_attn,
        grad_w_up,
        grad_bias_up,
        grad_w_down,
        grad_bias_down,
        grad_gain_ffn,
        grad_shift_ffn,
    )
    packed = [pack_rows(item, wide_count, narrow_count) for item in grads]
    shares = (
        lax.psum_scatter(packed[0], ("wide", "narrow"), scatter_dimension=0, tiled=True),
        lax.psum_scatter(packed[1], ("wide", "narrow"), scatter_dimension=0, tiled=True),
        lax.psum_scatter(packed[2], ("wide", "narrow"), scatter_dimension=0, tiled=True),
        lax.psum_scatter(packed[3], ("wide", "narrow"), scatter_dimension=0, tiled=True),
        lax.psum_scatter(packed[4], ("wide", "narrow"), scatter_dimension=0, tiled=True),
        lax.psum_scatter(packed[5], ("wide", "narrow"), scatter_dimension=0, tiled=True),
        lax.psum_scatter(packed[6], ("wide", "narrow"), scatter_dimension=0, tiled=True),
        lax.psum_scatter(packed[7], ("wide", "narrow"), scatter_dimension=0, tiled=True),
        lax.psum_scatter(packed[8], ("wide", "narrow"), scatter_dimension=0, tiled=True),
        lax.psum_scatter(packed[9], ("wide", "narrow"), scatter_dimension=0, tiled=True),
        lax.psum_scatter(packed[10], ("wide", "narrow"), scatter_dimension=0, tiled=True),
        lax.psum_scatter(packed[11], ("wide", "narrow"), scatter_dimension=0, tiled=True),
        lax.psum_scatter(packed[12], ("wide", "narrow"), scatter_dimension=0, tiled=True),
    )
    wholes = (
        lax.all_gather(shares[0].astype(jnp.bfloat16), "narrow", axis=0, tiled=True).astype(
            jnp.float32
        ),
        lax.all_gather(shares[1].astype(jnp.bfloat16), "narrow", axis=0, tiled=True).astype(
            jnp.float32
        ),
        lax.all_gather(shares[2].astype(jnp.bfloat16), "narrow", axis=0, tiled=True).astype(
            jnp.float32
        ),
        lax.all_gather(shares[3].astype(jnp.bfloat16), "narrow", axis=0, tiled=True).astype(
            jnp.float32
        ),
        lax.all_gather(shares[4].astype(jnp.bfloat16), "narrow", axis=0, tiled=True).astype(
            jnp.float32
        ),
        lax.all_gather(shares[5].astype(jnp.bfloat16), "narrow", axis=0, tiled=True).astype(
            jnp.float32
        ),
        lax.all_gather(shares[6].astype(jnp.bfloat16), "narrow", axis=0, tiled=True).astype(
            jnp.float32
        ),
        lax.all_gather(shares[7].astype(jnp.bfloat16), "narrow", axis=0, tiled=True).astype(
            jnp.float32
        ),
        lax.all_gather(shares[8].astype(jnp.bfloat16), "narrow", axis=0, tiled=True).astype(
            jnp.float32
        ),
        lax.all_gather(shares[9].astype(jnp.bfloat16), "narrow", axis=0, tiled=True).astype(
            jnp.float32
        ),
        lax.all_gather(shares[10].astype(jnp.bfloat16), "narrow", axis=0, tiled=True).astype(
            jnp.float32
        ),
        lax.all_gather(shares[11].astype(jnp.bfloat16), "narrow", axis=0, tiled=True).astype(
            jnp.float32
        ),
        lax.all_gather(shares[12].astype(jnp.bfloat16), "narrow", axis=0, tiled=True).astype(
            jnp.float32
        ),
    )
    summed = [unpack_rows(whole, item, wide_count) for whole, item in zip(wholes, grads)]
    return (
        encoded,
        grad_tokens,
        summed[0],
        summed[1],
        summed[2],
        summed[3],
        summed[4],
        summed[5],
        summed[6],
        summed[7],
        summed[8],
        summed[9],
        summed[10],
        summed[11],
        summed[12],
    )


def solution(mesh):
    in_specs = (
        P(("wide", "narrow"), None),
        P(("wide", "narrow")),
        P(("wide", "narrow")),
        P(("wide", "narrow"), None),
        P(("wide", "narrow")),
        P(),
        P(),
        P(),
        P(),
        P(),
        P(),
        P(),
        P(),
        P(),
        P(),
        P(),
        P(),
        P(),
    )
    out_specs = (
        P(("wide", "narrow"), None),
        P(("wide", "narrow"), None),
        P("wide", None),
        P("wide"),
        P("wide"),
        P("wide", None),
        P("wide"),
        P("wide"),
        P("wide"),
        P("wide", None),
        P("wide"),
        P("wide", None),
        P("wide"),
        P("wide"),
        P("wide"),
    )
    return jax.shard_map(body, mesh=mesh, in_specs=in_specs, out_specs=out_specs, check_vma=False)
```

profile of v0, /device:TPU:0, one launch (start us, length us, event | category | flops | bytes accessed | tf_op | source)
XLA Modules:
  0.0 907.4 jit_solution(4558167786938790751)
XLA Ops:
  11.8 7.3 all-to-all-start.1
  20.3 5.6 scatter_fusion
  25.9 6.0 all-to-all-start
  57.3 11.2 %all-to-all-done = bf16[8,128,768]{2,1,0:T(8,128)(2,1)} async-done(((bf16[8,128,768]{2,1,0:T(8,128)(2,1)}), bf16[8,128,768]{2,1,0:T(8,128)(2,1)}, u32[]{:S(2)}, u32[]{:S(2)}) %all-to-all-start) | async-done | bytes 1572896 | tf_op jit(solution)/shard_map/all_to_all | solution.py:128
  68.5 3.3 gather_fusion
  71.8 5.2 fusion.89
  78.4 2.3 fusion.12
  80.7 2.7 copy.92
  83.4 3.0 copy.116
  86.4 2.6 copy.94
  89.0 3.1 copy.118
  92.0 2.6 copy.93
  94.6 2.0 copy.117
  104.1 1.7 fusion.87
  106.5 1.9 copy-done.28
  108.4 35.0 %multiply_convert_fusion = (bf16[1024,3072]{1,0:T(8,128)(2,1)S(1)}, f32[1024,3072]{1,0:T(8,128)}, f32[1024,3072]{1,0:T(8,128)}) fusion(f32[3072]{0:T(1024)S(1)} %copy-done.40, bf16[768,3072]{1,0:T(8,128)(2,1)S(1)} %bitcast.167, f32[1024,768]{1,0:T(8,128)S(1)} %get-tuple-element.68, f32[768]{0:T(1024)S(1)} %copy-done.32, f32[768]{0:T(1024)S(1)} %copy-done.28, ...), kind=kOutput, calls=%fused_computation.20 | convolution fusion | flops 5043388416 | bytes 39348224 | tf_op jit(solution)/shard_map/dot_general | solution.py:173
  143.5 5.4 fusion.88
  149.7 1.7 multiply_convert_fusion.2
  151.5 2.4 fusion.44
  154.6 2.7 scatter_fusion.1
  157.3 1.7 convert_element_type.269
  159.0 4.0 all-to-all-start.2
  166.2 4.7 all-to-all-done.2
  170.9 1.7 reshape.449
  172.5 2.3 gather_fusion.3
  174.9 2.2 gather_fusion.4
  177.1 2.2 gather_fusion.5
  183.1 2.5 scatter_custom_fusion.5
  185.6 2.1 scatter_custom_fusion.6
  191.0 4.0 all-to-all-start.3
  200.4 2.5 all-to-all-done.3
  202.8 2.3 gather_fusion.6
  205.1 3.6 fusion.85
  212.1 7.7 fusion.77
  219.8 19.3 %convert_reduce_fusion = (f32[3072]{0:T(1024)}, bf16[1024,3072]{1,0:T(8,128)(2,1)}) fusion(f32[1024,3072]{1,0:T(8,128)} %get-tuple-element.59, bf16[3072,768]{1,0:T(8,128)(2,1)} %param.33, f32[1024,768]{1,0:T(8,128)} %copy-done.18, f32[1024,3072]{1,0:T(8,128)} %get-tuple-element.69, f32[3072]{0:T(1024)S(1)} %copy-done.41), kind=kOutput, calls=%fused_computation.18 | convolution fusion | flops 4886098944 | bytes 39346176 | tf_op jit(solution)/shard_map/dot_general | solution.py:27
  239.1 11.7 %multiply_reduce_fusion.1 = (f32[768]{0:T(1024)}, f32[1024]{0:T(1024)S(1)}, f32[1024]{0:T(1024)S(1)}, f32[768]{0:T(1024)}, f32[1024,768]{1,0:T(8,128)S(1)}) fusion(f32[1024,768]{1,0:T(8,128)} %copy-done.5, f32[1024]{0:T(1024)S(1)} %add_rsqrt_fusion.1, f32[1024]{0:T(1024)S(1)} %broadcast_multiply_fusion.4, f32[768]{0:T(1024)S(1)} %copy-done.29, ...), kind=kOutput, calls=%fused_computation.54 | convolution fusion | flops 4839698432 | bytes 20472832 | tf_op jit(solution)/shard_map/dot_general | solution.py:27
  250.9 8.5 convolution_bitcast_fusion
  260.8 2.8 fusion.24
  263.6 2.6 convolution_convert_fusion.2
  266.2 2.6 copy.100
  268.8 1.9 copy.120
  270.7 5.9 convert_reduce_fusion.3
  276.6 6.2 multiply_reduce_fusion
  282.9 5.1 multiply_convert_fusion.1
  287.9 2.2 fusion.28
  297.4 5.1 add_convert_fusion.1
  302.5 6.2 fusion.90
  308.7 10.8 %reshape.444 = f32[2359296]{0:T(1024)} reshape(f32[3072,768]{1,0:T(8,128)} %fusion.77) | data formatting | bytes 18874368 | tf_op jit(solution)/shard_map/reshape | solution.py:86
  319.5 9.5 %copy.124 = f32[96,24,8,128]{3,1,2,0:T(8,128)} copy(f32[96,24,8,128]{3,2,1,0:T(8,128)} %convolution_bitcast_fusion) | data formatting | bytes 18874368
  329.0 3.2 reshape.438
  335.5 5.5 scatter_fusion.2
  341.0 4.3 all-to-all-start.4
  345.3 8.0 reshape.435
  353.3 468.3 %all-reduce.25 = (bf16[1769472]{0:T(1024)(128)(2,1)}, bf16[768]{0:T(1024)(128)(2,1)}, bf16[768]{0:T(1024)(128)(2,1)}, bf16[589824]{0:T(1024)(128)(2,1)}, bf16[76...) all-reduce(f32[1769472]{0:T(1024)} %reshape.435, ...), channel_id=2, replica_groups=mesh['wide'=8,'narrow'=4] {'wide','narrow'}, use_global_device_ids=true, to_apply=%region_32.33.clone | all-reduce | flops 7087104 | bytes 42522624
  840.0 7.7 all-reduce.23
  858.3 5.9 all_gather.42
  864.2 1.8 reshape.453
  870.0 7.3 all_gather.39
  877.3 2.4 reshape.451
  879.7 9.2 %all_gather.46 = bf16[294912]{0:T(1024)(128)(2,1)} all-gather(bf16[73728]{0:T(1024)(128)(2,1)} %dynamic-slice.36), channel_id=1, replica_groups=mesh['wide'=8,'narrow'=4] {'narrow'}, dimensions={0}, use_global_device_ids=true | all-gather | bytes 737280 | tf_op jit(solution)/shard_map/all_gather | solution.py:342
  888.9 2.3 reshape.455
  891.1 10.3 %all_gather.48 = bf16[294912]{0:T(1024)(128)(2,1)} all-gather(bf16[73728]{0:T(1024)(128)(2,1)} %dynamic-slice.35), channel_id=1, replica_groups=mesh['wide'=8,'narrow'=4] {'narrow'}, dimensions={0}, use_global_device_ids=true | all-gather | bytes 737280 | tf_op jit(solution)/shard_map/all_gather | solution.py:348
  901.4 2.5 reshape.457
  903.9 3.3 gather_fusion.7
  (263 shorter events, 111.1 us)
Async XLA Ops:
  0.6 71.2 %copy-start = (bf16[768,2304]{1,0:T(8,128)(2,1)S(1)}, bf16[768,2304]{1,0:T(8,128)(2,1)}, u32[]{:S(2)}) copy-start(bf16[768,2304]{1,0:T(8,128)(2,1)} %param.24) | copy-start | bytes 10616836
  2.8 3.3 copy-start.48
  11.8 14.2 %all-to-all-start.1 = ((s32[8,1,128]{2,1,0:T(1,128)}), s32[8,1,128]{2,1,0:T(1,128)S(1)}, u32[]{:S(2)}, u32[]{:S(2)}) async-start(s32[8,1,128]{2,1,0:T(1,128)} %bitcast.5), calls=%async_computation.1 | async-start | bytes 8192 | tf_op jit(solution)/shard_map/all_to_all | solution.py:129
  20.3 11.6 %copy-start.54 = (s32[1,26]{1,0:T(1,128)S(1)}, s32[1,26]{1,0:T(1,128)}, u32[]{:S(2)}) copy-start(s32[1,26]{1,0:T(1,128)} %param.22) | copy-start | bytes 316
  20.3 13.5 %copy-start.1 = (s32[8]{0:T(128)S(1)}, s32[8]{0:T(128)}, u32[]{:S(2)}) copy-start(s32[8]{0:T(128)} %param.20) | copy-start | bytes 100
  20.3 14.7 %copy-start.46 = (bf16[768]{0:T(1024)(128)(2,1)S(1)}, bf16[768]{0:T(1024)(128)(2,1)}, u32[]{:S(2)}) copy-start(bf16[768]{0:T(1024)(128)(2,1)} %param.29) | copy-start | bytes 4612
  25.9 42.5 %all-to-all-start = ((bf16[8,128,768]{2,1,0:T(8,128)(2,1)}), bf16[8,128,768]{2,1,0:T(8,128)(2,1)}, u32[]{:S(2)}, u32[]{:S(2)}) async-start(bf16[8,128,768]{2,1,0:T(8,128)(2,1)} %scatter_fusion), calls=%async_computation | async-start | bytes 3145728 | tf_op jit(solution)/shard_map/all_to_all | solution.py:128
  94.6 2.0 copy-start.7
  94.6 2.0 copy-start.14
  96.6 1.4 copy-start.9
  98.1 2.7 copy-start.2
  98.1 2.7 copy-start.23
  98.1 2.7 copy-start.12
  99.7 2.6 copy-start.25
  102.3 1.4 copy-start.21
  102.3 1.4 copy-start.45
  102.3 1.7 copy-start.52
  103.6 2.2 copy-start.19
  103.6 2.9 slice-start.4
  104.1 2.4 slice-start.5
  104.1 39.4 %slice-start.2 = ((s8[4718592]{0:T(1024)(128)(4,1)}), s8[4194304]{0:T(1024)(128)(4,1)S(1)}, s32[]{:S(2)}) async-start(s8[4718592]{0:T(1024)(128)(4,1)} %bitcast.164), calls=%async_computation.7 | async-start | bytes 8388608
  105.8 37.6 %copy-start.5 = (f32[1024,768]{1,0:T(8,128)}, f32[1024,768]{1,0:T(8,128)S(1)}, u32[]{:S(2)}) copy-start(f32[1024,768]{1,0:T(8,128)S(1)} %get-tuple-element.68) | copy-start | bytes 9437188
  105.8 2.6 copy-start.28
  105.8 2.6 copy-start.32
  105.8 2.6 copy-start.40
  108.4 35.0 %copy-start.44 = (f32[768]{0:T(1024)S(1)}, f32[768]{0:T(1024)}, u32[]{:S(2)}) copy-start(f32[768]{0:T(1024)} %convert_element_type.262) | copy-start | bytes 9220
  108.4 35.0 %slice-start.3 = ((s8[4718592]{0:T(1024)(128)(4,1)}), s8[524288]{0:T(1024)(128)(4,1)S(1)}, s32[]{:S(2)}) async-start(s8[4718592]{0:T(1024)(128)(4,1)} %bitcast.164), calls=%async_computation.8 | async-start | bytes 1048576
  143.4 5.5 copy-start.56
  148.9 2.5 copy-start.3
  148.9 2.5 copy-start.26
  149.5 1.9 copy-start.30
  149.7 1.8 copy-start.34
  149.7 1.8 copy-start.43
  159.0 11.9 %all-to-all-start.2 = ((bf16[8,12,768]{2,1,0:T(8,128)(2,1)}), bf16[8,12,768]{2,1,0:T(8,128)(2,1)}, u32[]{:S(2)}, u32[]{:S(2)}) async-start(bf16[8,12,768]{2,1,0:T(8,128)(2,1)} %convert_element_type.269), calls=%async_computation.2 | async-start | bytes 393216 | tf_op jit(solution)/shard_map/all_to_all | solution.py:188
  191.0 11.8 %all-to-all-start.3 = ((bf16[8,12,768]{2,1,0:T(8,128)(2,1)}), bf16[8,12,768]{2,1,0:T(8,128)(2,1)}, u32[]{:S(2)}, u32[]{:S(2)}) async-start(bf16[8,12,768]{2,1,0:T(8,128)(2,1)} %convert_element_type.271), calls=%async_computation.3 | async-start | bytes 393216 | tf_op jit(solution)/shard_map/all_to_all | solution.py:218
  205.1 3.6 copy-start.4
  205.1 3.6 copy-start.27
  205.1 3.6 copy-start.31
  208.8 2.9 slice-start.6
  210.3 1.7 slice-start.7
  211.7 8.1 copy-start.18
  212.1 7.7 copy-start.41
  219.8 19.3 %copy-start.29 = (f32[768]{0:T(1024)S(1)}, f32[768]{0:T(1024)}, u32[]{:S(2)}) copy-start(f32[768]{0:T(1024)} %convert_element_type.257) | copy-start | bytes 9220
  239.1 11.8 %copy-start.6 = (f32[1024,768]{1,0:T(8,128)S(1)}, f32[1024,768]{1,0:T(8,128)}, u32[]{:S(2)}) copy-start(f32[1024,768]{1,0:T(8,128)} %copy-done.5) | copy-start | bytes 9437188
  239.1 11.8 %copy-start.11 = (bf16[1024,3072]{1,0:T(8,128)(2,1)S(1)}, bf16[1024,3072]{1,0:T(8,128)(2,1)}, u32[]{:S(2)}) copy-start(bf16[1024,3072]{1,0:T(8,128)(2,1)} %get-tuple-element.81) | copy-start | bytes 18874372
  239.1 11.8 %copy-start.33 = (f32[768]{0:T(1024)S(1)}, f32[768]{0:T(1024)}, u32[]{:S(2)}) copy-start(f32[768]{0:T(1024)} %convert_element_type.258) | copy-start | bytes 9220
  259.4 1.4 copy-start.20
  260.5 3.1 copy-start.16
  260.8 2.8 copy-start.53
  268.7 1.9 copy-start.15
  268.7 1.9 copy-start.24
  270.7 5.9 copy-start.13
  270.7 12.2 %slice-start = ((s8[6291456]{0:T(1024)(128)(4,1)}), s8[4194304]{0:T(1024)(128)(4,1)S(1)}, s32[]{:S(2)}) async-start(s8[6291456]{0:T(1024)(128)(4,1)} %bitcast.131), calls=%async_computation.5 | async-start | bytes 8388608
  276.6 6.3 slice-start.1
  282.9 5.1 copy-start.10
  287.9 2.3 copy-start.8
  295.5 1.9 copy-start.17
  297.4 5.1 copy-start.22
  341.0 562.9 %all-to-all-start.4 = ((bf16[8,128,768]{2,1,0:T(8,128)(2,1)}), bf16[8,128,768]{2,1,0:T(8,128)(2,1)}, u32[]{:S(2)}, u32[]{:S(2)}) async-start(bf16[8,128,768]{2,1,0:T(8,128)(2,1)} %scatter_fusion.2), calls=%async_computation.4 | async-start | bytes 3145728 | tf_op jit(solution)/shard_map/all_to_all | solution.py:287
  345.3 8.0 copy-start.37
  345.3 8.0 copy-start.38
  831.8 7.3 copy-start.49
  832.0 7.1 copy-start.50
  832.9 4.1 copy-start.51
  (6 other events, 5.1 us)
where the time goes:
time: 915 us; the launch traced here: 907 us
  blocking collectives  509 us (56%)
  local copies, waits for them, and re-layouts  145 us (16%)
  matrix products  136 us (15%)
  other arithmetic  71.2 us (8%)
  starting transfers between devices  25.6 us (3%)
  waiting for transfers between devices  18.3 us (2%)
    unnamed x2, blocking collectives  476 us
    unnamed x169, local copies, waits for them, and re-layouts  51.3 us
    dot_general x4, matrix products, times_transpose(): lax.dot_general(left, right, (((1,), (1,)), ((), ())), preferred_element_...  38.7 us
    dot_general x1, matrix products, body(): jnp.dot(hidden_low, w_up, preferred_element_type=jnp.float32) + bias_up  35 us
    dot_general x4, matrix products, contract_rows(): lax.dot_general(left, right, (((0,), (0,)), ((), ())), preferred_element_...  25.1 us
    reshape x3, local copies, waits for them, and re-layouts, pack_rows(): return blocks.reshape(-1)  22 us
  transfers between devices with their start and end apart: 5, of which 3 were waited for; matrix products, arithmetic and copies ran while one was open for 10% of the time, Pallas kernels for 0%

commit v1 on v0

--- a/solution.py
+++ b/solution.py
@@ -89,6 +89,98 @@
 def unpack_rows(whole, item, wide_count):
     extent = item.size // wide_count
     return whole[:extent].reshape((item.shape[0] // wide_count,) + item.shape[1:])
+
+
+def regroup_rows(rows, bucket, wide_count):
+    batches, span, width = rows.shape
+    send = jnp.zeros((wide_count, span, width), rows.dtype).at[bucket].set(rows)
+    got = lax.all_to_all(send, "wide", split_axis=0, concat_axis=0, tiled=True)
+    if wide_count == batches:
+        return got.reshape(batches * span, width)
+    marks = jnp.zeros((wide_count, 1), jnp.int32).at[bucket].set(1)
+    filled = lax.all_to_all(marks, "wide", split_axis=0, concat_axis=0, tiled=True)[:, 0]
+    place = jnp.where(filled > 0, jnp.cumsum(filled) - filled, batches)
+    chosen = (
+        jnp.zeros((batches,), jnp.int32)
+        .at[place]
+        .set(jnp.arange(wide_count, dtype=jnp.int32), mode="drop")
+    )
+    return got[chosen].reshape(batches * span, width)
+
+
+def swap(item, axis, step):
+    count = lax.axis_size(axis)
+    return lax.ppermute(item, axis, [(index, index ^ step) for index in range(count)])
+
+
+def bit(axis, step):
+    return (lax.axis_index(axis) // step) % 2
+
+
+def halves(item, dim, mine):
+    keep = lax.dynamic_index_in_dim(item, mine, dim, keepdims=False)
+    give = lax.dynamic_index_in_dim(item, 1 - mine, dim, keepdims=False)
+    return keep, give
+
+
+def fold(item, dim, axis, step):
+    keep, give = halves(item, dim, bit(axis, step))
+    got = swap(give.astype(jnp.bfloat16), axis, step)
+    return (keep.astype(jnp.float32) + got.astype(jnp.float32)).astype(jnp.bfloat16)
+
+
+def spread(item, axis, step):
+    got = swap(item, axis, step)
+    mine = bit(axis, step)
+    return jnp.stack([jnp.where(mine == 0, item, got), jnp.where(mine == 0, got, item)])
+
+
+def sum_matrix(grad):
+    rows, cols = grad.shape
+    part = rows // 32
+    cut = grad.reshape(2, 2, 2, 2, 2, part, cols)
+    cut = fold(cut, 3, "narrow", 1)
+    first, second = cut[..., : cols // 2], cut[..., cols // 2 :]
+    first = fold(first, 3, "narrow", 2)
+    first = fold(first, 2, "wide", 1)
+    second = fold(second, 2, "wide", 1)
+    second = fold(second, 2, "narrow", 2)
+    both = jnp.concatenate([first, second], axis=-1)
+    both = fold(both, 1, "wide", 2)
+    both = fold(both, 0, "wide", 4)
+    both = spread(both, "narrow", 2)
+    both = spread(both, "narrow", 1)
+    return both.reshape(rows // 8, cols).astype(jnp.float32)
+
+
+def sum_vectors(items, wide_count):
+    flat = jnp.concatenate([item.reshape(wide_count, -1) for item in items], axis=1)
+    for axis, step in (("narrow", 1), ("narrow", 2), ("wide", 1), ("wide", 2), ("wide", 4)):
+        flat = flat + swap(flat, axis, step)
+    mine = lax.dynamic_index_in_dim(flat, lax.axis_index("wide"), 0, keepdims=False)
+    sizes = [item.size // wide_count for item in items]
+    out, start = [], 0
+    for size in sizes:
+        out.append(mine[start : start + size])
+        start += size
+    return out
+
+
+def sum_terms(grads, wide_count, narrow_count):
+    if (wide_count, narrow_count) == (8, 4):
+        vectors = iter(sum_vectors([item for item in grads if item.ndim == 1], wide_count))
+        return [sum_matrix(item) if item.ndim == 2 else next(vectors) for item in grads]
+    out = []
+    for item in grads:
+        share = lax.psum_scatter(
+            pack_rows(item, wide_count, narrow_count),
+            ("wide", "narrow"),
+            scatter_dimension=0,
+            tiled=True,
+        )
+        whole = lax.all_gather(share.astype(jnp.bfloat16), "narrow", axis=0, tiled=True)
+        out.append(unpack_rows(whole.astype(jnp.float32), item, wide_count))
+    return out
 
 
 def body(
@@ -118,25 +210,8 @@
     width = w_out.shape[0]
     rows_count = batches * span
     source_tags, batch_of, within = source_layout(bucket, lengths, wide_count // batches, span)
-    send_rows = (
-        jnp.zeros((wide_count, span, width), jnp.bfloat16)
-        .at[bucket]
-        .set(tokens.reshape(batches, span, width))
-    )
-    send_tags = jnp.zeros((wide_count, span), jnp.int32).at[bucket].set(source_tags)
-    got_rows, got_tags = (
-        lax.all_to_all(send_rows, "wide", split_axis=0, concat_axis=0, tiled=True),
-        lax.all_to_all(send_tags, "wide", split_axis=0, concat_axis=0, tiled=True),
-    )
-    filled = (got_tags[:, 0] > 0).astype(jnp.int32)
-    place = jnp.where(filled > 0, jnp.cumsum(filled) - filled, batches)
-    chosen = (
-        jnp.zeros((batches,), jnp.int32)
-        .at[place]
-        .set(jnp.arange(wide_count, dtype=jnp.int32), mode="drop")
-    )
-    arrived = got_rows[chosen].reshape(rows_count, width)
-    row_tags = got_tags[chosen]
+    arrived = tokens
+    row_tags = source_tags
     allowed = allowed_pairs(row_tags)
     mixed = jnp.dot(arrived, w_qkv, preferred_element_type=jnp.float32)
     queries = (
@@ -184,12 +259,9 @@
     pooled = jnp.einsum(
         "bjl,bld->bjd", pooling, normed_out.reshape(batches, span, width), precision=EXACT
     )
-    back_rows = jnp.zeros((wide_count, KTOP, width), jnp.float32).at[chosen].set(pooled)
-    home_rows = lax.all_to_all(
-        back_rows.astype(jnp.bfloat16), "wide", split_axis=0, concat_axis=0, tiled=True
-    ).astype(back_rows.dtype)
-    sent_index = bucket[batch_of] * KTOP + within
-    home = home_rows.reshape(wide_count * KTOP, width)[sent_index]
+    encoded = regroup_rows(encoded.reshape(batches, span, width), bucket, wide_count)
+    sent_index = batch_of * KTOP + within
+    home = pooled.reshape(batches * KTOP, width)[sent_index]
     pair_ids = pairing[0]
     first_ids = pair_ids[0::2]
     partner_ids = pair_ids[1::2]
@@ -214,15 +286,12 @@
         .at[partner_ids]
         .add(grad_partner)
     )
-    grad_back = jnp.zeros((wide_count * KTOP, width), jnp.float32).at[sent_index].set(grad_home)
-    grad_slots = lax.all_to_all(
-        grad_back.reshape(wide_count, KTOP, width).astype(jnp.bfloat16),
-        "wide",
-        split_axis=0,
-        concat_axis=0,
-        tiled=True,
-    ).astype(jnp.float32)
-    grad_pooled = grad_slots[chosen]
+    grad_pooled = (
+        jnp.zeros((batches * KTOP, width), jnp.float32)
+        .at[sent_index]
+        .set(grad_home)
+        .reshape(batches, KTOP, width)
+    )
     grad_normed = jnp.einsum("bjl,bjd->bld", pooling, grad_pooled, precision=EXACT).reshape(
         rows_count, width
     )
@@ -279,13 +348,7 @@
     grad_bias_v = jnp.sum(grad_values_low.astype(jnp.float32), axis=0)
     grad_w_qkv = contract_rows(arrived, grad_mixed)
     grad_arrived = (times_transpose(grad_mixed, w_qkv) + grad_resid_attn).astype(jnp.bfloat16)
-    grad_send = (
-        jnp.zeros((wide_count, span, width), jnp.bfloat16)
-        .at[chosen]
-        .set(grad_arrived.reshape(batches, span, width))
-    )
-    returned = lax.all_to_all(grad_send, "wide", split_axis=0, concat_axis=0, tiled=True)
-    grad_tokens = returned[bucket].reshape(rows_count, width)
+    grad_tokens = grad_arrived
     grads = (
         grad_w_qkv,
         grad_bias_q,
@@ -301,64 +364,7 @@
         grad_gain_ffn,
         grad_shift_ffn,
     )
-    packed = [pack_rows(item, wide_count, narrow_count) for item in grads]
-    shares = (
-        lax.psum_scatter(packed[0], ("wide", "narrow"), scatter_dimension=0, tiled=True),
-        lax.psum_scatter(packed[1], ("wide", "narrow"), scatter_dimension=0, tiled=True),
-        lax.psum_scatter(packed[2], ("wide", "narrow"), scatter_dimension=0, tiled=True),
-        lax.psum_scatter(packed[3], ("wide", "narrow"), scatter_dimension=0, tiled=True),
-        lax.psum_scatter(packed[4], ("wide", "narrow"), scatter_dimension=0, tiled=True),
-        lax.psum_scatter(packed[5], ("wide", "narrow"), scatter_dimension=0, tiled=True),
-        lax.psum_scatter(packed[6], ("wide", "narrow"), scatter_dimension=0, tiled=True),
-        lax.psum_scatter(packed[7], ("wide", "narrow"), scatter_dimension=0, tiled=True),
-        lax.psum_scatter(packed[8], ("wide", "narrow"), scatter_dimension=0, tiled=True),
-        lax.psum_scatter(packed[9], ("wide", "narrow"), scatter_dimension=0, tiled=True),
-        lax.psum_scatter(packed[10], ("wide", "narrow"), scatter_dimension=0, tiled=True),
-        lax.psum_scatter(packed[11], ("wide", "narrow"), scatter_dimension=0, tiled=True),
-        lax.psum_scatter(packed[12], ("wide", "narrow"), scatter_dimension=0, tiled=True),
-    )
-    wholes = (
-        lax.all_gather(shares[0].astype(jnp.bfloat16), "narrow", axis=0, tiled=True).astype(
-            jnp.float32
-        ),
-        lax.all_gather(shares[1].astype(jnp.bfloat16), "narrow", axis=0, tiled=True).astype(
-            jnp.float32
-        ),
-        lax.all_gather(shares[2].astype(jnp.bfloat16), "narrow", axis=0, tiled=True).astype(
-            jnp.float32
-        ),
-        lax.all_gather(shares[3].astype(jnp.bfloat16), "narrow", axis=0, tiled=True).astype(
-            jnp.float32
-        ),
-        lax.all_gather(shares[4].astype(jnp.bfloat16), "narrow", axis=0, tiled=True).astype(
-            jnp.float32
-        ),
-        lax.all_gather(shares[5].astype(jnp.bfloat16), "narrow", axis=0, tiled=True).astype(
-            jnp.float32
-        ),
-        lax.all_gather(shares[6].astype(jnp.bfloat16), "narrow", axis=0, tiled=True).astype(
-            jnp.float32
-        ),
-        lax.all_gather(shares[7].astype(jnp.bfloat16), "narrow", axis=0, tiled=True).astype(
-            jnp.float32
-        ),
-        lax.all_gather(shares[8].astype(jnp.bfloat16), "narrow", axis=0, tiled=True).astype(
-            jnp.float32
-        ),
-        lax.all_gather(shares[9].astype(jnp.bfloat16), "narrow", axis=0, tiled=True).astype(
-            jnp.float32
-        ),
-        lax.all_gather(shares[10].astype(jnp.bfloat16), "narrow", axis=0, tiled=True).astype(
-            jnp.float32
-        ),
-        lax.all_gather(shares[11].astype(jnp.bfloat16), "narrow", axis=0, tiled=True).astype(
-            jnp.float32
-        ),
-        lax.all_gather(shares[12].astype(jnp.bfloat16), "narrow", axis=0, tiled=True).astype(
-            jnp.float32
-        ),
-    )
-    summed = [unpack_rows(whole, item, wide_count) for whole, item in zip(wholes, grads)]
+    summed = sum_terms(grads, wide_count, narrow_count)
     return (
         encoded,
         grad_tokens,

time: 915 us -> 449 us (0.49)
  blocking collectives: 509 us -> 0 us
  waiting for transfers between devices: 18.3 us -> 67.5 us
  local copies, waits for them, and re-layouts: 145 us -> 100 us
  starting transfers between devices: 25.6 us -> 44.7 us
  other arithmetic: 71.2 us -> 86.1 us
    unnamed x2 -> x0, blocking collectives: 476 us -> none
    ppermute x0 -> x41, waiting for transfers between devices: none -> 67.5 us  [swap(): lax.ppermute(item, axis, [(index, index ^ step) for index in range(count)])]
    ppermute x0 -> x41, starting transfers between devices: none -> 37.2 us  [swap(): lax.ppermute(item, axis, [(index, index ^ step) for index in range(count)])]
    all_gather x4 -> x0, blocking collectives: 32.6 us -> none  [the longest x1 10.3 us: body(): lax.all_gather(shares[9].astype(jnp.bfloat16), 'narrow', axis=0, tiled=True)]
    reshape x8 -> x11, local copies, waits for them, and re-layouts: 32.6 us -> 12.3 us  [the longest x9 8.84 us: sum_vectors(): item.reshape(wide_count, -1)]
    all_to_all x5 -> x1, waiting for transfers between devices: 18.3 us -> 0.01 us  [regroup_rows(): got = lax.all_to_all(send, 'wide', split_axis=0, concat_axis=0, tiled=True)]
    all_to_all x5 -> x1, starting transfers between devices: 25.6 us -> 7.53 us  [regroup_rows(): got = lax.all_to_all(send, 'wide', split_axis=0, concat_axis=0, tiled=True)]
    unnamed x169 -> x170, local copies, waits for them, and re-layouts: 51.3 us -> 33.7 us
  transfers between devices with their start and end apart: 5 -> 42, of which waited for: 3 -> 23; matrix products, arithmetic and copies ran while one was open for 10% -> 46% of each run, Pallas kernels for 0% -> 0%
where the time goes in v1:
time: 449 us; the launch traced here: 443 us
  matrix products  142 us (32%)
  local copies, waits for them, and re-layouts  100 us (22%)
  other arithmetic  86.1 us (19%)
  waiting for transfers between devices  67.5 us (15%)
  starting transfers between devices  44.7 us (10%)
    ppermute x41, waiting for transfers between devices, swap(): lax.ppermute(item, axis, [(index, index ^ step) for index in range(count)])  67.5 us
    dot_general x4, matrix products, times_transpose(): lax.dot_general(left, right, (((1,), (1,)), ((), ())), preferred_element_...  42.4 us
    ppermute x41, starting transfers between devices, swap(): lax.ppermute(item, axis, [(index, index ^ step) for index in range(count)])  37.2 us
    dot_general x1, matrix products, body(): jnp.dot(hidden_low, w_up, preferred_element_type=jnp.float32) + bias_up  35.4 us
    unnamed x170, local copies, waits for them, and re-layouts  33.7 us
    convert_element_type x28, other arithmetic, fold(): (keep.astype(jnp.float32) + got.astype(jnp.float32)).astype(jnp.bfloat16)  19.6 us
    dot_general x4, matrix products, contract_rows(): lax.dot_general(left, right, (((0,), (0,)), ((), ())), preferred_element_...  19.2 us
  transfers between devices with their start and end apart: 42, of which 23 were waited for; matrix products, arithmetic and copies ran while one was open for 46% of the time, Pallas kernels for 0%

profile of v1, /device:TPU:0, one launch (start us, length us, event | category | flops | bytes accessed | tf_op | source)
XLA Modules:
  0.0 443.0 jit_solution(5400054105830779181)
XLA Ops:
  22.3 5.2 %fusion.132 = f32[1024,2304]{1,0:T(8,128)S(1)} fusion(bf16[1024,768]{1,0:T(8,128)(2,1)} %param.19, bf16[768,2304]{1,0:T(8,128)(2,1)S(1)} %copy-done), kind=kOutput, calls=%fused_computation.356 | convolution fusion | flops 3623878656 | bytes 14548992 | tf_op jit(solution)/shard_map/dot_general | solution.py:216
  28.8 2.3 fusion.15
  31.1 2.9 copy.76
  34.0 3.0 copy.118
  37.0 2.6 copy.79
  39.6 3.0 copy.120
  42.6 2.6 copy.78
  45.2 2.0 copy.119
  57.3 1.9 copy-done.40
  59.2 35.4 %multiply_convert_fusion = (bf16[1024,3072]{1,0:T(8,128)(2,1)S(1)}, f32[1024,3072]{1,0:T(8,128)}, f32[1024,3072]{1,0:T(8,128)}) fusion(f32[3072]{0:T(1024)S(1)} %copy-done.53, bf16[768,3072]{1,0:T(8,128)(2,1)S(1)} %bitcast.385, f32[1024,768]{1,0:T(8,128)S(1)} %get-tuple-element.87, f32[768]{0:T(1024)S(1)} %copy-done.44, f32[768]{0:T(1024)S(1)} %copy-done.40, ...), kind=kOutput, calls=%fused_computation.11 | convolution fusion | flops 5043388416 | bytes 39348224 | tf_op jit(solution)/shard_map/dot_general | solution.py:248
  94.7 5.4 %fusion.131 = (f32[1024]{0:T(1024)S(1)}, f32[1024,768]{1,0:T(8,128)S(1)}) fusion(f32[768]{0:T(1024)S(1)} %copy-done.56, bf16[1024,3072]{1,0:T(8,128)(2,1)S(1)} %get-tuple-element.37, bf16[3072,768]{1,0:T(8,128)(2,1)S(1)} %bitcast.383, f32[768]{0:T(1024)S(1)} %copy-done.44, f32[768]{0:T(1024)S(1)} %copy-done.40, f32[1024]{0:T(1024)S(1)} %add_rsqrt_fusion.1, ...), kind=kOutput, calls=%fused_computation.355 | convolution fusion | flops 4837342208 | bytes 17323008 | tf_op jit(solution)/shard_map/dot_general | solution.py:251
  100.9 2.6 multiply_convert_fusion.2
  104.7 5.5 %scatter_fusion = bf16[8,128,768]{2,1,0:T(8,128)(2,1)} fusion(bf16[8,128,768]{2,1,0:T(8,128)(2,1)} %broadcast_in_dim.28, s32[8]{0:T(128)} %compare_select_fusion.3, bf16[8,128,768]{2,1,0:T(8,128)(2,1)} %bitcast.358), kind=kCustom, calls=%fused_computation.3 | custom fusion | bytes 4718624 | tf_op jit(solution)/shard_map/scatter | solution.py:96
  110.2 7.5 %all-to-all-start = ((bf16[8,128,768]{2,1,0:T(8,128)(2,1)}), bf16[8,128,768]{2,1,0:T(8,128)(2,1)}, u32[]{:S(2)}, u32[]{:S(2)}) async-start(bf16[8,128,768]{2,1,0:T(8,128)(2,1)} %scatter_fusion), calls=%async_computation | async-start | bytes 3145728 | tf_op jit(solution)/shard_map/all_to_all | solution.py:97
  120.8 3.0 copy.177
  128.9 4.3 fusion.89
  133.2 1.7 reshape.513
  134.9 2.3 gather_fusion
  137.3 2.2 gather_fusion.1
  139.5 2.2 gather_fusion.2
  145.5 2.5 scatter_custom_fusion.2
  151.5 4.9 %fusion.124 = (f32[768]{0:T(1024)}, f32[8,128]{1,0:T(8,128)S(1)}, f32[8,128,768]{2,1,0:T(8,128)S(1)}) fusion(f32[768]{0:T(1024)S(1)} %convert_element_type.536, f32[8,12,768]{2,1,0:T(8,128)} %reshape.514, f32[8,12]{1,0:T(8,128)} %copy-done.47, s32[8,128]{1,0:T(8,128)S(1)} %get-tuple-element.36, s32[12]{0:T(128)} %iota_add_fusion), kind=kOutput, calls=%fused_computation.349 | convolution fusion | flops 115640576 | bytes 3455408 | tf_op jit(solution)/shard_map/bjl,bjd->bld/dot_general | solution.py:295
  157.9 3.3 convert_reduce_fusion.1
  161.2 19.6 %convert_reduce_fusion = (f32[3072]{0:T(1024)}, bf16[1024,3072]{1,0:T(8,128)(2,1)}) fusion(f32[1024,3072]{1,0:T(8,128)} %get-tuple-element.38, bf16[3072,768]{1,0:T(8,128)(2,1)} %param.33, f32[1024,768]{1,0:T(8,128)} %get-tuple-element.29, f32[1024,3072]{1,0:T(8,128)} %get-tuple-element.88, f32[3072]{0:T(1024)S(1)} %copy-done.54), kind=kOutput, calls=%fused_computation.9 | convolution fusion | flops 4886098944 | bytes 39346176 | tf_op jit(solution)/shard_map/dot_general | solution.py:27
  180.8 12.4 %multiply_reduce_fusion.1 = (f32[768]{0:T(1024)}, f32[1024]{0:T(1024)S(1)}, f32[1024]{0:T(1024)S(1)}, f32[768]{0:T(1024)}, f32[1024,768]{1,0:T(8,128)}) fusion(f32[1024,768]{1,0:T(8,128)} %copy-done.4, f32[1024]{0:T(1024)S(1)} %add_rsqrt_fusion.1, f32[1024]{0:T(1024)S(1)} %broadcast_multiply_fusion.4, f32[768]{0:T(1024)S(1)} %copy-done.41, ...), kind=kOutput, calls=%fused_computation.53 | convolution fusion | flops 4839698432 | bytes 20472832 | tf_op jit(solution)/shard_map/dot_general | solution.py:27
  193.8 4.7 %convert_reduce_fusion.2 = (f32[768]{0:T(1024)}, f32[1024,768]{1,0:T(8,128)S(1)}) fusion(f32[1024]{0:T(1024)S(1)} %broadcast_multiply_fusion, f32[1024,768]{1,0:T(8,128)} %copy-done.4, f32[1024]{0:T(1024)S(1)} %broadcast_multiply_fusion.4, f32[1024]{0:T(1024)} %broadcast_multiply_fusion.1, f32[1024,768]{1,0:T(8,128)} %get-tuple-element.92, ...), kind=kLoop, calls=%fused_computation.54 | loop fusion | flops 7863552 | bytes 9459712 | tf_op jit(solution)/shard_map/reduce_sum | solution.py:313
  203.3 5.5 %fusion.115 = f32[3072,768]{1,0:T(8,128)S(1)} fusion(bf16[1024,3072]{1,0:T(8,128)(2,1)S(1)} %bitcast.389, f32[1024,768]{1,0:T(8,128)S(1)} %copy-done.22), kind=kOutput, calls=%fused_computation.342 | convolution fusion | flops 4832624640 | bytes 18874368 | tf_op jit(solution)/shard_map/dot_general | solution.py:21
  210.5 3.2 copy-done.15
  213.8 5.8 %fusion.120 = f32[768,3072]{1,0:T(8,128)S(1)} fusion(bf16[1024,3072]{1,0:T(8,128)(2,1)S(1)} %bitcast.357, f32[1024,768]{1,0:T(8,128)S(1)} %copy-done.5, f32[768]{0:T(1024)S(1)} %copy-done.45, f32[768]{0:T(1024)S(1)} %copy-done.41, f32[1024]{0:T(1024)S(1)} %add_rsqrt_fusion.1, f32[1024]{0:T(1024)S(1)} %broadcast_multiply_fusion.4), kind=kOutput, calls=%fused_computation.347 | convolution fusion | flops 4835770368 | bytes 18888704 | tf_op jit(solution)/shard_map/dot_general | solution.py:21
  219.6 3.6 copy-done.6
  226.1 2.6 convolution_convert_fusion.2
  228.7 2.6 copy.85
  231.3 1.9 copy.122
  233.2 6.9 %convert_reduce_fusion.3 = (f32[12,64]{1,0:T(8,128)}, bf16[8,12,64,128]{3,2,1,0:T(8,128)(2,1)}) fusion(f32[8,12,128,128]{2,3,1,0:T(8,128)} %copy-done.1, f32[8,12,128]{2,1,0:T(8,128)S(1)} %copy-done.33, pred[8,128,128]{1,2,0:T(8,128)(4,1)S(1)} %copy-done.20, bf16[8,128,12,64]{1,0,3,2:T(8,128)(2,1)S(1)} %bitcast.370), kind=kOutput, calls=%fused_computation.55 | convolution fusion | flops 208403712 | bytes 9620480 | tf_op jit(solution)/shard_map/bhqk,bqhd->bkhd/dot_general | solution.py:334
  240.2 6.3 %multiply_reduce_fusion = (f32[8,12,128]{2,1,0:T(8,128)}, f32[8,12,128,128]{2,3,1,0:T(8,128)}) fusion(f32[8,12,128,128]{2,3,1,0:T(8,128)} %copy-done.1, f32[8,12,128]{2,1,0:T(8,128)S(1)} %copy-done.33, pred[8,128,128]{1,2,0:T(8,128)(4,1)S(1)} %copy-done.20, bf16[8,128,12,64]{1,0,3,2:T(8,128)(2,1)S(1)} %bitcast.369, bf16[8,128,12,64]{1,0,3,2:T(8,128)(2,1)S(1)} %bitcast.371), kind=kOutput, calls=%fused_computation.26 | convolution fusion | flops 207605760 | bytes 15958016 | tf_op jit(solution)/shard_map/bqhd,bkhd->bhqk/dot_general | solution.py:323
  254.0 6.8 %multiply_convert_fusion.1 = bf16[8,12,128,128]{2,3,1,0:T(8,128)(2,1)S(1)} fusion(f32[8,12,128,128]{2,3,1,0:T(8,128)} %get-tuple-element.94, f32[8,12,128,128]{2,3,1,0:T(8,128)} %copy-done.1, f32[8,12,128]{2,1,0:T(8,128)} %get-tuple-element.93, f32[8,12,128]{2,1,0:T(8,128)} %log_add_fusion, pred[8,128,128]{1,2,0:T(8,128)(4,1)} %copy-done.19), kind=kLoop, calls=%fused_computation.25 | loop fusion | flops 7864320 | bytes 15958016 | tf_op jit(solution)/shard_map/convert_element_type | solution.py:327
  260.8 2.8 multiply_reduce_fusion.2
  266.3 4.7 %fusion.33 = bf16[8,128,12,64]{1,3,2,0:T(8,128)(2,1)S(1)} fusion(bf16[8,12,128,128]{2,3,1,0:T(8,128)(2,1)} %copy-done.7, bf16[8,128,12,64]{1,0,3,2:T(8,128)(2,1)} %bitcast.352), kind=kOutput, calls=%fused_computation.96 | convolution fusion | flops 202113024 | bytes 6291456 | tf_op jit(solution)/shard_map/bhqk,bqhd->bkhd/dot_general | solution.py:331
  278.4 6.4 %fusion.133 = f32[2304,768]{0,1:T(8,128)} fusion(bf16[1024,2304]{0,1:T(8,128)(2,1)S(1)} %bitcast_dynamic-update-slice_fusion, bf16[1024,768]{1,0:T(8,128)(2,1)S(1)} %copy-done.63), kind=kOutput, calls=%fused_computation.357 | convolution fusion | flops 3623878656 | bytes 13369344 | tf_op jit(solution)/shard_map/dot_general | solution.py:21
  286.3 2.0 collective-permute-start.11
  292.0 3.4 fusion.25
  296.9 1.9 collective-permute-start.12
  302.5 3.4 collective-permute-done.15
  307.5 2.8 collective-permute-done.18
  311.8 2.9 collective-permute-done.16
  315.7 7.8 %add_convert_fusion.1 = bf16[1024,768]{1,0:T(8,128)(2,1)} fusion(f32[1024,768]{1,0:T(8,128)} %copy-done.21, bf16[1024,2304]{0,1:T(8,128)(2,1)} %copy-done.34, bf16[768,2304]{1,0:T(8,128)(2,1)S(1)} %copy-done), kind=kOutput, calls=%fused_computation.57 | convolution fusion | flops 3625451520 | bytes 12976128 | tf_op jit(solution)/shard_map/dot_general | solution.py:27
  324.3 2.6 collective-permute-start.13
  329.6 3.2 collective-permute-done.20
  335.0 1.9 collective-permute-done.21
  338.2 2.9 fusion.10
  345.4 8.3 %collective-permute-done.3 = bf16[2,2,2,24,1152]{4,3,2,1,0:T(8,128)(2,1)S(1)} collective-permute-done((bf16[2,2,2,24,1152]{4,3,2,1,0:T(8,128)(2,1)S(1)}, bf16[2,2,2,24,1152]{4,3,2,1,0:T(8,128)(2,1)S(1)}, u32[]{:S(2)}, u32[]{:S(2)}) %collective-permute-start.3) | collective-permute-done | bytes 442400 | tf_op jit(solution)/shard_map/ppermute | solution.py:113
  357.1 3.8 fusion.7
  366.7 2.5 fusion.8
  371.2 4.2 collective-permute-done.5
  377.3 3.9 collective-permute-done.6
  386.2 1.9 collective-permute-done.7
  393.4 4.9 %collective-permute-done.26 = bf16[2,2,2,24,1536]{4,3,2,1,0:T(8,128)(2,1)} collective-permute-done((bf16[2,2,2,24,1536]{4,3,2,1,0:T(8,128)(2,1)}, bf16[2,2,2,24,1536]{4,3,2,1,0:T(8,128)(2,1)}, u32[]{:S(2)}, u32[]{:S(2)}) %collective-permute-start.26) | collective-permute-done | bytes 589856 | tf_op jit(solution)/shard_map/ppermute | solution.py:113
  405.1 2.8 collective-permute-done.36
  408.9 2.5 collective-permute-done.27
  412.0 7.3 %collective-permute-done.37 = bf16[2,96,768]{2,1,0:T(8,128)(2,1)S(1)} collective-permute-done((bf16[2,96,768]{2,1,0:T(8,128)(2,1)S(1)}, bf16[2,96,768]{2,1,0:T(8,128)(2,1)S(1)}, u32[]{:S(2)}, u32[]{:S(2)}) %collective-permute-start.37) | collective-permute-done | bytes 294944 | tf_op jit(solution)/shard_map/ppermute | solution.py:113
  419.6 3.0 collective-permute-done.28
  423.3 6.4 %collective-permute-done.38 = bf16[96,768]{1,0:T(8,128)(2,1)S(1)} collective-permute-done((bf16[96,768]{1,0:T(8,128)(2,1)S(1)}, bf16[96,768]{1,0:T(8,128)(2,1)S(1)}, u32[]{:S(2)}, u32[]{:S(2)}) %collective-permute-start.38) | collective-permute-done | bytes 147488 | tf_op jit(solution)/shard_map/ppermute | solution.py:113
  432.5 3.1 collective-permute-done.39
  440.1 2.7 copy.187
  (390 shorter events, 144.4 us)
Async XLA Ops:
  0.6 21.6 %copy-start = (bf16[768,2304]{1,0:T(8,128)(2,1)S(1)}, bf16[768,2304]{1,0:T(8,128)(2,1)}, u32[]{:S(2)}) copy-start(bf16[768,2304]{1,0:T(8,128)(2,1)} %param.24) | copy-start | bytes 10616836
  54.9 39.7 %slice-start.5 = ((s8[4718592]{0:T(1024)(128)(4,1)}), s8[4194304]{0:T(1024)(128)(4,1)S(1)}, s32[]{:S(2)}) async-start(s8[4718592]{0:T(1024)(128)(4,1)} %bitcast.382), calls=%async_computation.6 | async-start | bytes 8388608
  56.6 38.0 %copy-start.4 = (f32[1024,768]{1,0:T(8,128)}, f32[1024,768]{1,0:T(8,128)S(1)}, u32[]{:S(2)}) copy-start(f32[1024,768]{1,0:T(8,128)S(1)} %get-tuple-element.87) | copy-start | bytes 9437188
  59.2 35.4 %copy-start.56 = (f32[768]{0:T(1024)S(1)}, f32[768]{0:T(1024)}, u32[]{:S(2)}) copy-start(f32[768]{0:T(1024)} %convert_element_type.535) | copy-start | bytes 9220
  59.2 35.4 %slice-start.6 = ((s8[4718592]{0:T(1024)(128)(4,1)}), s8[524288]{0:T(1024)(128)(4,1)S(1)}, s32[]{:S(2)}) async-start(s8[4718592]{0:T(1024)(128)(4,1)} %bitcast.382), calls=%async_computation.7 | async-start | bytes 1048576
  110.2 276.0 %all-to-all-start = ((bf16[8,128,768]{2,1,0:T(8,128)(2,1)}), bf16[8,128,768]{2,1,0:T(8,128)(2,1)}, u32[]{:S(2)}, u32[]{:S(2)}) async-start(bf16[8,128,768]{2,1,0:T(8,128)(2,1)} %scatter_fusion), calls=%async_computation | async-start | bytes 3145728 | tf_op jit(solution)/shard_map/all_to_all | solution.py:97
  161.2 19.6 %copy-start.41 = (f32[768]{0:T(1024)S(1)}, f32[768]{0:T(1024)}, u32[]{:S(2)}) copy-start(f32[768]{0:T(1024)} %convert_element_type.530) | copy-start | bytes 9220
  193.8 7.7 %slice-start.9 = ((s8[6291456]{0:T(1024)(128)(4,1)}), s8[4194304]{0:T(1024)(128)(4,1)S(1)}, s32[]{:S(2)}) async-start(s8[6291456]{0:T(1024)(128)(4,1)} %bitcast.388), calls=%async_computation.10 | async-start | bytes 8388608
  198.5 27.6 %copy-start.21 = (f32[1024,768]{1,0:T(8,128)}, f32[1024,768]{1,0:T(8,128)S(1)}, u32[]{:S(2)}) copy-start(f32[1024,768]{1,0:T(8,128)S(1)} %get-tuple-element.31) | copy-start | bytes 9437188
  200.0 13.8 %slice-start.3 = ((s8[6291456]{0:T(1024)(128)(4,1)}), s8[4194304]{0:T(1024)(128)(4,1)S(1)}, s32[]{:S(2)}) async-start(s8[6291456]{0:T(1024)(128)(4,1)} %bitcast.356), calls=%async_computation.4 | async-start | bytes 8388608
  201.5 12.2 %slice-start.4 = ((s8[6291456]{0:T(1024)(128)(4,1)}), s8[2097152]{0:T(1024)(128)(4,1)S(1)}, s32[]{:S(2)}) async-start(s8[6291456]{0:T(1024)(128)(4,1)} %bitcast.356), calls=%async_computation.5 | async-start | bytes 4194304
  201.5 86.8 %collective-permute-start.14 = (bf16[2,2,2,2,24,768]{5,4,3,2,1,0:T(8,128)(2,1)}, bf16[2,2,2,2,24,768]{5,4,3,2,1,0:T(8,128)(2,1)}, u32[]{:S(2)}, u32[]{:S(2)}) collective-permute-start(bf16[2,2,2,2,24,768]{5,4,3,2,1,0:T(8,128)(2,1)} %fusion.51), channel_id=1, source_target_pairs={{0,1},{1,0},{2,3},{3,2},{4,5},{5,4},{6,7},{7,6},{8,9},{9,8},{10,11... | collective-permute-start | bytes 1769480 | tf_op jit(solution)/shard_map/ppermute | solution.py:113
  213.8 143.3 %collective-permute-start.32 = (bf16[2,2,2,2,96,768]{5,4,3,2,1,0:T(8,128)(2,1)}, bf16[2,2,2,2,96,768]{5,4,3,2,1,0:T(8,128)(2,1)}, u32[]{:S(2)}, u32[]{:S(2)}) collective-permute-start(bf16[2,2,2,2,96,768]{5,4,3,2,1,0:T(8,128)(2,1)} %fusion.24), channel_id=1, source_target_pairs={{0,1},{1,0},{2,3},{3,2},{4,5},{5,4},{6,7},{7,6},{8,9},{9,8},{10,11... | collective-permute-start | bytes 7077896 | tf_op jit(solution)/shard_map/ppermute | solution.py:113
  219.6 5.9 %copy-start.32 = (f32[8,12,128]{2,1,0:T(8,128)S(1)}, f32[8,12,128]{2,1,0:T(8,128)}, u32[]{:S(2)}) copy-start(f32[8,12,128]{2,1,0:T(8,128)} %copy-done.31) | copy-start | bytes 147460
  219.6 6.5 %copy-start.65 = (bf16[768,768]{1,0:T(8,128)(2,1)S(1)}, bf16[768,768]{1,0:T(8,128)(2,1)}, u32[]{:S(2)}) copy-start(bf16[768,768]{1,0:T(8,128)(2,1)} %param.27) | copy-start | bytes 3538948
  225.0 141.7 %collective-permute-start.23 = (bf16[2,2,2,2,24,3072]{5,4,3,2,1,0:T(8,128)(2,1)}, bf16[2,2,2,2,24,3072]{5,4,3,2,1,0:T(8,128)(2,1)}, u32[]{:S(2)}, u32[]{:S(2)}) collective-permute-start(bf16[2,2,2,2,24,3072]{5,4,3,2,1,0:T(8,128)(2,1)} %fusion.23), channel_id=1, source_target_pairs={{0,1},{1,0},{2,3},{3,2},{4,5},{5,4},{6,7},{7,6},{8,9},{9,8},{10,11... | collective-permute-start | bytes 7077896 | tf_op jit(solution)/shard_map/ppermute | solution.py:113
  233.2 6.9 %copy-start.14 = (bf16[96,8,8,128]{3,2,1,0:T(8,128)(2,1)S(1)}, bf16[96,8,8,128]{3,2,1,0:T(8,128)(2,1)}, u32[]{:S(2)}) copy-start(bf16[96,8,8,128]{3,2,1,0:T(8,128)(2,1)} %copy.118) | copy-start | bytes 4718596
  240.1 6.3 %copy-start.50 = (f32[768]{0:T(1024)S(1)}, f32[768]{0:T(1024)}, u32[]{:S(2)}) copy-start(f32[768]{0:T(1024)} %get-tuple-element.20) | copy-start | bytes 9220
  240.1 7.0 %copy-start.52 = (f32[768]{0:T(1024)S(1)}, f32[768]{0:T(1024)}, u32[]{:S(2)}) copy-start(f32[768]{0:T(1024)} %get-tuple-element.15) | copy-start | bytes 9220
  240.1 8.4 %copy-start.51 = (f32[768]{0:T(1024)S(1)}, f32[768]{0:T(1024)}, u32[]{:S(2)}) copy-start(f32[768]{0:T(1024)} %get-tuple-element.28) | copy-start | bytes 9220
  254.0 6.8 %copy-start.10 = (bf16[96,8,8,128]{3,2,1,0:T(8,128)(2,1)S(1)}, bf16[96,8,8,128]{3,2,1,0:T(8,128)(2,1)}, u32[]{:S(2)}) copy-start(bf16[96,8,8,128]{3,2,1,0:T(8,128)(2,1)} %copy.120) | copy-start | bytes 4718596
  266.3 9.8 %collective-permute-start.9 = (f32[8,1152]{1,0:T(8,128)}, f32[8,1152]{1,0:T(8,128)S(1)}, u32[]{:S(2)}, u32[]{:S(2)}) collective-permute-start(f32[8,1152]{1,0:T(8,128)} %concatenate.20), channel_id=1, source_target_pairs={{0,1},{1,0},{2,3},{3,2},{4,5},{5,4},{6,7},{7,6},{8,9},{9,8},{10,11... | collective-permute-start | bytes 110600 | tf_op jit(solution)/shard_map/ppermute | solution.py:113
  276.9 8.0 %collective-permute-start.10 = (f32[8,1152]{1,0:T(8,128)}, f32[8,1152]{1,0:T(8,128)}, u32[]{:S(2)}, u32[]{:S(2)}) collective-permute-start(f32[8,1152]{1,0:T(8,128)} %add.490), channel_id=1, source_target_pairs={{0,2},{1,3},{2,0},{3,1},{4,6},{5,7},{6,4},{7,5},{8,10},{9,11},{10,... | collective-permute-start | bytes 110600 | tf_op jit(solution)/shard_map/ppermute | solution.py:113
  286.3 9.3 %collective-permute-start.11 = (f32[8,1152]{1,0:T(8,128)}, f32[8,1152]{1,0:T(8,128)}, u32[]{:S(2)}, u32[]{:S(2)}) collective-permute-start(f32[8,1152]{1,0:T(8,128)} %add.491), channel_id=1, source_target_pairs={{0,4},{4,0},{8,12},{12,8},{16,20},{20,16},{24,28},{28,24},{1,5},{5... | collective-permute-start | bytes 110600 | tf_op jit(solution)/shard_map/ppermute | solution.py:113
  292.0 7.9 %collective-permute-start.17 = (bf16[2,2,2,24,384]{4,3,2,1,0:T(8,128)(2,1)}, bf16[2,2,2,24,384]{4,3,2,1,0:T(8,128)(2,1)}, u32[]{:S(2)}, u32[]{:S(2)}) collective-permute-start(bf16[2,2,2,24,384]{4,3,2,1,0:T(8,128)(2,1)} %dynamic-slice_bitcast_fusion.11), channel_id=1, source_target_pairs={{0,4},{4,0},{8,12},{12,8},{16,20},{20,16},{24,28},{28,24},{1,5},{5... | collective-permute-start | bytes 442376 | tf_op jit(solution)/shard_map/ppermute | solution.py:113
  295.4 42.8 %collective-permute-start = (bf16[2,2,2,2,24,2304]{5,4,3,2,1,0:T(8,128)(2,1)}, bf16[2,2,2,2,24,2304]{5,4,3,2,1,0:T(8,128)(2,1)}, u32[]{:S(2)}, u32[]{:S(2)}) collective-permute-start(bf16[2,2,2,2,24,2304]{5,4,3,2,1,0:T(8,128)(2,1)} %fusion.25), channel_id=1, source_target_pairs={{0,1},{1,0},{2,3},{3,2},{4,5},{5,4},{6,7},{7,6},{8,9},{9,8},{10,11... | collective-permute-start | bytes 5308424 | tf_op jit(solution)/shard_map/ppermute | solution.py:113
  296.9 26.6 %collective-permute-start.12 = (f32[8,1152]{1,0:T(8,128)}, f32[8,1152]{1,0:T(8,128)}, u32[]{:S(2)}, u32[]{:S(2)}) collective-permute-start(f32[8,1152]{1,0:T(8,128)} %add.492), channel_id=1, source_target_pairs={{0,8},{4,12},{8,0},{12,4},{16,24},{20,28},{24,16},{28,20},{1,9},{5... | collective-permute-start | bytes 110600 | tf_op jit(solution)/shard_map/ppermute | solution.py:113
  299.9 6.0 %collective-permute-start.15 = (bf16[2,2,2,24,384]{4,3,1,0,2:T(8,128)(2,1)S(1)}, bf16[2,2,2,24,384]{4,3,1,0,2:T(8,128)(2,1)S(1)}, u32[]{:S(2)}, u32[]{:S(2)}) collective-permute-start(bf16[2,2,2,24,384]{4,3,1,0,2:T(8,128)(2,1)S(1)} %bitcast.379), channel_id=1, source_target_pairs={{0,2},{1,3},{2,0},{3,1},{4,6},{5,7},{6,4},{7,5},{8,10},{9,11},{10,... | collective-permute-start | bytes 442376 | tf_op jit(solution)/shard_map/ppermute | solution.py:113
  306.0 4.4 collective-permute-start.18
  310.3 4.4 collective-permute-start.16
  315.4 11.5 %collective-permute-start.19 = (bf16[2,24,768]{2,1,0:T(8,128)(2,1)}, bf16[2,24,768]{2,1,0:T(8,128)(2,1)}, u32[]{:S(2)}, u32[]{:S(2)}) collective-permute-start(bf16[2,24,768]{2,1,0:T(8,128)(2,1)} %fusion.84), channel_id=1, source_target_pairs={{0,8},{4,12},{8,0},{12,4},{16,24},{20,28},{24,16},{28,20},{1,9},{5... | collective-permute-start | bytes 221192 | tf_op jit(solution)/shard_map/ppermute | solution.py:113
  324.3 5.3 %collective-permute-start.13 = (f32[8,1152]{1,0:T(8,128)S(1)}, f32[8,1152]{1,0:T(8,128)S(1)}, u32[]{:S(2)}, u32[]{:S(2)}) collective-permute-start(f32[8,1152]{1,0:T(8,128)S(1)} %add.493), channel_id=1, source_target_pairs={{0,16},{4,20},{8,24},{12,28},{16,0},{20,4},{24,8},{28,12},{1,17},{... | collective-permute-start | bytes 110600 | tf_op jit(solution)/shard_map/ppermute | solution.py:113
  327.9 4.9 %collective-permute-start.20 = (bf16[24,768]{1,0:T(8,128)(2,1)S(1)}, bf16[24,768]{1,0:T(8,128)(2,1)S(1)}, u32[]{:S(2)}, u32[]{:S(2)}) collective-permute-start(bf16[24,768]{1,0:T(8,128)(2,1)S(1)} %dynamic-slice_bitcast_fusion.15), channel_id=1, source_target_pairs={{0,16},{4,20},{8,24},{12,28},{16,0},{20,4},{24,8},{28,12},{1,17},{... | collective-permute-start | bytes 110600 | tf_op jit(solution)/shard_map/ppermute | solution.py:113
  332.8 4.0 collective-permute-start.21
  336.9 1.3 collective-permute-start.22
  341.4 12.3 %collective-permute-start.3 = (bf16[2,2,2,24,1152]{4,3,2,1,0:T(8,128)(2,1)S(1)}, bf16[2,2,2,24,1152]{4,3,2,1,0:T(8,128)(2,1)S(1)}, u32[]{:S(2)}, u32[]{:S(2)}) collective-permute-start(bf16[2,2,2,24,1152]{4,3,2,1,0:T(8,128)(2,1)S(1)} %dynamic-slice_bitcast_fusion.2), channel_id=1, source_target_pairs={{0,4},{4,0},{8,12},{12,8},{16,20},{20,16},{24,28},{28,24},{1,5},{5... | collective-permute-start | bytes 1327112 | tf_op jit(solution)/shard_map/ppermute | solution.py:113
  343.8 12.0 %collective-permute-start.1 = (bf16[2,2,2,24,1152]{4,3,1,0,2:T(8,128)(2,1)S(1)}, bf16[2,2,2,24,1152]{4,3,1,0,2:T(8,128)(2,1)S(1)}, u32[]{:S(2)}, u32[]{:S(2)}) collective-permute-start(bf16[2,2,2,24,1152]{4,3,1,0,2:T(8,128)(2,1)S(1)} %bitcast.378), channel_id=1, source_target_pairs={{0,2},{1,3},{2,0},{3,1},{4,6},{5,7},{6,4},{7,5},{8,10},{9,11},{10,... | collective-permute-start | bytes 1327112 | tf_op jit(solution)/shard_map/ppermute | solution.py:113
  353.8 15.4 %collective-permute-start.4 = (bf16[2,2,24,1152]{3,2,1,0:T(8,128)(2,1)S(1)}, bf16[2,2,24,1152]{3,2,1,0:T(8,128)(2,1)S(1)}, u32[]{:S(2)}, u32[]{:S(2)}) collective-permute-start(bf16[2,2,24,1152]{3,2,1,0:T(8,128)(2,1)S(1)} %dynamic-slice_bitcast_fusion.7), channel_id=1, source_target_pairs={{0,2},{1,3},{2,0},{3,1},{4,6},{5,7},{6,4},{7,5},{8,10},{9,11},{10,... | collective-permute-start | bytes 663560 | tf_op jit(solution)/shard_map/ppermute | solution.py:113
  356.0 13.3 %collective-permute-start.2 = (bf16[2,2,24,1152]{3,2,1,0:T(8,128)(2,1)S(1)}, bf16[2,2,24,1152]{3,2,1,0:T(8,128)(2,1)S(1)}, u32[]{:S(2)}, u32[]{:S(2)}) collective-permute-start(bf16[2,2,24,1152]{3,2,1,0:T(8,128)(2,1)S(1)} %dynamic-slice_bitcast_fusion.8), channel_id=1, source_target_pairs={{0,4},{4,0},{8,12},{12,8},{16,20},{20,16},{24,28},{28,24},{1,5},{5... | collective-permute-start | bytes 663560 | tf_op jit(solution)/shard_map/ppermute | solution.py:113
  357.1 9.6 %slice-start = ((s8[9437184]{0:T(1024)(128)(4,1)}), s8[4194304]{0:T(1024)(128)(4,1)S(1)}, s32[]{:S(2)}) async-start(s8[9437184]{0:T(1024)(128)(4,1)} %bitcast.348), calls=%async_computation.1 | async-start | bytes 8388608
  357.1 9.6 %slice-start.1 = ((s8[9437184]{0:T(1024)(128)(4,1)}), s8[4194304]{0:T(1024)(128)(4,1)S(1)}, s32[]{:S(2)}) async-start(s8[9437184]{0:T(1024)(128)(4,1)} %bitcast.348), calls=%async_computation.2 | async-start | bytes 8388608
  364.1 25.1 %collective-permute-start.35 = (bf16[2,2,2,96,384]{4,3,2,1,0:T(8,128)(2,1)}, bf16[2,2,2,96,384]{4,3,2,1,0:T(8,128)(2,1)}, u32[]{:S(2)}, u32[]{:S(2)}) collective-permute-start(bf16[2,2,2,96,384]{4,3,2,1,0:T(8,128)(2,1)} %dynamic-slice_bitcast_fusion), channel_id=1, source_target_pairs={{0,4},{4,0},{8,12},{12,8},{16,20},{20,16},{24,28},{28,24},{1,5},{5... | collective-permute-start | bytes 1769480 | tf_op jit(solution)/shard_map/ppermute | solution.py:113
  365.1 26.2 %collective-permute-start.33 = (bf16[2,2,2,96,384]{4,3,1,0,2:T(8,128)(2,1)}, bf16[2,2,2,96,384]{4,3,1,0,2:T(8,128)(2,1)}, u32[]{:S(2)}, u32[]{:S(2)}) collective-permute-start(bf16[2,2,2,96,384]{4,3,1,0,2:T(8,128)(2,1)} %bitcast.341), channel_id=1, source_target_pairs={{0,2},{1,3},{2,0},{3,1},{4,6},{5,7},{6,4},{7,5},{8,10},{9,11},{10,... | collective-permute-start | bytes 1769480 | tf_op jit(solution)/shard_map/ppermute | solution.py:113
  369.4 6.0 %collective-permute-start.5 = (bf16[2,24,2304]{2,1,0:T(8,128)(2,1)S(1)}, bf16[2,24,2304]{2,1,0:T(8,128)(2,1)S(1)}, u32[]{:S(2)}, u32[]{:S(2)}) collective-permute-start(bf16[2,24,2304]{2,1,0:T(8,128)(2,1)S(1)} %fusion.74), channel_id=1, source_target_pairs={{0,8},{4,12},{8,0},{12,4},{16,24},{20,28},{24,16},{28,20},{1,9},{5... | collective-permute-start | bytes 663560 | tf_op jit(solution)/shard_map/ppermute | solution.py:113
  371.2 11.2 %copy-start.17 = (bf16[2,2,2,2,24,1536]{5,4,3,2,1,0:T(8,128)(2,1)}, bf16[2,2,2,2,24,1536]{5,4,3,2,1,0:T(8,128)(2,1)S(1)}, u32[]{:S(2)}) copy-start(bf16[2,2,2,2,24,1536]{5,4,3,2,1,0:T(8,128)(2,1)S(1)} %get-tuple-element.43) | copy-start | bytes 3538948
  375.5 5.7 %collective-permute-start.6 = (bf16[24,2304]{1,0:T(8,128)(2,1)S(1)}, bf16[24,2304]{1,0:T(8,128)(2,1)S(1)}, u32[]{:S(2)}, u32[]{:S(2)}) collective-permute-start(bf16[24,2304]{1,0:T(8,128)(2,1)S(1)} %dynamic-slice_bitcast_fusion.12), channel_id=1, source_target_pairs={{0,16},{4,20},{8,24},{12,28},{16,0},{20,4},{24,8},{28,12},{1,17},{... | collective-permute-start | bytes 331784 | tf_op jit(solution)/shard_map/ppermute | solution.py:113
  381.8 6.2 %collective-permute-start.7 = (bf16[24,2304]{1,0:T(8,128)(2,1)}, bf16[24,2304]{1,0:T(8,128)(2,1)}, u32[]{:S(2)}, u32[]{:S(2)}) collective-permute-start(bf16[24,2304]{1,0:T(8,128)(2,1)} %fusion.77), channel_id=1, source_target_pairs={{0,2},{1,3},{2,0},{3,1},{4,6},{5,7},{6,4},{7,5},{8,10},{9,11},{10,... | collective-permute-start | bytes 331784 | tf_op jit(solution)/shard_map/ppermute | solution.py:113
  384.2 14.1 %collective-permute-start.26 = (bf16[2,2,2,24,1536]{4,3,2,1,0:T(8,128)(2,1)}, bf16[2,2,2,24,1536]{4,3,2,1,0:T(8,128)(2,1)}, u32[]{:S(2)}, u32[]{:S(2)}) collective-permute-start(bf16[2,2,2,24,1536]{4,3,2,1,0:T(8,128)(2,1)} %dynamic-slice_bitcast_fusion.1), channel_id=1, source_target_pairs={{0,4},{4,0},{8,12},{12,8},{16,20},{20,16},{24,28},{28,24},{1,5},{5... | collective-permute-start | bytes 1769480 | tf_op jit(solution)/shard_map/ppermute | solution.py:113
  385.2 16.5 %collective-permute-start.24 = (bf16[2,2,2,24,1536]{4,3,1,0,2:T(8,128)(2,1)}, bf16[2,2,2,24,1536]{4,3,1,0,2:T(8,128)(2,1)}, u32[]{:S(2)}, u32[]{:S(2)}) collective-permute-start(bf16[2,2,2,24,1536]{4,3,1,0,2:T(8,128)(2,1)} %bitcast.342), channel_id=1, source_target_pairs={{0,2},{1,3},{2,0},{3,1},{4,6},{5,7},{6,4},{7,5},{8,10},{9,11},{10,... | collective-permute-start | bytes 1769480 | tf_op jit(solution)/shard_map/ppermute | solution.py:113
  386.2 12.1 %copy-start.18 = (bf16[2,2,2,2,24,1536]{5,4,3,2,1,0:T(8,128)(2,1)S(1)}, bf16[2,2,2,2,24,1536]{5,4,3,2,1,0:T(8,128)(2,1)}, u32[]{:S(2)}) copy-start(bf16[2,2,2,2,24,1536]{5,4,3,2,1,0:T(8,128)(2,1)} %copy-done.17) | copy-start | bytes 3538948
  389.1 12.6 %copy-start.24 = (bf16[2,2,2,1,24,1536]{5,4,3,2,1,0:T(8,128)(2,1)S(1)}, bf16[2,2,2,1,24,1536]{5,4,3,2,1,0:T(8,128)(2,1)}, u32[]{:S(2)}) copy-start(bf16[2,2,2,1,24,1536]{5,4,3,2,1,0:T(8,128)(2,1)} %get-tuple-element.49) | copy-start | bytes 1769476
  389.1 14.9 %collective-permute-start.8 = (bf16[2,24,2304]{2,1,0:T(8,128)(2,1)S(1)}, bf16[2,24,2304]{2,1,0:T(8,128)(2,1)S(1)}, u32[]{:S(2)}, u32[]{:S(2)}) collective-permute-start(bf16[2,24,2304]{2,1,0:T(8,128)(2,1)S(1)} %pad_maximum_fusion.5), channel_id=1, source_target_pairs={{0,1},{1,0},{2,3},{3,2},{4,5},{5,4},{6,7},{7,6},{8,9},{9,8},{10,11... | collective-permute-start | bytes 663560 | tf_op jit(solution)/shard_map/ppermute | solution.py:113
  390.7 17.2 %collective-permute-start.36 = (bf16[2,2,96,384]{3,2,1,0:T(8,128)(2,1)S(1)}, bf16[2,2,96,384]{3,2,1,0:T(8,128)(2,1)S(1)}, u32[]{:S(2)}, u32[]{:S(2)}) collective-permute-start(bf16[2,2,96,384]{3,2,1,0:T(8,128)(2,1)S(1)} %dynamic-slice_bitcast_fusion.3), channel_id=1, source_target_pairs={{0,2},{1,3},{2,0},{3,1},{4,6},{5,7},{6,4},{7,5},{8,10},{9,11},{10,... | collective-permute-start | bytes 884744 | tf_op jit(solution)/shard_map/ppermute | solution.py:113
  392.6 15.4 %collective-permute-start.34 = (bf16[2,2,96,384]{3,2,1,0:T(8,128)(2,1)S(1)}, bf16[2,2,96,384]{3,2,1,0:T(8,128)(2,1)S(1)}, u32[]{:S(2)}, u32[]{:S(2)}) collective-permute-start(bf16[2,2,96,384]{3,2,1,0:T(8,128)(2,1)S(1)} %dynamic-slice_bitcast_fusion.4), channel_id=1, source_target_pairs={{0,4},{4,0},{8,12},{12,8},{16,20},{20,16},{24,28},{28,24},{1,5},{5... | collective-permute-start | bytes 884744 | tf_op jit(solution)/shard_map/ppermute | solution.py:113
  399.5 11.8 %collective-permute-start.27 = (bf16[2,2,24,1536]{3,2,1,0:T(8,128)(2,1)S(1)}, bf16[2,2,24,1536]{3,2,1,0:T(8,128)(2,1)S(1)}, u32[]{:S(2)}, u32[]{:S(2)}) collective-permute-start(bf16[2,2,24,1536]{3,2,1,0:T(8,128)(2,1)S(1)} %dynamic-slice_bitcast_fusion.5), channel_id=1, source_target_pairs={{0,2},{1,3},{2,0},{3,1},{4,6},{5,7},{6,4},{7,5},{8,10},{9,11},{10,... | collective-permute-start | bytes 884744 | tf_op jit(solution)/shard_map/ppermute | solution.py:113
  402.9 8.5 %collective-permute-start.25 = (bf16[2,2,24,1536]{3,2,1,0:T(8,128)(2,1)S(1)}, bf16[2,2,24,1536]{3,2,1,0:T(8,128)(2,1)S(1)}, u32[]{:S(2)}, u32[]{:S(2)}) collective-permute-start(bf16[2,2,24,1536]{3,2,1,0:T(8,128)(2,1)S(1)} %dynamic-slice_bitcast_fusion.6), channel_id=1, source_target_pairs={{0,4},{4,0},{8,12},{12,8},{16,20},{20,16},{24,28},{28,24},{1,5},{5... | collective-permute-start | bytes 884744 | tf_op jit(solution)/shard_map/ppermute | solution.py:113
  408.2 11.2 %collective-permute-start.37 = (bf16[2,96,768]{2,1,0:T(8,128)(2,1)S(1)}, bf16[2,96,768]{2,1,0:T(8,128)(2,1)S(1)}, u32[]{:S(2)}, u32[]{:S(2)}) collective-permute-start(bf16[2,96,768]{2,1,0:T(8,128)(2,1)S(1)} %fusion.62), channel_id=1, source_target_pairs={{0,8},{4,12},{8,0},{12,4},{16,24},{20,28},{24,16},{28,20},{1,9},{5... | collective-permute-start | bytes 884744 | tf_op jit(solution)/shard_map/ppermute | solution.py:113
  411.6 10.9 %collective-permute-start.28 = (bf16[2,24,3072]{2,1,0:T(8,128)(2,1)S(1)}, bf16[2,24,3072]{2,1,0:T(8,128)(2,1)S(1)}, u32[]{:S(2)}, u32[]{:S(2)}) collective-permute-start(bf16[2,24,3072]{2,1,0:T(8,128)(2,1)S(1)} %fusion.66), channel_id=1, source_target_pairs={{0,8},{4,12},{8,0},{12,4},{16,24},{20,28},{24,16},{28,20},{1,9},{5... | collective-permute-start | bytes 884744 | tf_op jit(solution)/shard_map/ppermute | solution.py:113
  419.5 10.2 %collective-permute-start.38 = (bf16[96,768]{1,0:T(8,128)(2,1)S(1)}, bf16[96,768]{1,0:T(8,128)(2,1)S(1)}, u32[]{:S(2)}, u32[]{:S(2)}) collective-permute-start(bf16[96,768]{1,0:T(8,128)(2,1)S(1)} %dynamic-slice_bitcast_fusion.9), channel_id=1, source_target_pairs={{0,16},{4,20},{8,24},{12,28},{16,0},{20,4},{24,8},{28,12},{1,17},{... | collective-permute-start | bytes 442376 | tf_op jit(solution)/shard_map/ppermute | solution.py:113
  422.6 8.7 %collective-permute-start.29 = (bf16[24,3072]{1,0:T(8,128)(2,1)S(1)}, bf16[24,3072]{1,0:T(8,128)(2,1)S(1)}, u32[]{:S(2)}, u32[]{:S(2)}) collective-permute-start(bf16[24,3072]{1,0:T(8,128)(2,1)S(1)} %dynamic-slice_bitcast_fusion.10), channel_id=1, source_target_pairs={{0,16},{4,20},{8,24},{12,28},{16,0},{20,4},{24,8},{28,12},{1,17},{... | collective-permute-start | bytes 442376 | tf_op jit(solution)/shard_map/ppermute | solution.py:113
  429.7 5.8 %collective-permute-start.39 = (bf16[96,768]{1,0:T(8,128)(2,1)S(1)}, bf16[96,768]{1,0:T(8,128)(2,1)S(1)}, u32[]{:S(2)}, u32[]{:S(2)}) collective-permute-start(bf16[96,768]{1,0:T(8,128)(2,1)S(1)} %fusion.69), channel_id=1, source_target_pairs={{0,2},{1,3},{2,0},{3,1},{4,6},{5,7},{6,4},{7,5},{8,10},{9,11},{10,... | collective-permute-start | bytes 442376 | tf_op jit(solution)/shard_map/ppermute | solution.py:113
  431.3 5.8 %collective-permute-start.30 = (bf16[24,3072]{1,0:T(8,128)(2,1)S(1)}, bf16[24,3072]{1,0:T(8,128)(2,1)S(1)}, u32[]{:S(2)}, u32[]{:S(2)}) collective-permute-start(bf16[24,3072]{1,0:T(8,128)(2,1)S(1)} %fusion.70), channel_id=1, source_target_pairs={{0,2},{1,3},{2,0},{3,1},{4,6},{5,7},{6,4},{7,5},{8,10},{9,11},{10,... | collective-permute-start | bytes 442376 | tf_op jit(solution)/shard_map/ppermute | solution.py:113
  435.6 1.7 collective-permute-start.40
  437.2 1.6 collective-permute-start.31
  (57 other events, 167.1 us)

commit v2 on v1

v2 whole, which is shorter than its diff:
```python
from functools import partial

import jax
import jax.numpy as jnp
from jax import lax
from jax.experimental import pallas as pl
from jax.experimental.pallas import tpu as pltpu
from jax.sharding import PartitionSpec as P

HDIM = 64
KTOP = 12
NORM_EPS = 1e-12
COS_EPS = 1e-06
MASKED = -1000000000.0
LOSS_SCALE = 1024.0
F32 = jnp.float32
BF16 = jnp.bfloat16
LANES = 128
VMEM_LIMIT = 60 * 1024 * 1024
ERF_P = 0.3275911
ERF_A = (0.254829592, -0.284496736, 1.421413741, -1.453152027, 1.061405429)
HALF_ROOT = 0.7071067811865476
PEAK = 0.3989422804014327
ROW_BQ, ROW_BV, ROW_BO, ROW_GA, ROW_SA, ROW_BD, ROW_GF, ROW_SF = range(8)


def dot(left, right):
    return jnp.dot(left, right, preferred_element_type=F32)


def dot_t(left, right):
    return lax.dot_general(left, right, (((1,), (1,)), ((), ())), preferred_element_type=F32)


def t_dot(left, right):
    return lax.dot_general(left, right, (((0,), (0,)), ((), ())), preferred_element_type=F32)


def full(shape):
    return pl.BlockSpec(shape, lambda *_: (0,) * len(shape))


def once(shape):
    return pl.BlockSpec(shape, lambda *_: (0,) * len(shape), pipeline_mode=pl.Buffered(1))


def shaped(shape, dtype):
    return jax.ShapeDtypeStruct(shape, dtype)


def call(kernel, name, grid, prefetch, in_specs, out_specs, out_shape, scratch, flops, moved, args):
    return pl.pallas_call(
        kernel,
        grid_spec=pltpu.PrefetchScalarGridSpec(
            num_scalar_prefetch=len(prefetch),
            grid=grid,
            in_specs=in_specs,
            out_specs=out_specs,
            scratch_shapes=scratch,
        ),
        out_shape=out_shape,
        compiler_params=pltpu.CompilerParams(
            dimension_semantics=("arbitrary",) * len(grid), vmem_limit_bytes=VMEM_LIMIT
        ),
        cost_estimate=pl.CostEstimate(flops=int(flops), bytes_accessed=int(moved), transcendentals=0),
        name=name,
    )(*prefetch, *args)


def norm_forward(values):
    center = values - jnp.mean(values, axis=-1, keepdims=True)
    spread = lax.rsqrt(jnp.mean(center * center, axis=-1, keepdims=True) + NORM_EPS)
    return center * spread, spread


def norm_backward(grad_out, normed, spread, gain):
    scaled = grad_out * gain
    mean_scaled = jnp.mean(scaled, axis=-1, keepdims=True)
    mean_product = jnp.mean(scaled * normed, axis=-1, keepdims=True)
    return spread * (scaled - mean_scaled - normed * mean_product)


def column_sum(values):
    return jnp.sum(values, axis=0, keepdims=True)


def gelu_pair(v):
    t = 1.0 / (1.0 + (ERF_P * HALF_ROOT) * jnp.abs(v))
    bell = jnp.exp(-0.5 * (v * v))
    poly = 0.5 * ERF_A[4]
    for coef in ERF_A[3::-1]:
        poly = poly * t + 0.5 * coef
    tail = poly * t * bell
    phi = jnp.where(v > 0, 1.0 - tail, tail)
    return v * phi, phi + v * (PEAK * bell)


def head_masks():
    lane = lax.broadcasted_iota(jnp.int32, (1, LANES), 1)
    low = (lane < HDIM).astype(F32)
    return low.astype(BF16), (1.0 - low).astype(BF16), lane < HDIM


def sentence_count(bucket_s, number, group_size):
    kind = bucket_s[number]
    if group_size > 1:
        kind = kind // group_size
    return jnp.maximum(1, lax.shift_right_logical(jnp.int32(KTOP), kind))


def row_sentences(batch, bucket_s, lengths_s, group_size, batches, sent, span):
    start = jnp.int32(0)
    for other in range(batches):
        start += jnp.where(other < batch, sentence_count(bucket_s, other, group_size), 0)
    count = sentence_count(bucket_s, batch, group_size)
    lane = lax.broadcasted_iota(jnp.int32, (8, span), 1)
    row = lax.broadcasted_iota(jnp.int32, (span, span), 0)
    passed_lane = jnp.zeros((8, span), jnp.int32)
    passed_row = jnp.zeros((span, span), jnp.int32)
    finish = jnp.int32(0)
    for number in range(KTOP):
        finish += lengths_s[jnp.minimum(start + number, sent - 1)]
        bound = jnp.where(number < count, finish, span)
        passed_lane += (lane >= bound).astype(jnp.int32)
        passed_row += (row >= bound).astype(jnp.int32)
    sid_lane = jnp.where(passed_lane < count, start + passed_lane, -1)
    sid_row = jnp.where(passed_row < count, start + passed_row, -1)
    return sid_lane, sid_row


def attention_forward(x, w_qkv, w_out, table, bucket, lengths, group_size, span, rows_step):
    rows, width = x.shape
    batches = rows // span
    pairs = width // LANES
    sent = lengths.shape[0]
    per_step = rows_step // span

    def kernel(bucket_s, lengths_s, x_ref, wq_ref, wo_ref, tab_ref, qkv_ref, p_ref, att_ref, n_ref, s_ref, sid_ref):
        step = pl.program_id(0)
        low_b, high_b, low_m = head_masks()
        x_in = x_ref[...]
        mixed = dot(x_in, wq_ref[:, :width]) + tab_ref[ROW_BQ : ROW_BQ + 1, :]
        qkv_ref[:, :width] = (mixed * 0.125).astype(BF16)
        qkv_ref[:, width : 2 * width] = dot(x_in, wq_ref[:, width : 2 * width]).astype(BF16)
        mixed = dot(x_in, wq_ref[:, 2 * width :]) + tab_ref[ROW_BV : ROW_BV + 1, :]
        qkv_ref[:, 2 * width :] = mixed.astype(BF16)
        eye = lax.broadcasted_iota(jnp.int32, (span, span), 0) == lax.broadcasted_iota(
            jnp.int32, (span, span), 1
        )
        for inner in range(per_step):
            sid_lane, sid_row = row_sentences(
                step * per_step + inner, bucket_s, lengths_s, group_size, batches, sent, span
            )
            sid_ref[inner] = sid_lane
            same = (sid_row == sid_lane[0:1, :]) & (sid_row >= 0)
            bias = jnp.where(same | eye, 0.0, MASKED)
            bias = jnp.concatenate([bias, bias], axis=0)
            base = slice(inner * span, (inner + 1) * span)
            for pair in range(pairs):
                cols = slice(pair * LANES, (pair + 1) * LANES)
                q = qkv_ref[base, cols]
                k = qkv_ref[base, width + pair * LANES : width + (pair + 1) * LANES]
                v = qkv_ref[base, 2 * width + pair * LANES : 2 * width + (pair + 1) * LANES]
                both = jnp.concatenate([q * low_b, q * high_b], axis=0)
                logits = dot_t(both, k) + bias
                raised = jnp.exp(logits - jnp.max(logits, axis=-1, keepdims=True))
                total = jnp.sum(raised, axis=-1, keepdims=True)
                probs = (raised * (1.0 / total)).astype(BF16)
                p_ref[inner, pair] = probs
                mix = dot(probs, v)
                att_ref[base, cols] = jnp.where(low_m, mix[:span], mix[span:]).astype(BF16)
        branch = dot(att_ref[...], wo_ref[...]) + tab_ref[ROW_BO : ROW_BO + 1, :]
        normed, spread = norm_forward(x_in.astype(F32) + branch)
        n_ref[...] = normed
        s_ref[...] = jnp.broadcast_to(spread, (rows_step, LANES))

    return call(
        kernel,
        "attn_fwd",
        (rows // rows_step,),
        (bucket, lengths),
        [
            pl.BlockSpec((rows_step, width), lambda i, *_: (i, 0)),
            once((width, 3 * width)),
            once((width, width)),
            once((8, width)),
        ],
        [
            pl.BlockSpec((rows_step, 3 * width), lambda i, *_: (i, 0)),
            pl.BlockSpec((per_step, pairs, 2 * span, span), lambda i, *_: (i, 0, 0, 0)),
            pl.BlockSpec((rows_step, width), lambda i, *_: (i, 0)),
            pl.BlockSpec((rows_step, width), lambda i, *_: (i, 0)),
            pl.BlockSpec((rows_step, LANES), lambda i, *_: (i, 0)),
            pl.BlockSpec((per_step, 8, span), lambda i, *_: (i, 0, 0)),
        ],
        [
            shaped((rows, 3 * width), BF16),
            shaped((batches, pairs, 2 * span, span), BF16),
            shaped((rows, width), BF16),
            shaped((rows, width), F32),
            shaped((rows, LANES), F32),
            shaped((batches, 8, span), jnp.int32),
        ],
        [],
        8 * rows * width * width * 2,
        30e6,
        (x, w_qkv, w_out, table),
    )


def feed_forward(n_attn, w_up, w_down, bias_up, table, sid, slots, pairing, targets, slot_count, chunk, block):
    rows, width = n_attn.shape
    ff = w_up.shape[1]
    batches, _, span = sid.shape
    pair_count = targets.shape[0]
    side = -(-pair_count // 8) * 8
    steps = ff // chunk
    blocks = rows // block
    per_block = block // span

    def kernel(
        slots_s, pairing_s, targets_s, n_ref, wu_ref, wd_ref, bu_ref, tab_ref, sid_ref,
        act_ref, dg_ref, ht_ref, enc_ref, gres_ref, gsl_ref, vec_ref, low_scr, acc_scr, spread_scr,
    ):
        step = pl.program_id(0)
        gain = tab_ref[ROW_GA : ROW_GA + 1, :]
        shift = tab_ref[ROW_SA : ROW_SA + 1, :]

        @pl.when(step == 0)
        def _():
            hidden = (n_ref[...] * gain + shift).astype(BF16)
            low_scr[...] = hidden
            ht_ref[...] = hidden.T
            acc_scr[...] = jnp.zeros_like(acc_scr)

        for number in range(blocks):
            base = slice(number * block, (number + 1) * block)
            inner = dot(low_scr[base, :], wu_ref[...]) + bu_ref[...].astype(F32)
            active, slope = gelu_pair(inner)
            active = active.astype(BF16)
            act_ref[base, :] = active
            dg_ref[base, :] = slope.astype(BF16)
            acc_scr[base, :] += dot(active, wd_ref[...])

        @pl.when(step == steps - 1)
        def _():
            gain_out = tab_ref[ROW_GF : ROW_GF + 1, :]
            shift_out = tab_ref[ROW_SF : ROW_SF + 1, :]
            slot = lax.broadcasted_iota(jnp.int32, (2 * side, span), 0)
            wanted = jnp.full((2 * side, span), -2, jnp.int32)
            goal = jnp.zeros((side, LANES), F32)
            goal_slot = lax.broadcasted_iota(jnp.int32, (side, LANES), 0)
            for number in range(pair_count):
                wanted = jnp.where(slot == number, pairing_s[0, 2 * number], wanted)
                wanted = jnp.where(slot == side + number, pairing_s[0, 2 * number + 1], wanted)
                goal = jnp.where(goal_slot == number, targets_s[number], goal)
            members = [
                (sid_ref[number][0:1, :] == wanted).astype(F32) for number in range(batches)
            ]
            sizes = jnp.zeros((2 * side, 1), F32)
            for member in members:
                sizes += jnp.sum(member, axis=-1, keepdims=True)
            share = 1.0 / jnp.maximum(sizes, 1.0)
            picks = [
                jnp.concatenate(members[number * per_block : (number + 1) * per_block], axis=1).astype(BF16)
                for number in range(blocks)
            ]
            ones = jnp.ones((2 * side, LANES), BF16)
            pooled = jnp.zeros((2 * side, width), F32)
            for number in range(blocks):
                base = slice(number * block, (number + 1) * block)
                resid = (
                    n_ref[base, :] * gain + shift + acc_scr[base, :] + tab_ref[ROW_BD : ROW_BD + 1, :]
                )
                normed, spread = norm_forward(resid)
                acc_scr[base, :] = normed
                spread_scr[base, :] = jnp.broadcast_to(spread, (block, LANES))
                out = normed * gain_out + shift_out
                high = out.astype(BF16)
                rest = (out - high.astype(F32)).astype(BF16)
                pooled += dot(picks[number], high) + dot(picks[number], rest)
                valid = t_dot(picks[number], ones)
                for col in range(width // LANES):
                    cols = slice(col * LANES, (col + 1) * LANES)
                    kept = (out[:, cols] * valid).astype(BF16)
                    for inner in range(per_block):
                        enc_ref[slots_s[number * per_block + inner], :, cols] = kept[
                            inner * span : (inner + 1) * span
                        ]
            pooled = pooled * share
            first, partner = pooled[:side], pooled[side:]
            cross = jnp.sum(first * partner, axis=-1, keepdims=True)
            scale_first = lax.rsqrt(jnp.sum(first * first, axis=-1, keepdims=True) + COS_EPS)
            scale_partner = lax.rsqrt(jnp.sum(partner * partner, axis=-1, keepdims=True) + COS_EPS)
            cosine = cross * scale_first * scale_partner
            factor = 2.0 * LOSS_SCALE * (cosine - goal[:, :1])
            both_scales = factor * scale_first * scale_partner
            grad_first = both_scales * partner - (factor * cosine * scale_first * scale_first) * first
            grad_partner = (
                both_scales * first - (factor * cosine * scale_partner * scale_partner) * partner
            )
            grad_home = jnp.concatenate([grad_first, grad_partner], axis=0) * share
            high = grad_home.astype(BF16)
            rest = (grad_home - high.astype(F32)).astype(BF16)
            vec_ref[...] = jnp.zeros_like(vec_ref)
            for number in range(blocks):
                base = slice(number * block, (number + 1) * block)
                grad_out = t_dot(picks[number], high) + t_dot(picks[number], rest)
                normed = acc_scr[base, :]
                resid = norm_backward(grad_out, normed, spread_scr[base, :1], gain_out)
                gres_ref[base, :] = resid
                low = resid.astype(BF16)
                gsl_ref[base, :] = low
                vec_ref[0:1, :] += column_sum(grad_out * normed)
                vec_ref[1:2, :] += column_sum(grad_out)
                vec_ref[2:3, :] += column_sum(low.astype(F32))

    return call(
        kernel,
        "ffn_fwd",
        (steps,),
        (slots, pairing, targets),
        [
            once((rows, width)),
            pl.BlockSpec((width, chunk), lambda j, *_: (0, j)),
            pl.BlockSpec((chunk, width), lambda j, *_: (j, 0)),
            pl.BlockSpec((1, chunk), lambda j, *_: (0, j)),
            once((8, width)),
            once((batches, 8, span)),
        ],
        [
            pl.BlockSpec((rows, chunk), lambda j, *_: (0, j)),
            pl.BlockSpec((rows, chunk), lambda j, *_: (0, j)),
            once((width, rows)),
            once((slot_count, span, width)),
            once((rows, width)),
            once((rows, width)),
            once((8, width)),
        ],
        [
            shaped((rows, ff), BF16),
            shaped((rows, ff), BF16),
            shaped((width, rows), BF16),
            shaped((slot_count, span, width), BF16),
            shaped((rows, width), F32),
            shaped((rows, width), BF16),
            shaped((8, width), F32),
        ],
        [
            pltpu.VMEM((rows, width), BF16),
            pltpu.VMEM((rows, width), F32),
            pltpu.VMEM((rows, LANES), F32),
        ],
        8 * rows * width * ff,
        40e6,
        (n_attn, w_up, w_down, bias_up, table, sid),
    )


def deal(scratch, here_s, outs, z_count, pieces):
    send_a, keep_a, send_b, keep_b = outs
    x, y = here_s[2], here_s[3]
    for z in range(z_count):
        for other in range(2):
            at = pl.ds((z * 2 + other) * pieces, pieces)
            send_a[at] = scratch[z, other, 1 - x, 0].astype(BF16)
            keep_a[at] = scratch[z, other, x, 0].astype(BF16)
            send_b[at] = scratch[z, 1 - y, other, 1].astype(BF16)
            keep_b[at] = scratch[z, y, other, 1].astype(BF16)


def down_terms(active, grad_second, here, which, got=None):
    rows, ff = active.shape
    half = grad_second.shape[1] // 2
    steps = 4
    tall = ff // steps
    pieces = ff // 32 // 8

    def give(here_s, act_ref, gs_ref, out_ref):
        out_ref[...] = t_dot(act_ref[...], gs_ref[...]).astype(BF16)

    def own(here_s, act_ref, gs_ref, got_ref, *rest):
        outs, scratch = rest[:4], rest[4]
        term = t_dot(act_ref[...], gs_ref[...]) + got_ref[...].astype(F32)
        scratch[...] = term.reshape(scratch.shape)
        deal(scratch, here_s, outs, 1, pieces)

    in_specs = [
        pl.BlockSpec((rows, tall), lambda i, here_s: (0, i)),
        pl.BlockSpec((rows, half), lambda i, here_s: (0, here_s[which]), pipeline_mode=pl.Buffered(1)),
    ]
    flops = 2 * rows * ff * half
    if got is None:
        return call(
            give, "down_give", (steps,), (here,), in_specs,
            pl.BlockSpec((tall, half), lambda i, *_: (i, 0)),
            shaped((ff, half), BF16), [], flops, 9e6, (active, grad_second),
        )
    block = (2 * pieces, 8, half)
    return call(
        own, "down_own", (steps,), (here,),
        in_specs + [pl.BlockSpec((tall, half), lambda i, *_: (i, 0))],
        [pl.BlockSpec(block, lambda i, *_: (i, 0, 0))] * 4,
        [shaped((8 * pieces, 8, half), BF16)] * 4,
        [pltpu.VMEM((1, 2, 2, 2, pieces, 8, half), F32)],
        flops, 11e6, (active, grad_second, got),
    )


def up_terms(grad_second, slope, hidden_t, w_up, w_down, here, which, chunk, block, so_far=None, got=None):
    rows, width = grad_second.shape
    ff = w_up.shape[1]
    half = ff // 2
    steps = half // chunk
    blocks = rows // block
    pieces = width // 32 // 8
    more = so_far is not None

    def kernel(here_s, *refs):
        gs_ref, dg_ref, ht_ref, wu_ref, wd_ref = refs[:5]
        refs = refs[5:]
        if more:
            so_far_ref, refs = refs[0], refs[1:]
        if got is not None:
            got_ref, refs = refs[0], refs[1:]
            outs, refs = refs[:4], refs[4:]
        else:
            out_ref, refs = refs[0], refs[1:]
        gh_ref, bu_ref, gi_scr = refs[:3]
        step = pl.program_id(0)

        @pl.when(step == 0)
        def _():
            gh_ref[...] = so_far_ref[...] if more else jnp.zeros_like(gh_ref)

        sums = jnp.zeros((1, chunk), F32)
        for number in range(blocks):
            base = slice(number * block, (number + 1) * block)
            grad_active = dot_t(gs_ref[base, :], wd_ref[...])
            low = (grad_active * dg_ref[base, :].astype(F32)).astype(BF16)
            gi_scr[base, :] = low
            sums += column_sum(low.astype(F32))
            gh_ref[base, :] += dot_t(low, wu_ref[...])
        bu_ref[...] = sums
        term = dot(ht_ref[...], gi_scr[...])
        if got is None:
            out_ref[...] = term.astype(BF16)
        else:
            scratch = refs[3]
            term += got_ref[...].astype(F32)
            scratch[...] = term.reshape(scratch.shape)
            deal(scratch, here_s, outs, 4, pieces)

    def col(i, here_s):
        return here_s[which] * steps + i

    in_specs = [
        once((rows, width)),
        pl.BlockSpec((rows, chunk), lambda i, h: (0, col(i, h))),
        once((width, rows)),
        pl.BlockSpec((width, chunk), lambda i, h: (0, col(i, h))),
        pl.BlockSpec((chunk, width), lambda i, h: (col(i, h), 0)),
    ]
    args = [grad_second, slope, hidden_t, w_up, w_down]
    if more:
        in_specs.append(once((rows, width)))
        args.append(so_far)
    scratch = [pltpu.VMEM((rows, chunk), BF16)]
    if got is None:
        out_specs = [pl.BlockSpec((width, chunk), lambda i, *_: (0, i))]
        out_shape = [shaped((width, half), BF16)]
    else:
        in_specs.append(pl.BlockSpec((width, chunk), lambda i, *_: (0, i)))
        args.append(got)
        out_specs = [pl.BlockSpec((8 * pieces, 8, chunk), lambda i, *_: (0, 0, i))] * 4
        out_shape = [shaped((8 * pieces, 8, half), BF16)] * 4
        scratch.append(pltpu.VMEM((4, 2, 2, 2, pieces, 8, chunk), F32))
    return call(
        kernel, "up_give" if got is None else "up_own", (steps,), (here,), in_specs,
        out_specs + [once((rows, width)), pl.BlockSpec((1, chunk), lambda i, *_: (0, i))],
        out_shape + [shaped((rows, width), F32), shaped((1, half), F32)],
        scratch, 6 * rows * width * half, 20e6, args,
    )


def attention_backward(gh, gres, n_attn, spread, table, w_out, qkv, probs, span, rows_step):
    rows, width = gh.shape
    pairs = width // LANES
    per_step = rows_step // span

    def kernel(gh_ref, gres_ref, n_ref, s_ref, tab_ref, wo_ref, qkv_ref, p_ref, gr_ref, gb_ref, gm_ref, vec_ref, ga_scr):
        step = pl.program_id(0)
        low_b, high_b, low_m = head_masks()

        @pl.when(step == 0)
        def _():
            vec_ref[...] = jnp.zeros_like(vec_ref)

        normed = n_ref[...]
        grad_hidden = gh_ref[...] + gres_ref[...]
        resid = norm_backward(grad_hidden, normed, s_ref[:, :1], tab_ref[ROW_GA : ROW_GA + 1, :])
        gr_ref[...] = resid
        low = resid.astype(BF16)
        gb_ref[...] = low
        vec_ref[2:3, :] += column_sum(low.astype(F32))
        vec_ref[3:4, :] += column_sum(grad_hidden * normed)
        vec_ref[4:5, :] += column_sum(grad_hidden)
        ga_scr[...] = dot_t(low, wo_ref[...]).astype(BF16)
        for inner in range(per_step):
            base = slice(inner * span, (inner + 1) * span)
            for pair in range(pairs):
                cols = slice(pair * LANES, (pair + 1) * LANES)
                k_cols = slice(width + pair * LANES, width + (pair + 1) * LANES)
                v_cols = slice(2 * width + pair * LANES, 2 * width + (pair + 1) * LANES)
                q, k, v = qkv_ref[base, cols], qkv_ref[base, k_cols], qkv_ref[base, v_cols]
                grad = ga_scr[base, cols]
                grads = jnp.concatenate([grad * low_b, grad * high_b], axis=0)
                both = jnp.concatenate([q * low_b, q * high_b], axis=0)
                weights = p_ref[inner, pair]
                wide = weights.astype(F32)
                grad_probs = dot_t(grads, v)
                balance = jnp.sum(wide * grad_probs, axis=-1, keepdims=True)
                grad_logits = (wide * (grad_probs - balance)).astype(BF16)
                mix = dot(grad_logits, k)
                grad_q = jnp.where(low_m, mix[:span], mix[span:]).astype(BF16) * jnp.bfloat16(0.125)
                grad_v = t_dot(weights, grads).astype(BF16)
                gm_ref[base, cols] = grad_q
                gm_ref[base, k_cols] = t_dot(grad_logits, both).astype(BF16)
                gm_ref[base, v_cols] = grad_v
                vec_ref[0:1, cols] += column_sum(grad_q.astype(F32))
                vec_ref[1:2, cols] += column_sum(grad_v.astype(F32))

    def rows_of(cols):
        return pl.BlockSpec((rows_step, cols), lambda i: (i, 0))

    return call(
        kernel,
        "attn_bwd",
        (rows // rows_step,),
        (),
        [
            rows_of(width), rows_of(width), rows_of(width), rows_of(LANES),
            once((8, width)), once((width, width)), rows_of(3 * width),
            pl.BlockSpec((per_step, pairs, 2 * span, span), lambda i: (i, 0, 0, 0)),
        ],
        [rows_of(width), rows_of(width), rows_of(3 * width), full((8, width))],
        [
            shaped((rows, width), F32), shaped((rows, width), BF16),
            shaped((rows, 3 * width), BF16), shaped((8, width), F32),
        ],
        [pltpu.VMEM((rows_step, width), BF16)],
        8 * rows * width * width * 2,
        34e6,
        (gh, gres, n_attn, spread, table, w_out, qkv, probs),
    )


def projection_terms(x, grad_mixed, attended, grad_branch, vectors, here, which, got=None):
    rows, width = x.shape
    part = width // 2
    pieces = width // 32 // 8

    def product(refs):
        x_ref, gm_ref, att_ref, gb_ref, scr = refs
        step = pl.program_id(0)

        @pl.when(step < 3)
        def _():
            scr[...] = t_dot(x_ref[...], gm_ref[...])

        @pl.when(step == 3)
        def _():
            scr[...] = t_dot(att_ref[...], gb_ref[...])

    def give(here_s, x_ref, gm_ref, att_ref, gb_ref, vec_ref, out_ref, scr):
        product((x_ref, gm_ref, att_ref, gb_ref, scr))
        out_ref[:width, :] = scr[...].astype(BF16)
        out_ref[width:, :] = vec_ref[...].astype(BF16)

    def own(here_s, x_ref, gm_ref, att_ref, gb_ref, vec_ref, got_ref, send_a, keep_a, send_b, keep_b, scr, cut):
        product((x_ref, gm_ref, att_ref, gb_ref, scr))
        term = scr[...] + got_ref[:width, :].astype(F32)
        cut[...] = term.reshape(cut.shape)
        deal(cut, here_s, (send_a, keep_a, send_b, keep_b), 4, pieces)
        extra = (vec_ref[...] + got_ref[width:, :].astype(F32)).astype(BF16)
        send_a[8 * pieces] = extra
        keep_a[8 * pieces] = extra

    in_specs = [
        once((rows, width)),
        pl.BlockSpec((rows, part), lambda i, h: (0, h[which] * 3 + jnp.minimum(i, 2))),
        once((rows, width)),
        pl.BlockSpec((rows, part), lambda i, h: (0, h[which]), pipeline_mode=pl.Buffered(1)),
        pl.BlockSpec((8, part), lambda i, h: (0, i)),
    ]
    args = [x, grad_mixed, attended, grad_branch, vectors]
    flops = 4 * rows * width * width
    if got is None:
        return call(
            give, "proj_give", (4,), (here,), in_specs,
            pl.BlockSpec((width + 8, part), lambda i, *_: (0, i)),
            shaped((width + 8, 4 * part), BF16),
            [pltpu.VMEM((width, part), F32)], flops, 9e6, args,
        )
    return call(
        own, "proj_own", (4,), (here,),
        in_specs + [pl.BlockSpec((width + 8, part), lambda i, *_: (0, i))],
        [
            pl.BlockSpec((8 * pieces + extra, 8, part), lambda i, *_: (0, 0, i))
            for extra in (1, 1, 0, 0)
        ],
        [shaped((8 * pieces + extra, 8, 4 * part), BF16) for extra in (1, 1, 0, 0)],
        [pltpu.VMEM((width, part), F32), pltpu.VMEM((4, 2, 2, 2, pieces, 8, part), F32)],
        flops, 11e6, args + [got],
    )


def input_gradient(grad_mixed, w_qkv, grad_resid, rows_step):
    rows, width = grad_resid.shape

    def kernel(gm_ref, wq_ref, gr_ref, out_ref):
        out_ref[...] = (dot_t(gm_ref[...], wq_ref[...]) + gr_ref[...]).astype(BF16)

    return call(
        kernel, "input_grad", (rows // rows_step,), (),
        [
            pl.BlockSpec((rows_step, 3 * width), lambda i: (i, 0)),
            once((width, 3 * width)),
            pl.BlockSpec((rows_step, width), lambda i: (i, 0)),
        ],
        pl.BlockSpec((rows_step, width), lambda i: (i, 0)),
        shaped((rows, width), BF16), [], 6 * rows * width * width, 13e6,
        (grad_mixed, w_qkv, grad_resid),
    )


def add_call(kernel, name, here, args, outs):
    moved = sum(item.size * 2 for item in args) + sum(2 * a * b * c for a, b, c in outs)
    return call(
        kernel, name, (), (here,), [pl.BlockSpec(memory_space=pltpu.VMEM)] * len(args),
        [pl.BlockSpec(memory_space=pltpu.VMEM)] * len(outs),
        [shaped(shape, BF16) for shape in outs], [], moved // 4, moved, args,
    )


def add(left, right):
    return (left.astype(F32) + right.astype(F32)).astype(BF16)


def fold_second(keep_a, got_a, keep_b, got_b, here, pieces, extra):
    cols = keep_a.shape[2]

    def kernel(here_s, ka, ga, kb, gb, send_a, left_a, send_b, left_b):
        x, y = here_s[2], here_s[3]
        for z in range(4):
            at = pl.ds(z * pieces, pieces)

            def sum_of(keep, got, other):
                rows = pl.ds(z * 2 * pieces + other * pieces, pieces)
                return add(keep[rows], got[rows])

            send_a[at] = sum_of(ka, ga, 1 - y)
            left_a[at] = sum_of(ka, ga, y)
            send_b[at] = sum_of(kb, gb, 1 - x)
            left_b[at] = sum_of(kb, gb, x)
        if extra:
            total = add(ka[8 * pieces], ga[8 * pieces])
            send_a[4 * pieces] = total
            left_a[4 * pieces] = total

    a_shape, b_shape = (4 * pieces + extra, 8, cols), (4 * pieces, 8, cols)
    return add_call(
        kernel, "fold_second", here, (keep_a, got_a, keep_b, got_b), (a_shape, a_shape, b_shape, b_shape)
    )


def fold_third(keep_a, got_a, keep_b, got_b, here, pieces, extra):
    cols = keep_a.shape[2]

    def kernel(here_s, ka, ga, kb, gb, send, left):
        low = here_s[4]
        for high in range(2):
            for number, (keep, got) in enumerate(((ka, ga), (kb, gb))):
                at = pl.ds((high * 2 + number) * pieces, pieces)
                for out, pick in ((send, 1 - low), (left, low)):
                    rows = pl.ds((high * 2 + pick) * pieces, pieces)
                    out[at] = add(keep[rows], got[rows])
        if extra:
            total = add(ka[4 * pieces], ga[4 * pieces])
            send[4 * pieces] = total
            left[4 * pieces] = total

    shape = (4 * pieces + extra, 8, cols)
    return add_call(kernel, "fold_third", here, (keep_a, got_a, keep_b, got_b), (shape, shape))


def fold_fourth(keep, got, here, pieces, extra):
    cols = keep.shape[2]

    def kernel(here_s, keep_ref, got_ref, send, left):
        high = here_s[5]
        for out, pick in ((send, 1 - high), (left, high)):
            rows = pl.ds(pick * 2 * pieces, 2 * pieces)
            out[: 2 * pieces] = add(keep_ref[rows], got_ref[rows])
        if extra:
            total = add(keep_ref[4 * pieces], got_ref[4 * pieces])
            send[2 * pieces] = total
            left[2 * pieces] = total

    shape = (2 * pieces + extra, 8, cols)
    return add_call(kernel, "fold_fourth", here, (keep, got), (shape, shape))


def fold_last(keep, got, here, pieces, extra):
    cols = keep.shape[2]

    def kernel(here_s, keep_ref, got_ref, *outs):
        outs[0][...] = add(keep_ref[: 2 * pieces], got_ref[: 2 * pieces])
        if extra:
            outs[1][0] = add(keep_ref[2 * pieces], got_ref[2 * pieces])

    shapes = [(2 * pieces, 8, cols)] + [(1, 8, cols)] * extra
    return add_call(kernel, "fold_last", here, (keep, got), shapes)


def whole_block(mine, over_x, over_core, over_both, here, vectors=None):
    count, _, cols = mine.shape
    rows = 8 * count

    def pick(here_s, refs, core, side):
        me, gx, gc, gd = [item[...].astype(F32).reshape(rows, cols) for item in refs]
        same_core, same_side = here_s[0] == core, here_s[2] == side
        return jnp.where(
            same_core, jnp.where(same_side, me, gx), jnp.where(same_side, gc, gd)
        )

    def kernel(here_s, me, gx, gc, gd, *rest):
        outs = rest[1:] if vectors is not None else rest
        for core in range(2):
            for side in range(2):
                value = pick(here_s, (me, gx, gc, gd), core, side)
                at = slice(side * rows, (side + 1) * rows)
                if vectors is None:
                    outs[0][at, core * cols : (core + 1) * cols] = value
                else:
                    cut = cols // 4 * 3
                    outs[0][at, core * cut : (core + 1) * cut] = value[:, :cut]
                    outs[1][at, core * (cols - cut) : (core + 1) * (cols - cut)] = value[:, cut:]
        if vectors is not None:
            table = rest[0][0].astype(F32)
            wide = here_s[6]
            width = cols // 2
            small = width // 8
            left = pltpu.roll(table[:, :width], lax.rem(width - wide * small, width), 1)
            right = pltpu.roll(table[:, width:], lax.rem(width - wide * small, width), 1)
            for row in range(4):
                outs[2 + 2 * row][...] = left[row : row + 1, :small]
                outs[3 + 2 * row][...] = right[row : row + 1, :small]
            large = 2 * cols // 8
            turned = pltpu.roll(table, lax.rem(cols - lax.rem(wide, 4) * large, cols), 1)
            outs[10][...] = jnp.where(wide < 4, turned[4:5, :large], turned[5:6, :large])

    if vectors is None:
        shapes = [(2 * rows, 2 * cols)]
        args = (mine, over_x, over_core, over_both)
    else:
        cut = cols // 4 * 3
        shapes = [(2 * rows, 2 * cut), (2 * rows, 2 * (cols - cut))]
        shapes += [(1, cols // 16)] * 8 + [(1, cols // 4)]
        args = (mine, over_x, over_core, over_both, vectors)
    return call(
        kernel, "whole_block", (), (here,), [pl.BlockSpec(memory_space=pltpu.VMEM)] * len(args),
        [pl.BlockSpec(memory_space=pltpu.VMEM)] * len(shapes),
        [shaped(shape, F32) for shape in shapes], [], 1e6, 4e6, args,
    )


def swap(item, axis, step):
    count = lax.axis_size(axis)
    return lax.ppermute(item, axis, [(index, index ^ step) for index in range(count)])


def finish(dealt, here, pieces, extra):
    send_a, keep_a, send_b, keep_b = dealt
    got_a, got_b = swap(send_a, "narrow", 2), swap(send_b, "wide", 1)
    send_a, keep_a, send_b, keep_b = fold_second(keep_a, got_a, keep_b, got_b, here, pieces, extra)
    got_a, got_b = swap(send_a, "wide", 1), swap(send_b, "narrow", 2)
    send, keep = fold_third(keep_a, got_a, keep_b, got_b, here, pieces, extra)
    send, keep = fold_fourth(keep, swap(send, "wide", 2), here, pieces, extra)
    last = fold_last(keep, swap(send, "wide", 4), here, pieces, extra)
    mine = last[0]
    parts = (mine, swap(mine, "narrow", 2), swap(mine, "narrow", 1), swap(mine, "narrow", 3))
    return whole_block(*parts, here, *last[1:])


def regroup_rows(sent, bucket, wide_count, batches):
    span, width = sent.shape[1:]
    if wide_count == batches:
        got = lax.all_to_all(sent, "wide", split_axis=0, concat_axis=0, tiled=True)
        return got.reshape(batches * span, width)
    send = jnp.zeros((wide_count, span, width), sent.dtype).at[bucket].set(sent)
    got = lax.all_to_all(send, "wide", split_axis=0, concat_axis=0, tiled=True)
    marks = jnp.zeros((wide_count, 1), jnp.int32).at[bucket].set(1)
    filled = lax.all_to_all(marks, "wide", split_axis=0, concat_axis=0, tiled=True)[:, 0]
    place = jnp.where(filled > 0, jnp.cumsum(filled) - filled, batches)
    chosen = (
        jnp.zeros((batches,), jnp.int32)
        .at[place]
        .set(jnp.arange(wide_count, dtype=jnp.int32), mode="drop")
    )
    return got[chosen].reshape(batches * span, width)


def sum_anywhere(item, wide_count, narrow_count):
    blocks = item.astype(F32).reshape(wide_count, -1)
    extent = blocks.shape[1]
    padded = (extent + narrow_count - 1) // narrow_count * narrow_count
    blocks = jnp.pad(blocks, ((0, 0), (0, padded - extent))).reshape(-1)
    share = lax.psum_scatter(blocks, ("wide", "narrow"), scatter_dimension=0, tiled=True)
    whole = lax.all_gather(share.astype(BF16), "narrow", axis=0, tiled=True).astype(F32)
    return whole[:extent].reshape((item.shape[0] // wide_count,) + item.shape[1:])


def body(
    tokens, bucket, lengths, pairing, targets, w_qkv, bias_q, bias_v, w_out, bias_out,
    gain_attn, shift_attn, w_up, bias_up, w_down, bias_down, gain_ffn, shift_ffn,
):
    wide_count, narrow_count = lax.axis_size("wide"), lax.axis_size("narrow")
    batches = bucket.shape[0]
    rows, width = tokens.shape
    span = rows // batches
    paired = (wide_count, narrow_count) == (8, 4)
    wide, narrow = lax.axis_index("wide"), lax.axis_index("narrow")
    if paired:
        core = narrow % 2
        here = jnp.stack(
            [core, 1 - core, narrow // 2, wide % 2, wide // 2 % 2, wide // 4, wide, narrow]
        ).astype(jnp.int32)
    else:
        here = jnp.arange(8, dtype=jnp.int32)
    table = jnp.stack(
        [bias_q, bias_v, bias_out, gain_attn, shift_attn, bias_down, gain_ffn, shift_ffn]
    ).astype(F32)
    ordered = wide_count == batches
    slots = bucket if ordered else jnp.arange(batches, dtype=jnp.int32)

    qkv, probs, attended, n_attn, spread, sid = attention_forward(
        tokens, w_qkv, w_out, table, bucket, lengths, wide_count // batches, span, 2 * span
    )
    active, slope, hidden_t, sent, gres, grad_second, vec_ffn = feed_forward(
        n_attn, w_up, w_down, bias_up.reshape(1, -1), table, sid, slots, pairing, targets,
        batches, 512, 256,
    )
    encoded = regroup_rows(sent, bucket, wide_count, batches)
    ups = (grad_second, slope, hidden_t, w_up, w_down, here)
    down_sent = down_terms(active, grad_second, here, 1)
    up_sent, gh, bup_sent = up_terms(*ups, 1, 512, 256)
    if paired:
        down_dealt = down_terms(active, grad_second, here, 0, swap(down_sent, "narrow", 1))
        *up_dealt, gh, bup_kept = up_terms(*ups, 0, 512, 256, gh, swap(up_sent, "narrow", 1))
    else:
        down_kept = down_terms(active, grad_second, here, 0)
        up_kept, gh, bup_kept = up_terms(*ups, 0, 512, 256, gh)
    gr, gb, gm, vec_attn = attention_backward(
        gh, gres, n_attn, spread, table, w_out, qkv, probs, span, 2 * span
    )
    if paired:
        first_up = jnp.where(here[0] == 0, bup_kept, bup_sent)
        second_up = jnp.where(here[0] == 0, bup_sent, bup_kept)
    else:
        first_up, second_up = bup_kept, bup_sent
    vectors = jnp.concatenate(
        [
            vec_ffn[:2].reshape(1, -1),
            jnp.concatenate([vec_ffn[2:3], vec_attn[0:1]], axis=1),
            vec_attn[1:5].reshape(2, -1),
            first_up,
            second_up,
            jnp.zeros((2, 2 * width), F32),
        ],
        axis=0,
    )
    projections = (tokens, gm, attended, gb, vectors, here)
    proj_sent = projection_terms(*projections, 1)
    grad_tokens = input_gradient(gm, w_qkv, gr, 2 * span)
    if paired:
        proj_dealt = projection_terms(*projections, 0, swap(proj_sent, "narrow", 1))
        (grad_w_down,) = finish(down_dealt, here, 12, 0)
        (grad_w_up,) = finish(up_dealt, here, 3, 0)
        grad_w_qkv, grad_w_out, *small = finish(proj_dealt, here, 3, 1)
        small = [item.reshape(-1) for item in small]
    else:
        proj_kept = projection_terms(*projections, 0)
        total = partial(sum_anywhere, wide_count=wide_count, narrow_count=narrow_count)
        cut = width // 2 * 3
        grad_w_down = total(jnp.concatenate([down_kept, down_sent], axis=1))
        grad_w_up = total(jnp.concatenate([up_kept, up_sent], axis=1))
        grad_w_qkv = total(jnp.concatenate([proj_kept[:width, :cut], proj_sent[:width, :cut]], axis=1))
        grad_w_out = total(jnp.concatenate([proj_kept[:width, cut:], proj_sent[:width, cut:]], axis=1))
        small = [total(item) for item in vectors[:4].reshape(8, width)]
        small.append(total(vectors[4:6].reshape(-1)))
    gain_out, shift_out, b_down, b_q, b_v, b_out, g_attn, s_attn, b_up = small
    return (
        encoded, grad_tokens, grad_w_qkv, b_q, b_v, grad_w_out, b_out, g_attn, s_attn,
        grad_w_up, b_up, grad_w_down, b_down, gain_out, shift_out,
    )


def solution(mesh):
    split = P(("wide", "narrow"))
    in_specs = (
        P(("wide", "narrow"), None), split, split, P(("wide", "narrow"), None), split,
    ) + (P(),) * 13
    out_specs = (
        P(("wide", "narrow"), None), P(("wide", "narrow"), None),
        P("wide", None), P("wide"), P("wide"), P("wide", None), P("wide"), P("wide"), P("wide"),
        P("wide", None), P("wide"), P("wide", None), P("wide"), P("wide"), P("wide"),
    )
    return jax.shard_map(body, mesh=mesh, in_specs=in_specs, out_specs=out_specs, check_vma=False)
```

time: 449 us -> 277 us (0.62)
  Pallas kernels: 0 us -> 180 us
  matrix products: 142 us -> 0 us
  other arithmetic: 86.1 us -> 1.89 us
  local copies, waits for them, and re-layouts: 100 us -> 23.3 us
  waiting for transfers between devices: 67.5 us -> 27.5 us
    pallas_call x0 -> x25, Pallas kernels: none -> 180 us  [call(): pl.pallas_call(kernel, grid_spec=pltpu.PrefetchScalarGridSpec(num_scalar_...]
    dot_general x20 -> x0, matrix products: 142 us -> none  [the longest x4 42.4 us: times_transpose(): lax.dot_general(left, right, (((1,), (1,)), ((), ())), preferred_element_...]
    convert_element_type x45 -> x1, other arithmetic: 46.3 us -> 0.61 us  [body(): table = jnp.stack([bias_q, bias_v, bias_out, gain_attn, shift_attn, bias_...]
    ppermute x41 -> x30, waiting for transfers between devices: 67.5 us -> 27.5 us  [swap(): lax.ppermute(item, axis, [(index, index ^ step) for index in range(count)])]
    unnamed x170 -> x55, local copies, waits for them, and re-layouts: 33.7 us -> 12.9 us
    convert_element_type x10 -> x0, local copies, waits for them, and re-layouts: 19.5 us -> none  [the longest x4 7.74 us: fold(): got = swap(give.astype(jnp.bfloat16), axis, step)]
    reduce_sum x13 -> x0, other arithmetic: 16.9 us -> none  [the longest x1 4.69 us: body(): grad_bias_out = jnp.sum(grad_branch_low.astype(jnp.float32), axis=0)]
    reshape x11 -> x2, local copies, waits for them, and re-layouts: 12.3 us -> 1.32 us  [the longest x1 1.29 us: body(): bias_up.reshape(1, -1)]
  transfers between devices with their start and end apart: 42 -> 31, of which waited for: 23 -> 8; matrix products, arithmetic and copies ran while one was open for 46% -> 1% of each run, Pallas kernels for 0% -> 41%
where the time goes in v2:
time: 277 us; the launch traced here: 275 us
  Pallas kernels  180 us (65%)
  starting transfers between devices  41.1 us (15%)
  waiting for transfers between devices  27.5 us (10%)
  local copies, waits for them, and re-layouts  23.3 us (8%)
    pallas_call x25, Pallas kernels, call(): pl.pallas_call(kernel, grid_spec=pltpu.PrefetchScalarGridSpec(num_scalar_...  180 us
    ppermute x30, starting transfers between devices, swap(): lax.ppermute(item, axis, [(index, index ^ step) for index in range(count)])  34.3 us
    ppermute x30, waiting for transfers between devices, swap(): lax.ppermute(item, axis, [(index, index ^ step) for index in range(count)])  27.5 us
    unnamed x55, local copies, waits for them, and re-layouts  12.9 us
    all_to_all x1, starting transfers between devices, regroup_rows(): got = lax.all_to_all(sent, 'wide', split_axis=0, concat_axis=0, tiled=True)  6.83 us
  transfers between devices with their start and end apart: 31, of which 8 were waited for; matrix products, arithmetic and copies ran while one was open for 1% of the time, Pallas kernels for 41%

profile of v2, /device:TPU:0, one launch (start us, length us, event | category | flops | bytes accessed | tf_op | source)
XLA Modules:
  0.0 274.5 jit_solution(8504567143694751705)
XLA Ops:
  6.8 1.3 reshape.69.bu_ref
  8.1 16.6 %attn_fwd.1 = (bf16[1024,2304]{1,0:T(8,128)(2,1)}, bf16[8,6,256,128]{3,2,1,0:T(8,128)(2,1)}, bf16[1024,768]{1,0:T(8,128)(2,1)}, f32[1024,768]{1,0:T(8,128)}, f32[1024,128]{1,0:T(8,128)}, /*index=5*/s32[8,8,128]{2,1,0:T(8,128)}) custom-call(s32[8]{0:T(128)} %slots_s.1, s32[26]{0:T(128)} %lengths_s.1, bf16[1024,768]{1,0:T(8,128)(2,1)} %x_ref.5, ...), custom_call_target="tpu_custom_call" | custom-call | flops 9663676416 | bytes 30000000 | tf_op jit(solution)/shard_map/attn_fwd/pallas_call | solution.py:52
  24.8 32.3 %ffn_fwd.1 = (bf16[1024,3072]{1,0:T(8,128)(2,1)}, bf16[1024,3072]{1,0:T(8,128)(2,1)}, bf16[768,1024]{1,0:T(8,128)(2,1)}, bf16[8,128,768]{2,1,0:T(8,128)(2,1)}, f...) custom-call(s32[8]{0:T(128)} %slots_s.1, s32[1,26]{1,0:T(1,128)} %pairing_s.1, f32[13]{0:T(128)} %targets_s.1, ...), custom_call_target="tpu_custom_call" | custom-call | flops 19327352832 | bytes 40000000 | tf_op jit(solution)/shard_map/ffn_fwd/pallas_call | solution.py:52
  57.7 14.1 %up_give.1 = (bf16[768,1536]{1,0:T(8,128)(2,1)}, f32[1024,768]{1,0:T(8,128)}, f32[1,1536]{1,0:T(1,128)}) custom-call(s32[8]{0:T(128)} %stack.71.here_s, bf16[1024,768]{1,0:T(8,128)(2,1)} %get-tuple-element.89.refs_0_.gs_ref, bf16[1024,3072]{1,0:T(8,128)(2,1)} %get-tuple-element.90.refs_1_, bf16[768,1024]{1,0:T(8,128)(2,1)} %get-tuple-element.91.refs_2_, ...), custom_call_target="tpu_custom_call" | custom-call | flops 7247757312 | bytes 20000000 | tf_op jit(solution)/shard_map/up_give/pallas_call | solution.py:52
  72.3 7.9 %down_give.1 = bf16[3072,384]{1,0:T(8,128)(2,1)} custom-call(s32[8]{0:T(128)} %stack.71.here_s, bf16[1024,3072]{1,0:T(8,128)(2,1)} %get-tuple-element.141.act_ref, bf16[1024,768]{1,0:T(8,128)(2,1)} %get-tuple-element.89.refs_0_.gs_ref), custom_call_target="tpu_custom_call" | custom-call | flops 2415919104 | bytes 9000000 | tf_op jit(solution)/shard_map/down_give/pallas_call | solution.py:52
  80.2 0.7 slice.13
  81.0 0.7 slice_bitcast_fusion
  81.7 1.4 copy-done.25
  83.1 16.2 %up_own.1 = (bf16[24,8,1536]{2,1,0:T(8,128)(2,1)}, bf16[24,8,1536]{2,1,0:T(8,128)(2,1)}, bf16[24,8,1536]{2,1,0:T(8,128)(2,1)}, bf16[24,8,1536]{2,1,0:T(8,128)(2,...) custom-call(s32[8]{0:T(128)} %stack.71.here_s, bf16[1024,768]{1,0:T(8,128)(2,1)} %get-tuple-element.89.refs_0_.gs_ref, ...), custom_call_target="tpu_custom_call" | custom-call | flops 7247757312 | bytes 20000000 | tf_op jit(solution)/shard_map/up_own/pallas_call | solution.py:52
  99.3 14.9 %attn_bwd.1 = (f32[1024,768]{1,0:T(8,128)}, bf16[1024,768]{1,0:T(8,128)(2,1)}, bf16[1024,2304]{1,0:T(8,128)(2,1)}, f32[8,768]{1,0:T(8,128)}) custom-call(f32[1024,768]{1,0:T(8,128)} %get-tuple-element.94.gh_ref, f32[1024,768]{1,0:T(8,128)} %get-tuple-element.95.gres_ref, f32[1024,768]{1,0:T(8,128)} %get-tuple-element.86.n_ref, ...), custom_call_target="tpu_custom_call" | custom-call | flops 9663676416 | bytes 34000000 | tf_op jit(solution)/shard_map/attn_bwd/pallas_call | solution.py:52
  114.2 0.7 slice.14
  114.9 0.7 slice.15
  116.4 8.5 %proj_give.1 = bf16[776,1536]{1,0:T(8,128)(2,1)} custom-call(s32[8]{0:T(128)} %stack.71.here_s, bf16[1024,768]{1,0:T(8,128)(2,1)} %x_ref.5, bf16[1024,2304]{1,0:T(8,128)(2,1)} %get-tuple-element.99.gm_ref, bf16[1024,768]{1,0:T(8,128)(2,1)} %get-tuple-element.101.att_ref, bf16[1024,768]{1,0:T(8,128)(2,1)} %get-tuple-element.102.gb_ref, ...), custom_call_target="tpu_custom_call" | custom-call | flops 2415919104 | bytes 9000000 | tf_op jit(solution)/shard_map/proj_give/pallas_call | solution.py:52
  125.4 6.8 %all-to-all-start = ((bf16[8,128,768]{2,1,0:T(8,128)(2,1)}), bf16[8,128,768]{2,1,0:T(8,128)(2,1)S(1)}, u32[]{:S(2)}, u32[]{:S(2)}) async-start(bf16[8,128,768]{2,1,0:T(8,128)(2,1)} %get-tuple-element.88), calls=%async_computation | async-start | bytes 3145728 | tf_op jit(solution)/shard_map/all_to_all | solution.py:799
  132.3 8.4 %down_own.1 = (bf16[96,8,384]{2,1,0:T(8,128)(2,1)}, bf16[96,8,384]{2,1,0:T(8,128)(2,1)}, bf16[96,8,384]{2,1,0:T(8,128)(2,1)}, bf16[96,8,384]{2,1,0:T(8,128)(2,1)}) custom-call(s32[8]{0:T(128)} %stack.71.here_s, bf16[1024,3072]{1,0:T(8,128)(2,1)} %get-tuple-element.141.act_ref, bf16[1024,768]{1,0:T(8,128)(2,1)} %get-tuple-element.89.refs_0_.gs_ref, ...), custom_call_target="tpu_custom_call" | custom-call | flops 2415919104 | bytes 11000000 | tf_op jit(solution)/shard_map/down_own/pallas_call | solution.py:52
  140.7 1.5 collective-permute-start.21
  142.2 2.0 collective-permute-start.22
  144.7 9.2 %proj_own.1 = (bf16[25,8,1536]{2,1,0:T(8,128)(2,1)}, bf16[25,8,1536]{2,1,0:T(8,128)(2,1)}, bf16[24,8,1536]{2,1,0:T(8,128)(2,1)}, bf16[24,8,1536]{2,1,0:T(8,128)(2,1)}) custom-call(s32[8]{0:T(128)} %stack.71.here_s, bf16[1024,768]{1,0:T(8,128)(2,1)} %x_ref.5, bf16[1024,2304]{1,0:T(8,128)(2,1)} %get-tuple-element.99.gm_ref, ...), custom_call_target="tpu_custom_call" | custom-call | flops 2415919104 | bytes 11000000 | tf_op jit(solution)/shard_map/proj_own/pallas_call | solution.py:52
  153.9 2.0 collective-permute-start.3
  156.0 1.1 collective-permute-done.21.ga
  157.1 0.8 copy-done.3
  157.9 1.5 collective-permute-start.2
  159.4 6.5 %collective-permute-done.22.gb = bf16[96,8,384]{2,1,0:T(8,128)(2,1)} collective-permute-done((bf16[96,8,384]{2,1,0:T(8,128)(2,1)}, bf16[96,8,384]{2,1,0:T(8,128)(2,1)}, u32[]{:S(2)}, u32[]{:S(2)}) %collective-permute-start.22) | collective-permute-done | bytes 589856 | tf_op jit(solution)/shard_map/ppermute | solution.py:780
  165.9 3.4 %fold_second.5 = (bf16[48,8,384]{2,1,0:T(8,128)(2,1)}, bf16[48,8,384]{2,1,0:T(8,128)(2,1)}, bf16[48,8,384]{2,1,0:T(8,128)(2,1)}, bf16[48,8,384]{2,1,0:T(8,128)(2,1)}) custom-call(s32[8]{0:T(128)} %stack.71.here_s, bf16[96,8,384]{2,1,0:T(8,128)(2,1)} %get-tuple-element.142.ka, bf16[96,8,384]{2,1,0:T(8,128)(2,1)} %copy-done.3, ...), custom_call_target="tpu_custom_call" | custom-call | flops 884736 | bytes 3538944 | tf_op jit(solution)/shard_map/fold_second/pallas_call | solution.py:52
  169.7 1.5 collective-permute-start.24
  171.2 7.2 %collective-permute-done.12.gb = bf16[24,8,1536]{2,1,0:T(8,128)(2,1)S(1)} collective-permute-done((bf16[24,8,1536]{2,1,0:T(8,128)(2,1)}, bf16[24,8,1536]{2,1,0:T(8,128)(2,1)S(1)}, u32[]{:S(2)}, u32[]{:S(2)}) %collective-permute-start.12) | collective-permute-done | bytes 589856 | tf_op jit(solution)/shard_map/ppermute | solution.py:780
  178.4 0.8 copy-done.2
  179.2 3.5 %fold_second.4 = (bf16[12,8,1536]{2,1,0:T(8,128)(2,1)}, bf16[12,8,1536]{2,1,0:T(8,128)(2,1)}, bf16[12,8,1536]{2,1,0:T(8,128)(2,1)}, bf16[12,8,1536]{2,1,0:T(8,128)(2,1)}) custom-call(s32[8]{0:T(128)} %stack.71.here_s, bf16[24,8,1536]{2,1,0:T(8,128)(2,1)} %get-tuple-element.128.ka, bf16[24,8,1536]{2,1,0:T(8,128)(2,1)} %copy-done.1, ...), custom_call_target="tpu_custom_call" | custom-call | flops 884736 | bytes 3538944 | tf_op jit(solution)/shard_map/fold_second/pallas_call | solution.py:52
  182.7 8.4 %collective-permute-done.3.gb = bf16[24,8,1536]{2,1,0:T(8,128)(2,1)} collective-permute-done((bf16[24,8,1536]{2,1,0:T(8,128)(2,1)}, bf16[24,8,1536]{2,1,0:T(8,128)(2,1)}, u32[]{:S(2)}, u32[]{:S(2)}) %collective-permute-start.3) | collective-permute-done | bytes 589856 | tf_op jit(solution)/shard_map/ppermute | solution.py:780
  191.2 1.5 collective-permute-start.14
  192.6 0.8 copy-done
  193.5 3.5 %fold_second.3 = (bf16[13,8,1536]{2,1,0:T(8,128)(2,1)}, bf16[13,8,1536]{2,1,0:T(8,128)(2,1)}, bf16[12,8,1536]{2,1,0:T(8,128)(2,1)}, bf16[12,8,1536]{2,1,0:T(8,128)(2,1)}) custom-call(s32[8]{0:T(128)} %stack.71.here_s, bf16[25,8,1536]{2,1,0:T(8,128)(2,1)} %get-tuple-element.107.ka, bf16[25,8,1536]{2,1,0:T(8,128)(2,1)} %copy-done, ...), custom_call_target="tpu_custom_call" | custom-call | flops 909312 | bytes 3637248 | tf_op jit(solution)/shard_map/fold_second/pallas_call | solution.py:52
  197.5 1.5 collective-permute-start.5
  199.0 2.9 %fold_third.5 = (bf16[48,8,384]{2,1,0:T(8,128)(2,1)}, bf16[48,8,384]{2,1,0:T(8,128)(2,1)}) custom-call(s32[8]{0:T(128)} %stack.71.here_s, bf16[48,8,384]{2,1,0:T(8,128)(2,1)} %get-tuple-element.146.ka, bf16[48,8,384]{2,1,0:T(8,128)(2,1)} %collective-permute-done.23.ga, bf16[48,8,384]{2,1,0:T(8,128)(2,1)} %get-tuple-element.148.kb, ...), custom_call_target="tpu_custom_call" | custom-call | flops 442368 | bytes 1769472 | tf_op jit(solution)/shard_map/fold_third/pallas_call | solution.py:52
  201.8 2.3 collective-permute-start.25
  204.2 0.7 copy-done.8
  204.9 2.8 %fold_third.4 = (bf16[12,8,1536]{2,1,0:T(8,128)(2,1)}, bf16[12,8,1536]{2,1,0:T(8,128)(2,1)}) custom-call(s32[8]{0:T(128)} %stack.71.here_s, bf16[12,8,1536]{2,1,0:T(8,128)(2,1)} %get-tuple-element.132.ka, bf16[12,8,1536]{2,1,0:T(8,128)(2,1)} %copy-done.8, bf16[12,8,1536]{2,1,0:T(8,128)(2,1)} %get-tuple-element.134.kb, bf16[12,8,1536]{2,1,0:T(8,128)(2,1)} %copy-done.9), custom_call_target="tpu_custom_call" | custom-call | flops 442368 | bytes 1769472 | tf_op jit(solution)/shard_map/fold_third/pallas_call | solution.py:52
  207.8 2.8 %collective-permute-start.15 = (bf16[12,8,1536]{2,1,0:T(8,128)(2,1)}, bf16[12,8,1536]{2,1,0:T(8,128)(2,1)S(1)}, u32[]{:S(2)}, u32[]{:S(2)}) collective-permute-start(bf16[12,8,1536]{2,1,0:T(8,128)(2,1)} %get-tuple-element.137), channel_id=1, source_target_pairs={{0,8},{4,12},{8,0},{12,4},{16,24},{20,28},{24,16},{28,20},{1,9},{5... | collective-permute-start | bytes 884744 | tf_op jit(solution)/shard_map/ppermute | solution.py:780
  210.6 0.7 copy-done.10
  211.4 2.9 %fold_third.3 = (bf16[13,8,1536]{2,1,0:T(8,128)(2,1)}, bf16[13,8,1536]{2,1,0:T(8,128)(2,1)}) custom-call(s32[8]{0:T(128)} %stack.71.here_s, bf16[13,8,1536]{2,1,0:T(8,128)(2,1)} %get-tuple-element.111.ka, bf16[13,8,1536]{2,1,0:T(8,128)(2,1)} %copy-done.4, bf16[12,8,1536]{2,1,0:T(8,128)(2,1)} %get-tuple-element.113.kb, bf16[12,8,1536]{2,1,0:T(8,128)(2,1)} %copy-done.10), custom_call_target="tpu_custom_call" | custom-call | flops 466944 | bytes 1867776 | tf_op jit(solution)/shard_map/fold_third/pallas_call | solution.py:52
  214.3 1.8 collective-permute-start.6
  216.1 0.7 copy-done.6
  216.8 2.5 fold_fourth.5
  219.2 4.8 %collective-permute-start.26 = (bf16[24,8,384]{2,1,0:T(8,128)(2,1)}, bf16[24,8,384]{2,1,0:T(8,128)(2,1)S(1)}, u32[]{:S(2)}, u32[]{:S(2)}) collective-permute-start(bf16[24,8,384]{2,1,0:T(8,128)(2,1)} %get-tuple-element.153), channel_id=1, source_target_pairs={{0,16},{4,20},{8,24},{12,28},{16,0},{20,4},{24,8},{28,12},{1,17},{... | collective-permute-start | bytes 442376 | tf_op jit(solution)/shard_map/ppermute | solution.py:780
  224.1 0.7 copy-done.7
  224.8 2.5 fold_fourth.4
  227.2 0.7 copy-done.5
  228.0 2.5 fold_fourth.3
  230.5 2.9 %collective-permute-start.7 = (bf16[7,8,1536]{2,1,0:T(8,128)(2,1)}, bf16[7,8,1536]{2,1,0:T(8,128)(2,1)S(1)}, u32[]{:S(2)}, u32[]{:S(2)}) collective-permute-start(bf16[7,8,1536]{2,1,0:T(8,128)(2,1)} %get-tuple-element.118), channel_id=1, source_target_pairs={{0,16},{4,20},{8,24},{12,28},{16,0},{20,4},{24,8},{28,12},{1,17},{... | collective-permute-start | bytes 516104 | tf_op jit(solution)/shard_map/ppermute | solution.py:780
  234.1 2.3 fold_last.5.me
  236.4 1.4 collective-permute-start.28
  237.8 0.7 collective-permute-start.27
  238.6 2.9 %collective-permute-done.16.got_ref = bf16[6,8,1536]{2,1,0:T(8,128)(2,1)S(1)} collective-permute-done((bf16[6,8,1536]{2,1,0:T(8,128)(2,1)}, bf16[6,8,1536]{2,1,0:T(8,128)(2,1)S(1)}, u32[]{:S(2)}, u32[]{:S(2)}) %collective-permute-start.16) | collective-permute-done | bytes 147488 | tf_op jit(solution)/shard_map/ppermute | solution.py:780
  242.1 2.3 fold_last.4.me
  245.8 2.4 fold_last.3
  248.2 1.1 collective-permute-start.17
  249.3 0.9 collective-permute-start.10
  250.7 1.1 collective-permute-start.8
  251.8 8.9 %input_grad.1 = bf16[1024,768]{1,0:T(8,128)(2,1)} custom-call(bf16[1024,2304]{1,0:T(8,128)(2,1)} %get-tuple-element.99.gm_ref, bf16[768,2304]{1,0:T(8,128)(2,1)} %wq_ref.3, f32[1024,768]{1,0:T(8,128)} %get-tuple-element.100.gr_ref), custom_call_target="tpu_custom_call" | custom-call | flops 3623878656 | bytes 13000000 | tf_op jit(solution)/shard_map/input_grad/pallas_call | solution.py:52
  260.7 3.1 %whole_block.5 = f32[384,768]{1,0:T(8,128)} custom-call(s32[8]{0:T(128)} %stack.71.here_s, bf16[24,8,384]{2,1,0:T(8,128)(2,1)} %fold_last.5.me, bf16[24,8,384]{2,1,0:T(8,128)(2,1)} %copy-done.14, bf16[24,8,384]{2,1,0:T(8,128)(2,1)} %copy-done.13, bf16[24,8,384]{2,1,0:T(8,128)(2,1)} %copy-done.12), custom_call_target="tpu_custom_call" | custom-call | flops 1000000 | bytes 4000000 | tf_op jit(solution)/shard_map/whole_block/pallas_call | solution.py:52
  265.1 3.1 %whole_block.4 = f32[96,3072]{1,0:T(8,128)} custom-call(s32[8]{0:T(128)} %stack.71.here_s, bf16[6,8,1536]{2,1,0:T(8,128)(2,1)} %fold_last.4.me, bf16[6,8,1536]{2,1,0:T(8,128)(2,1)} %copy-done.20, bf16[6,8,1536]{2,1,0:T(8,128)(2,1)} %copy-done.18, bf16[6,8,1536]{2,1,0:T(8,128)(2,1)} %copy-done.15), custom_call_target="tpu_custom_call" | custom-call | flops 1000000 | bytes 4000000 | tf_op jit(solution)/shard_map/whole_block/pallas_call | solution.py:52
  269.0 3.1 %whole_block.3 = (f32[96,2304]{1,0:T(8,128)}, f32[96,768]{1,0:T(8,128)}, f32[1,96]{1,0:T(1,128)}, f32[1,96]{1,0:T(1,128)}, f32[1,96]{1,0:T(1,128)}, /*index=5*/f...) custom-call(s32[8]{0:T(128)} %stack.71.here_s, ...), custom_call_target="tpu_custom_call" | custom-call | flops 1000000 | bytes 4000000 | tf_op jit(solution)/shard_map/whole_block/pallas_call | solution.py:52
  272.1 1.3 reduce
  273.4 1.1 copy.35
  (99 shorter events, 15.5 us)
Async XLA Ops:
  71.8 9.9 %collective-permute-start = (bf16[768,1536]{1,0:T(8,128)(2,1)}, bf16[768,1536]{1,0:T(8,128)(2,1)S(1)}, u32[]{:S(2)}, u32[]{:S(2)}) collective-permute-start(bf16[768,1536]{1,0:T(8,128)(2,1)} %get-tuple-element.93), channel_id=1, source_target_pairs={{0,1},{1,0},{2,3},{3,2},{4,5},{5,4},{6,7},{7,6},{8,9},{9,8},{10,11... | collective-permute-start | bytes 7077896 | tf_op jit(solution)/shard_map/ppermute | solution.py:780
  80.2 52.1 %collective-permute-start.20 = (bf16[3072,384]{1,0:T(8,128)(2,1)}, bf16[3072,384]{1,0:T(8,128)(2,1)}, u32[]{:S(2)}, u32[]{:S(2)}) collective-permute-start(bf16[3072,384]{1,0:T(8,128)(2,1)} %down_give.1), channel_id=1, source_target_pairs={{0,1},{1,0},{2,3},{3,2},{4,5},{5,4},{6,7},{7,6},{8,9},{9,8},{10,11... | collective-permute-start | bytes 7077896 | tf_op jit(solution)/shard_map/ppermute | solution.py:780
  81.7 1.4 copy-start.25
  99.3 14.9 %copy-start.23 = (f32[1,1536]{1,0:T(1,128)S(1)}, f32[1,1536]{1,0:T(1,128)}, u32[]{:S(2)}) copy-start(f32[1,1536]{1,0:T(1,128)} %get-tuple-element.106) | copy-start | bytes 18436
  99.3 14.9 %copy-start.24 = (f32[1,1536]{1,0:T(1,128)S(1)}, f32[1,1536]{1,0:T(1,128)}, u32[]{:S(2)}) copy-start(f32[1,1536]{1,0:T(1,128)} %get-tuple-element.105) | copy-start | bytes 18436
  124.9 19.8 %collective-permute-start.1 = (bf16[776,1536]{1,0:T(8,128)(2,1)}, bf16[776,1536]{1,0:T(8,128)(2,1)}, u32[]{:S(2)}, u32[]{:S(2)}) collective-permute-start(bf16[776,1536]{1,0:T(8,128)(2,1)} %proj_give.1), channel_id=1, source_target_pairs={{0,1},{1,0},{2,3},{3,2},{4,5},{5,4},{6,7},{7,6},{8,9},{9,8},{10,11... | collective-permute-start | bytes 7151624 | tf_op jit(solution)/shard_map/ppermute | solution.py:780
  125.4 135.3 %all-to-all-start = ((bf16[8,128,768]{2,1,0:T(8,128)(2,1)}), bf16[8,128,768]{2,1,0:T(8,128)(2,1)S(1)}, u32[]{:S(2)}, u32[]{:S(2)}) async-start(bf16[8,128,768]{2,1,0:T(8,128)(2,1)} %get-tuple-element.88), calls=%async_computation | async-start | bytes 3145728 | tf_op jit(solution)/shard_map/all_to_all | solution.py:799
  140.7 16.4 %collective-permute-start.21 = (bf16[96,8,384]{2,1,0:T(8,128)(2,1)}, bf16[96,8,384]{2,1,0:T(8,128)(2,1)S(1)}, u32[]{:S(2)}, u32[]{:S(2)}) collective-permute-start(bf16[96,8,384]{2,1,0:T(8,128)(2,1)} %get-tuple-element.143), channel_id=1, source_target_pairs={{0,2},{1,3},{2,0},{3,1},{4,6},{5,7},{6,4},{7,5},{8,10},{9,11},{10,... | collective-permute-start | bytes 1769480 | tf_op jit(solution)/shard_map/ppermute | solution.py:780
  142.2 23.7 %collective-permute-start.22 = (bf16[96,8,384]{2,1,0:T(8,128)(2,1)}, bf16[96,8,384]{2,1,0:T(8,128)(2,1)}, u32[]{:S(2)}, u32[]{:S(2)}) collective-permute-start(bf16[96,8,384]{2,1,0:T(8,128)(2,1)} %get-tuple-element.145), channel_id=1, source_target_pairs={{0,4},{4,0},{8,12},{12,8},{16,20},{20,16},{24,28},{28,24},{1,5},{5... | collective-permute-start | bytes 1769480 | tf_op jit(solution)/shard_map/ppermute | solution.py:780
  144.2 25.5 %collective-permute-start.11 = (bf16[24,8,1536]{2,1,0:T(8,128)(2,1)}, bf16[24,8,1536]{2,1,0:T(8,128)(2,1)S(1)}, u32[]{:S(2)}, u32[]{:S(2)}) collective-permute-start(bf16[24,8,1536]{2,1,0:T(8,128)(2,1)} %get-tuple-element.129), channel_id=1, source_target_pairs={{0,2},{1,3},{2,0},{3,1},{4,6},{5,7},{6,4},{7,5},{8,10},{9,11},{10,... | collective-permute-start | bytes 1769480 | tf_op jit(solution)/shard_map/ppermute | solution.py:780
  144.7 33.7 %collective-permute-start.12 = (bf16[24,8,1536]{2,1,0:T(8,128)(2,1)}, bf16[24,8,1536]{2,1,0:T(8,128)(2,1)S(1)}, u32[]{:S(2)}, u32[]{:S(2)}) collective-permute-start(bf16[24,8,1536]{2,1,0:T(8,128)(2,1)} %get-tuple-element.131), channel_id=1, source_target_pairs={{0,4},{4,0},{8,12},{12,8},{16,20},{20,16},{24,28},{28,24},{1,5},{5... | collective-permute-start | bytes 1769480 | tf_op jit(solution)/shard_map/ppermute | solution.py:780
  153.9 37.2 %collective-permute-start.3 = (bf16[24,8,1536]{2,1,0:T(8,128)(2,1)}, bf16[24,8,1536]{2,1,0:T(8,128)(2,1)}, u32[]{:S(2)}, u32[]{:S(2)}) collective-permute-start(bf16[24,8,1536]{2,1,0:T(8,128)(2,1)} %get-tuple-element.110), channel_id=1, source_target_pairs={{0,4},{4,0},{8,12},{12,8},{16,20},{20,16},{24,28},{28,24},{1,5},{5... | collective-permute-start | bytes 1769480 | tf_op jit(solution)/shard_map/ppermute | solution.py:780
  157.1 0.8 copy-start.3
  157.9 34.7 %collective-permute-start.2 = (bf16[25,8,1536]{2,1,0:T(8,128)(2,1)}, bf16[25,8,1536]{2,1,0:T(8,128)(2,1)S(1)}, u32[]{:S(2)}, u32[]{:S(2)}) collective-permute-start(bf16[25,8,1536]{2,1,0:T(8,128)(2,1)} %get-tuple-element.108), channel_id=1, source_target_pairs={{0,2},{1,3},{2,0},{3,1},{4,6},{5,7},{6,4},{7,5},{8,10},{9,11},{10,... | collective-permute-start | bytes 1843208 | tf_op jit(solution)/shard_map/ppermute | solution.py:780
  169.3 28.2 %collective-permute-start.23 = (bf16[48,8,384]{2,1,0:T(8,128)(2,1)}, bf16[48,8,384]{2,1,0:T(8,128)(2,1)}, u32[]{:S(2)}, u32[]{:S(2)}) collective-permute-start(bf16[48,8,384]{2,1,0:T(8,128)(2,1)} %get-tuple-element.147), channel_id=1, source_target_pairs={{0,4},{4,0},{8,12},{12,8},{16,20},{20,16},{24,28},{28,24},{1,5},{5... | collective-permute-start | bytes 884744 | tf_op jit(solution)/shard_map/ppermute | solution.py:780
  169.7 8.7 %copy-start.1 = (bf16[24,8,1536]{2,1,0:T(8,128)(2,1)}, bf16[24,8,1536]{2,1,0:T(8,128)(2,1)S(1)}, u32[]{:S(2)}) copy-start(bf16[24,8,1536]{2,1,0:T(8,128)(2,1)S(1)} %collective-permute-done.11.ga) | copy-start | bytes 1769476
  169.7 29.2 %collective-permute-start.24 = (bf16[48,8,384]{2,1,0:T(8,128)(2,1)}, bf16[48,8,384]{2,1,0:T(8,128)(2,1)}, u32[]{:S(2)}, u32[]{:S(2)}) collective-permute-start(bf16[48,8,384]{2,1,0:T(8,128)(2,1)} %get-tuple-element.149), channel_id=1, source_target_pairs={{0,2},{1,3},{2,0},{3,1},{4,6},{5,7},{6,4},{7,5},{8,10},{9,11},{10,... | collective-permute-start | bytes 884744 | tf_op jit(solution)/shard_map/ppermute | solution.py:780
  178.4 0.8 copy-start.2
  182.7 21.4 %collective-permute-start.13 = (bf16[12,8,1536]{2,1,0:T(8,128)(2,1)}, bf16[12,8,1536]{2,1,0:T(8,128)(2,1)S(1)}, u32[]{:S(2)}, u32[]{:S(2)}) collective-permute-start(bf16[12,8,1536]{2,1,0:T(8,128)(2,1)} %get-tuple-element.133), channel_id=1, source_target_pairs={{0,4},{4,0},{8,12},{12,8},{16,20},{20,16},{24,28},{28,24},{1,5},{5... | collective-permute-start | bytes 884744 | tf_op jit(solution)/shard_map/ppermute | solution.py:780
  191.2 13.0 %collective-permute-start.14 = (bf16[12,8,1536]{2,1,0:T(8,128)(2,1)}, bf16[12,8,1536]{2,1,0:T(8,128)(2,1)S(1)}, u32[]{:S(2)}, u32[]{:S(2)}) collective-permute-start(bf16[12,8,1536]{2,1,0:T(8,128)(2,1)} %get-tuple-element.135), channel_id=1, source_target_pairs={{0,2},{1,3},{2,0},{3,1},{4,6},{5,7},{6,4},{7,5},{8,10},{9,11},{10,... | collective-permute-start | bytes 884744 | tf_op jit(solution)/shard_map/ppermute | solution.py:780
  192.6 0.8 copy-start
  197.0 13.6 %collective-permute-start.4 = (bf16[13,8,1536]{2,1,0:T(8,128)(2,1)}, bf16[13,8,1536]{2,1,0:T(8,128)(2,1)S(1)}, u32[]{:S(2)}, u32[]{:S(2)}) collective-permute-start(bf16[13,8,1536]{2,1,0:T(8,128)(2,1)} %get-tuple-element.112), channel_id=1, source_target_pairs={{0,4},{4,0},{8,12},{12,8},{16,20},{20,16},{24,28},{28,24},{1,5},{5... | collective-permute-start | bytes 958472 | tf_op jit(solution)/shard_map/ppermute | solution.py:780
  197.5 13.1 %collective-permute-start.5 = (bf16[12,8,1536]{2,1,0:T(8,128)(2,1)}, bf16[12,8,1536]{2,1,0:T(8,128)(2,1)S(1)}, u32[]{:S(2)}, u32[]{:S(2)}) collective-permute-start(bf16[12,8,1536]{2,1,0:T(8,128)(2,1)} %get-tuple-element.114), channel_id=1, source_target_pairs={{0,2},{1,3},{2,0},{3,1},{4,6},{5,7},{6,4},{7,5},{8,10},{9,11},{10,... | collective-permute-start | bytes 884744 | tf_op jit(solution)/shard_map/ppermute | solution.py:780
  201.8 14.2 %collective-permute-start.25 = (bf16[48,8,384]{2,1,0:T(8,128)(2,1)}, bf16[48,8,384]{2,1,0:T(8,128)(2,1)S(1)}, u32[]{:S(2)}, u32[]{:S(2)}) collective-permute-start(bf16[48,8,384]{2,1,0:T(8,128)(2,1)} %get-tuple-element.151), channel_id=1, source_target_pairs={{0,8},{4,12},{8,0},{12,4},{16,24},{20,28},{24,16},{28,20},{1,9},{5... | collective-permute-start | bytes 884744 | tf_op jit(solution)/shard_map/ppermute | solution.py:780
  204.1 0.7 copy-start.8
  204.1 0.8 copy-start.9
  207.8 16.3 %collective-permute-start.15 = (bf16[12,8,1536]{2,1,0:T(8,128)(2,1)}, bf16[12,8,1536]{2,1,0:T(8,128)(2,1)S(1)}, u32[]{:S(2)}, u32[]{:S(2)}) collective-permute-start(bf16[12,8,1536]{2,1,0:T(8,128)(2,1)} %get-tuple-element.137), channel_id=1, source_target_pairs={{0,8},{4,12},{8,0},{12,4},{16,24},{20,28},{24,16},{28,20},{1,9},{5... | collective-permute-start | bytes 884744 | tf_op jit(solution)/shard_map/ppermute | solution.py:780
  210.6 0.7 copy-start.10
  210.6 0.8 copy-start.4
  214.3 13.0 %collective-permute-start.6 = (bf16[13,8,1536]{2,1,0:T(8,128)(2,1)}, bf16[13,8,1536]{2,1,0:T(8,128)(2,1)S(1)}, u32[]{:S(2)}, u32[]{:S(2)}) collective-permute-start(bf16[13,8,1536]{2,1,0:T(8,128)(2,1)} %get-tuple-element.116), channel_id=1, source_target_pairs={{0,8},{4,12},{8,0},{12,4},{16,24},{20,28},{24,16},{28,20},{1,9},{5... | collective-permute-start | bytes 958472 | tf_op jit(solution)/shard_map/ppermute | solution.py:780
  216.1 0.7 copy-start.6
  219.2 14.2 %collective-permute-start.26 = (bf16[24,8,384]{2,1,0:T(8,128)(2,1)}, bf16[24,8,384]{2,1,0:T(8,128)(2,1)S(1)}, u32[]{:S(2)}, u32[]{:S(2)}) collective-permute-start(bf16[24,8,384]{2,1,0:T(8,128)(2,1)} %get-tuple-element.153), channel_id=1, source_target_pairs={{0,16},{4,20},{8,24},{12,28},{16,0},{20,4},{24,8},{28,12},{1,17},{... | collective-permute-start | bytes 442376 | tf_op jit(solution)/shard_map/ppermute | solution.py:780
  224.1 0.7 copy-start.7
  227.2 14.3 %collective-permute-start.16 = (bf16[6,8,1536]{2,1,0:T(8,128)(2,1)}, bf16[6,8,1536]{2,1,0:T(8,128)(2,1)S(1)}, u32[]{:S(2)}, u32[]{:S(2)}) collective-permute-start(bf16[6,8,1536]{2,1,0:T(8,128)(2,1)} %get-tuple-element.139), channel_id=1, source_target_pairs={{0,16},{4,20},{8,24},{12,28},{16,0},{20,4},{24,8},{28,12},{1,17},{... | collective-permute-start | bytes 442376 | tf_op jit(solution)/shard_map/ppermute | solution.py:780
  227.2 0.7 copy-start.5
  230.5 14.6 %collective-permute-start.7 = (bf16[7,8,1536]{2,1,0:T(8,128)(2,1)}, bf16[7,8,1536]{2,1,0:T(8,128)(2,1)S(1)}, u32[]{:S(2)}, u32[]{:S(2)}) collective-permute-start(bf16[7,8,1536]{2,1,0:T(8,128)(2,1)} %get-tuple-element.118), channel_id=1, source_target_pairs={{0,16},{4,20},{8,24},{12,28},{16,0},{20,4},{24,8},{28,12},{1,17},{... | collective-permute-start | bytes 516104 | tf_op jit(solution)/shard_map/ppermute | solution.py:780
  233.4 0.7 copy-start.22
  236.4 11.7 %collective-permute-start.29 = (bf16[24,8,384]{2,1,0:T(8,128)(2,1)}, bf16[24,8,384]{2,1,0:T(8,128)(2,1)S(1)}, u32[]{:S(2)}, u32[]{:S(2)}) collective-permute-start(bf16[24,8,384]{2,1,0:T(8,128)(2,1)} %fold_last.5.me), channel_id=1, source_target_pairs={{0,3},{1,2},{2,1},{3,0},{4,7},{5,6},{6,5},{7,4},{8,11},{9,10},{10,... | collective-permute-start | bytes 442376 | tf_op jit(solution)/shard_map/ppermute | solution.py:780
  236.4 12.9 %collective-permute-start.28 = (bf16[24,8,384]{2,1,0:T(8,128)(2,1)}, bf16[24,8,384]{2,1,0:T(8,128)(2,1)S(1)}, u32[]{:S(2)}, u32[]{:S(2)}) collective-permute-start(bf16[24,8,384]{2,1,0:T(8,128)(2,1)} %fold_last.5.me), channel_id=1, source_target_pairs={{0,1},{1,0},{2,3},{3,2},{4,5},{5,4},{6,7},{7,6},{8,9},{9,8},{10,11... | collective-permute-start | bytes 442376 | tf_op jit(solution)/shard_map/ppermute | solution.py:780
  237.8 12.3 %collective-permute-start.27 = (bf16[24,8,384]{2,1,0:T(8,128)(2,1)}, bf16[24,8,384]{2,1,0:T(8,128)(2,1)S(1)}, u32[]{:S(2)}, u32[]{:S(2)}) collective-permute-start(bf16[24,8,384]{2,1,0:T(8,128)(2,1)} %fold_last.5.me), channel_id=1, source_target_pairs={{0,2},{1,3},{2,0},{3,1},{4,6},{5,7},{6,4},{7,5},{8,10},{9,11},{10,... | collective-permute-start | bytes 442376 | tf_op jit(solution)/shard_map/ppermute | solution.py:780
  241.5 0.7 copy-start.21
  244.5 6.3 %collective-permute-start.19 = (bf16[6,8,1536]{2,1,0:T(8,128)(2,1)}, bf16[6,8,1536]{2,1,0:T(8,128)(2,1)S(1)}, u32[]{:S(2)}, u32[]{:S(2)}) collective-permute-start(bf16[6,8,1536]{2,1,0:T(8,128)(2,1)} %fold_last.4.me), channel_id=1, source_target_pairs={{0,3},{1,2},{2,1},{3,0},{4,7},{5,6},{6,5},{7,4},{8,11},{9,10},{10,... | collective-permute-start | bytes 442376 | tf_op jit(solution)/shard_map/ppermute | solution.py:780
  245.1 0.7 copy-start.11
  245.1 18.7 %collective-permute-start.18 = (bf16[6,8,1536]{2,1,0:T(8,128)(2,1)}, bf16[6,8,1536]{2,1,0:T(8,128)(2,1)S(1)}, u32[]{:S(2)}, u32[]{:S(2)}) collective-permute-start(bf16[6,8,1536]{2,1,0:T(8,128)(2,1)} %fold_last.4.me), channel_id=1, source_target_pairs={{0,1},{1,0},{2,3},{3,2},{4,5},{5,4},{6,7},{7,6},{8,9},{9,8},{10,11... | collective-permute-start | bytes 442376 | tf_op jit(solution)/shard_map/ppermute | solution.py:780
  248.1 12.5 %copy-start.12 = (bf16[24,8,384]{2,1,0:T(8,128)(2,1)}, bf16[24,8,384]{2,1,0:T(8,128)(2,1)S(1)}, u32[]{:S(2)}) copy-start(bf16[24,8,384]{2,1,0:T(8,128)(2,1)S(1)} %collective-permute-done.29.gd) | copy-start | bytes 442372
  248.2 15.7 %collective-permute-start.17 = (bf16[6,8,1536]{2,1,0:T(8,128)(2,1)}, bf16[6,8,1536]{2,1,0:T(8,128)(2,1)S(1)}, u32[]{:S(2)}, u32[]{:S(2)}) collective-permute-start(bf16[6,8,1536]{2,1,0:T(8,128)(2,1)} %fold_last.4.me), channel_id=1, source_target_pairs={{0,2},{1,3},{2,0},{3,1},{4,6},{5,7},{6,4},{7,5},{8,10},{9,11},{10,... | collective-permute-start | bytes 442376 | tf_op jit(solution)/shard_map/ppermute | solution.py:780
  249.3 11.4 %copy-start.13 = (bf16[24,8,384]{2,1,0:T(8,128)(2,1)}, bf16[24,8,384]{2,1,0:T(8,128)(2,1)S(1)}, u32[]{:S(2)}) copy-start(bf16[24,8,384]{2,1,0:T(8,128)(2,1)S(1)} %collective-permute-done.28.gc) | copy-start | bytes 442372
  249.3 18.9 %collective-permute-start.10 = (bf16[6,8,1536]{2,1,0:T(8,128)(2,1)}, bf16[6,8,1536]{2,1,0:T(8,128)(2,1)S(1)}, u32[]{:S(2)}, u32[]{:S(2)}) collective-permute-start(bf16[6,8,1536]{2,1,0:T(8,128)(2,1)} %get-tuple-element.119.me), channel_id=1, source_target_pairs={{0,3},{1,2},{2,1},{3,0},{4,7},{5,6},{6,5},{7,4},{8,11},{9,10},{10,... | collective-permute-start | bytes 442376 | tf_op jit(solution)/shard_map/ppermute | solution.py:780
  250.2 10.5 %copy-start.14 = (bf16[24,8,384]{2,1,0:T(8,128)(2,1)}, bf16[24,8,384]{2,1,0:T(8,128)(2,1)S(1)}, u32[]{:S(2)}) copy-start(bf16[24,8,384]{2,1,0:T(8,128)(2,1)S(1)} %collective-permute-done.27.gx) | copy-start | bytes 442372
  250.2 18.0 %collective-permute-start.9 = (bf16[6,8,1536]{2,1,0:T(8,128)(2,1)}, bf16[6,8,1536]{2,1,0:T(8,128)(2,1)S(1)}, u32[]{:S(2)}, u32[]{:S(2)}) collective-permute-start(bf16[6,8,1536]{2,1,0:T(8,128)(2,1)} %get-tuple-element.119.me), channel_id=1, source_target_pairs={{0,1},{1,0},{2,3},{3,2},{4,5},{5,4},{6,7},{7,6},{8,9},{9,8},{10,11... | collective-permute-start | bytes 442376 | tf_op jit(solution)/shard_map/ppermute | solution.py:780
  250.7 10.0 %copy-start.15 = (bf16[6,8,1536]{2,1,0:T(8,128)(2,1)}, bf16[6,8,1536]{2,1,0:T(8,128)(2,1)S(1)}, u32[]{:S(2)}) copy-start(bf16[6,8,1536]{2,1,0:T(8,128)(2,1)S(1)} %collective-permute-done.19.gd) | copy-start | bytes 442372
  250.7 17.5 %collective-permute-start.8 = (bf16[6,8,1536]{2,1,0:T(8,128)(2,1)}, bf16[6,8,1536]{2,1,0:T(8,128)(2,1)S(1)}, u32[]{:S(2)}, u32[]{:S(2)}) collective-permute-start(bf16[6,8,1536]{2,1,0:T(8,128)(2,1)} %get-tuple-element.119.me), channel_id=1, source_target_pairs={{0,2},{1,3},{2,0},{3,1},{4,6},{5,7},{6,4},{7,5},{8,10},{9,11},{10,... | collective-permute-start | bytes 442376 | tf_op jit(solution)/shard_map/ppermute | solution.py:780
  263.8 0.7 copy-start.18
  264.5 0.7 copy-start.20
  268.2 0.6 copy-start.16
  268.2 0.7 copy-start.17
  268.2 0.7 copy-start.19

commit v3 on v2

--- a/solution.py
+++ b/solution.py
@@ -16,12 +16,14 @@
 F32 = jnp.float32
 BF16 = jnp.bfloat16
 LANES = 128
-VMEM_LIMIT = 60 * 1024 * 1024
+MIB = 1024 * 1024
+LARGE = 100000
+COST = 0.05
 ERF_P = 0.3275911
 ERF_A = (0.254829592, -0.284496736, 1.421413741, -1.453152027, 1.061405429)
 HALF_ROOT = 0.7071067811865476
 PEAK = 0.3989422804014327
-ROW_BQ, ROW_BV, ROW_BO, ROW_GA, ROW_SA, ROW_BD, ROW_GF, ROW_SF = range(8)
+ROW_BQ, ROW_BV, ROW_BO, ROW_GA, ROW_SA, ROW_BD, ROW_GF, ROW_SF, ROW_BU = range(9)
 
 
 def dot(left, right):
@@ -44,11 +46,28 @@
     return pl.BlockSpec(shape, lambda *_: (0,) * len(shape), pipeline_mode=pl.Buffered(1))
 
 
+def large(item):
+    return item.size >= LARGE
+
+
 def shaped(shape, dtype):
     return jax.ShapeDtypeStruct(shape, dtype)
 
 
-def call(kernel, name, grid, prefetch, in_specs, out_specs, out_shape, scratch, flops, moved, args):
+def call(
+    kernel, name, grid, prefetch, in_specs, out_specs, out_shape, scratch, flops, moved, args, vmem=24, free=0, loose=0
+):
+    single = not isinstance(out_shape, list)
+    shapes = [out_shape] if single else out_shape
+    shapes = [
+        pltpu.HBM(item.shape, item.dtype) if large(item) and number >= loose else item
+        for number, item in enumerate(shapes)
+    ]
+    out_shape = shapes[0] if single else shapes
+    args = [
+        pltpu.with_memory_space_constraint(item, pltpu.HBM) if large(item) and number < len(args) - free else item
+        for number, item in enumerate(args)
+    ]
     return pl.pallas_call(
         kernel,
         grid_spec=pltpu.PrefetchScalarGridSpec(
@@ -60,11 +79,11 @@
         ),
         out_shape=out_shape,
         compiler_params=pltpu.CompilerParams(
-            dimension_semantics=("arbitrary",) * len(grid), vmem_limit_bytes=VMEM_LIMIT
+            dimension_semantics=("arbitrary",) * len(grid), vmem_limit_bytes=vmem * MIB
         ),
-        cost_estimate=pl.CostEstimate(flops=int(flops), bytes_accessed=int(moved), transcendentals=0),
+        cost_estimate=pl.CostEstimate(flops=int(flops * COST), bytes_accessed=int(moved * COST), transcendentals=0),
         name=name,
-    )(*prefetch, *args)
+    )(*[pltpu.with_memory_space_constraint(item, pltpu.HBM) for item in prefetch], *args)
 
 
 def norm_forward(values):
@@ -126,6 +145,27 @@
     sid_lane = jnp.where(passed_lane < count, start + passed_lane, -1)
     sid_row = jnp.where(passed_row < count, start + passed_row, -1)
     return sid_lane, sid_row
+
+
+def vector_table(vectors, width):
+    def kernel(*refs):
+        out_ref = refs[-1]
+        at = 0
+        for ref in refs[:-1]:
+            for part in range(ref.shape[0] // width):
+                out_ref[at : at + 1, :] = ref[part * width : (part + 1) * width].astype(F32).reshape(1, width)
+                at += 1
+
+    rows = sum(item.shape[0] for item in vectors) // width
+    return pl.pallas_call(
+        kernel,
+        grid=(1,),
+        in_specs=[full(item.shape) for item in vectors],
+        out_specs=full((rows, width)),
+        out_shape=shaped((rows, width), F32),
+        compiler_params=pltpu.CompilerParams(vmem_limit_bytes=4 * MIB),
+        name="vector_table",
+    )(*[pltpu.with_memory_space_constraint(item, pltpu.HBM) for item in vectors])
 
 
 def attention_forward(x, w_qkv, w_out, table, bucket, lengths, group_size, span, rows_step):
@@ -183,7 +223,7 @@
             pl.BlockSpec((rows_step, width), lambda i, *_: (i, 0)),
             once((width, 3 * width)),
             once((width, width)),
-            once((8, width)),
+            once(table.shape),
         ],
         [
             pl.BlockSpec((rows_step, 3 * width), lambda i, *_: (i, 0)),
@@ -205,21 +245,23 @@
         8 * rows * width * width * 2,
         30e6,
         (x, w_qkv, w_out, table),
-    )
-
-
-def feed_forward(n_attn, w_up, w_down, bias_up, table, sid, slots, pairing, targets, slot_count, chunk, block):
+        26,
+    )
+
+
+def feed_forward(n_attn, w_up, w_down, table, sid, slots, pairing, targets, slot_count, block):
     rows, width = n_attn.shape
     ff = w_up.shape[1]
     batches, _, span = sid.shape
     pair_count = targets.shape[0]
     side = -(-pair_count // 8) * 8
+    chunk = width
     steps = ff // chunk
     blocks = rows // block
     per_block = block // span
 
     def kernel(
-        slots_s, pairing_s, targets_s, n_ref, wu_ref, wd_ref, bu_ref, tab_ref, sid_ref,
+        slots_s, pairing_s, targets_s, n_ref, wu_ref, wd_ref, tab_ref, sid_ref,
         act_ref, dg_ref, ht_ref, enc_ref, gres_ref, gsl_ref, vec_ref, low_scr, acc_scr, spread_scr,
     ):
         step = pl.program_id(0)
@@ -235,7 +277,7 @@
 
         for number in range(blocks):
             base = slice(number * block, (number + 1) * block)
-            inner = dot(low_scr[base, :], wu_ref[...]) + bu_ref[...].astype(F32)
+            inner = dot(low_scr[base, :], wu_ref[...]) + tab_ref[pl.ds(ROW_BU + step, 1), :]
             active, slope = gelu_pair(inner)
             active = active.astype(BF16)
             act_ref[base, :] = active
@@ -324,8 +366,7 @@
             once((rows, width)),
             pl.BlockSpec((width, chunk), lambda j, *_: (0, j)),
             pl.BlockSpec((chunk, width), lambda j, *_: (j, 0)),
-            pl.BlockSpec((1, chunk), lambda j, *_: (0, j)),
-            once((8, width)),
+            once(table.shape),
             once((batches, 8, span)),
         ],
         [
@@ -353,28 +394,35 @@
         ],
         8 * rows * width * ff,
         40e6,
-        (n_attn, w_up, w_down, bias_up, table, sid),
-    )
-
-
-def deal(scratch, here_s, outs, z_count, pieces):
+        (n_attn, w_up, w_down, table, sid),
+        44,
+    )
+
+
+def deal(scratch, here_s, outs, z_count, pieces, folds=1):
     send_a, keep_a, send_b, keep_b = outs
     x, y = here_s[2], here_s[3]
+    cols = scratch.shape[-1]
     for z in range(z_count):
         for other in range(2):
             at = pl.ds((z * 2 + other) * pieces, pieces)
-            send_a[at] = scratch[z, other, 1 - x, 0].astype(BF16)
-            keep_a[at] = scratch[z, other, x, 0].astype(BF16)
-            send_b[at] = scratch[z, 1 - y, other, 1].astype(BF16)
-            keep_b[at] = scratch[z, y, other, 1].astype(BF16)
+            for fold in range(folds):
+                part = pl.ds(fold * pieces, pieces)
+                to = slice(fold * cols, (fold + 1) * cols)
+                send_a[at, :, to] = scratch[z, other, 1 - x, 0, part].astype(BF16)
+                keep_a[at, :, to] = scratch[z, other, x, 0, part].astype(BF16)
+                send_b[at, :, to] = scratch[z, 1 - y, other, 1, part].astype(BF16)
+                keep_b[at, :, to] = scratch[z, y, other, 1, part].astype(BF16)
 
 
 def down_terms(active, grad_second, here, which, got=None):
     rows, ff = active.shape
-    half = grad_second.shape[1] // 2
+    width = grad_second.shape[1]
+    half = width // 2
     steps = 4
     tall = ff // steps
-    pieces = ff // 32 // 8
+    pieces = width // 32 // 8
+    folds = ff // width
 
     def give(here_s, act_ref, gs_ref, out_ref):
         out_ref[...] = t_dot(act_ref[...], gs_ref[...]).astype(BF16)
@@ -383,7 +431,7 @@
         outs, scratch = rest[:4], rest[4]
         term = t_dot(act_ref[...], gs_ref[...]) + got_ref[...].astype(F32)
         scratch[...] = term.reshape(scratch.shape)
-        deal(scratch, here_s, outs, 1, pieces)
+        deal(scratch, here_s, outs, 1, pieces, folds)
 
     in_specs = [
         pl.BlockSpec((rows, tall), lambda i, here_s: (0, i)),
@@ -394,59 +442,48 @@
         return call(
             give, "down_give", (steps,), (here,), in_specs,
             pl.BlockSpec((tall, half), lambda i, *_: (i, 0)),
-            shaped((ff, half), BF16), [], flops, 9e6, (active, grad_second),
-        )
-    block = (2 * pieces, 8, half)
+            shaped((ff, half), BF16), [], flops, 9e6, (active, grad_second), 20, 0, 1,
+        )
+    block = (2 * pieces, 8, folds * half)
     return call(
         own, "down_own", (steps,), (here,),
         in_specs + [pl.BlockSpec((tall, half), lambda i, *_: (i, 0))],
         [pl.BlockSpec(block, lambda i, *_: (i, 0, 0))] * 4,
-        [shaped((8 * pieces, 8, half), BF16)] * 4,
-        [pltpu.VMEM((1, 2, 2, 2, pieces, 8, half), F32)],
-        flops, 11e6, (active, grad_second, got),
-    )
-
-
-def up_terms(grad_second, slope, hidden_t, w_up, w_down, here, which, chunk, block, so_far=None, got=None):
+        [shaped((8 * pieces, 8, folds * half), BF16)] * 4,
+        [pltpu.VMEM((1, 2, 2, 2, folds * pieces, 8, half), F32)],
+        flops, 11e6, (active, grad_second, got), 24, 1, 4,
+    )
+
+
+def up_terms(grad_second, slope, hidden_t, w_down, here, which, got=None):
     rows, width = grad_second.shape
-    ff = w_up.shape[1]
+    ff = w_down.shape[0]
     half = ff // 2
+    chunk = width
     steps = half // chunk
-    blocks = rows // block
+    block = rows // 4
     pieces = width // 32 // 8
-    more = so_far is not None
-
-    def kernel(here_s, *refs):
-        gs_ref, dg_ref, ht_ref, wu_ref, wd_ref = refs[:5]
-        refs = refs[5:]
-        if more:
-            so_far_ref, refs = refs[0], refs[1:]
+
+    def kernel(here_s, gs_ref, dg_ref, ht_ref, wd_ref, *refs):
         if got is not None:
             got_ref, refs = refs[0], refs[1:]
             outs, refs = refs[:4], refs[4:]
         else:
             out_ref, refs = refs[0], refs[1:]
-        gh_ref, bu_ref, gi_scr = refs[:3]
-        step = pl.program_id(0)
-
-        @pl.when(step == 0)
-        def _():
-            gh_ref[...] = so_far_ref[...] if more else jnp.zeros_like(gh_ref)
-
+        gi_ref, bu_ref = refs[:2]
         sums = jnp.zeros((1, chunk), F32)
-        for number in range(blocks):
+        for number in range(rows // block):
             base = slice(number * block, (number + 1) * block)
             grad_active = dot_t(gs_ref[base, :], wd_ref[...])
             low = (grad_active * dg_ref[base, :].astype(F32)).astype(BF16)
-            gi_scr[base, :] = low
+            gi_ref[base, :] = low
             sums += column_sum(low.astype(F32))
-            gh_ref[base, :] += dot_t(low, wu_ref[...])
         bu_ref[...] = sums
-        term = dot(ht_ref[...], gi_scr[...])
+        term = dot(ht_ref[...], gi_ref[...])
         if got is None:
             out_ref[...] = term.astype(BF16)
         else:
-            scratch = refs[3]
+            scratch = refs[2]
             term += got_ref[...].astype(F32)
             scratch[...] = term.reshape(scratch.shape)
             deal(scratch, here_s, outs, 4, pieces)
@@ -458,14 +495,10 @@
         once((rows, width)),
         pl.BlockSpec((rows, chunk), lambda i, h: (0, col(i, h))),
         once((width, rows)),
-        pl.BlockSpec((width, chunk), lambda i, h: (0, col(i, h))),
         pl.BlockSpec((chunk, width), lambda i, h: (col(i, h), 0)),
     ]
-    args = [grad_second, slope, hidden_t, w_up, w_down]
-    if more:
-        in_specs.append(once((rows, width)))
-        args.append(so_far)
-    scratch = [pltpu.VMEM((rows, chunk), BF16)]
+    args = [grad_second, slope, hidden_t, w_down]
+    scratch = []
     if got is None:
         out_specs = [pl.BlockSpec((width, chunk), lambda i, *_: (0, i))]
         out_shape = [shaped((width, half), BF16)]
@@ -477,18 +510,42 @@
         scratch.append(pltpu.VMEM((4, 2, 2, 2, pieces, 8, chunk), F32))
     return call(
         kernel, "up_give" if got is None else "up_own", (steps,), (here,), in_specs,
-        out_specs + [once((rows, width)), pl.BlockSpec((1, chunk), lambda i, *_: (0, i))],
-        out_shape + [shaped((rows, width), F32), shaped((1, half), F32)],
-        scratch, 6 * rows * width * half, 20e6, args,
-    )
-
-
-def attention_backward(gh, gres, n_attn, spread, table, w_out, qkv, probs, span, rows_step):
+        out_specs
+        + [
+            pl.BlockSpec((rows, chunk), lambda i, *_: (0, i)),
+            pl.BlockSpec((1, chunk), lambda i, *_: (0, i)),
+        ],
+        out_shape + [shaped((rows, half), BF16), shaped((1, half), F32)],
+        scratch, 4 * rows * width * half, 16e6, args, 34, 0 if got is None else 1, 1 if got is None else 4,
+    )
+
+
+def hidden_gradient(grad_inner, w_up, here, which):
+    rows, half = grad_inner.shape
+    width = w_up.shape[0]
+    block = rows // 2
+
+    def kernel(here_s, gi_ref, wu_ref, out_ref):
+        out_ref[...] = dot_t(gi_ref[...], wu_ref[...])
+
+    return call(
+        kernel, "hidden_grad", (rows // block,), (here,),
+        [
+            pl.BlockSpec((block, half), lambda i, h: (i, 0)),
+            pl.BlockSpec((width, half), lambda i, h: (0, h[which]), pipeline_mode=pl.Buffered(1)),
+        ],
+        pl.BlockSpec((block, width), lambda i, h: (i, 0)),
+        shaped((rows, width), F32), [], 2 * rows * width * half, 9e6, (grad_inner, w_up), 16,
+    )
+
+
+def attention_backward(gh, gres, grad_inner, w_up, n_attn, spread, table, w_out, qkv, probs, here, which, span, rows_step):
     rows, width = gh.shape
+    half = grad_inner.shape[1]
     pairs = width // LANES
     per_step = rows_step // span
 
-    def kernel(gh_ref, gres_ref, n_ref, s_ref, tab_ref, wo_ref, qkv_ref, p_ref, gr_ref, gb_ref, gm_ref, vec_ref, ga_scr):
+    def kernel(here_s, gh_ref, gres_ref, gi_ref, wu_ref, n_ref, s_ref, tab_ref, wo_ref, qkv_ref, p_ref, gr_ref, gb_ref, gm_ref, vec_ref, ga_scr):
         step = pl.program_id(0)
         low_b, high_b, low_m = head_masks()
 
@@ -497,7 +554,7 @@
             vec_ref[...] = jnp.zeros_like(vec_ref)
 
         normed = n_ref[...]
-        grad_hidden = gh_ref[...] + gres_ref[...]
+        grad_hidden = dot_t(gi_ref[...], wu_ref[...]) + gh_ref[...] + gres_ref[...]
         resid = norm_backward(grad_hidden, normed, s_ref[:, :1], tab_ref[ROW_GA : ROW_GA + 1, :])
         gr_ref[...] = resid
         low = resid.astype(BF16)
@@ -531,17 +588,19 @@
                 vec_ref[1:2, cols] += column_sum(grad_v.astype(F32))
 
     def rows_of(cols):
-        return pl.BlockSpec((rows_step, cols), lambda i: (i, 0))
+        return pl.BlockSpec((rows_step, cols), lambda i, h: (i, 0))
 
     return call(
         kernel,
         "attn_bwd",
         (rows // rows_step,),
-        (),
-        [
-            rows_of(width), rows_of(width), rows_of(width), rows_of(LANES),
-            once((8, width)), once((width, width)), rows_of(3 * width),
-            pl.BlockSpec((per_step, pairs, 2 * span, span), lambda i: (i, 0, 0, 0)),
+        (here,),
+        [
+            rows_of(width), rows_of(width), rows_of(half),
+            pl.BlockSpec((width, half), lambda i, h: (0, h[which]), pipeline_mode=pl.Buffered(1)),
+            rows_of(width), rows_of(LANES),
+            once(table.shape), once((width, width)), rows_of(3 * width),
+            pl.BlockSpec((per_step, pairs, 2 * span, span), lambda i, h: (i, 0, 0, 0)),
         ],
         [rows_of(width), rows_of(width), rows_of(3 * width), full((8, width))],
         [
@@ -550,8 +609,9 @@
         ],
         [pltpu.VMEM((rows_step, width), BF16)],
         8 * rows * width * width * 2,
-        34e6,
-        (gh, gres, n_attn, spread, table, w_out, qkv, probs),
+        40e6,
+        (gh, gres, grad_inner, w_up, n_attn, spread, table, w_out, qkv, probs),
+        34,
     )
 
 
@@ -560,8 +620,7 @@
     part = width // 2
     pieces = width // 32 // 8
 
-    def product(refs):
-        x_ref, gm_ref, att_ref, gb_ref, scr = refs
+    def product(x_ref, gm_ref, att_ref, gb_ref, scr):
         step = pl.program_id(0)
 
         @pl.when(step < 3)
@@ -572,35 +631,61 @@
         def _():
             scr[...] = t_dot(att_ref[...], gb_ref[...])
 
-    def give(here_s, x_ref, gm_ref, att_ref, gb_ref, vec_ref, out_ref, scr):
-        product((x_ref, gm_ref, att_ref, gb_ref, scr))
+    def small(here_s, ffn_ref, attn_ref, sent_ref, kept_ref, store):
+        first = here_s[0] == 0
+        for step in range(4):
+
+            @pl.when(pl.program_id(0) == step)
+            def _():
+                side, at = step // 2, slice(step % 2 * part, (step % 2 + 1) * part)
+                wide = slice(step * part, (step + 1) * part)
+                rows_of = (
+                    (ffn_ref[0:1, at], ffn_ref[2:3, at], attn_ref[1:2, at], attn_ref[3:4, at]),
+                    (ffn_ref[1:2, at], attn_ref[0:1, at], attn_ref[2:3, at], attn_ref[4:5, at]),
+                )[side]
+                sent, kept = sent_ref[:, wide], kept_ref[:, wide]
+                ups = (jnp.where(first, kept, sent), jnp.where(first, sent, kept))
+                store(jnp.concatenate(rows_of + ups + (jnp.zeros((2, part), F32),), axis=0))
+
+    def give(here_s, x_ref, gm_ref, att_ref, gb_ref, ffn_ref, attn_ref, sent_ref, kept_ref, out_ref, scr):
+        product(x_ref, gm_ref, att_ref, gb_ref, scr)
         out_ref[:width, :] = scr[...].astype(BF16)
-        out_ref[width:, :] = vec_ref[...].astype(BF16)
-
-    def own(here_s, x_ref, gm_ref, att_ref, gb_ref, vec_ref, got_ref, send_a, keep_a, send_b, keep_b, scr, cut):
-        product((x_ref, gm_ref, att_ref, gb_ref, scr))
+
+        def store(value):
+            out_ref[width:, :] = value.astype(BF16)
+
+        small(here_s, ffn_ref, attn_ref, sent_ref, kept_ref, store)
+
+    def own(
+        here_s, x_ref, gm_ref, att_ref, gb_ref, ffn_ref, attn_ref, sent_ref, kept_ref, got_ref,
+        send_a, keep_a, send_b, keep_b, scr, cut,
+    ):
+        product(x_ref, gm_ref, att_ref, gb_ref, scr)
         term = scr[...] + got_ref[:width, :].astype(F32)
         cut[...] = term.reshape(cut.shape)
         deal(cut, here_s, (send_a, keep_a, send_b, keep_b), 4, pieces)
-        extra = (vec_ref[...] + got_ref[width:, :].astype(F32)).astype(BF16)
-        send_a[8 * pieces] = extra
-        keep_a[8 * pieces] = extra
+
+        def store(value):
+            extra = (value + got_ref[width:, :].astype(F32)).astype(BF16)
+            send_a[8 * pieces] = extra
+            keep_a[8 * pieces] = extra
+
+        small(here_s, ffn_ref, attn_ref, sent_ref, kept_ref, store)
 
     in_specs = [
         once((rows, width)),
         pl.BlockSpec((rows, part), lambda i, h: (0, h[which] * 3 + jnp.minimum(i, 2))),
         once((rows, width)),
         pl.BlockSpec((rows, part), lambda i, h: (0, h[which]), pipeline_mode=pl.Buffered(1)),
-        pl.BlockSpec((8, part), lambda i, h: (0, i)),
-    ]
-    args = [x, grad_mixed, attended, grad_branch, vectors]
+    ] + [once(item.shape) for item in vectors]
+    args = [x, grad_mixed, attended, grad_branch, *vectors]
     flops = 4 * rows * width * width
     if got is None:
         return call(
             give, "proj_give", (4,), (here,), in_specs,
             pl.BlockSpec((width + 8, part), lambda i, *_: (0, i)),
             shaped((width + 8, 4 * part), BF16),
-            [pltpu.VMEM((width, part), F32)], flops, 9e6, args,
+            [pltpu.VMEM((width, part), F32)], flops, 9e6, args, 20, 0, 1,
         )
     return call(
         own, "proj_own", (4,), (here,),
@@ -611,7 +696,7 @@
         ],
         [shaped((8 * pieces + extra, 8, 4 * part), BF16) for extra in (1, 1, 0, 0)],
         [pltpu.VMEM((width, part), F32), pltpu.VMEM((4, 2, 2, 2, pieces, 8, part), F32)],
-        flops, 11e6, args + [got],
+        flops, 11e6, args + [got], 24, 1, 4,
     )
 
 
@@ -630,17 +715,34 @@
         ],
         pl.BlockSpec((rows_step, width), lambda i: (i, 0)),
         shaped((rows, width), BF16), [], 6 * rows * width * width, 13e6,
-        (grad_mixed, w_qkv, grad_resid),
-    )
-
-
-def add_call(kernel, name, here, args, outs):
-    moved = sum(item.size * 2 for item in args) + sum(2 * a * b * c for a, b, c in outs)
+        (grad_mixed, w_qkv, grad_resid), 20,
+    )
+
+
+def copied(item, here, block):
+    rows, width = item.shape
+
+    def kernel(here_s, in_ref, out_ref):
+        out_ref[...] = in_ref[...]
+
+    spec = pl.BlockSpec((block, width), lambda i, *_: (i, 0))
     return call(
-        kernel, name, (), (here,), [pl.BlockSpec(memory_space=pltpu.VMEM)] * len(args),
-        [pl.BlockSpec(memory_space=pltpu.VMEM)] * len(outs),
-        [shaped(shape, BF16) for shape in outs], [], moved // 4, moved, args,
-    )
+        kernel, "copied", (rows // block,), (here,), [spec], spec,
+        shaped((rows, width), item.dtype), [], 1, 3e6, (item,), 4,
+    )
+
+
+def small_call(kernel, name, here, args, outs, vmem=12):
+    return pl.pallas_call(
+        kernel,
+        in_specs=[pl.BlockSpec(memory_space=pltpu.SMEM)]
+        + [pl.BlockSpec(memory_space=pltpu.VMEM)] * len(args),
+        out_specs=[pl.BlockSpec(memory_space=pltpu.VMEM)] * len(outs),
+        out_shape=outs,
+        compiler_params=pltpu.CompilerParams(vmem_limit_bytes=vmem * MIB),
+        cost_estimate=pl.CostEstimate(flops=int(1e6 * COST), bytes_accessed=int(4e6 * COST), transcendentals=0),
+        name=name,
+    )(here, *args)
 
 
 def add(left, right):
@@ -668,111 +770,134 @@
             send_a[4 * pieces] = total
             left_a[4 * pieces] = total
 
-    a_shape, b_shape = (4 * pieces + extra, 8, cols), (4 * pieces, 8, cols)
-    return add_call(
-        kernel, "fold_second", here, (keep_a, got_a, keep_b, got_b), (a_shape, a_shape, b_shape, b_shape)
-    )
-
-
-def fold_third(keep_a, got_a, keep_b, got_b, here, pieces, extra):
-    cols = keep_a.shape[2]
-
-    def kernel(here_s, ka, ga, kb, gb, send, left):
+    a_out = shaped((4 * pieces + extra, 8, cols), BF16)
+    b_out = shaped((4 * pieces, 8, cols), BF16)
+    return small_call(
+        kernel, "fold_second", here, (keep_a, got_a, keep_b, got_b), [a_out, a_out, b_out, b_out]
+    )
+
+
+def fold_third(terms, here, pieces, extra):
+    cols = terms[0][0].shape[2]
+    count = len(terms)
+
+    def kernel(here_s, *refs):
+        ins, (send, left) = refs[:-2], refs[-2:]
         low = here_s[4]
         for high in range(2):
-            for number, (keep, got) in enumerate(((ka, ga), (kb, gb))):
-                at = pl.ds((high * 2 + number) * pieces, pieces)
+            for number in range(2 * count):
+                keep, got = ins[2 * number : 2 * number + 2]
+                at = pl.ds((high * 2 * count + number) * pieces, pieces)
                 for out, pick in ((send, 1 - low), (left, low)):
                     rows = pl.ds((high * 2 + pick) * pieces, pieces)
                     out[at] = add(keep[rows], got[rows])
         if extra:
-            total = add(ka[4 * pieces], ga[4 * pieces])
-            send[4 * pieces] = total
-            left[4 * pieces] = total
-
-    shape = (4 * pieces + extra, 8, cols)
-    return add_call(kernel, "fold_third", here, (keep_a, got_a, keep_b, got_b), (shape, shape))
-
-
-def fold_fourth(keep, got, here, pieces, extra):
+            total = add(ins[0][4 * pieces], ins[1][4 * pieces])
+            send[4 * count * pieces] = total
+            left[4 * count * pieces] = total
+
+    out = shaped((4 * count * pieces + extra, 8, cols), BF16)
+    args = [item for term in terms for item in term]
+    return small_call(kernel, "fold_third", here, args, [out, out])
+
+
+def fold_fourth(keep, got, here, extra):
     cols = keep.shape[2]
+    count = (keep.shape[0] - extra) // 2
 
     def kernel(here_s, keep_ref, got_ref, send, left):
         high = here_s[5]
         for out, pick in ((send, 1 - high), (left, high)):
-            rows = pl.ds(pick * 2 * pieces, 2 * pieces)
-            out[: 2 * pieces] = add(keep_ref[rows], got_ref[rows])
+            rows = pl.ds(pick * count, count)
+            out[:count] = add(keep_ref[rows], got_ref[rows])
         if extra:
-            total = add(keep_ref[4 * pieces], got_ref[4 * pieces])
-            send[2 * pieces] = total
-            left[2 * pieces] = total
-
-    shape = (2 * pieces + extra, 8, cols)
-    return add_call(kernel, "fold_fourth", here, (keep, got), (shape, shape))
-
-
-def fold_last(keep, got, here, pieces, extra):
+            total = add(keep_ref[2 * count], got_ref[2 * count])
+            send[count] = total
+            left[count] = total
+
+    out = shaped((count + extra, 8, cols), BF16)
+    return small_call(kernel, "fold_fourth", here, (keep, got), [out, out])
+
+
+def fold_last(keep, got, here, extra):
     cols = keep.shape[2]
+    count = keep.shape[0] - extra
 
     def kernel(here_s, keep_ref, got_ref, *outs):
-        outs[0][...] = add(keep_ref[: 2 * pieces], got_ref[: 2 * pieces])
+        outs[0][...] = add(keep_ref[:count], got_ref[:count])
         if extra:
-            outs[1][0] = add(keep_ref[2 * pieces], got_ref[2 * pieces])
-
-    shapes = [(2 * pieces, 8, cols)] + [(1, 8, cols)] * extra
-    return add_call(kernel, "fold_last", here, (keep, got), shapes)
-
-
-def whole_block(mine, over_x, over_core, over_both, here, vectors=None):
-    count, _, cols = mine.shape
-    rows = 8 * count
-
-    def pick(here_s, refs, core, side):
-        me, gx, gc, gd = [item[...].astype(F32).reshape(rows, cols) for item in refs]
-        same_core, same_side = here_s[0] == core, here_s[2] == side
-        return jnp.where(
-            same_core, jnp.where(same_side, me, gx), jnp.where(same_side, gc, gd)
-        )
-
-    def kernel(here_s, me, gx, gc, gd, *rest):
-        outs = rest[1:] if vectors is not None else rest
+            outs[1][0] = add(keep_ref[count], got_ref[count])
+
+    outs = [shaped((count, 8, cols), BF16)] + [shaped((1, 8, cols), BF16)] * extra
+    return small_call(kernel, "fold_last", here, (keep, got), outs)
+
+
+def chosen_part(here_s, refs, core, side, at):
+    me, gx, gc, gd = [item[at].astype(F32) for item in refs]
+    same_core, same_side = here_s[0] == core, here_s[2] == side
+    return jnp.where(same_core, jnp.where(same_side, me, gx), jnp.where(same_side, gc, gd))
+
+
+def feed_blocks(parts, here, pieces, width):
+    cols = parts[0].shape[2]
+    half = width // 2
+    folds = cols // half
+    rows = 2 * pieces * 8
+
+    def kernel(here_s, me, gx, gc, gd, down_ref, up_ref):
+        refs = (me, gx, gc, gd)
         for core in range(2):
             for side in range(2):
-                value = pick(here_s, (me, gx, gc, gd), core, side)
+                tall = side * folds * rows
+                for ab in range(2):
+                    at = pl.ds(ab * pieces, pieces)
+                    value = chosen_part(here_s, refs, core, side, at).reshape(rows // 2, cols)
+                    for fold in range(folds):
+                        start = tall + (ab * folds + fold) * (rows // 2)
+                        down_ref[start : start + rows // 2, core * half : (core + 1) * half] = value[
+                            :, fold * half : (fold + 1) * half
+                        ]
+                at = pl.ds(2 * pieces, 2 * pieces)
+                value = chosen_part(here_s, refs, core, side, at).reshape(rows, cols)
+                up_ref[side * rows : (side + 1) * rows, core * cols : (core + 1) * cols] = value
+
+    outs = [shaped((2 * folds * rows, width), F32), shaped((2 * rows, 2 * cols), F32)]
+    return small_call(kernel, "feed_blocks", here, parts, outs, 16)
+
+
+def projection_blocks(parts, vectors, here, pieces):
+    cols = parts[0].shape[2]
+    rows = 2 * pieces * 8
+    cut = cols // 4 * 3
+    width = cols // 2
+    small = width // 8
+    large = cols // 4
+
+    def kernel(here_s, me, gx, gc, gd, vec_ref, qkv_ref, out_ref, *outs):
+        refs = (me, gx, gc, gd)
+        for core in range(2):
+            for side in range(2):
+                value = chosen_part(here_s, refs, core, side, slice(None)).reshape(rows, cols)
                 at = slice(side * rows, (side + 1) * rows)
-                if vectors is None:
-                    outs[0][at, core * cols : (core + 1) * cols] = value
-                else:
-                    cut = cols // 4 * 3
-                    outs[0][at, core * cut : (core + 1) * cut] = value[:, :cut]
-                    outs[1][at, core * (cols - cut) : (core + 1) * (cols - cut)] = value[:, cut:]
-        if vectors is not None:
-            table = rest[0][0].astype(F32)
-            wide = here_s[6]
-            width = cols // 2
-            small = width // 8
-            left = pltpu.roll(table[:, :width], lax.rem(width - wide * small, width), 1)
-            right = pltpu.roll(table[:, width:], lax.rem(width - wide * small, width), 1)
-            for row in range(4):
-                outs[2 + 2 * row][...] = left[row : row + 1, :small]
-                outs[3 + 2 * row][...] = right[row : row + 1, :small]
-            large = 2 * cols // 8
-            turned = pltpu.roll(table, lax.rem(cols - lax.rem(wide, 4) * large, cols), 1)
-            outs[10][...] = jnp.where(wide < 4, turned[4:5, :large], turned[5:6, :large])
-
-    if vectors is None:
-        shapes = [(2 * rows, 2 * cols)]
-        args = (mine, over_x, over_core, over_both)
-    else:
-        cut = cols // 4 * 3
-        shapes = [(2 * rows, 2 * cut), (2 * rows, 2 * (cols - cut))]
-        shapes += [(1, cols // 16)] * 8 + [(1, cols // 4)]
-        args = (mine, over_x, over_core, over_both, vectors)
-    return call(
-        kernel, "whole_block", (), (here,), [pl.BlockSpec(memory_space=pltpu.VMEM)] * len(args),
-        [pl.BlockSpec(memory_space=pltpu.VMEM)] * len(shapes),
-        [shaped(shape, F32) for shape in shapes], [], 1e6, 4e6, args,
-    )
+                qkv_ref[at, core * cut : (core + 1) * cut] = value[:, :cut]
+                out_ref[at, core * (cols - cut) : (core + 1) * (cols - cut)] = value[:, cut:]
+        table = vec_ref[0].astype(F32)
+        wide = here_s[6]
+        shift = lax.rem(width - wide * small, width)
+        left, right = pltpu.roll(table[:, :width], shift, 1), pltpu.roll(table[:, width:], shift, 1)
+        for row in range(4):
+            outs[2 * row][...] = left[row : row + 1, :small]
+            outs[2 * row + 1][...] = right[row : row + 1, :small]
+        turned = pltpu.roll(table, lax.rem(cols - lax.rem(wide, 4) * large, cols), 1)
+        outs[8][...] = jnp.where(wide < 4, turned[4:5, :large], turned[5:6, :large])
+
+    outs = [shaped((2 * rows, 2 * cut), F32), shaped((2 * rows, 2 * (cols - cut)), F32)]
+    outs += [shaped((1, small), F32)] * 8 + [shaped((1, large), F32)]
+    return small_call(kernel, "projection_blocks", here, (*parts, vectors), outs, 16)
+
+
+def after(item, *earlier):
+    return lax.optimization_barrier((item, *earlier))[0]
 
 
 def swap(item, axis, step):
@@ -780,17 +905,8 @@
     return lax.ppermute(item, axis, [(index, index ^ step) for index in range(count)])
 
 
-def finish(dealt, here, pieces, extra):
-    send_a, keep_a, send_b, keep_b = dealt
-    got_a, got_b = swap(send_a, "narrow", 2), swap(send_b, "wide", 1)
-    send_a, keep_a, send_b, keep_b = fold_second(keep_a, got_a, keep_b, got_b, here, pieces, extra)
-    got_a, got_b = swap(send_a, "wide", 1), swap(send_b, "narrow", 2)
-    send, keep = fold_third(keep_a, got_a, keep_b, got_b, here, pieces, extra)
-    send, keep = fold_fourth(keep, swap(send, "wide", 2), here, pieces, extra)
-    last = fold_last(keep, swap(send, "wide", 4), here, pieces, extra)
-    mine = last[0]
-    parts = (mine, swap(mine, "narrow", 2), swap(mine, "narrow", 1), swap(mine, "narrow", 3))
-    return whole_block(*parts, here, *last[1:])
+def quarters(mine):
+    return mine, swap(mine, "narrow", 2), swap(mine, "narrow", 1), swap(mine, "narrow", 3)
 
 
 def regroup_rows(sent, bucket, wide_count, batches):
@@ -838,67 +954,96 @@
         ).astype(jnp.int32)
     else:
         here = jnp.arange(8, dtype=jnp.int32)
-    table = jnp.stack(
-        [bias_q, bias_v, bias_out, gain_attn, shift_attn, bias_down, gain_ffn, shift_ffn]
-    ).astype(F32)
+    table = vector_table(
+        [bias_q, bias_v, bias_out, gain_attn, shift_attn, bias_down, gain_ffn, shift_ffn, bias_up], width
+    )
     ordered = wide_count == batches
     slots = bucket if ordered else jnp.arange(batches, dtype=jnp.int32)
+    pieces = width // 32 // 8
 
     qkv, probs, attended, n_attn, spread, sid = attention_forward(
         tokens, w_qkv, w_out, table, bucket, lengths, wide_count // batches, span, 2 * span
     )
     active, slope, hidden_t, sent, gres, grad_second, vec_ffn = feed_forward(
-        n_attn, w_up, w_down, bias_up.reshape(1, -1), table, sid, slots, pairing, targets,
-        batches, 512, 256,
-    )
-    encoded = regroup_rows(sent, bucket, wide_count, batches)
-    ups = (grad_second, slope, hidden_t, w_up, w_down, here)
+        n_attn, w_up, w_down, table, sid, slots, pairing, targets, batches, 2 * span
+    )
+    ups = (grad_second, slope, hidden_t, w_down)
+    heads = (n_attn, spread, table, w_out, qkv, probs)
     down_sent = down_terms(active, grad_second, here, 1)
-    up_sent, gh, bup_sent = up_terms(*ups, 1, 512, 256)
+    encoded = regroup_rows(after(sent, down_sent), bucket, wide_count, batches)
     if paired:
         down_dealt = down_terms(active, grad_second, here, 0, swap(down_sent, "narrow", 1))
-        *up_dealt, gh, bup_kept = up_terms(*ups, 0, 512, 256, gh, swap(up_sent, "narrow", 1))
+        down_a, down_b = swap(down_dealt[0], "narrow", 2), swap(down_dealt[2], "wide", 1)
+        up_sent, gi_sent, bup_sent = up_terms(*ups, after(here, down_dealt[1]), 1)
+        gh = hidden_gradient(gi_sent, w_up, here, 1)
+        *up_dealt, gi_kept, bup_kept = up_terms(
+            *ups, after(here, gh), 0, swap(up_sent, "narrow", 1)
+        )
+        up_a, up_b = swap(up_dealt[0], "narrow", 2), swap(up_dealt[2], "wide", 1)
+        down_dealt = fold_second(
+            down_dealt[1], down_a, down_dealt[3], down_b, after(here, bup_kept), pieces, 0
+        )
+        down_a, down_b = swap(down_dealt[0], "wide", 1), swap(down_dealt[2], "narrow", 2)
+        gr, gb, gm, vec_attn = attention_backward(
+            gh, gres, gi_kept, w_up, *heads, after(here, down_dealt[1]), 0, span, 2 * span
+        )
+        up_dealt = fold_second(
+            up_dealt[1], up_a, up_dealt[3], up_b, after(here, vec_attn, encoded), pieces, 0
+        )
+        up_a, up_b = swap(up_dealt[0], "wide", 1), swap(up_dealt[2], "narrow", 2)
+        projections = (tokens, gm, attended, gb, (vec_ffn, vec_attn, bup_sent, bup_kept))
+        proj_sent = projection_terms(*projections, after(here, up_dealt[1]), 1)
+        grad_tokens = input_gradient(after(gm, proj_sent), w_qkv, gr, 2 * span)
+        send, feed = fold_third(
+            [(down_dealt[1], down_a, down_dealt[3], down_b), (up_dealt[1], up_a, up_dealt[3], up_b)],
+            after(here, grad_tokens), pieces, 0,
+        )
+        feed_got = swap(send, "wide", 2)
+        proj_dealt = projection_terms(
+            *projections, after(here, feed), 0, swap(proj_sent, "narrow", 1)
+        )
+        proj_a, proj_b = swap(proj_dealt[0], "narrow", 2), swap(proj_dealt[2], "wide", 1)
+        encoded = copied(encoded, after(here, proj_dealt[1]), span)
+        send, feed = fold_fourth(feed, feed_got, after(here, encoded), 0)
+        feed_got = swap(send, "wide", 4)
+        proj_dealt = fold_second(
+            proj_dealt[1], proj_a, proj_dealt[3], proj_b, after(here, feed), pieces, 1
+        )
+        proj_a, proj_b = swap(proj_dealt[0], "wide", 1), swap(proj_dealt[2], "narrow", 2)
+        (feed,) = fold_last(feed, feed_got, after(here, proj_dealt[1]), 0)
+        feed = quarters(feed)
+        send, proj = fold_third(
+            [(proj_dealt[1], proj_a, proj_dealt[3], proj_b)], after(here, feed[0]), pieces, 1
+        )
+        proj_got = swap(send, "wide", 2)
+        grad_w_down, grad_w_up = feed_blocks(feed, after(here, proj), pieces, width)
+        send, proj = fold_fourth(proj, proj_got, after(here, grad_w_down), 1)
+        proj_got = swap(send, "wide", 4)
+        proj, vectors = fold_last(proj, proj_got, here, 1)
+        proj = quarters(proj)
+        grad_w_qkv, grad_w_out, *small = projection_blocks(proj, vectors, here, pieces)
+        small = [item.reshape(-1) for item in small]
     else:
         down_kept = down_terms(active, grad_second, here, 0)
-        up_kept, gh, bup_kept = up_terms(*ups, 0, 512, 256, gh)
-    gr, gb, gm, vec_attn = attention_backward(
-        gh, gres, n_attn, spread, table, w_out, qkv, probs, span, 2 * span
-    )
-    if paired:
-        first_up = jnp.where(here[0] == 0, bup_kept, bup_sent)
-        second_up = jnp.where(here[0] == 0, bup_sent, bup_kept)
-    else:
-        first_up, second_up = bup_kept, bup_sent
-    vectors = jnp.concatenate(
-        [
-            vec_ffn[:2].reshape(1, -1),
-            jnp.concatenate([vec_ffn[2:3], vec_attn[0:1]], axis=1),
-            vec_attn[1:5].reshape(2, -1),
-            first_up,
-            second_up,
-            jnp.zeros((2, 2 * width), F32),
-        ],
-        axis=0,
-    )
-    projections = (tokens, gm, attended, gb, vectors, here)
-    proj_sent = projection_terms(*projections, 1)
-    grad_tokens = input_gradient(gm, w_qkv, gr, 2 * span)
-    if paired:
-        proj_dealt = projection_terms(*projections, 0, swap(proj_sent, "narrow", 1))
-        (grad_w_down,) = finish(down_dealt, here, 12, 0)
-        (grad_w_up,) = finish(up_dealt, here, 3, 0)
-        grad_w_qkv, grad_w_out, *small = finish(proj_dealt, here, 3, 1)
-        small = [item.reshape(-1) for item in small]
-    else:
-        proj_kept = projection_terms(*projections, 0)
+        up_sent, gi_sent, bup_sent = up_terms(*ups, here, 1)
+        up_kept, gi_kept, bup_kept = up_terms(*ups, here, 0)
+        gh = hidden_gradient(gi_sent, w_up, here, 1)
+        gr, gb, gm, vec_attn = attention_backward(
+            gh, gres, gi_kept, w_up, *heads, here, 0, span, 2 * span
+        )
+        projections = (tokens, gm, attended, gb, (vec_ffn, vec_attn, bup_sent, bup_kept), here)
+        grad_tokens = input_gradient(gm, w_qkv, gr, 2 * span)
+        proj_sent, proj_kept = projection_terms(*projections, 1), projection_terms(*projections, 0)
         total = partial(sum_anywhere, wide_count=wide_count, narrow_count=narrow_count)
         cut = width // 2 * 3
         grad_w_down = total(jnp.concatenate([down_kept, down_sent], axis=1))
         grad_w_up = total(jnp.concatenate([up_kept, up_sent], axis=1))
         grad_w_qkv = total(jnp.concatenate([proj_kept[:width, :cut], proj_sent[:width, :cut]], axis=1))
         grad_w_out = total(jnp.concatenate([proj_kept[:width, cut:], proj_sent[:width, cut:]], axis=1))
-        small = [total(item) for item in vectors[:4].reshape(8, width)]
-        small.append(total(vectors[4:6].reshape(-1)))
+        small = [
+            total(item)
+            for item in (*vec_ffn[:3], *vec_attn[:5], jnp.concatenate([bup_kept[0], bup_sent[0]]))
+        ]
     gain_out, shift_out, b_down, b_q, b_v, b_out, g_attn, s_attn, b_up = small
     return (
         encoded, grad_tokens, grad_w_qkv, b_q, b_v, grad_w_out, b_out, g_attn, s_attn,

time: 277 us -> 254 us (0.917)
  waiting for transfers between devices: 27.5 us -> 63.7 us
  Pallas kernels: 180 us -> 152 us
  local copies, waits for them, and re-layouts: 23.3 us -> 3.8 us
  starting transfers between devices: 41.1 us -> 32.3 us
    pallas_call x25 -> x12, Pallas kernels: 180 us -> 140 us  [call(): pl.pallas_call(kernel, grid_spec=pltpu.PrefetchScalarGridSpec(num_scalar_...]
    ppermute x30 -> x25, waiting for transfers between devices: 27.5 us -> 63.7 us  [swap(): lax.ppermute(item, axis, [(index, index ^ step) for index in range(count)])]
    pallas_call x0 -> x12, Pallas kernels: none -> 11.7 us  [the longest x11 10.8 us: small_call(): pl.pallas_call(kernel, in_specs=[pl.BlockSpec(memory_space=pltpu.SMEM)] +...]
    unnamed x55 -> x24, local copies, waits for them, and re-layouts: 12.9 us -> 3.19 us
    ppermute x30 -> x25, starting transfers between devices: 34.3 us -> 25.3 us  [swap(): lax.ppermute(item, axis, [(index, index ^ step) for index in range(count)])]
    another operation x9 -> x0, local copies, waits for them, and re-layouts: 5.53 us -> none  [body(): jnp.stack([bias_q, bias_v, bias_out, gain_attn, shift_attn, bias_down, ga...]
  transfers between devices with their start and end apart: 31 -> 26, of which waited for: 8 -> 11; matrix products, arithmetic and copies ran while one was open for 1% -> 0% of each run, Pallas kernels for 41% -> 23%
where the time goes in v3:
time: 254 us; the launch traced here: 253 us
  Pallas kernels  152 us (60%)
  waiting for transfers between devices  63.7 us (25%)
  starting transfers between devices  32.3 us (13%)
  local copies, waits for them, and re-layouts  3.8 us (1%)
    pallas_call x12, Pallas kernels, call(): pl.pallas_call(kernel, grid_spec=pltpu.PrefetchScalarGridSpec(num_scalar_...  140 us
    ppermute x25, waiting for transfers between devices, swap(): lax.ppermute(item, axis, [(index, index ^ step) for index in range(count)])  63.7 us
    ppermute x25, starting transfers between devices, swap(): lax.ppermute(item, axis, [(index, index ^ step) for index in range(count)])  25.3 us
    pallas_call x11, Pallas kernels, small_call(): pl.pallas_call(kernel, in_specs=[pl.BlockSpec(memory_space=pltpu.SMEM)] +...  10.8 us
    all_to_all x1, starting transfers between devices, regroup_rows(): got = lax.all_to_all(sent, 'wide', split_axis=0, concat_axis=0, tiled=True)  6.96 us
  transfers between devices with their start and end apart: 26, of which 11 were waited for; matrix products, arithmetic and copies ran while one was open for 0% of the time, Pallas kernels for 23%

profile of v3, /device:TPU:0, one launch (start us, length us, event | category | flops | bytes accessed | tf_op | source)
XLA Modules:
  0.0 253.1 jit_solution(6069583708949109727)
XLA Ops:
  0.7 0.9 vector_table.1.tab_ref
  1.6 16.5 %attn_fwd.1 = (bf16[1024,2304]{1,0:T(8,128)(2,1)}, bf16[8,6,256,128]{3,2,1,0:T(8,128)(2,1)}, bf16[1024,768]{1,0:T(8,128)(2,1)}, f32[1024,768]{1,0:T(8,128)}, f32...) custom-call(s32[8]{0:T(128)} %slots_s.1, s32[26]{0:T(128)} %lengths_s.1, bf16[1024,768]{1,0:T(8,128)(2,1)} %x_ref.5, ...), custom_call_target="tpu_custom_call" | custom-call | flops 483183808 | bytes 1500000 | tf_op jit(solution)/shard_map/attn_fwd/pallas_call | solution.py:71
  18.1 30.5 %ffn_fwd.1 = (bf16[1024,3072]{1,0:T(8,128)(2,1)}, bf16[1024,3072]{1,0:T(8,128)(2,1)}, bf16[768,1024]{1,0:T(8,128)(2,1)}, bf16[8,128,768]{2,1,0:T(8,128)(2,1)}, f...) custom-call(s32[8]{0:T(128)} %slots_s.1, s32[1,26]{1,0:T(1,128)} %pairing_s.1, f32[13]{0:T(128)} %targets_s.1, ...), custom_call_target="tpu_custom_call" | custom-call | flops 966367616 | bytes 2000000 | tf_op jit(solution)/shard_map/ffn_fwd/pallas_call | solution.py:71
  48.6 0.6 stack.35.here_s
  49.3 6.9 %down_give.1 = bf16[3072,384]{1,0:T(8,128)(2,1)S(1)} custom-call(s32[8]{0:T(128)} %stack.35.here_s, bf16[1024,3072]{1,0:T(8,128)(2,1)} %get-tuple-element.103.act_ref, bf16[1024,768]{1,0:T(8,128)(2,1)} %get-tuple-element.104.gs_ref), custom_call_target="tpu_custom_call" | custom-call | flops 120795952 | bytes 450000 | tf_op jit(solution)/shard_map/down_give/pallas_call | solution.py:71
  56.1 0.6 collective-permute-start
  56.7 4.2 %collective-permute-done.got_ref = bf16[3072,384]{1,0:T(8,128)(2,1)S(1)} collective-permute-done((bf16[3072,384]{1,0:T(8,128)(2,1)S(1)}, bf16[3072,384]{1,0:T(8,128)(2,1)S(1)}, u32[]{:S(2)}, u32[]{:S(2)}) %collective-permute-start) | collective-permute-done | bytes 2359328 | tf_op jit(solution)/shard_map/ppermute | solution.py:905
  60.8 7.8 %down_own.1 = (bf16[24,8,1536]{2,1,0:T(8,128)(2,1)}, bf16[24,8,1536]{2,1,0:T(8,128)(2,1)S(1)}, bf16[24,8,1536]{2,1,0:T(8,128)(2,1)}, bf16[24,8,1536]{2,1,0:T(8,128)(2,1)S(1)}) custom-call(s32[8]{0:T(128)} %stack.35.here_s, bf16[1024,3072]{1,0:T(8,128)(2,1)} %get-tuple-element.103.act_ref, bf16[1024,768]{1,0:T(8,128)(2,1)} %get-tuple-element.104.gs_ref, ...), custom_call_target="tpu_custom_call" | custom-call | flops 120795952 | bytes 550000 | tf_op jit(solution)/shard_map/down_own/pallas_call | solution.py:71
  68.6 0.8 copy-done.2
  69.5 0.8 copy-done.4
  70.3 10.0 %up_give.1 = (bf16[768,1536]{1,0:T(8,128)(2,1)}, bf16[1024,1536]{1,0:T(8,128)(2,1)}, f32[1,1536]{1,0:T(1,128)S(1)}) custom-call(s32[8]{0:T(128)} %stack.35.here_s, bf16[1024,768]{1,0:T(8,128)(2,1)} %get-tuple-element.104.gs_ref, bf16[1024,3072]{1,0:T(8,128)(2,1)} %get-tuple-element.107.dg_ref, bf16[768,1024]{1,0:T(8,128)(2,1)} %get-tuple-element.108.ht_ref, ...), custom_call_target="tpu_custom_call" | custom-call | flops 241591904 | bytes 800000 | tf_op jit(solution)/shard_map/up_give/pallas_call | solution.py:71
  80.3 0.4 collective-permute-start.1
  80.6 7.0 %all-to-all-start = ((bf16[8,128,768]{2,1,0:T(8,128)(2,1)}), bf16[8,128,768]{2,1,0:T(8,128)(2,1)}, u32[]{:S(2)}, u32[]{:S(2)}) async-start(bf16[8,128,768]{2,1,0:T(8,128)(2,1)} %get-tuple-element.127), calls=%async_computation | async-start | bytes 3145728 | tf_op jit(solution)/shard_map/all_to_all | solution.py:915
  87.6 1.5 collective-permute-start.2
  89.1 2.0 collective-permute-start.3
  91.1 6.9 %hidden_grad.1.gh_ref = f32[1024,768]{1,0:T(8,128)} custom-call(s32[8]{0:T(128)} %stack.35.here_s, bf16[1024,1536]{1,0:T(8,128)(2,1)} %get-tuple-element.109.gi_ref, bf16[768,3072]{1,0:T(8,128)(2,1)} %wu_ref.5), custom_call_target="tpu_custom_call" | custom-call | flops 120795952 | bytes 450000 | tf_op jit(solution)/shard_map/hidden_grad/pallas_call | solution.py:71
  98.0 10.8 %up_own.1 = (bf16[24,8,1536]{2,1,0:T(8,128)(2,1)}, bf16[24,8,1536]{2,1,0:T(8,128)(2,1)S(1)}, bf16[24,8,1536]{2,1,0:T(8,128)(2,1)}, bf16[24,8,1536]{2,1,0:T(8,128...) custom-call(s32[8]{0:T(128)} %stack.35.here_s, bf16[1024,768]{1,0:T(8,128)(2,1)} %get-tuple-element.104.gs_ref, ...), custom_call_target="tpu_custom_call" | custom-call | flops 241591904 | bytes 800000 | tf_op jit(solution)/shard_map/up_own/pallas_call | solution.py:71
  108.8 0.8 copy-done
  109.6 0.5 collective-permute-start.4
  110.2 10.7 %collective-permute-done.3.gb = bf16[24,8,1536]{2,1,0:T(8,128)(2,1)S(1)} collective-permute-done((bf16[24,8,1536]{2,1,0:T(8,128)(2,1)}, bf16[24,8,1536]{2,1,0:T(8,128)(2,1)S(1)}, u32[]{:S(2)}, u32[]{:S(2)}) %collective-permute-start.3) | collective-permute-done | bytes 589856 | tf_op jit(solution)/shard_map/ppermute | solution.py:905
  120.8 0.8 fold_second.3
  121.7 0.7 copy-done.10
  122.4 19.3 %attn_bwd.1 = (f32[1024,768]{1,0:T(8,128)}, bf16[1024,768]{1,0:T(8,128)(2,1)}, bf16[1024,2304]{1,0:T(8,128)(2,1)}, f32[8,768]{1,0:T(8,128)S(1)}) custom-call(s32[8]{0:T(128)} %stack.35.here_s, f32[1024,768]{1,0:T(8,128)} %hidden_grad.1.gh_ref, f32[1024,768]{1,0:T(8,128)} %get-tuple-element.119.gres_ref, bf16[1024,1536]{1,0:T(8,128)(2,1)} %get-tuple-element.120.gi_ref, ...), custom_call_target="tpu_custom_call" | custom-call | flops 483183808 | bytes 2000000 | tf_op jit(solution)/shard_map/attn_bwd/pallas_call | solution.py:71
  141.8 0.8 fold_second.4
  142.6 7.9 %proj_give.1 = bf16[776,1536]{1,0:T(8,128)(2,1)S(1)} custom-call(s32[8]{0:T(128)} %stack.35.here_s, bf16[1024,768]{1,0:T(8,128)(2,1)} %x_ref.5, bf16[1024,2304]{1,0:T(8,128)(2,1)} %get-tuple-element.139.gm_ref, bf16[1024,768]{1,0:T(8,128)(2,1)} %get-tuple-element.135.att_ref, bf16[1024,768]{1,0:T(8,128)(2,1)} %get-tuple-element.136.gb_ref, ...), custom_call_target="tpu_custom_call" | custom-call | flops 120795952 | bytes 450000 | tf_op jit(solution)/shard_map/proj_give/pallas_call | solution.py:71
  150.6 0.1 collective-permute-start.6
  150.7 1.6 collective-permute-start.7
  152.2 1.9 collective-permute-start.8
  154.2 0.5 collective-permute-start.9
  154.7 8.9 %input_grad.1 = bf16[1024,768]{1,0:T(8,128)(2,1)} custom-call(bf16[1024,2304]{1,0:T(8,128)(2,1)} %get-tuple-element.139.gm_ref, bf16[768,2304]{1,0:T(8,128)(2,1)} %wq_ref.3, f32[1024,768]{1,0:T(8,128)} %get-tuple-element.140.gr_ref), custom_call_target="tpu_custom_call" | custom-call | flops 181193936 | bytes 650000 | tf_op jit(solution)/shard_map/input_grad/pallas_call | solution.py:71
  163.6 2.7 %collective-permute-done.8.refs_5_ = bf16[12,8,1536]{2,1,0:T(8,128)(2,1)S(1)} collective-permute-done((bf16[12,8,1536]{2,1,0:T(8,128)(2,1)S(1)}, bf16[12,8,1536]{2,1,0:T(8,128)(2,1)S(1)}, u32[]{:S(2)}, u32[]{:S(2)}) %collective-permute-start.8) | collective-permute-done | bytes 294944 | tf_op jit(solution)/shard_map/ppermute | solution.py:905
  166.3 0.8 fold_third.2
  167.2 8.5 %proj_own.1 = (bf16[25,8,1536]{2,1,0:T(8,128)(2,1)S(1)}, bf16[25,8,1536]{2,1,0:T(8,128)(2,1)S(1)}, bf16[24,8,1536]{2,1,0:T(8,128)(2,1)S(1)}, bf16[24,8,1536]{2,1,0:T(8,128)(2,1)S(1)}) custom-call(s32[8]{0:T(128)} %stack.35.here_s, bf16[1024,768]{1,0:T(8,128)(2,1)} %x_ref.5, bf16[1024,2304]{1,0:T(8,128)(2,1)} %get-tuple-element.139.gm_ref, ...), custom_call_target="tpu_custom_call" | custom-call | flops 120795952 | bytes 550000 | tf_op jit(solution)/shard_map/proj_own/pallas_call | solution.py:71
  175.7 1.6 collective-permute-start.12
  177.3 1.7 collective-permute-start.11
  179.0 0.3 collective-permute-start.13
  179.3 6.1 %copied.1 = bf16[1024,768]{1,0:T(8,128)(2,1)} custom-call(s32[8]{0:T(128)} %stack.35.here_s, bf16[1024,768]{1,0:T(8,128)(2,1)} %bitcast.8.in_ref), custom_call_target="tpu_custom_call" | custom-call | bytes 150000 | tf_op jit(solution)/shard_map/copied/pallas_call | solution.py:71
  185.4 6.4 %collective-permute-done.11.got_ref = bf16[24,8,1536]{2,1,0:T(8,128)(2,1)S(1)} collective-permute-done((bf16[24,8,1536]{2,1,0:T(8,128)(2,1)S(1)}, bf16[24,8,1536]{2,1,0:T(8,128)(2,1)S(1)}, u32[]{:S(2)}, u32[]{:S(2)}) %collective-permute-start.11) | collective-permute-done | bytes 589856 | tf_op jit(solution)/shard_map/ppermute | solution.py:905
  191.8 0.7 fold_fourth.2
  192.5 0.5 collective-permute-done.13.gb
  193.0 0.9 fold_second.5
  193.8 1.1 collective-permute-start.15
  194.9 2.7 %collective-permute-start.14 = (bf16[12,8,1536]{2,1,0:T(8,128)(2,1)S(1)}, bf16[12,8,1536]{2,1,0:T(8,128)(2,1)S(1)}, u32[]{:S(2)}, u32[]{:S(2)}) collective-permute-start(bf16[12,8,1536]{2,1,0:T(8,128)(2,1)S(1)} %get-tuple-element.161), channel_id=1, source_target_pairs={{0,16},{4,20},{8,24},{12,28},{16,0},{20,4},{24,8},{28,12},{1,17},{... | collective-permute-start | bytes 884744 | tf_op jit(solution)/shard_map/ppermute | solution.py:905
  197.7 0.5 collective-permute-start.16
  198.2 10.7 %collective-permute-done.14.got_ref = bf16[12,8,1536]{2,1,0:T(8,128)(2,1)S(1)} collective-permute-done((bf16[12,8,1536]{2,1,0:T(8,128)(2,1)S(1)}, bf16[12,8,1536]{2,1,0:T(8,128)(2,1)S(1)}, u32[]{:S(2)}, u32[]{:S(2)}) %collective-permute-start.14) | collective-permute-done | bytes 294944 | tf_op jit(solution)/shard_map/ppermute | solution.py:905
  208.9 0.6 fold_last.2.me
  209.6 0.7 fold_third.3
  210.3 0.4 collective-permute-start.20
  210.7 0.6 collective-permute-start.18
  211.3 1.5 collective-permute-start.17
  212.8 7.2 %collective-permute-done.19.gd = bf16[12,8,1536]{2,1,0:T(8,128)(2,1)S(1)} collective-permute-done((bf16[12,8,1536]{2,1,0:T(8,128)(2,1)S(1)}, bf16[12,8,1536]{2,1,0:T(8,128)(2,1)S(1)}, u32[]{:S(2)}, u32[]{:S(2)}) %collective-permute-start.19) | collective-permute-done | bytes 294944 | tf_op jit(solution)/shard_map/ppermute | solution.py:905
  220.0 5.8 %collective-permute-done.17.gx = bf16[12,8,1536]{2,1,0:T(8,128)(2,1)S(1)} collective-permute-done((bf16[12,8,1536]{2,1,0:T(8,128)(2,1)S(1)}, bf16[12,8,1536]{2,1,0:T(8,128)(2,1)S(1)}, u32[]{:S(2)}, u32[]{:S(2)}) %collective-permute-start.17) | collective-permute-done | bytes 294944 | tf_op jit(solution)/shard_map/ppermute | solution.py:905
  225.8 2.4 feed_blocks.1
  228.2 0.6 fold_fourth.3
  228.9 3.4 %collective-permute-start.21 = (bf16[7,8,1536]{2,1,0:T(8,128)(2,1)S(1)}, bf16[7,8,1536]{2,1,0:T(8,128)(2,1)S(1)}, u32[]{:S(2)}, u32[]{:S(2)}) collective-permute-start(bf16[7,8,1536]{2,1,0:T(8,128)(2,1)S(1)} %get-tuple-element.172), channel_id=1, source_target_pairs={{0,16},{4,20},{8,24},{12,28},{16,0},{20,4},{24,8},{28,12},{1,17},{... | collective-permute-start | bytes 516104 | tf_op jit(solution)/shard_map/ppermute | solution.py:905
  232.3 8.3 %collective-permute-done.21.got_ref = bf16[7,8,1536]{2,1,0:T(8,128)(2,1)S(1)} collective-permute-done((bf16[7,8,1536]{2,1,0:T(8,128)(2,1)S(1)}, bf16[7,8,1536]{2,1,0:T(8,128)(2,1)S(1)}, u32[]{:S(2)}, u32[]{:S(2)}) %collective-permute-start.21) | collective-permute-done | bytes 172064 | tf_op jit(solution)/shard_map/ppermute | solution.py:905
  240.6 0.6 fold_last.3
  241.2 0.3 collective-permute-start.24
  241.6 0.9 collective-permute-start.23
  242.4 1.0 collective-permute-start.22
  243.4 3.8 %collective-permute-done.24.gd = bf16[6,8,1536]{2,1,0:T(8,128)(2,1)S(1)} collective-permute-done((bf16[6,8,1536]{2,1,0:T(8,128)(2,1)S(1)}, bf16[6,8,1536]{2,1,0:T(8,128)(2,1)S(1)}, u32[]{:S(2)}, u32[]{:S(2)}) %collective-permute-start.24) | collective-permute-done | bytes 147488 | tf_op jit(solution)/shard_map/ppermute | solution.py:905
  247.2 3.4 %collective-permute-done.22.gx = bf16[6,8,1536]{2,1,0:T(8,128)(2,1)S(1)} collective-permute-done((bf16[6,8,1536]{2,1,0:T(8,128)(2,1)S(1)}, bf16[6,8,1536]{2,1,0:T(8,128)(2,1)S(1)}, u32[]{:S(2)}, u32[]{:S(2)}) %collective-permute-start.22) | collective-permute-done | bytes 147488 | tf_op jit(solution)/shard_map/ppermute | solution.py:905
  250.6 1.9 projection_blocks.1
  252.5 0.6 reduce
  (38 shorter events, 0.2 us)
Async XLA Ops:
  56.1 4.7 %collective-permute-start = (bf16[3072,384]{1,0:T(8,128)(2,1)S(1)}, bf16[3072,384]{1,0:T(8,128)(2,1)S(1)}, u32[]{:S(2)}, u32[]{:S(2)}) collective-permute-start(bf16[3072,384]{1,0:T(8,128)(2,1)S(1)} %down_give.1), channel_id=1, source_target_pairs={{0,1},{1,0},{2,3},{3,2},{4,5},{5,4},{6,7},{7,6},{8,9},{9,8},{10,11... | collective-permute-start | bytes 7077896 | tf_op jit(solution)/shard_map/ppermute | solution.py:905
  68.6 0.8 copy-start.2
  69.5 0.8 copy-start.4
  80.3 17.7 %collective-permute-start.1 = (bf16[768,1536]{1,0:T(8,128)(2,1)}, bf16[768,1536]{1,0:T(8,128)(2,1)S(1)}, u32[]{:S(2)}, u32[]{:S(2)}) collective-permute-start(bf16[768,1536]{1,0:T(8,128)(2,1)} %get-tuple-element.111), channel_id=1, source_target_pairs={{0,1},{1,0},{2,3},{3,2},{4,5},{5,4},{6,7},{7,6},{8,9},{9,8},{10,11... | collective-permute-start | bytes 7077896 | tf_op jit(solution)/shard_map/ppermute | solution.py:905
  80.6 61.1 %all-to-all-start = ((bf16[8,128,768]{2,1,0:T(8,128)(2,1)}), bf16[8,128,768]{2,1,0:T(8,128)(2,1)}, u32[]{:S(2)}, u32[]{:S(2)}) async-start(bf16[8,128,768]{2,1,0:T(8,128)(2,1)} %get-tuple-element.127), calls=%async_computation | async-start | bytes 3145728 | tf_op jit(solution)/shard_map/all_to_all | solution.py:915
  87.6 22.6 %collective-permute-start.2 = (bf16[24,8,1536]{2,1,0:T(8,128)(2,1)}, bf16[24,8,1536]{2,1,0:T(8,128)(2,1)S(1)}, u32[]{:S(2)}, u32[]{:S(2)}) collective-permute-start(bf16[24,8,1536]{2,1,0:T(8,128)(2,1)} %get-tuple-element.114), channel_id=1, source_target_pairs={{0,2},{1,3},{2,0},{3,1},{4,6},{5,7},{6,4},{7,5},{8,10},{9,11},{10,... | collective-permute-start | bytes 1769480 | tf_op jit(solution)/shard_map/ppermute | solution.py:905
  89.1 31.8 %collective-permute-start.3 = (bf16[24,8,1536]{2,1,0:T(8,128)(2,1)}, bf16[24,8,1536]{2,1,0:T(8,128)(2,1)S(1)}, u32[]{:S(2)}, u32[]{:S(2)}) collective-permute-start(bf16[24,8,1536]{2,1,0:T(8,128)(2,1)} %get-tuple-element.116), channel_id=1, source_target_pairs={{0,4},{4,0},{8,12},{12,8},{16,20},{20,16},{24,28},{28,24},{1,5},{5... | collective-permute-start | bytes 1769480 | tf_op jit(solution)/shard_map/ppermute | solution.py:905
  98.0 22.9 %copy-start.3 = (bf16[24,8,1536]{2,1,0:T(8,128)(2,1)S(1)}, bf16[24,8,1536]{2,1,0:T(8,128)(2,1)}, u32[]{:S(2)}) copy-start(bf16[24,8,1536]{2,1,0:T(8,128)(2,1)} %copy-done.2) | copy-start | bytes 1769476
  98.0 22.9 %copy-start.5 = (bf16[24,8,1536]{2,1,0:T(8,128)(2,1)S(1)}, bf16[24,8,1536]{2,1,0:T(8,128)(2,1)}, u32[]{:S(2)}) copy-start(bf16[24,8,1536]{2,1,0:T(8,128)(2,1)} %copy-done.4) | copy-start | bytes 1769476
  98.0 22.9 %copy-start.6 = (s32[8]{0:T(128)S(1)}, s32[8]{0:T(128)}, u32[]{:S(2)}) copy-start(s32[8]{0:T(128)} %stack.35.here_s) | copy-start | bytes 100
  108.8 0.8 copy-start
  109.6 32.1 %collective-permute-start.4 = (bf16[24,8,1536]{2,1,0:T(8,128)(2,1)}, bf16[24,8,1536]{2,1,0:T(8,128)(2,1)S(1)}, u32[]{:S(2)}, u32[]{:S(2)}) collective-permute-start(bf16[24,8,1536]{2,1,0:T(8,128)(2,1)} %get-tuple-element.130), channel_id=1, source_target_pairs={{0,2},{1,3},{2,0},{3,1},{4,6},{5,7},{6,4},{7,5},{8,10},{9,11},{10,... | collective-permute-start | bytes 1769480 | tf_op jit(solution)/shard_map/ppermute | solution.py:905
  110.1 31.6 %collective-permute-start.5 = (bf16[24,8,1536]{2,1,0:T(8,128)(2,1)}, bf16[24,8,1536]{2,1,0:T(8,128)(2,1)S(1)}, u32[]{:S(2)}, u32[]{:S(2)}) collective-permute-start(bf16[24,8,1536]{2,1,0:T(8,128)(2,1)} %get-tuple-element.132), channel_id=1, source_target_pairs={{0,4},{4,0},{8,12},{12,8},{16,20},{20,16},{24,28},{28,24},{1,5},{5... | collective-permute-start | bytes 1769480 | tf_op jit(solution)/shard_map/ppermute | solution.py:905
  121.7 0.7 copy-start.10
  122.4 19.4 %copy-start.1 = (bf16[24,8,1536]{2,1,0:T(8,128)(2,1)S(1)}, bf16[24,8,1536]{2,1,0:T(8,128)(2,1)}, u32[]{:S(2)}) copy-start(bf16[24,8,1536]{2,1,0:T(8,128)(2,1)} %copy-done) | copy-start | bytes 1769476
  122.4 19.4 %copy-start.7 = (s32[8]{0:T(128)S(1)}, s32[8]{0:T(128)}, u32[]{:S(2)}) copy-start(s32[8]{0:T(128)} %stack.35.here_s) | copy-start | bytes 100
  142.6 8.0 %copy-start.11 = (bf16[12,8,1536]{2,1,0:T(8,128)(2,1)S(1)}, bf16[12,8,1536]{2,1,0:T(8,128)(2,1)}, u32[]{:S(2)}) copy-start(bf16[12,8,1536]{2,1,0:T(8,128)(2,1)} %copy-done.10) | copy-start | bytes 884740
  150.5 16.6 %collective-permute-start.10 = (bf16[776,1536]{1,0:T(8,128)(2,1)S(1)}, bf16[776,1536]{1,0:T(8,128)(2,1)S(1)}, u32[]{:S(2)}, u32[]{:S(2)}) collective-permute-start(bf16[776,1536]{1,0:T(8,128)(2,1)S(1)} %proj_give.1), channel_id=1, source_target_pairs={{0,1},{1,0},{2,3},{3,2},{4,5},{5,4},{6,7},{7,6},{8,9},{9,8},{10,11... | collective-permute-start | bytes 7151624 | tf_op jit(solution)/shard_map/ppermute | solution.py:905
  150.6 13.0 %collective-permute-start.6 = (bf16[12,8,1536]{2,1,0:T(8,128)(2,1)S(1)}, bf16[12,8,1536]{2,1,0:T(8,128)(2,1)S(1)}, u32[]{:S(2)}, u32[]{:S(2)}) collective-permute-start(bf16[12,8,1536]{2,1,0:T(8,128)(2,1)S(1)} %copy-done.11), channel_id=1, source_target_pairs={{0,4},{4,0},{8,12},{12,8},{16,20},{20,16},{24,28},{28,24},{1,5},{5... | collective-permute-start | bytes 884744 | tf_op jit(solution)/shard_map/ppermute | solution.py:905
  150.7 12.9 %collective-permute-start.7 = (bf16[12,8,1536]{2,1,0:T(8,128)(2,1)S(1)}, bf16[12,8,1536]{2,1,0:T(8,128)(2,1)S(1)}, u32[]{:S(2)}, u32[]{:S(2)}) collective-permute-start(bf16[12,8,1536]{2,1,0:T(8,128)(2,1)S(1)} %get-tuple-element.144), channel_id=1, source_target_pairs={{0,2},{1,3},{2,0},{3,1},{4,6},{5,7},{6,4},{7,5},{8,10},{9,11},{10,... | collective-permute-start | bytes 884744 | tf_op jit(solution)/shard_map/ppermute | solution.py:905
  152.2 14.1 %collective-permute-start.8 = (bf16[12,8,1536]{2,1,0:T(8,128)(2,1)S(1)}, bf16[12,8,1536]{2,1,0:T(8,128)(2,1)S(1)}, u32[]{:S(2)}, u32[]{:S(2)}) collective-permute-start(bf16[12,8,1536]{2,1,0:T(8,128)(2,1)S(1)} %get-tuple-element.145), channel_id=1, source_target_pairs={{0,4},{4,0},{8,12},{12,8},{16,20},{20,16},{24,28},{28,24},{1,5},{5... | collective-permute-start | bytes 884744 | tf_op jit(solution)/shard_map/ppermute | solution.py:905
  154.2 12.1 %collective-permute-start.9 = (bf16[12,8,1536]{2,1,0:T(8,128)(2,1)S(1)}, bf16[12,8,1536]{2,1,0:T(8,128)(2,1)S(1)}, u32[]{:S(2)}, u32[]{:S(2)}) collective-permute-start(bf16[12,8,1536]{2,1,0:T(8,128)(2,1)S(1)} %get-tuple-element.147), channel_id=1, source_target_pairs={{0,2},{1,3},{2,0},{3,1},{4,6},{5,7},{6,4},{7,5},{8,10},{9,11},{10,... | collective-permute-start | bytes 884744 | tf_op jit(solution)/shard_map/ppermute | solution.py:905
  154.7 11.6 %copy-start.8 = (s32[8]{0:T(128)S(1)}, s32[8]{0:T(128)}, u32[]{:S(2)}) copy-start(s32[8]{0:T(128)} %stack.35.here_s) | copy-start | bytes 100
  175.7 16.1 %copy-start.9 = (s32[8]{0:T(128)S(1)}, s32[8]{0:T(128)}, u32[]{:S(2)}) copy-start(s32[8]{0:T(128)} %stack.35.here_s) | copy-start | bytes 100
  175.7 17.3 %collective-permute-start.12 = (bf16[25,8,1536]{2,1,0:T(8,128)(2,1)S(1)}, bf16[25,8,1536]{2,1,0:T(8,128)(2,1)S(1)}, u32[]{:S(2)}, u32[]{:S(2)}) collective-permute-start(bf16[25,8,1536]{2,1,0:T(8,128)(2,1)S(1)} %get-tuple-element.156), channel_id=1, source_target_pairs={{0,2},{1,3},{2,0},{3,1},{4,6},{5,7},{6,4},{7,5},{8,10},{9,11},{10,... | collective-permute-start | bytes 1843208 | tf_op jit(solution)/shard_map/ppermute | solution.py:905
  177.3 14.5 %collective-permute-start.11 = (bf16[24,8,1536]{2,1,0:T(8,128)(2,1)S(1)}, bf16[24,8,1536]{2,1,0:T(8,128)(2,1)S(1)}, u32[]{:S(2)}, u32[]{:S(2)}) collective-permute-start(bf16[24,8,1536]{2,1,0:T(8,128)(2,1)S(1)} %get-tuple-element.153), channel_id=1, source_target_pairs={{0,8},{4,12},{8,0},{12,4},{16,24},{20,28},{24,16},{28,20},{1,9},{5... | collective-permute-start | bytes 1769480 | tf_op jit(solution)/shard_map/ppermute | solution.py:905
  179.0 14.0 %collective-permute-start.13 = (bf16[24,8,1536]{2,1,0:T(8,128)(2,1)S(1)}, bf16[24,8,1536]{2,1,0:T(8,128)(2,1)S(1)}, u32[]{:S(2)}, u32[]{:S(2)}) collective-permute-start(bf16[24,8,1536]{2,1,0:T(8,128)(2,1)S(1)} %get-tuple-element.158), channel_id=1, source_target_pairs={{0,4},{4,0},{8,12},{12,8},{16,20},{20,16},{24,28},{28,24},{1,5},{5... | collective-permute-start | bytes 1769480 | tf_op jit(solution)/shard_map/ppermute | solution.py:905
  193.8 15.7 %collective-permute-start.15 = (bf16[13,8,1536]{2,1,0:T(8,128)(2,1)S(1)}, bf16[13,8,1536]{2,1,0:T(8,128)(2,1)S(1)}, u32[]{:S(2)}, u32[]{:S(2)}) collective-permute-start(bf16[13,8,1536]{2,1,0:T(8,128)(2,1)S(1)} %get-tuple-element.163), channel_id=1, source_target_pairs={{0,4},{4,0},{8,12},{12,8},{16,20},{20,16},{24,28},{28,24},{1,5},{5... | collective-permute-start | bytes 958472 | tf_op jit(solution)/shard_map/ppermute | solution.py:905
  194.9 14.0 %collective-permute-start.14 = (bf16[12,8,1536]{2,1,0:T(8,128)(2,1)S(1)}, bf16[12,8,1536]{2,1,0:T(8,128)(2,1)S(1)}, u32[]{:S(2)}, u32[]{:S(2)}) collective-permute-start(bf16[12,8,1536]{2,1,0:T(8,128)(2,1)S(1)} %get-tuple-element.161), channel_id=1, source_target_pairs={{0,16},{4,20},{8,24},{12,28},{16,0},{20,4},{24,8},{28,12},{1,17},{... | collective-permute-start | bytes 884744 | tf_op jit(solution)/shard_map/ppermute | solution.py:905
  197.7 11.9 %collective-permute-start.16 = (bf16[12,8,1536]{2,1,0:T(8,128)(2,1)S(1)}, bf16[12,8,1536]{2,1,0:T(8,128)(2,1)S(1)}, u32[]{:S(2)}, u32[]{:S(2)}) collective-permute-start(bf16[12,8,1536]{2,1,0:T(8,128)(2,1)S(1)} %get-tuple-element.165), channel_id=1, source_target_pairs={{0,2},{1,3},{2,0},{3,1},{4,6},{5,7},{6,4},{7,5},{8,10},{9,11},{10,... | collective-permute-start | bytes 884744 | tf_op jit(solution)/shard_map/ppermute | solution.py:905
  210.3 18.0 %collective-permute-start.20 = (bf16[13,8,1536]{2,1,0:T(8,128)(2,1)S(1)}, bf16[13,8,1536]{2,1,0:T(8,128)(2,1)S(1)}, u32[]{:S(2)}, u32[]{:S(2)}) collective-permute-start(bf16[13,8,1536]{2,1,0:T(8,128)(2,1)S(1)} %get-tuple-element.170), channel_id=1, source_target_pairs={{0,8},{4,12},{8,0},{12,4},{16,24},{20,28},{24,16},{28,20},{1,9},{5... | collective-permute-start | bytes 958472 | tf_op jit(solution)/shard_map/ppermute | solution.py:905
  210.7 9.3 %collective-permute-start.19 = (bf16[12,8,1536]{2,1,0:T(8,128)(2,1)S(1)}, bf16[12,8,1536]{2,1,0:T(8,128)(2,1)S(1)}, u32[]{:S(2)}, u32[]{:S(2)}) collective-permute-start(bf16[12,8,1536]{2,1,0:T(8,128)(2,1)S(1)} %fold_last.2.me), channel_id=1, source_target_pairs={{0,3},{1,2},{2,1},{3,0},{4,7},{5,6},{6,5},{7,4},{8,11},{9,10},{10,... | collective-permute-start | bytes 884744 | tf_op jit(solution)/shard_map/ppermute | solution.py:905
  210.7 9.3 %collective-permute-start.18 = (bf16[12,8,1536]{2,1,0:T(8,128)(2,1)S(1)}, bf16[12,8,1536]{2,1,0:T(8,128)(2,1)S(1)}, u32[]{:S(2)}, u32[]{:S(2)}) collective-permute-start(bf16[12,8,1536]{2,1,0:T(8,128)(2,1)S(1)} %fold_last.2.me), channel_id=1, source_target_pairs={{0,1},{1,0},{2,3},{3,2},{4,5},{5,4},{6,7},{7,6},{8,9},{9,8},{10,11... | collective-permute-start | bytes 884744 | tf_op jit(solution)/shard_map/ppermute | solution.py:905
  211.3 14.5 %collective-permute-start.17 = (bf16[12,8,1536]{2,1,0:T(8,128)(2,1)S(1)}, bf16[12,8,1536]{2,1,0:T(8,128)(2,1)S(1)}, u32[]{:S(2)}, u32[]{:S(2)}) collective-permute-start(bf16[12,8,1536]{2,1,0:T(8,128)(2,1)S(1)} %fold_last.2.me), channel_id=1, source_target_pairs={{0,2},{1,3},{2,0},{3,1},{4,6},{5,7},{6,4},{7,5},{8,10},{9,11},{10,... | collective-permute-start | bytes 884744 | tf_op jit(solution)/shard_map/ppermute | solution.py:905
  228.9 11.8 %collective-permute-start.21 = (bf16[7,8,1536]{2,1,0:T(8,128)(2,1)S(1)}, bf16[7,8,1536]{2,1,0:T(8,128)(2,1)S(1)}, u32[]{:S(2)}, u32[]{:S(2)}) collective-permute-start(bf16[7,8,1536]{2,1,0:T(8,128)(2,1)S(1)} %get-tuple-element.172), channel_id=1, source_target_pairs={{0,16},{4,20},{8,24},{12,28},{16,0},{20,4},{24,8},{28,12},{1,17},{... | collective-permute-start | bytes 516104 | tf_op jit(solution)/shard_map/ppermute | solution.py:905
  241.2 6.0 %collective-permute-start.24 = (bf16[6,8,1536]{2,1,0:T(8,128)(2,1)S(1)}, bf16[6,8,1536]{2,1,0:T(8,128)(2,1)S(1)}, u32[]{:S(2)}, u32[]{:S(2)}) collective-permute-start(bf16[6,8,1536]{2,1,0:T(8,128)(2,1)S(1)} %get-tuple-element.173.me), channel_id=1, source_target_pairs={{0,3},{1,2},{2,1},{3,0},{4,7},{5,6},{6,5},{7,4},{8,11},{9,10},{10,... | collective-permute-start | bytes 442376 | tf_op jit(solution)/shard_map/ppermute | solution.py:905
  241.6 5.7 %collective-permute-start.23 = (bf16[6,8,1536]{2,1,0:T(8,128)(2,1)S(1)}, bf16[6,8,1536]{2,1,0:T(8,128)(2,1)S(1)}, u32[]{:S(2)}, u32[]{:S(2)}) collective-permute-start(bf16[6,8,1536]{2,1,0:T(8,128)(2,1)S(1)} %get-tuple-element.173.me), channel_id=1, source_target_pairs={{0,1},{1,0},{2,3},{3,2},{4,5},{5,4},{6,7},{7,6},{8,9},{9,8},{10,11... | collective-permute-start | bytes 442376 | tf_op jit(solution)/shard_map/ppermute | solution.py:905
  242.4 8.2 %collective-permute-start.22 = (bf16[6,8,1536]{2,1,0:T(8,128)(2,1)S(1)}, bf16[6,8,1536]{2,1,0:T(8,128)(2,1)S(1)}, u32[]{:S(2)}, u32[]{:S(2)}) collective-permute-start(bf16[6,8,1536]{2,1,0:T(8,128)(2,1)S(1)} %get-tuple-element.173.me), channel_id=1, source_target_pairs={{0,2},{1,3},{2,0},{3,1},{4,6},{5,7},{6,4},{7,5},{8,10},{9,11},{10,... | collective-permute-start | bytes 442376 | tf_op jit(solution)/shard_map/ppermute | solution.py:905

commit v4 on v3

--- a/solution.py
+++ b/solution.py
@@ -55,12 +55,12 @@
 
 
 def call(
-    kernel, name, grid, prefetch, in_specs, out_specs, out_shape, scratch, flops, moved, args, vmem=24, free=0, loose=0
+    kernel, name, grid, prefetch, in_specs, out_specs, out_shape, scratch, flops, moved, args, vmem=24, free=0, loose=()
 ):
     single = not isinstance(out_shape, list)
     shapes = [out_shape] if single else out_shape
     shapes = [
-        pltpu.HBM(item.shape, item.dtype) if large(item) and number >= loose else item
+        pltpu.HBM(item.shape, item.dtype) if large(item) and number not in loose else item
         for number, item in enumerate(shapes)
     ]
     out_shape = shapes[0] if single else shapes
@@ -442,7 +442,7 @@
         return call(
             give, "down_give", (steps,), (here,), in_specs,
             pl.BlockSpec((tall, half), lambda i, *_: (i, 0)),
-            shaped((ff, half), BF16), [], flops, 9e6, (active, grad_second), 20, 0, 1,
+            shaped((ff, half), BF16), [], flops, 9e6, (active, grad_second), 20, 0, (0,),
         )
     block = (2 * pieces, 8, folds * half)
     return call(
@@ -451,7 +451,7 @@
         [pl.BlockSpec(block, lambda i, *_: (i, 0, 0))] * 4,
         [shaped((8 * pieces, 8, folds * half), BF16)] * 4,
         [pltpu.VMEM((1, 2, 2, 2, folds * pieces, 8, half), F32)],
-        flops, 11e6, (active, grad_second, got), 24, 1, 4,
+        flops, 11e6, (active, grad_second, got), 24, 1, (0, 2),
     )
 
 
@@ -516,7 +516,7 @@
             pl.BlockSpec((1, chunk), lambda i, *_: (0, i)),
         ],
         out_shape + [shaped((rows, half), BF16), shaped((1, half), F32)],
-        scratch, 4 * rows * width * half, 16e6, args, 34, 0 if got is None else 1, 1 if got is None else 4,
+        scratch, 4 * rows * width * half, 16e6, args, 34, 0 if got is None else 1, (0,) if got is None else (0, 2),
     )
 
 
@@ -685,7 +685,7 @@
             give, "proj_give", (4,), (here,), in_specs,
             pl.BlockSpec((width + 8, part), lambda i, *_: (0, i)),
             shaped((width + 8, 4 * part), BF16),
-            [pltpu.VMEM((width, part), F32)], flops, 9e6, args, 20, 0, 1,
+            [pltpu.VMEM((width, part), F32)], flops, 9e6, args, 20, 0, (0,),
         )
     return call(
         own, "proj_own", (4,), (here,),
@@ -696,7 +696,7 @@
         ],
         [shaped((8 * pieces + extra, 8, 4 * part), BF16) for extra in (1, 1, 0, 0)],
         [pltpu.VMEM((width, part), F32), pltpu.VMEM((4, 2, 2, 2, pieces, 8, part), F32)],
-        flops, 11e6, args + [got], 24, 1, 4,
+        flops, 11e6, args + [got], 24, 1, (0, 1, 2, 3),
     )
 
 
@@ -906,7 +906,8 @@
 
 
 def quarters(mine):
-    return mine, swap(mine, "narrow", 2), swap(mine, "narrow", 1), swap(mine, "narrow", 3)
+    across = swap(mine, "narrow", 2)
+    return mine, across, swap(mine, "narrow", 1), swap(across, "narrow", 1)
 
 
 def regroup_rows(sent, bucket, wide_count, batches):
@@ -970,12 +971,12 @@
     ups = (grad_second, slope, hidden_t, w_down)
     heads = (n_attn, spread, table, w_out, qkv, probs)
     down_sent = down_terms(active, grad_second, here, 1)
-    encoded = regroup_rows(after(sent, down_sent), bucket, wide_count, batches)
     if paired:
-        down_dealt = down_terms(active, grad_second, here, 0, swap(down_sent, "narrow", 1))
+        up_sent, gi_sent, bup_sent = up_terms(*ups, after(here, down_sent), 1)
+        down_dealt = down_terms(active, grad_second, after(here, bup_sent), 0, swap(down_sent, "narrow", 1))
         down_a, down_b = swap(down_dealt[0], "narrow", 2), swap(down_dealt[2], "wide", 1)
-        up_sent, gi_sent, bup_sent = up_terms(*ups, after(here, down_dealt[1]), 1)
-        gh = hidden_gradient(gi_sent, w_up, here, 1)
+        encoded = regroup_rows(after(sent, down_dealt[1]), bucket, wide_count, batches)
+        gh = hidden_gradient(gi_sent, w_up, after(here, down_dealt[1]), 1)
         *up_dealt, gi_kept, bup_kept = up_terms(
             *ups, after(here, gh), 0, swap(up_sent, "narrow", 1)
         )
@@ -1003,17 +1004,17 @@
             *projections, after(here, feed), 0, swap(proj_sent, "narrow", 1)
         )
         proj_a, proj_b = swap(proj_dealt[0], "narrow", 2), swap(proj_dealt[2], "wide", 1)
-        encoded = copied(encoded, after(here, proj_dealt[1]), span)
-        send, feed = fold_fourth(feed, feed_got, after(here, encoded), 0)
+        send, feed = fold_fourth(feed, feed_got, after(here, proj_dealt[1]), 0)
         feed_got = swap(send, "wide", 4)
+        encoded = copied(encoded, after(here, feed), span)
+        (feed,) = fold_last(feed, feed_got, after(here, encoded), 0)
         proj_dealt = fold_second(
             proj_dealt[1], proj_a, proj_dealt[3], proj_b, after(here, feed), pieces, 1
         )
         proj_a, proj_b = swap(proj_dealt[0], "wide", 1), swap(proj_dealt[2], "narrow", 2)
-        (feed,) = fold_last(feed, feed_got, after(here, proj_dealt[1]), 0)
-        feed = quarters(feed)
+        feed = quarters(after(feed, proj_dealt[1]))
         send, proj = fold_third(
-            [(proj_dealt[1], proj_a, proj_dealt[3], proj_b)], after(here, feed[0]), pieces, 1
+            [(proj_dealt[1], proj_a, proj_dealt[3], proj_b)], here, pieces, 1
         )
         proj_got = swap(send, "wide", 2)
         grad_w_down, grad_w_up = feed_blocks(feed, after(here, proj), pieces, width)
@@ -1024,6 +1025,7 @@
         grad_w_qkv, grad_w_out, *small = projection_blocks(proj, vectors, here, pieces)
         small = [item.reshape(-1) for item in small]
     else:
+        encoded = regroup_rows(sent, bucket, wide_count, batches)
         down_kept = down_terms(active, grad_second, here, 0)
         up_sent, gi_sent, bup_sent = up_terms(*ups, here, 1)
         up_kept, gi_kept, bup_kept = up_terms(*ups, here, 0)

time: 254 us -> 236 us (0.929)
  waiting for transfers between devices: 63.7 us -> 50.4 us
  starting transfers between devices: 32.3 us -> 29 us
    ppermute x25, waiting for transfers between devices: 63.7 us -> 50.4 us  [swap(): lax.ppermute(item, axis, [(index, index ^ step) for index in range(count)])]
    ppermute x25, starting transfers between devices: 25.3 us -> 21.7 us  [swap(): lax.ppermute(item, axis, [(index, index ^ step) for index in range(count)])]
  transfers between devices with their start and end apart: 26 -> 26, of which waited for: 11 -> 10; matrix products, arithmetic and copies ran while one was open for 0% -> 0% of each run, Pallas kernels for 23% -> 36%
where the time goes in v4:
time: 236 us; the launch traced here: 235 us
  Pallas kernels  152 us (64%)
  waiting for transfers between devices  50.4 us (21%)
  starting transfers between devices  29 us (12%)
    pallas_call x12, Pallas kernels, call(): pl.pallas_call(kernel, grid_spec=pltpu.PrefetchScalarGridSpec(num_scalar_...  140 us
    ppermute x25, waiting for transfers between devices, swap(): lax.ppermute(item, axis, [(index, index ^ step) for index in range(count)])  50.4 us
    ppermute x25, starting transfers between devices, swap(): lax.ppermute(item, axis, [(index, index ^ step) for index in range(count)])  21.7 us
    pallas_call x11, Pallas kernels, small_call(): pl.pallas_call(kernel, in_specs=[pl.BlockSpec(memory_space=pltpu.SMEM)] +...  10.8 us
    all_to_all x1, starting transfers between devices, regroup_rows(): got = lax.all_to_all(sent, 'wide', split_axis=0, concat_axis=0, tiled=True)  7.31 us
  transfers between devices with their start and end apart: 26, of which 10 were waited for; matrix products, arithmetic and copies ran while one was open for 0% of the time, Pallas kernels for 36%

profile of v4, /device:TPU:0, one launch (start us, length us, event | category | flops | bytes accessed | tf_op | source)
XLA Modules:
  0.0 235.2 jit_solution(555554062377918127)
XLA Ops:
  0.7 0.9 vector_table.1.tab_ref
  1.6 16.5 %attn_fwd.1 = (bf16[1024,2304]{1,0:T(8,128)(2,1)}, bf16[8,6,256,128]{3,2,1,0:T(8,128)(2,1)}, bf16[1024,768]{1,0:T(8,128)(2,1)}, f32[1024,768]{1,0:T(8,128)}, f32...) custom-call(s32[8]{0:T(128)} %slots_s.1, s32[26]{0:T(128)} %lengths_s.1, bf16[1024,768]{1,0:T(8,128)(2,1)} %x_ref.5, ...), custom_call_target="tpu_custom_call" | custom-call | flops 483183808 | bytes 1500000 | tf_op jit(solution)/shard_map/attn_fwd/pallas_call | solution.py:71
  18.1 30.5 %ffn_fwd.1 = (bf16[1024,3072]{1,0:T(8,128)(2,1)}, bf16[1024,3072]{1,0:T(8,128)(2,1)}, bf16[768,1024]{1,0:T(8,128)(2,1)}, bf16[8,128,768]{2,1,0:T(8,128)(2,1)}, f...) custom-call(s32[8]{0:T(128)} %slots_s.1, s32[1,26]{1,0:T(1,128)} %pairing_s.1, f32[13]{0:T(128)} %targets_s.1, ...), custom_call_target="tpu_custom_call" | custom-call | flops 966367616 | bytes 2000000 | tf_op jit(solution)/shard_map/ffn_fwd/pallas_call | solution.py:71
  48.7 0.6 stack.35.here_s
  49.3 6.9 %down_give.1 = bf16[3072,384]{1,0:T(8,128)(2,1)S(1)} custom-call(s32[8]{0:T(128)} %stack.35.here_s, bf16[1024,3072]{1,0:T(8,128)(2,1)} %get-tuple-element.105.act_ref, bf16[1024,768]{1,0:T(8,128)(2,1)} %get-tuple-element.106.gs_ref), custom_call_target="tpu_custom_call" | custom-call | flops 120795952 | bytes 450000 | tf_op jit(solution)/shard_map/down_give/pallas_call | solution.py:71
  56.1 0.6 collective-permute-start
  56.7 10.0 %up_give.1 = (bf16[768,1536]{1,0:T(8,128)(2,1)}, bf16[1024,1536]{1,0:T(8,128)(2,1)}, f32[1,1536]{1,0:T(1,128)S(1)}) custom-call(s32[8]{0:T(128)} %stack.35.here_s, bf16[1024,768]{1,0:T(8,128)(2,1)} %get-tuple-element.106.gs_ref, bf16[1024,3072]{1,0:T(8,128)(2,1)} %get-tuple-element.108.dg_ref, bf16[768,1024]{1,0:T(8,128)(2,1)} %get-tuple-element.109.ht_ref, ...), custom_call_target="tpu_custom_call" | custom-call | flops 241591904 | bytes 800000 | tf_op jit(solution)/shard_map/up_give/pallas_call | solution.py:71
  66.7 0.0 collective-permute-start.1
  66.7 7.8 %down_own.1 = (bf16[24,8,1536]{2,1,0:T(8,128)(2,1)S(1)}, bf16[24,8,1536]{2,1,0:T(8,128)(2,1)}, bf16[24,8,1536]{2,1,0:T(8,128)(2,1)S(1)}, bf16[24,8,1536]{2,1,0:T(8,128)(2,1)}) custom-call(s32[8]{0:T(128)} %stack.35.here_s, bf16[1024,3072]{1,0:T(8,128)(2,1)} %get-tuple-element.105.act_ref, bf16[1024,768]{1,0:T(8,128)(2,1)} %get-tuple-element.106.gs_ref, ...), custom_call_target="tpu_custom_call" | custom-call | flops 120795952 | bytes 550000 | tf_op jit(solution)/shard_map/down_own/pallas_call | solution.py:71
  74.5 0.8 copy-done.9
  75.3 7.3 %all-to-all-start = ((bf16[8,128,768]{2,1,0:T(8,128)(2,1)}), bf16[8,128,768]{2,1,0:T(8,128)(2,1)}, u32[]{:S(2)}, u32[]{:S(2)}) async-start(bf16[8,128,768]{2,1,0:T(8,128)(2,1)} %get-tuple-element.132), calls=%async_computation | async-start | bytes 3145728 | tf_op jit(solution)/shard_map/all_to_all | solution.py:916
  82.6 1.5 collective-permute-start.2
  84.1 2.0 collective-permute-start.3
  86.1 6.9 %hidden_grad.1.gh_ref = f32[1024,768]{1,0:T(8,128)} custom-call(s32[8]{0:T(128)} %stack.35.here_s, bf16[1024,1536]{1,0:T(8,128)(2,1)} %get-tuple-element.114.gi_ref, bf16[768,3072]{1,0:T(8,128)(2,1)} %wu_ref.5), custom_call_target="tpu_custom_call" | custom-call | flops 120795952 | bytes 450000 | tf_op jit(solution)/shard_map/hidden_grad/pallas_call | solution.py:71
  93.1 10.8 %up_own.1 = (bf16[24,8,1536]{2,1,0:T(8,128)(2,1)}, bf16[24,8,1536]{2,1,0:T(8,128)(2,1)}, bf16[24,8,1536]{2,1,0:T(8,128)(2,1)}, bf16[24,8,1536]{2,1,0:T(8,128)(2,...) custom-call(s32[8]{0:T(128)} %stack.35.here_s, bf16[1024,768]{1,0:T(8,128)(2,1)} %get-tuple-element.106.gs_ref, ...), custom_call_target="tpu_custom_call" | custom-call | flops 241591904 | bytes 800000 | tf_op jit(solution)/shard_map/up_own/pallas_call | solution.py:71
  103.8 0.6 collective-permute-start.4
  104.4 0.0 collective-permute-start.5
  104.4 11.5 %collective-permute-done.3.gb = bf16[24,8,1536]{2,1,0:T(8,128)(2,1)S(1)} collective-permute-done((bf16[24,8,1536]{2,1,0:T(8,128)(2,1)S(1)}, bf16[24,8,1536]{2,1,0:T(8,128)(2,1)S(1)}, u32[]{:S(2)}, u32[]{:S(2)}) %collective-permute-start.3) | collective-permute-done | bytes 589856 | tf_op jit(solution)/shard_map/ppermute | solution.py:905
  115.9 0.8 fold_second.3
  116.7 0.0 copy-start.10
  116.7 0.7 copy-done.10
  117.4 19.3 %attn_bwd.1 = (f32[1024,768]{1,0:T(8,128)}, bf16[1024,768]{1,0:T(8,128)(2,1)}, bf16[1024,2304]{1,0:T(8,128)(2,1)}, f32[8,768]{1,0:T(8,128)S(1)}) custom-call(s32[8]{0:T(128)} %stack.35.here_s, f32[1024,768]{1,0:T(8,128)} %hidden_grad.1.gh_ref, f32[1024,768]{1,0:T(8,128)} %get-tuple-element.124.gres_ref, bf16[1024,1536]{1,0:T(8,128)(2,1)} %get-tuple-element.125.gi_ref, ...), custom_call_target="tpu_custom_call" | custom-call | flops 483183808 | bytes 2000000 | tf_op jit(solution)/shard_map/attn_bwd/pallas_call | solution.py:71
  136.8 0.8 fold_second.4
  137.7 0.0 copy-start.11
  137.7 7.9 %proj_give.1 = bf16[776,1536]{1,0:T(8,128)(2,1)S(1)} custom-call(s32[8]{0:T(128)} %stack.35.here_s, bf16[1024,768]{1,0:T(8,128)(2,1)} %x_ref.5, bf16[1024,2304]{1,0:T(8,128)(2,1)} %get-tuple-element.143.gm_ref, bf16[1024,768]{1,0:T(8,128)(2,1)} %get-tuple-element.140.att_ref, bf16[1024,768]{1,0:T(8,128)(2,1)} %get-tuple-element.141.gb_ref, ...), custom_call_target="tpu_custom_call" | custom-call | flops 120795952 | bytes 450000 | tf_op jit(solution)/shard_map/proj_give/pallas_call | solution.py:71
  145.5 0.1 collective-permute-start.10
  145.6 0.1 collective-permute-start.6
  145.7 1.6 collective-permute-start.7
  147.3 1.9 collective-permute-start.8
  149.2 0.5 collective-permute-start.9
  149.8 8.9 %input_grad.1 = bf16[1024,768]{1,0:T(8,128)(2,1)} custom-call(bf16[1024,2304]{1,0:T(8,128)(2,1)} %get-tuple-element.143.gm_ref, bf16[768,2304]{1,0:T(8,128)(2,1)} %wq_ref.3, f32[1024,768]{1,0:T(8,128)} %get-tuple-element.144.gr_ref), custom_call_target="tpu_custom_call" | custom-call | flops 181193936 | bytes 650000 | tf_op jit(solution)/shard_map/input_grad/pallas_call | solution.py:71
  158.6 2.7 %collective-permute-done.8.refs_5_ = bf16[12,8,1536]{2,1,0:T(8,128)(2,1)S(1)} collective-permute-done((bf16[12,8,1536]{2,1,0:T(8,128)(2,1)S(1)}, bf16[12,8,1536]{2,1,0:T(8,128)(2,1)S(1)}, u32[]{:S(2)}, u32[]{:S(2)}) %collective-permute-start.8) | collective-permute-done | bytes 294944 | tf_op jit(solution)/shard_map/ppermute | solution.py:905
  161.4 0.0 collective-permute-done.9.refs_7_
  161.4 0.8 fold_third.2
  162.2 1.6 collective-permute-start.11
  163.8 8.9 %proj_own.1 = (bf16[25,8,1536]{2,1,0:T(8,128)(2,1)S(1)}, bf16[25,8,1536]{2,1,0:T(8,128)(2,1)S(1)}, bf16[24,8,1536]{2,1,0:T(8,128)(2,1)S(1)}, bf16[24,8,1536]{2,1,0:T(8,128)(2,1)S(1)}) custom-call(s32[8]{0:T(128)} %stack.35.here_s, bf16[1024,768]{1,0:T(8,128)(2,1)} %x_ref.5, bf16[1024,2304]{1,0:T(8,128)(2,1)} %get-tuple-element.143.gm_ref, ...), custom_call_target="tpu_custom_call" | custom-call | flops 120795952 | bytes 550000 | tf_op jit(solution)/shard_map/proj_own/pallas_call | solution.py:71
  172.7 0.0 copy-start.8
  172.7 1.6 collective-permute-start.13
  174.2 0.9 collective-permute-start.14
  175.2 1.9 collective-permute-done.11.got_ref
  177.1 0.7 fold_fourth.2
  177.7 2.1 collective-permute-start.12
  179.9 6.1 %copied.1 = bf16[1024,768]{1,0:T(8,128)(2,1)} custom-call(s32[8]{0:T(128)} %stack.35.here_s, bf16[1024,768]{1,0:T(8,128)(2,1)} %bitcast.8.in_ref), custom_call_target="tpu_custom_call" | custom-call | bytes 150000 | tf_op jit(solution)/shard_map/copied/pallas_call | solution.py:71
  185.9 6.7 %collective-permute-done.12.got_ref = bf16[12,8,1536]{2,1,0:T(8,128)(2,1)S(1)} collective-permute-done((bf16[12,8,1536]{2,1,0:T(8,128)(2,1)S(1)}, bf16[12,8,1536]{2,1,0:T(8,128)(2,1)S(1)}, u32[]{:S(2)}, u32[]{:S(2)}) %collective-permute-start.12) | collective-permute-done | bytes 294944 | tf_op jit(solution)/shard_map/ppermute | solution.py:905
  192.7 0.6 fold_last.2.me
  193.3 0.8 fold_second.5
  194.1 1.2 collective-permute-start.15
  195.4 1.5 collective-permute-start.16
  196.9 0.5 collective-permute-start.17
  197.4 7.9 %collective-permute-done.16.refs_3_ = bf16[12,8,1536]{2,1,0:T(8,128)(2,1)S(1)} collective-permute-done((bf16[12,8,1536]{2,1,0:T(8,128)(2,1)S(1)}, bf16[12,8,1536]{2,1,0:T(8,128)(2,1)S(1)}, u32[]{:S(2)}, u32[]{:S(2)}) %collective-permute-start.16) | collective-permute-done | bytes 294944 | tf_op jit(solution)/shard_map/ppermute | solution.py:905
  205.3 0.7 fold_third.3
  205.9 0.4 collective-permute-start.20
  206.4 3.4 %collective-permute-done.17.gx = bf16[12,8,1536]{2,1,0:T(8,128)(2,1)S(1)} collective-permute-done((bf16[12,8,1536]{2,1,0:T(8,128)(2,1)S(1)}, bf16[12,8,1536]{2,1,0:T(8,128)(2,1)S(1)}, u32[]{:S(2)}, u32[]{:S(2)}) %collective-permute-start.17) | collective-permute-done | bytes 294944 | tf_op jit(solution)/shard_map/ppermute | solution.py:905
  209.8 1.6 collective-permute-done.19.gd
  211.4 2.4 %feed_blocks.1 = (f32[384,768]{1,0:T(8,128)}, f32[96,3072]{1,0:T(8,128)}) custom-call(s32[8]{0:T(128)S(1)} %copy-done.8, bf16[12,8,1536]{2,1,0:T(8,128)(2,1)S(1)} %fold_last.2.me, bf16[12,8,1536]{2,1,0:T(8,128)(2,1)S(1)} %collective-permute-done.17.gx, bf16[12,8,1536]{2,1,0:T(8,128)(2,1)S(1)} %collective-permute-done.18.gc, ...), custom_call_target="tpu_custom_call" | custom-call | flops 50000 | bytes 200000 | tf_op jit(solution)/shard_map/feed_blocks/pallas_call | solution.py:736
  213.8 0.6 fold_fourth.3
  214.4 1.4 collective-permute-start.21
  215.8 9.7 %collective-permute-done.21.got_ref = bf16[7,8,1536]{2,1,0:T(8,128)(2,1)S(1)} collective-permute-done((bf16[7,8,1536]{2,1,0:T(8,128)(2,1)S(1)}, bf16[7,8,1536]{2,1,0:T(8,128)(2,1)S(1)}, u32[]{:S(2)}, u32[]{:S(2)}) %collective-permute-start.21) | collective-permute-done | bytes 172064 | tf_op jit(solution)/shard_map/ppermute | solution.py:905
  225.5 0.6 fold_last.3
  226.1 1.6 collective-permute-start.22
  227.7 3.6 %collective-permute-done.22.gx = bf16[6,8,1536]{2,1,0:T(8,128)(2,1)S(1)} collective-permute-done((bf16[6,8,1536]{2,1,0:T(8,128)(2,1)S(1)}, bf16[6,8,1536]{2,1,0:T(8,128)(2,1)S(1)}, u32[]{:S(2)}, u32[]{:S(2)}) %collective-permute-start.22) | collective-permute-done | bytes 147488 | tf_op jit(solution)/shard_map/ppermute | solution.py:905
  231.3 1.4 collective-permute-done.24.gd
  232.7 1.9 projection_blocks.1
  234.6 0.6 reduce
  (38 shorter events, 0.1 us)
Async XLA Ops:
  56.1 10.6 %collective-permute-start = (bf16[3072,384]{1,0:T(8,128)(2,1)S(1)}, bf16[3072,384]{1,0:T(8,128)(2,1)S(1)}, u32[]{:S(2)}, u32[]{:S(2)}) collective-permute-start(bf16[3072,384]{1,0:T(8,128)(2,1)S(1)} %down_give.1), channel_id=1, source_target_pairs={{0,1},{1,0},{2,3},{3,2},{4,5},{5,4},{6,7},{7,6},{8,9},{9,8},{10,11... | collective-permute-start | bytes 7077896 | tf_op jit(solution)/shard_map/ppermute | solution.py:905
  66.7 26.4 %collective-permute-start.1 = (bf16[768,1536]{1,0:T(8,128)(2,1)}, bf16[768,1536]{1,0:T(8,128)(2,1)S(1)}, u32[]{:S(2)}, u32[]{:S(2)}) collective-permute-start(bf16[768,1536]{1,0:T(8,128)(2,1)} %get-tuple-element.116), channel_id=1, source_target_pairs={{0,1},{1,0},{2,3},{3,2},{4,5},{5,4},{6,7},{7,6},{8,9},{9,8},{10,11... | collective-permute-start | bytes 7077896 | tf_op jit(solution)/shard_map/ppermute | solution.py:905
  74.5 0.8 copy-start.9
  75.3 61.5 %all-to-all-start = ((bf16[8,128,768]{2,1,0:T(8,128)(2,1)}), bf16[8,128,768]{2,1,0:T(8,128)(2,1)}, u32[]{:S(2)}, u32[]{:S(2)}) async-start(bf16[8,128,768]{2,1,0:T(8,128)(2,1)} %get-tuple-element.132), calls=%async_computation | async-start | bytes 3145728 | tf_op jit(solution)/shard_map/all_to_all | solution.py:916
  82.6 21.8 %collective-permute-start.2 = (bf16[24,8,1536]{2,1,0:T(8,128)(2,1)}, bf16[24,8,1536]{2,1,0:T(8,128)(2,1)S(1)}, u32[]{:S(2)}, u32[]{:S(2)}) collective-permute-start(bf16[24,8,1536]{2,1,0:T(8,128)(2,1)} %copy-done.9), channel_id=1, source_target_pairs={{0,2},{1,3},{2,0},{3,1},{4,6},{5,7},{6,4},{7,5},{8,10},{9,11},{10,... | collective-permute-start | bytes 1769480 | tf_op jit(solution)/shard_map/ppermute | solution.py:905
  84.1 31.8 %collective-permute-start.3 = (bf16[24,8,1536]{2,1,0:T(8,128)(2,1)S(1)}, bf16[24,8,1536]{2,1,0:T(8,128)(2,1)S(1)}, u32[]{:S(2)}, u32[]{:S(2)}) collective-permute-start(bf16[24,8,1536]{2,1,0:T(8,128)(2,1)S(1)} %get-tuple-element.121), channel_id=1, source_target_pairs={{0,4},{4,0},{8,12},{12,8},{16,20},{20,16},{24,28},{28,24},{1,5},{5... | collective-permute-start | bytes 1769480 | tf_op jit(solution)/shard_map/ppermute | solution.py:905
  93.0 22.8 %copy-start.2 = (bf16[24,8,1536]{2,1,0:T(8,128)(2,1)S(1)}, bf16[24,8,1536]{2,1,0:T(8,128)(2,1)}, u32[]{:S(2)}) copy-start(bf16[24,8,1536]{2,1,0:T(8,128)(2,1)} %get-tuple-element.112.ka) | copy-start | bytes 1769476
  93.0 22.8 %copy-start.3 = (bf16[24,8,1536]{2,1,0:T(8,128)(2,1)S(1)}, bf16[24,8,1536]{2,1,0:T(8,128)(2,1)}, u32[]{:S(2)}) copy-start(bf16[24,8,1536]{2,1,0:T(8,128)(2,1)} %get-tuple-element.120.kb) | copy-start | bytes 1769476
  93.0 22.8 %copy-start.4 = (s32[8]{0:T(128)S(1)}, s32[8]{0:T(128)}, u32[]{:S(2)}) copy-start(s32[8]{0:T(128)} %stack.35.here_s) | copy-start | bytes 100
  103.8 33.0 %collective-permute-start.4 = (bf16[24,8,1536]{2,1,0:T(8,128)(2,1)}, bf16[24,8,1536]{2,1,0:T(8,128)(2,1)S(1)}, u32[]{:S(2)}, u32[]{:S(2)}) collective-permute-start(bf16[24,8,1536]{2,1,0:T(8,128)(2,1)} %get-tuple-element.135), channel_id=1, source_target_pairs={{0,2},{1,3},{2,0},{3,1},{4,6},{5,7},{6,4},{7,5},{8,10},{9,11},{10,... | collective-permute-start | bytes 1769480 | tf_op jit(solution)/shard_map/ppermute | solution.py:905
  104.4 32.4 %collective-permute-start.5 = (bf16[24,8,1536]{2,1,0:T(8,128)(2,1)}, bf16[24,8,1536]{2,1,0:T(8,128)(2,1)S(1)}, u32[]{:S(2)}, u32[]{:S(2)}) collective-permute-start(bf16[24,8,1536]{2,1,0:T(8,128)(2,1)} %get-tuple-element.137), channel_id=1, source_target_pairs={{0,4},{4,0},{8,12},{12,8},{16,20},{20,16},{24,28},{28,24},{1,5},{5... | collective-permute-start | bytes 1769480 | tf_op jit(solution)/shard_map/ppermute | solution.py:905
  116.7 0.7 copy-start.10
  117.4 19.4 %copy-start = (bf16[24,8,1536]{2,1,0:T(8,128)(2,1)S(1)}, bf16[24,8,1536]{2,1,0:T(8,128)(2,1)}, u32[]{:S(2)}) copy-start(bf16[24,8,1536]{2,1,0:T(8,128)(2,1)} %get-tuple-element.134.ka) | copy-start | bytes 1769476
  117.4 19.4 %copy-start.1 = (bf16[24,8,1536]{2,1,0:T(8,128)(2,1)S(1)}, bf16[24,8,1536]{2,1,0:T(8,128)(2,1)}, u32[]{:S(2)}) copy-start(bf16[24,8,1536]{2,1,0:T(8,128)(2,1)} %get-tuple-element.136.kb) | copy-start | bytes 1769476
  117.4 19.4 %copy-start.5 = (s32[8]{0:T(128)S(1)}, s32[8]{0:T(128)}, u32[]{:S(2)}) copy-start(s32[8]{0:T(128)} %stack.35.here_s) | copy-start | bytes 100
  137.7 8.0 %copy-start.11 = (bf16[12,8,1536]{2,1,0:T(8,128)(2,1)S(1)}, bf16[12,8,1536]{2,1,0:T(8,128)(2,1)}, u32[]{:S(2)}) copy-start(bf16[12,8,1536]{2,1,0:T(8,128)(2,1)} %copy-done.10) | copy-start | bytes 884740
  145.5 18.2 %collective-permute-start.10 = (bf16[776,1536]{1,0:T(8,128)(2,1)S(1)}, bf16[776,1536]{1,0:T(8,128)(2,1)S(1)}, u32[]{:S(2)}, u32[]{:S(2)}) collective-permute-start(bf16[776,1536]{1,0:T(8,128)(2,1)S(1)} %proj_give.1), channel_id=1, source_target_pairs={{0,1},{1,0},{2,3},{3,2},{4,5},{5,4},{6,7},{7,6},{8,9},{9,8},{10,11... | collective-permute-start | bytes 7151624 | tf_op jit(solution)/shard_map/ppermute | solution.py:905
  145.6 13.0 %collective-permute-start.6 = (bf16[12,8,1536]{2,1,0:T(8,128)(2,1)S(1)}, bf16[12,8,1536]{2,1,0:T(8,128)(2,1)S(1)}, u32[]{:S(2)}, u32[]{:S(2)}) collective-permute-start(bf16[12,8,1536]{2,1,0:T(8,128)(2,1)S(1)} %copy-done.11), channel_id=1, source_target_pairs={{0,4},{4,0},{8,12},{12,8},{16,20},{20,16},{24,28},{28,24},{1,5},{5... | collective-permute-start | bytes 884744 | tf_op jit(solution)/shard_map/ppermute | solution.py:905
  145.7 12.9 %collective-permute-start.7 = (bf16[12,8,1536]{2,1,0:T(8,128)(2,1)S(1)}, bf16[12,8,1536]{2,1,0:T(8,128)(2,1)S(1)}, u32[]{:S(2)}, u32[]{:S(2)}) collective-permute-start(bf16[12,8,1536]{2,1,0:T(8,128)(2,1)S(1)} %get-tuple-element.148), channel_id=1, source_target_pairs={{0,2},{1,3},{2,0},{3,1},{4,6},{5,7},{6,4},{7,5},{8,10},{9,11},{10,... | collective-permute-start | bytes 884744 | tf_op jit(solution)/shard_map/ppermute | solution.py:905
  147.3 14.1 %collective-permute-start.8 = (bf16[12,8,1536]{2,1,0:T(8,128)(2,1)S(1)}, bf16[12,8,1536]{2,1,0:T(8,128)(2,1)S(1)}, u32[]{:S(2)}, u32[]{:S(2)}) collective-permute-start(bf16[12,8,1536]{2,1,0:T(8,128)(2,1)S(1)} %get-tuple-element.149), channel_id=1, source_target_pairs={{0,4},{4,0},{8,12},{12,8},{16,20},{20,16},{24,28},{28,24},{1,5},{5... | collective-permute-start | bytes 884744 | tf_op jit(solution)/shard_map/ppermute | solution.py:905
  149.2 12.1 %collective-permute-start.9 = (bf16[12,8,1536]{2,1,0:T(8,128)(2,1)S(1)}, bf16[12,8,1536]{2,1,0:T(8,128)(2,1)S(1)}, u32[]{:S(2)}, u32[]{:S(2)}) collective-permute-start(bf16[12,8,1536]{2,1,0:T(8,128)(2,1)S(1)} %get-tuple-element.151), channel_id=1, source_target_pairs={{0,2},{1,3},{2,0},{3,1},{4,6},{5,7},{6,4},{7,5},{8,10},{9,11},{10,... | collective-permute-start | bytes 884744 | tf_op jit(solution)/shard_map/ppermute | solution.py:905
  149.8 11.6 %copy-start.6 = (s32[8]{0:T(128)S(1)}, s32[8]{0:T(128)}, u32[]{:S(2)}) copy-start(s32[8]{0:T(128)} %stack.35.here_s) | copy-start | bytes 100
  162.2 14.9 %collective-permute-start.11 = (bf16[24,8,1536]{2,1,0:T(8,128)(2,1)S(1)}, bf16[24,8,1536]{2,1,0:T(8,128)(2,1)S(1)}, u32[]{:S(2)}, u32[]{:S(2)}) collective-permute-start(bf16[24,8,1536]{2,1,0:T(8,128)(2,1)S(1)} %get-tuple-element.156), channel_id=1, source_target_pairs={{0,8},{4,12},{8,0},{12,4},{16,24},{20,28},{24,16},{28,20},{1,9},{5... | collective-permute-start | bytes 1769480 | tf_op jit(solution)/shard_map/ppermute | solution.py:905
  163.8 13.3 %copy-start.7 = (s32[8]{0:T(128)S(1)}, s32[8]{0:T(128)}, u32[]{:S(2)}) copy-start(s32[8]{0:T(128)} %stack.35.here_s) | copy-start | bytes 100
  172.7 20.0 %copy-start.8 = (s32[8]{0:T(128)S(1)}, s32[8]{0:T(128)}, u32[]{:S(2)}) copy-start(s32[8]{0:T(128)} %stack.35.here_s) | copy-start | bytes 100
  172.7 20.6 %collective-permute-start.13 = (bf16[25,8,1536]{2,1,0:T(8,128)(2,1)S(1)}, bf16[25,8,1536]{2,1,0:T(8,128)(2,1)S(1)}, u32[]{:S(2)}, u32[]{:S(2)}) collective-permute-start(bf16[25,8,1536]{2,1,0:T(8,128)(2,1)S(1)} %get-tuple-element.162), channel_id=1, source_target_pairs={{0,2},{1,3},{2,0},{3,1},{4,6},{5,7},{6,4},{7,5},{8,10},{9,11},{10,... | collective-permute-start | bytes 1843208 | tf_op jit(solution)/shard_map/ppermute | solution.py:905
  174.2 19.0 %collective-permute-start.14 = (bf16[24,8,1536]{2,1,0:T(8,128)(2,1)S(1)}, bf16[24,8,1536]{2,1,0:T(8,128)(2,1)S(1)}, u32[]{:S(2)}, u32[]{:S(2)}) collective-permute-start(bf16[24,8,1536]{2,1,0:T(8,128)(2,1)S(1)} %get-tuple-element.164), channel_id=1, source_target_pairs={{0,4},{4,0},{8,12},{12,8},{16,20},{20,16},{24,28},{28,24},{1,5},{5... | collective-permute-start | bytes 1769480 | tf_op jit(solution)/shard_map/ppermute | solution.py:905
  177.7 14.9 %collective-permute-start.12 = (bf16[12,8,1536]{2,1,0:T(8,128)(2,1)S(1)}, bf16[12,8,1536]{2,1,0:T(8,128)(2,1)S(1)}, u32[]{:S(2)}, u32[]{:S(2)}) collective-permute-start(bf16[12,8,1536]{2,1,0:T(8,128)(2,1)S(1)} %get-tuple-element.160), channel_id=1, source_target_pairs={{0,16},{4,20},{8,24},{12,28},{16,0},{20,4},{24,8},{28,12},{1,17},{... | collective-permute-start | bytes 884744 | tf_op jit(solution)/shard_map/ppermute | solution.py:905
  194.1 11.1 %collective-permute-start.15 = (bf16[13,8,1536]{2,1,0:T(8,128)(2,1)S(1)}, bf16[13,8,1536]{2,1,0:T(8,128)(2,1)S(1)}, u32[]{:S(2)}, u32[]{:S(2)}) collective-permute-start(bf16[13,8,1536]{2,1,0:T(8,128)(2,1)S(1)} %get-tuple-element.166), channel_id=1, source_target_pairs={{0,4},{4,0},{8,12},{12,8},{16,20},{20,16},{24,28},{28,24},{1,5},{5... | collective-permute-start | bytes 958472 | tf_op jit(solution)/shard_map/ppermute | solution.py:905
  195.4 9.9 %collective-permute-start.16 = (bf16[12,8,1536]{2,1,0:T(8,128)(2,1)S(1)}, bf16[12,8,1536]{2,1,0:T(8,128)(2,1)S(1)}, u32[]{:S(2)}, u32[]{:S(2)}) collective-permute-start(bf16[12,8,1536]{2,1,0:T(8,128)(2,1)S(1)} %get-tuple-element.168), channel_id=1, source_target_pairs={{0,2},{1,3},{2,0},{3,1},{4,6},{5,7},{6,4},{7,5},{8,10},{9,11},{10,... | collective-permute-start | bytes 884744 | tf_op jit(solution)/shard_map/ppermute | solution.py:905
  196.9 12.9 %collective-permute-start.17 = (bf16[12,8,1536]{2,1,0:T(8,128)(2,1)S(1)}, bf16[12,8,1536]{2,1,0:T(8,128)(2,1)S(1)}, u32[]{:S(2)}, u32[]{:S(2)}) collective-permute-start(bf16[12,8,1536]{2,1,0:T(8,128)(2,1)S(1)} %fold_last.2.me), channel_id=1, source_target_pairs={{0,2},{1,3},{2,0},{3,1},{4,6},{5,7},{6,4},{7,5},{8,10},{9,11},{10,... | collective-permute-start | bytes 884744 | tf_op jit(solution)/shard_map/ppermute | solution.py:905
  205.9 7.9 %collective-permute-start.20 = (bf16[13,8,1536]{2,1,0:T(8,128)(2,1)S(1)}, bf16[13,8,1536]{2,1,0:T(8,128)(2,1)S(1)}, u32[]{:S(2)}, u32[]{:S(2)}) collective-permute-start(bf16[13,8,1536]{2,1,0:T(8,128)(2,1)S(1)} %get-tuple-element.174), channel_id=1, source_target_pairs={{0,8},{4,12},{8,0},{12,4},{16,24},{20,28},{24,16},{28,20},{1,9},{5... | collective-permute-start | bytes 958472 | tf_op jit(solution)/shard_map/ppermute | solution.py:905
  206.4 3.4 %collective-permute-start.18 = (bf16[12,8,1536]{2,1,0:T(8,128)(2,1)S(1)}, bf16[12,8,1536]{2,1,0:T(8,128)(2,1)S(1)}, u32[]{:S(2)}, u32[]{:S(2)}) collective-permute-start(bf16[12,8,1536]{2,1,0:T(8,128)(2,1)S(1)} %fold_last.2.me), channel_id=1, source_target_pairs={{0,1},{1,0},{2,3},{3,2},{4,5},{5,4},{6,7},{7,6},{8,9},{9,8},{10,11... | collective-permute-start | bytes 884744 | tf_op jit(solution)/shard_map/ppermute | solution.py:905
  209.8 1.6 collective-permute-start.19
  214.4 11.1 %collective-permute-start.21 = (bf16[7,8,1536]{2,1,0:T(8,128)(2,1)S(1)}, bf16[7,8,1536]{2,1,0:T(8,128)(2,1)S(1)}, u32[]{:S(2)}, u32[]{:S(2)}) collective-permute-start(bf16[7,8,1536]{2,1,0:T(8,128)(2,1)S(1)} %get-tuple-element.176), channel_id=1, source_target_pairs={{0,16},{4,20},{8,24},{12,28},{16,0},{20,4},{24,8},{28,12},{1,17},{... | collective-permute-start | bytes 516104 | tf_op jit(solution)/shard_map/ppermute | solution.py:905
  226.1 5.2 %collective-permute-start.22 = (bf16[6,8,1536]{2,1,0:T(8,128)(2,1)S(1)}, bf16[6,8,1536]{2,1,0:T(8,128)(2,1)S(1)}, u32[]{:S(2)}, u32[]{:S(2)}) collective-permute-start(bf16[6,8,1536]{2,1,0:T(8,128)(2,1)S(1)} %get-tuple-element.177.me), channel_id=1, source_target_pairs={{0,2},{1,3},{2,0},{3,1},{4,6},{5,7},{6,4},{7,5},{8,10},{9,11},{10,... | collective-permute-start | bytes 442376 | tf_op jit(solution)/shard_map/ppermute | solution.py:905
  227.6 3.7 %collective-permute-start.23 = (bf16[6,8,1536]{2,1,0:T(8,128)(2,1)S(1)}, bf16[6,8,1536]{2,1,0:T(8,128)(2,1)S(1)}, u32[]{:S(2)}, u32[]{:S(2)}) collective-permute-start(bf16[6,8,1536]{2,1,0:T(8,128)(2,1)S(1)} %get-tuple-element.177.me), channel_id=1, source_target_pairs={{0,1},{1,0},{2,3},{3,2},{4,5},{5,4},{6,7},{7,6},{8,9},{9,8},{10,11... | collective-permute-start | bytes 442376 | tf_op jit(solution)/shard_map/ppermute | solution.py:905
  231.3 1.4 collective-permute-start.24

commit v5 on v4

--- a/solution.py
+++ b/solution.py
@@ -19,10 +19,9 @@
 MIB = 1024 * 1024
 LARGE = 100000
 COST = 0.05
-ERF_P = 0.3275911
-ERF_A = (0.254829592, -0.284496736, 1.421413741, -1.453152027, 1.061405429)
 HALF_ROOT = 0.7071067811865476
-PEAK = 0.3989422804014327
+BELL_RATE = -0.7213475204444817
+BELL_PEAK = -1.3257480647361595
 ROW_BQ, ROW_BV, ROW_BO, ROW_GA, ROW_SA, ROW_BD, ROW_GF, ROW_SF, ROW_BU = range(9)
 
 
@@ -104,14 +103,9 @@
 
 
 def gelu_pair(v):
-    t = 1.0 / (1.0 + (ERF_P * HALF_ROOT) * jnp.abs(v))
-    bell = jnp.exp(-0.5 * (v * v))
-    poly = 0.5 * ERF_A[4]
-    for coef in ERF_A[3::-1]:
-        poly = poly * t + 0.5 * coef
-    tail = poly * t * bell
-    phi = jnp.where(v > 0, 1.0 - tail, tail)
-    return v * phi, phi + v * (PEAK * bell)
+    phi = 0.5 + 0.5 * lax.erf(v * HALF_ROOT)
+    bell = jnp.exp2((v * v) * BELL_RATE + BELL_PEAK)
+    return v * phi, phi + v * bell
 
 
 def head_masks():
@@ -972,10 +966,10 @@
     heads = (n_attn, spread, table, w_out, qkv, probs)
     down_sent = down_terms(active, grad_second, here, 1)
     if paired:
+        encoded = regroup_rows(after(sent, down_sent), bucket, wide_count, batches)
         up_sent, gi_sent, bup_sent = up_terms(*ups, after(here, down_sent), 1)
         down_dealt = down_terms(active, grad_second, after(here, bup_sent), 0, swap(down_sent, "narrow", 1))
         down_a, down_b = swap(down_dealt[0], "narrow", 2), swap(down_dealt[2], "wide", 1)
-        encoded = regroup_rows(after(sent, down_dealt[1]), bucket, wide_count, batches)
         gh = hidden_gradient(gi_sent, w_up, after(here, down_dealt[1]), 1)
         *up_dealt, gi_kept, bup_kept = up_terms(
             *ups, after(here, gh), 0, swap(up_sent, "narrow", 1)
@@ -994,25 +988,25 @@
         up_a, up_b = swap(up_dealt[0], "wide", 1), swap(up_dealt[2], "narrow", 2)
         projections = (tokens, gm, attended, gb, (vec_ffn, vec_attn, bup_sent, bup_kept))
         proj_sent = projection_terms(*projections, after(here, up_dealt[1]), 1)
-        grad_tokens = input_gradient(after(gm, proj_sent), w_qkv, gr, 2 * span)
         send, feed = fold_third(
             [(down_dealt[1], down_a, down_dealt[3], down_b), (up_dealt[1], up_a, up_dealt[3], up_b)],
-            after(here, grad_tokens), pieces, 0,
+            after(here, proj_sent), pieces, 0,
         )
         feed_got = swap(send, "wide", 2)
+        grad_tokens = input_gradient(after(gm, feed), w_qkv, gr, 2 * span)
         proj_dealt = projection_terms(
-            *projections, after(here, feed), 0, swap(proj_sent, "narrow", 1)
+            *projections, after(here, grad_tokens), 0, swap(proj_sent, "narrow", 1)
         )
         proj_a, proj_b = swap(proj_dealt[0], "narrow", 2), swap(proj_dealt[2], "wide", 1)
         send, feed = fold_fourth(feed, feed_got, after(here, proj_dealt[1]), 0)
         feed_got = swap(send, "wide", 4)
         encoded = copied(encoded, after(here, feed), span)
-        (feed,) = fold_last(feed, feed_got, after(here, encoded), 0)
         proj_dealt = fold_second(
-            proj_dealt[1], proj_a, proj_dealt[3], proj_b, after(here, feed), pieces, 1
+            proj_dealt[1], proj_a, proj_dealt[3], proj_b, after(here, encoded), pieces, 1
         )
         proj_a, proj_b = swap(proj_dealt[0], "wide", 1), swap(proj_dealt[2], "narrow", 2)
-        feed = quarters(after(feed, proj_dealt[1]))
+        (feed,) = fold_last(feed, feed_got, after(here, proj_dealt[1]), 0)
+        feed = quarters(feed)
         send, proj = fold_third(
             [(proj_dealt[1], proj_a, proj_dealt[3], proj_b)], here, pieces, 1
         )

time: 236 us -> 229 us (0.970)
  waiting for transfers between devices: 50.4 us -> 37 us
  starting transfers between devices: 29 us -> 39.8 us
  Pallas kernels: 152 us -> 148 us
    ppermute x25, waiting for transfers between devices: 50.4 us -> 37 us  [swap(): lax.ppermute(item, axis, [(index, index ^ step) for index in range(count)])]
    ppermute x25, starting transfers between devices: 21.7 us -> 32.5 us  [swap(): lax.ppermute(item, axis, [(index, index ^ step) for index in range(count)])]
    pallas_call x12, Pallas kernels: 140 us -> 137 us  [call(): pl.pallas_call(kernel, grid_spec=pltpu.PrefetchScalarGridSpec(num_scalar_...]
  transfers between devices with their start and end apart: 26 -> 26, of which waited for: 10 -> 12; matrix products, arithmetic and copies ran while one was open for 0% -> 0% of each run, Pallas kernels for 36% -> 38%
where the time goes in v5:
time: 229 us; the launch traced here: 228 us
  Pallas kernels  148 us (65%)
  starting transfers between devices  39.8 us (17%)
  waiting for transfers between devices  37 us (16%)
    pallas_call x12, Pallas kernels, call(): pl.pallas_call(kernel, grid_spec=pltpu.PrefetchScalarGridSpec(num_scalar_...  137 us
    ppermute x25, waiting for transfers between devices, swap(): lax.ppermute(item, axis, [(index, index ^ step) for index in range(count)])  37 us
    ppermute x25, starting transfers between devices, swap(): lax.ppermute(item, axis, [(index, index ^ step) for index in range(count)])  32.5 us
    pallas_call x11, Pallas kernels, small_call(): pl.pallas_call(kernel, in_specs=[pl.BlockSpec(memory_space=pltpu.SMEM)] +...  10.8 us
    all_to_all x1, starting transfers between devices, regroup_rows(): got = lax.all_to_all(sent, 'wide', split_axis=0, concat_axis=0, tiled=True)  7.31 us
  transfers between devices with their start and end apart: 26, of which 12 were waited for; matrix products, arithmetic and copies ran while one was open for 0% of the time, Pallas kernels for 38%

profile of v5, /device:TPU:0, one launch (start us, length us, event | category | flops | bytes accessed | tf_op | source)
XLA Modules:
  0.0 228.0 jit_solution(13087389234999596232)
XLA Ops:
  0.7 0.9 vector_table.1.tab_ref
  1.6 16.6 %attn_fwd.1 = (bf16[1024,2304]{1,0:T(8,128)(2,1)}, bf16[8,6,256,128]{3,2,1,0:T(8,128)(2,1)}, bf16[1024,768]{1,0:T(8,128)(2,1)}, f32[1024,768]{1,0:T(8,128)}, f32...) custom-call(s32[8]{0:T(128)} %slots_s.1, s32[26]{0:T(128)} %lengths_s.1, bf16[1024,768]{1,0:T(8,128)(2,1)} %x_ref.5, ...), custom_call_target="tpu_custom_call" | custom-call | flops 483183808 | bytes 1500000 | tf_op jit(solution)/shard_map/attn_fwd/pallas_call | solution.py:70
  18.1 25.2 %ffn_fwd.1 = (bf16[1024,3072]{1,0:T(8,128)(2,1)}, bf16[1024,3072]{1,0:T(8,128)(2,1)}, bf16[768,1024]{1,0:T(8,128)(2,1)}, bf16[8,128,768]{2,1,0:T(8,128)(2,1)}, f...) custom-call(s32[8]{0:T(128)} %slots_s.1, s32[1,26]{1,0:T(1,128)} %pairing_s.1, f32[13]{0:T(128)} %targets_s.1, ...), custom_call_target="tpu_custom_call" | custom-call | flops 966367616 | bytes 2000000 | tf_op jit(solution)/shard_map/ffn_fwd/pallas_call | solution.py:70
  43.3 0.6 stack.35.here_s
  43.9 7.9 %down_give.1 = bf16[3072,384]{1,0:T(8,128)(2,1)} custom-call(s32[8]{0:T(128)} %stack.35.here_s, bf16[1024,3072]{1,0:T(8,128)(2,1)} %get-tuple-element.104.act_ref, bf16[1024,768]{1,0:T(8,128)(2,1)} %get-tuple-element.105.gs_ref), custom_call_target="tpu_custom_call" | custom-call | flops 120795952 | bytes 450000 | tf_op jit(solution)/shard_map/down_give/pallas_call | solution.py:70
  51.9 0.5 collective-permute-start
  52.4 10.2 %up_give.1 = (bf16[768,1536]{1,0:T(8,128)(2,1)}, bf16[1024,1536]{1,0:T(8,128)(2,1)}, f32[1,1536]{1,0:T(1,128)S(1)}) custom-call(s32[8]{0:T(128)} %stack.35.here_s, bf16[1024,768]{1,0:T(8,128)(2,1)} %get-tuple-element.105.gs_ref, bf16[1024,3072]{1,0:T(8,128)(2,1)} %get-tuple-element.107.dg_ref, bf16[768,1024]{1,0:T(8,128)(2,1)} %get-tuple-element.108.ht_ref, ...), custom_call_target="tpu_custom_call" | custom-call | flops 241591904 | bytes 800000 | tf_op jit(solution)/shard_map/up_give/pallas_call | solution.py:70
  62.6 0.0 collective-permute-start.1
  62.6 7.3 %all-to-all-start = ((bf16[8,128,768]{2,1,0:T(8,128)(2,1)}), bf16[8,128,768]{2,1,0:T(8,128)(2,1)}, u32[]{:S(2)}, u32[]{:S(2)}) async-start(bf16[8,128,768]{2,1,0:T(8,128)(2,1)} %get-tuple-element.131), calls=%async_computation | async-start | bytes 3145728 | tf_op jit(solution)/shard_map/all_to_all | solution.py:910
  69.9 8.2 %down_own.1 = (bf16[24,8,1536]{2,1,0:T(8,128)(2,1)S(1)}, bf16[24,8,1536]{2,1,0:T(8,128)(2,1)}, bf16[24,8,1536]{2,1,0:T(8,128)(2,1)S(1)}, bf16[24,8,1536]{2,1,0:T(8,128)(2,1)}) custom-call(s32[8]{0:T(128)} %stack.35.here_s, bf16[1024,3072]{1,0:T(8,128)(2,1)} %get-tuple-element.104.act_ref, bf16[1024,768]{1,0:T(8,128)(2,1)} %get-tuple-element.105.gs_ref, ...), custom_call_target="tpu_custom_call" | custom-call | flops 120795952 | bytes 550000 | tf_op jit(solution)/shard_map/down_own/pallas_call | solution.py:70
  78.1 1.5 collective-permute-start.2
  79.6 2.0 collective-permute-start.3
  81.6 6.9 %hidden_grad.1.gh_ref = f32[1024,768]{1,0:T(8,128)} custom-call(s32[8]{0:T(128)} %stack.35.here_s, bf16[1024,1536]{1,0:T(8,128)(2,1)} %get-tuple-element.113.gi_ref, bf16[768,3072]{1,0:T(8,128)(2,1)} %wu_ref.5), custom_call_target="tpu_custom_call" | custom-call | flops 120795952 | bytes 450000 | tf_op jit(solution)/shard_map/hidden_grad/pallas_call | solution.py:70
  88.5 10.8 %up_own.1 = (bf16[24,8,1536]{2,1,0:T(8,128)(2,1)}, bf16[24,8,1536]{2,1,0:T(8,128)(2,1)}, bf16[24,8,1536]{2,1,0:T(8,128)(2,1)}, bf16[24,8,1536]{2,1,0:T(8,128)(2,...) custom-call(s32[8]{0:T(128)} %stack.35.here_s, bf16[1024,768]{1,0:T(8,128)(2,1)} %get-tuple-element.105.gs_ref, ...), custom_call_target="tpu_custom_call" | custom-call | flops 241591904 | bytes 800000 | tf_op jit(solution)/shard_map/up_own/pallas_call | solution.py:70
  99.3 0.6 collective-permute-start.4
  99.8 0.0 collective-permute-start.5
  99.9 3.3 %collective-permute-done.3.gb = bf16[24,8,1536]{2,1,0:T(8,128)(2,1)S(1)} collective-permute-done((bf16[24,8,1536]{2,1,0:T(8,128)(2,1)S(1)}, bf16[24,8,1536]{2,1,0:T(8,128)(2,1)S(1)}, u32[]{:S(2)}, u32[]{:S(2)}) %collective-permute-start.3) | collective-permute-done | bytes 589856 | tf_op jit(solution)/shard_map/ppermute | solution.py:899
  103.2 0.8 fold_second.3
  104.0 0.7 copy-done.9
  104.7 19.3 %attn_bwd.1 = (f32[1024,768]{1,0:T(8,128)}, bf16[1024,768]{1,0:T(8,128)(2,1)}, bf16[1024,2304]{1,0:T(8,128)(2,1)}, f32[8,768]{1,0:T(8,128)S(1)}) custom-call(s32[8]{0:T(128)} %stack.35.here_s, f32[1024,768]{1,0:T(8,128)} %hidden_grad.1.gh_ref, f32[1024,768]{1,0:T(8,128)} %get-tuple-element.123.gres_ref, bf16[1024,1536]{1,0:T(8,128)(2,1)} %get-tuple-element.124.gi_ref, ...), custom_call_target="tpu_custom_call" | custom-call | flops 483183808 | bytes 2000000 | tf_op jit(solution)/shard_map/attn_bwd/pallas_call | solution.py:70
  124.1 0.8 fold_second.4
  125.0 0.0 copy-start.6
  125.0 7.9 %proj_give.1 = bf16[776,1536]{1,0:T(8,128)(2,1)S(1)} custom-call(s32[8]{0:T(128)} %stack.35.here_s, bf16[1024,768]{1,0:T(8,128)(2,1)} %x_ref.5, bf16[1024,2304]{1,0:T(8,128)(2,1)} %get-tuple-element.150.gm_ref, bf16[1024,768]{1,0:T(8,128)(2,1)} %get-tuple-element.139.att_ref, bf16[1024,768]{1,0:T(8,128)(2,1)} %get-tuple-element.140.gb_ref, ...), custom_call_target="tpu_custom_call" | custom-call | flops 120795952 | bytes 450000 | tf_op jit(solution)/shard_map/proj_give/pallas_call | solution.py:70
  132.9 0.1 collective-permute-start.10
  132.9 0.1 collective-permute-start.6
  133.0 1.3 collective-permute-start.7
  134.3 1.9 collective-permute-start.8
  136.3 0.8 collective-permute-start.9
  137.1 5.8 %collective-permute-done.6.refs_1_ = bf16[12,8,1536]{2,1,0:T(8,128)(2,1)S(1)} collective-permute-done((bf16[12,8,1536]{2,1,0:T(8,128)(2,1)S(1)}, bf16[12,8,1536]{2,1,0:T(8,128)(2,1)S(1)}, u32[]{:S(2)}, u32[]{:S(2)}) %collective-permute-start.6) | collective-permute-done | bytes 294944 | tf_op jit(solution)/shard_map/ppermute | solution.py:899
  142.9 0.1 collective-permute-done.7.refs_3_
  143.0 5.7 %collective-permute-done.8.refs_5_ = bf16[12,8,1536]{2,1,0:T(8,128)(2,1)S(1)} collective-permute-done((bf16[12,8,1536]{2,1,0:T(8,128)(2,1)S(1)}, bf16[12,8,1536]{2,1,0:T(8,128)(2,1)S(1)}, u32[]{:S(2)}, u32[]{:S(2)}) %collective-permute-start.8) | collective-permute-done | bytes 294944 | tf_op jit(solution)/shard_map/ppermute | solution.py:899
  148.7 0.8 fold_third.2
  149.5 1.2 collective-permute-start.11
  150.7 8.9 %input_grad.1 = bf16[1024,768]{1,0:T(8,128)(2,1)} custom-call(bf16[1024,2304]{1,0:T(8,128)(2,1)} %get-tuple-element.150.gm_ref, bf16[768,2304]{1,0:T(8,128)(2,1)} %wq_ref.3, f32[1024,768]{1,0:T(8,128)} %get-tuple-element.151.gr_ref), custom_call_target="tpu_custom_call" | custom-call | flops 181193936 | bytes 650000 | tf_op jit(solution)/shard_map/input_grad/pallas_call | solution.py:70
  159.6 8.8 %proj_own.1 = (bf16[25,8,1536]{2,1,0:T(8,128)(2,1)S(1)}, bf16[25,8,1536]{2,1,0:T(8,128)(2,1)S(1)}, bf16[24,8,1536]{2,1,0:T(8,128)(2,1)S(1)}, bf16[24,8,1536]{2,1,0:T(8,128)(2,1)S(1)}) custom-call(s32[8]{0:T(128)} %stack.35.here_s, bf16[1024,768]{1,0:T(8,128)(2,1)} %x_ref.5, bf16[1024,2304]{1,0:T(8,128)(2,1)} %get-tuple-element.150.gm_ref, ...), custom_call_target="tpu_custom_call" | custom-call | flops 120795952 | bytes 550000 | tf_op jit(solution)/shard_map/proj_own/pallas_call | solution.py:70
  168.4 0.0 copy-start.8
  168.4 1.6 collective-permute-start.12
  169.9 0.4 collective-permute-start.13
  170.3 0.7 fold_fourth.2
  171.0 6.7 %collective-permute-start.16 = (bf16[12,8,1536]{2,1,0:T(8,128)(2,1)S(1)}, bf16[12,8,1536]{2,1,0:T(8,128)(2,1)S(1)}, u32[]{:S(2)}, u32[]{:S(2)}) collective-permute-start(bf16[12,8,1536]{2,1,0:T(8,128)(2,1)S(1)} %get-tuple-element.169), channel_id=1, source_target_pairs={{0,16},{4,20},{8,24},{12,28},{16,0},{20,4},{24,8},{28,12},{1,17},{... | collective-permute-start | bytes 884744 | tf_op jit(solution)/shard_map/ppermute | solution.py:899
  177.7 6.1 %copied.1 = bf16[1024,768]{1,0:T(8,128)(2,1)} custom-call(s32[8]{0:T(128)} %stack.35.here_s, bf16[1024,768]{1,0:T(8,128)(2,1)} %bitcast.8.in_ref), custom_call_target="tpu_custom_call" | custom-call | bytes 150000 | tf_op jit(solution)/shard_map/copied/pallas_call | solution.py:70
  183.8 0.1 collective-permute-done.13.gb
  183.9 0.8 fold_second.5
  184.7 0.7 collective-permute-start.14
  185.5 0.8 collective-permute-start.15
  186.3 3.1 %collective-permute-done.16.got_ref = bf16[12,8,1536]{2,1,0:T(8,128)(2,1)S(1)} collective-permute-done((bf16[12,8,1536]{2,1,0:T(8,128)(2,1)S(1)}, bf16[12,8,1536]{2,1,0:T(8,128)(2,1)S(1)}, u32[]{:S(2)}, u32[]{:S(2)}) %collective-permute-start.16) | collective-permute-done | bytes 294944 | tf_op jit(solution)/shard_map/ppermute | solution.py:899
  189.4 0.6 fold_last.2.me
  190.0 0.6 collective-permute-start.17
  190.6 1.7 collective-permute-done.15.refs_3_
  192.3 0.0 collective-permute-done.14.refs_1_
  192.3 0.7 fold_third.3
  193.0 4.3 %collective-permute-start.20 = (bf16[13,8,1536]{2,1,0:T(8,128)(2,1)S(1)}, bf16[13,8,1536]{2,1,0:T(8,128)(2,1)S(1)}, u32[]{:S(2)}, u32[]{:S(2)}) collective-permute-start(bf16[13,8,1536]{2,1,0:T(8,128)(2,1)S(1)} %get-tuple-element.172), channel_id=1, source_target_pairs={{0,8},{4,12},{8,0},{12,4},{16,24},{20,28},{24,16},{28,20},{1,9},{5... | collective-permute-start | bytes 958472 | tf_op jit(solution)/shard_map/ppermute | solution.py:899
  197.3 1.7 collective-permute-done.17.gx
  199.0 1.6 collective-permute-done.19.gd
  200.6 2.4 %feed_blocks.1 = (f32[384,768]{1,0:T(8,128)}, f32[96,3072]{1,0:T(8,128)}) custom-call(s32[8]{0:T(128)S(1)} %copy-done.8, bf16[12,8,1536]{2,1,0:T(8,128)(2,1)S(1)} %fold_last.2.me, bf16[12,8,1536]{2,1,0:T(8,128)(2,1)S(1)} %collective-permute-done.17.gx, bf16[12,8,1536]{2,1,0:T(8,128)(2,1)S(1)} %collective-permute-done.18.gc, ...), custom_call_target="tpu_custom_call" | custom-call | flops 50000 | bytes 200000 | tf_op jit(solution)/shard_map/feed_blocks/pallas_call | solution.py:730
  203.0 0.6 fold_fourth.3
  203.6 6.3 %collective-permute-start.21 = (bf16[7,8,1536]{2,1,0:T(8,128)(2,1)S(1)}, bf16[7,8,1536]{2,1,0:T(8,128)(2,1)S(1)}, u32[]{:S(2)}, u32[]{:S(2)}) collective-permute-start(bf16[7,8,1536]{2,1,0:T(8,128)(2,1)S(1)} %get-tuple-element.174), channel_id=1, source_target_pairs={{0,16},{4,20},{8,24},{12,28},{16,0},{20,4},{24,8},{28,12},{1,17},{... | collective-permute-start | bytes 516104 | tf_op jit(solution)/shard_map/ppermute | solution.py:899
  209.9 7.8 %collective-permute-done.21.got_ref = bf16[7,8,1536]{2,1,0:T(8,128)(2,1)S(1)} collective-permute-done((bf16[7,8,1536]{2,1,0:T(8,128)(2,1)S(1)}, bf16[7,8,1536]{2,1,0:T(8,128)(2,1)S(1)}, u32[]{:S(2)}, u32[]{:S(2)}) %collective-permute-start.21) | collective-permute-done | bytes 172064 | tf_op jit(solution)/shard_map/ppermute | solution.py:899
  217.7 0.6 fold_last.3
  218.3 1.1 collective-permute-start.22
  219.4 4.7 %collective-permute-done.22.gx = bf16[6,8,1536]{2,1,0:T(8,128)(2,1)S(1)} collective-permute-done((bf16[6,8,1536]{2,1,0:T(8,128)(2,1)S(1)}, bf16[6,8,1536]{2,1,0:T(8,128)(2,1)S(1)}, u32[]{:S(2)}, u32[]{:S(2)}) %collective-permute-start.22) | collective-permute-done | bytes 147488 | tf_op jit(solution)/shard_map/ppermute | solution.py:899
  224.1 1.4 collective-permute-done.24.gd
  225.5 1.9 projection_blocks.1
  227.4 0.6 reduce
  (36 shorter events, 0.1 us)
Async XLA Ops:
  51.9 18.0 %collective-permute-start = (bf16[3072,384]{1,0:T(8,128)(2,1)}, bf16[3072,384]{1,0:T(8,128)(2,1)}, u32[]{:S(2)}, u32[]{:S(2)}) collective-permute-start(bf16[3072,384]{1,0:T(8,128)(2,1)} %down_give.1), channel_id=1, source_target_pairs={{0,1},{1,0},{2,3},{3,2},{4,5},{5,4},{6,7},{7,6},{8,9},{9,8},{10,11... | collective-permute-start | bytes 7077896 | tf_op jit(solution)/shard_map/ppermute | solution.py:899
  62.6 25.9 %collective-permute-start.1 = (bf16[768,1536]{1,0:T(8,128)(2,1)}, bf16[768,1536]{1,0:T(8,128)(2,1)S(1)}, u32[]{:S(2)}, u32[]{:S(2)}) collective-permute-start(bf16[768,1536]{1,0:T(8,128)(2,1)} %get-tuple-element.115), channel_id=1, source_target_pairs={{0,1},{1,0},{2,3},{3,2},{4,5},{5,4},{6,7},{7,6},{8,9},{9,8},{10,11... | collective-permute-start | bytes 7077896 | tf_op jit(solution)/shard_map/ppermute | solution.py:899
  62.6 61.5 %all-to-all-start = ((bf16[8,128,768]{2,1,0:T(8,128)(2,1)}), bf16[8,128,768]{2,1,0:T(8,128)(2,1)}, u32[]{:S(2)}, u32[]{:S(2)}) async-start(bf16[8,128,768]{2,1,0:T(8,128)(2,1)} %get-tuple-element.131), calls=%async_computation | async-start | bytes 3145728 | tf_op jit(solution)/shard_map/all_to_all | solution.py:910
  78.1 21.8 %collective-permute-start.2 = (bf16[24,8,1536]{2,1,0:T(8,128)(2,1)S(1)}, bf16[24,8,1536]{2,1,0:T(8,128)(2,1)S(1)}, u32[]{:S(2)}, u32[]{:S(2)}) collective-permute-start(bf16[24,8,1536]{2,1,0:T(8,128)(2,1)S(1)} %get-tuple-element.118), channel_id=1, source_target_pairs={{0,2},{1,3},{2,0},{3,1},{4,6},{5,7},{6,4},{7,5},{8,10},{9,11},{10,... | collective-permute-start | bytes 1769480 | tf_op jit(solution)/shard_map/ppermute | solution.py:899
  79.6 23.6 %collective-permute-start.3 = (bf16[24,8,1536]{2,1,0:T(8,128)(2,1)S(1)}, bf16[24,8,1536]{2,1,0:T(8,128)(2,1)S(1)}, u32[]{:S(2)}, u32[]{:S(2)}) collective-permute-start(bf16[24,8,1536]{2,1,0:T(8,128)(2,1)S(1)} %get-tuple-element.120), channel_id=1, source_target_pairs={{0,4},{4,0},{8,12},{12,8},{16,20},{20,16},{24,28},{28,24},{1,5},{5... | collective-permute-start | bytes 1769480 | tf_op jit(solution)/shard_map/ppermute | solution.py:899
  88.5 14.7 %copy-start.2 = (bf16[24,8,1536]{2,1,0:T(8,128)(2,1)S(1)}, bf16[24,8,1536]{2,1,0:T(8,128)(2,1)}, u32[]{:S(2)}) copy-start(bf16[24,8,1536]{2,1,0:T(8,128)(2,1)} %get-tuple-element.111.ka) | copy-start | bytes 1769476
  88.5 14.7 %copy-start.3 = (bf16[24,8,1536]{2,1,0:T(8,128)(2,1)S(1)}, bf16[24,8,1536]{2,1,0:T(8,128)(2,1)}, u32[]{:S(2)}) copy-start(bf16[24,8,1536]{2,1,0:T(8,128)(2,1)} %get-tuple-element.119.kb) | copy-start | bytes 1769476
  88.5 14.7 %copy-start.4 = (s32[8]{0:T(128)S(1)}, s32[8]{0:T(128)}, u32[]{:S(2)}) copy-start(s32[8]{0:T(128)} %stack.35.here_s) | copy-start | bytes 100
  99.3 24.8 %collective-permute-start.4 = (bf16[24,8,1536]{2,1,0:T(8,128)(2,1)}, bf16[24,8,1536]{2,1,0:T(8,128)(2,1)S(1)}, u32[]{:S(2)}, u32[]{:S(2)}) collective-permute-start(bf16[24,8,1536]{2,1,0:T(8,128)(2,1)} %get-tuple-element.134), channel_id=1, source_target_pairs={{0,2},{1,3},{2,0},{3,1},{4,6},{5,7},{6,4},{7,5},{8,10},{9,11},{10,... | collective-permute-start | bytes 1769480 | tf_op jit(solution)/shard_map/ppermute | solution.py:899
  99.8 24.2 %collective-permute-start.5 = (bf16[24,8,1536]{2,1,0:T(8,128)(2,1)}, bf16[24,8,1536]{2,1,0:T(8,128)(2,1)S(1)}, u32[]{:S(2)}, u32[]{:S(2)}) collective-permute-start(bf16[24,8,1536]{2,1,0:T(8,128)(2,1)} %get-tuple-element.136), channel_id=1, source_target_pairs={{0,4},{4,0},{8,12},{12,8},{16,20},{20,16},{24,28},{28,24},{1,5},{5... | collective-permute-start | bytes 1769480 | tf_op jit(solution)/shard_map/ppermute | solution.py:899
  104.0 0.7 copy-start.9
  104.7 19.4 %copy-start = (bf16[24,8,1536]{2,1,0:T(8,128)(2,1)S(1)}, bf16[24,8,1536]{2,1,0:T(8,128)(2,1)}, u32[]{:S(2)}) copy-start(bf16[24,8,1536]{2,1,0:T(8,128)(2,1)} %get-tuple-element.133.ka) | copy-start | bytes 1769476
  104.7 19.4 %copy-start.1 = (bf16[24,8,1536]{2,1,0:T(8,128)(2,1)S(1)}, bf16[24,8,1536]{2,1,0:T(8,128)(2,1)}, u32[]{:S(2)}) copy-start(bf16[24,8,1536]{2,1,0:T(8,128)(2,1)} %get-tuple-element.135.kb) | copy-start | bytes 1769476
  104.7 19.4 %copy-start.5 = (s32[8]{0:T(128)S(1)}, s32[8]{0:T(128)}, u32[]{:S(2)}) copy-start(s32[8]{0:T(128)} %stack.35.here_s) | copy-start | bytes 100
  124.9 8.0 %copy-start.10 = (bf16[12,8,1536]{2,1,0:T(8,128)(2,1)S(1)}, bf16[12,8,1536]{2,1,0:T(8,128)(2,1)}, u32[]{:S(2)}) copy-start(bf16[12,8,1536]{2,1,0:T(8,128)(2,1)} %copy-done.9) | copy-start | bytes 884740
  125.0 23.7 %copy-start.6 = (s32[8]{0:T(128)S(1)}, s32[8]{0:T(128)}, u32[]{:S(2)}) copy-start(s32[8]{0:T(128)} %stack.35.here_s) | copy-start | bytes 100
  132.9 26.7 %collective-permute-start.10 = (bf16[776,1536]{1,0:T(8,128)(2,1)S(1)}, bf16[776,1536]{1,0:T(8,128)(2,1)S(1)}, u32[]{:S(2)}, u32[]{:S(2)}) collective-permute-start(bf16[776,1536]{1,0:T(8,128)(2,1)S(1)} %proj_give.1), channel_id=1, source_target_pairs={{0,1},{1,0},{2,3},{3,2},{4,5},{5,4},{6,7},{7,6},{8,9},{9,8},{10,11... | collective-permute-start | bytes 7151624 | tf_op jit(solution)/shard_map/ppermute | solution.py:899
  132.9 9.9 %collective-permute-start.6 = (bf16[12,8,1536]{2,1,0:T(8,128)(2,1)S(1)}, bf16[12,8,1536]{2,1,0:T(8,128)(2,1)S(1)}, u32[]{:S(2)}, u32[]{:S(2)}) collective-permute-start(bf16[12,8,1536]{2,1,0:T(8,128)(2,1)S(1)} %copy-done.10), channel_id=1, source_target_pairs={{0,4},{4,0},{8,12},{12,8},{16,20},{20,16},{24,28},{28,24},{1,5},{5... | collective-permute-start | bytes 884744 | tf_op jit(solution)/shard_map/ppermute | solution.py:899
  133.0 9.9 %collective-permute-start.7 = (bf16[12,8,1536]{2,1,0:T(8,128)(2,1)S(1)}, bf16[12,8,1536]{2,1,0:T(8,128)(2,1)S(1)}, u32[]{:S(2)}, u32[]{:S(2)}) collective-permute-start(bf16[12,8,1536]{2,1,0:T(8,128)(2,1)S(1)} %get-tuple-element.145), channel_id=1, source_target_pairs={{0,2},{1,3},{2,0},{3,1},{4,6},{5,7},{6,4},{7,5},{8,10},{9,11},{10,... | collective-permute-start | bytes 884744 | tf_op jit(solution)/shard_map/ppermute | solution.py:899
  134.3 14.3 %collective-permute-start.8 = (bf16[12,8,1536]{2,1,0:T(8,128)(2,1)S(1)}, bf16[12,8,1536]{2,1,0:T(8,128)(2,1)S(1)}, u32[]{:S(2)}, u32[]{:S(2)}) collective-permute-start(bf16[12,8,1536]{2,1,0:T(8,128)(2,1)S(1)} %get-tuple-element.146), channel_id=1, source_target_pairs={{0,4},{4,0},{8,12},{12,8},{16,20},{20,16},{24,28},{28,24},{1,5},{5... | collective-permute-start | bytes 884744 | tf_op jit(solution)/shard_map/ppermute | solution.py:899
  136.3 12.4 %collective-permute-start.9 = (bf16[12,8,1536]{2,1,0:T(8,128)(2,1)S(1)}, bf16[12,8,1536]{2,1,0:T(8,128)(2,1)S(1)}, u32[]{:S(2)}, u32[]{:S(2)}) collective-permute-start(bf16[12,8,1536]{2,1,0:T(8,128)(2,1)S(1)} %get-tuple-element.148), channel_id=1, source_target_pairs={{0,2},{1,3},{2,0},{3,1},{4,6},{5,7},{6,4},{7,5},{8,10},{9,11},{10,... | collective-permute-start | bytes 884744 | tf_op jit(solution)/shard_map/ppermute | solution.py:899
  149.5 20.8 %collective-permute-start.11 = (bf16[24,8,1536]{2,1,0:T(8,128)(2,1)S(1)}, bf16[24,8,1536]{2,1,0:T(8,128)(2,1)S(1)}, u32[]{:S(2)}, u32[]{:S(2)}) collective-permute-start(bf16[24,8,1536]{2,1,0:T(8,128)(2,1)S(1)} %get-tuple-element.155), channel_id=1, source_target_pairs={{0,8},{4,12},{8,0},{12,4},{16,24},{20,28},{24,16},{28,20},{1,9},{5... | collective-permute-start | bytes 1769480 | tf_op jit(solution)/shard_map/ppermute | solution.py:899
  159.5 10.8 %copy-start.7 = (s32[8]{0:T(128)S(1)}, s32[8]{0:T(128)}, u32[]{:S(2)}) copy-start(s32[8]{0:T(128)} %stack.35.here_s) | copy-start | bytes 100
  168.4 15.5 %copy-start.8 = (s32[8]{0:T(128)S(1)}, s32[8]{0:T(128)}, u32[]{:S(2)}) copy-start(s32[8]{0:T(128)} %stack.35.here_s) | copy-start | bytes 100
  168.4 15.5 %collective-permute-start.12 = (bf16[25,8,1536]{2,1,0:T(8,128)(2,1)S(1)}, bf16[25,8,1536]{2,1,0:T(8,128)(2,1)S(1)}, u32[]{:S(2)}, u32[]{:S(2)}) collective-permute-start(bf16[25,8,1536]{2,1,0:T(8,128)(2,1)S(1)} %get-tuple-element.159), channel_id=1, source_target_pairs={{0,2},{1,3},{2,0},{3,1},{4,6},{5,7},{6,4},{7,5},{8,10},{9,11},{10,... | collective-permute-start | bytes 1843208 | tf_op jit(solution)/shard_map/ppermute | solution.py:899
  169.9 14.0 %collective-permute-start.13 = (bf16[24,8,1536]{2,1,0:T(8,128)(2,1)S(1)}, bf16[24,8,1536]{2,1,0:T(8,128)(2,1)S(1)}, u32[]{:S(2)}, u32[]{:S(2)}) collective-permute-start(bf16[24,8,1536]{2,1,0:T(8,128)(2,1)S(1)} %get-tuple-element.161), channel_id=1, source_target_pairs={{0,4},{4,0},{8,12},{12,8},{16,20},{20,16},{24,28},{28,24},{1,5},{5... | collective-permute-start | bytes 1769480 | tf_op jit(solution)/shard_map/ppermute | solution.py:899
  171.0 18.3 %collective-permute-start.16 = (bf16[12,8,1536]{2,1,0:T(8,128)(2,1)S(1)}, bf16[12,8,1536]{2,1,0:T(8,128)(2,1)S(1)}, u32[]{:S(2)}, u32[]{:S(2)}) collective-permute-start(bf16[12,8,1536]{2,1,0:T(8,128)(2,1)S(1)} %get-tuple-element.169), channel_id=1, source_target_pairs={{0,16},{4,20},{8,24},{12,28},{16,0},{20,4},{24,8},{28,12},{1,17},{... | collective-permute-start | bytes 884744 | tf_op jit(solution)/shard_map/ppermute | solution.py:899
  184.7 7.5 %collective-permute-start.14 = (bf16[13,8,1536]{2,1,0:T(8,128)(2,1)S(1)}, bf16[13,8,1536]{2,1,0:T(8,128)(2,1)S(1)}, u32[]{:S(2)}, u32[]{:S(2)}) collective-permute-start(bf16[13,8,1536]{2,1,0:T(8,128)(2,1)S(1)} %get-tuple-element.163), channel_id=1, source_target_pairs={{0,4},{4,0},{8,12},{12,8},{16,20},{20,16},{24,28},{28,24},{1,5},{5... | collective-permute-start | bytes 958472 | tf_op jit(solution)/shard_map/ppermute | solution.py:899
  185.5 6.8 %collective-permute-start.15 = (bf16[12,8,1536]{2,1,0:T(8,128)(2,1)S(1)}, bf16[12,8,1536]{2,1,0:T(8,128)(2,1)S(1)}, u32[]{:S(2)}, u32[]{:S(2)}) collective-permute-start(bf16[12,8,1536]{2,1,0:T(8,128)(2,1)S(1)} %get-tuple-element.165), channel_id=1, source_target_pairs={{0,2},{1,3},{2,0},{3,1},{4,6},{5,7},{6,4},{7,5},{8,10},{9,11},{10,... | collective-permute-start | bytes 884744 | tf_op jit(solution)/shard_map/ppermute | solution.py:899
  190.0 9.0 %collective-permute-start.17 = (bf16[12,8,1536]{2,1,0:T(8,128)(2,1)S(1)}, bf16[12,8,1536]{2,1,0:T(8,128)(2,1)S(1)}, u32[]{:S(2)}, u32[]{:S(2)}) collective-permute-start(bf16[12,8,1536]{2,1,0:T(8,128)(2,1)S(1)} %fold_last.2.me), channel_id=1, source_target_pairs={{0,2},{1,3},{2,0},{3,1},{4,6},{5,7},{6,4},{7,5},{8,10},{9,11},{10,... | collective-permute-start | bytes 884744 | tf_op jit(solution)/shard_map/ppermute | solution.py:899
  193.0 10.0 %collective-permute-start.20 = (bf16[13,8,1536]{2,1,0:T(8,128)(2,1)S(1)}, bf16[13,8,1536]{2,1,0:T(8,128)(2,1)S(1)}, u32[]{:S(2)}, u32[]{:S(2)}) collective-permute-start(bf16[13,8,1536]{2,1,0:T(8,128)(2,1)S(1)} %get-tuple-element.172), channel_id=1, source_target_pairs={{0,8},{4,12},{8,0},{12,4},{16,24},{20,28},{24,16},{28,20},{1,9},{5... | collective-permute-start | bytes 958472 | tf_op jit(solution)/shard_map/ppermute | solution.py:899
  197.3 1.7 collective-permute-start.18
  199.0 1.6 collective-permute-start.19
  203.6 14.1 %collective-permute-start.21 = (bf16[7,8,1536]{2,1,0:T(8,128)(2,1)S(1)}, bf16[7,8,1536]{2,1,0:T(8,128)(2,1)S(1)}, u32[]{:S(2)}, u32[]{:S(2)}) collective-permute-start(bf16[7,8,1536]{2,1,0:T(8,128)(2,1)S(1)} %get-tuple-element.174), channel_id=1, source_target_pairs={{0,16},{4,20},{8,24},{12,28},{16,0},{20,4},{24,8},{28,12},{1,17},{... | collective-permute-start | bytes 516104 | tf_op jit(solution)/shard_map/ppermute | solution.py:899
  218.3 5.8 %collective-permute-start.22 = (bf16[6,8,1536]{2,1,0:T(8,128)(2,1)S(1)}, bf16[6,8,1536]{2,1,0:T(8,128)(2,1)S(1)}, u32[]{:S(2)}, u32[]{:S(2)}) collective-permute-start(bf16[6,8,1536]{2,1,0:T(8,128)(2,1)S(1)} %get-tuple-element.175.me), channel_id=1, source_target_pairs={{0,2},{1,3},{2,0},{3,1},{4,6},{5,7},{6,4},{7,5},{8,10},{9,11},{10,... | collective-permute-start | bytes 442376 | tf_op jit(solution)/shard_map/ppermute | solution.py:899
  219.4 4.7 %collective-permute-start.23 = (bf16[6,8,1536]{2,1,0:T(8,128)(2,1)S(1)}, bf16[6,8,1536]{2,1,0:T(8,128)(2,1)S(1)}, u32[]{:S(2)}, u32[]{:S(2)}) collective-permute-start(bf16[6,8,1536]{2,1,0:T(8,128)(2,1)S(1)} %get-tuple-element.175.me), channel_id=1, source_target_pairs={{0,1},{1,0},{2,3},{3,2},{4,5},{5,4},{6,7},{7,6},{8,9},{9,8},{10,11... | collective-permute-start | bytes 442376 | tf_op jit(solution)/shard_map/ppermute | solution.py:899
  224.1 1.4 collective-permute-start.24

commit v6 on v5

--- a/solution.py
+++ b/solution.py
@@ -54,7 +54,7 @@
 
 
 def call(
-    kernel, name, grid, prefetch, in_specs, out_specs, out_shape, scratch, flops, moved, args, vmem=24, free=0, loose=()
+    kernel, name, grid, prefetch, in_specs, out_specs, out_shape, scratch, flops, moved, args, vmem=24, free=0, loose=(), near=()
 ):
     single = not isinstance(out_shape, list)
     shapes = [out_shape] if single else out_shape
@@ -64,7 +64,9 @@
     ]
     out_shape = shapes[0] if single else shapes
     args = [
-        pltpu.with_memory_space_constraint(item, pltpu.HBM) if large(item) and number < len(args) - free else item
+        pltpu.with_memory_space_constraint(item, pltpu.HBM)
+        if large(item) and number < len(args) - free and number not in near
+        else item
         for number, item in enumerate(args)
     ]
     return pl.pallas_call(
@@ -389,7 +391,7 @@
         8 * rows * width * ff,
         40e6,
         (n_attn, w_up, w_down, table, sid),
-        44,
+        38, 0, (2, 5),
     )
 
 
@@ -436,7 +438,7 @@
         return call(
             give, "down_give", (steps,), (here,), in_specs,
             pl.BlockSpec((tall, half), lambda i, *_: (i, 0)),
-            shaped((ff, half), BF16), [], flops, 9e6, (active, grad_second), 20, 0, (0,),
+            shaped((ff, half), BF16), [], flops, 9e6, (active, grad_second), 20, 0, (0,), (1,),
         )
     block = (2 * pieces, 8, folds * half)
     return call(
@@ -445,7 +447,7 @@
         [pl.BlockSpec(block, lambda i, *_: (i, 0, 0))] * 4,
         [shaped((8 * pieces, 8, folds * half), BF16)] * 4,
         [pltpu.VMEM((1, 2, 2, 2, folds * pieces, 8, half), F32)],
-        flops, 11e6, (active, grad_second, got), 24, 1, (0, 2),
+        flops, 11e6, (active, grad_second, got), 24, 1, (0, 2), (1,),
     )
 
 
@@ -510,7 +512,7 @@
             pl.BlockSpec((1, chunk), lambda i, *_: (0, i)),
         ],
         out_shape + [shaped((rows, half), BF16), shaped((1, half), F32)],
-        scratch, 4 * rows * width * half, 16e6, args, 34, 0 if got is None else 1, (0,) if got is None else (0, 2),
+        scratch, 4 * rows * width * half, 16e6, args, 26, 0 if got is None else 1, (0,) if got is None else (0, 2, 4), (0, 2),
     )
 
 
@@ -529,7 +531,7 @@
             pl.BlockSpec((width, half), lambda i, h: (0, h[which]), pipeline_mode=pl.Buffered(1)),
         ],
         pl.BlockSpec((block, width), lambda i, h: (i, 0)),
-        shaped((rows, width), F32), [], 2 * rows * width * half, 9e6, (grad_inner, w_up), 16,
+        shaped((rows, width), F32), [], 2 * rows * width * half, 9e6, (grad_inner, w_up), 16, 0, (0,),
     )
 
 
@@ -605,7 +607,7 @@
         8 * rows * width * width * 2,
         40e6,
         (gh, gres, grad_inner, w_up, n_attn, spread, table, w_out, qkv, probs),
-        34,
+        24, 0, (1,), (0, 2),
     )
 
 
@@ -679,7 +681,7 @@
             give, "proj_give", (4,), (here,), in_specs,
             pl.BlockSpec((width + 8, part), lambda i, *_: (0, i)),
             shaped((width + 8, 4 * part), BF16),
-            [pltpu.VMEM((width, part), F32)], flops, 9e6, args, 20, 0, (0,),
+            [pltpu.VMEM((width, part), F32)], flops, 9e6, args, 20, 0, (0,), (3,),
         )
     return call(
         own, "proj_own", (4,), (here,),
@@ -690,7 +692,7 @@
         ],
         [shaped((8 * pieces + extra, 8, 4 * part), BF16) for extra in (1, 1, 0, 0)],
         [pltpu.VMEM((width, part), F32), pltpu.VMEM((4, 2, 2, 2, pieces, 8, part), F32)],
-        flops, 11e6, args + [got], 24, 1, (0, 1, 2, 3),
+        flops, 11e6, args + [got], 24, 1, (0, 1, 2, 3), (3,),
     )
 
 
@@ -743,7 +745,7 @@
     return (left.astype(F32) + right.astype(F32)).astype(BF16)
 
 
-def fold_second(keep_a, got_a, keep_b, got_b, here, pieces, extra):
+def fold_second(keep_a, got_a, keep_b, got_b, here, pieces, extra, far=False):
     cols = keep_a.shape[2]
 
     def kernel(here_s, ka, ga, kb, gb, send_a, left_a, send_b, left_b):
@@ -766,8 +768,11 @@
 
     a_out = shaped((4 * pieces + extra, 8, cols), BF16)
     b_out = shaped((4 * pieces, 8, cols), BF16)
+    a_left, b_left = a_out, b_out
+    if far:
+        a_left, b_left = pltpu.HBM(a_out.shape, BF16), pltpu.HBM(b_out.shape, BF16)
     return small_call(
-        kernel, "fold_second", here, (keep_a, got_a, keep_b, got_b), [a_out, a_out, b_out, b_out]
+        kernel, "fold_second", here, (keep_a, got_a, keep_b, got_b), [a_out, a_left, b_out, b_left]
     )
 
 
@@ -976,7 +981,7 @@
         )
         up_a, up_b = swap(up_dealt[0], "narrow", 2), swap(up_dealt[2], "wide", 1)
         down_dealt = fold_second(
-            down_dealt[1], down_a, down_dealt[3], down_b, after(here, bup_kept), pieces, 0
+            down_dealt[1], down_a, down_dealt[3], down_b, after(here, bup_kept), pieces, 0, True
         )
         down_a, down_b = swap(down_dealt[0], "wide", 1), swap(down_dealt[2], "narrow", 2)
         gr, gb, gm, vec_attn = attention_backward(
@@ -988,21 +993,21 @@
         up_a, up_b = swap(up_dealt[0], "wide", 1), swap(up_dealt[2], "narrow", 2)
         projections = (tokens, gm, attended, gb, (vec_ffn, vec_attn, bup_sent, bup_kept))
         proj_sent = projection_terms(*projections, after(here, up_dealt[1]), 1)
+        proj_dealt = projection_terms(
+            *projections, after(here, proj_sent), 0, swap(proj_sent, "narrow", 1)
+        )
+        proj_a, proj_b = swap(proj_dealt[0], "narrow", 2), swap(proj_dealt[2], "wide", 1)
         send, feed = fold_third(
             [(down_dealt[1], down_a, down_dealt[3], down_b), (up_dealt[1], up_a, up_dealt[3], up_b)],
-            after(here, proj_sent), pieces, 0,
+            after(here, proj_dealt[1]), pieces, 0,
         )
         feed_got = swap(send, "wide", 2)
         grad_tokens = input_gradient(after(gm, feed), w_qkv, gr, 2 * span)
-        proj_dealt = projection_terms(
-            *projections, after(here, grad_tokens), 0, swap(proj_sent, "narrow", 1)
-        )
-        proj_a, proj_b = swap(proj_dealt[0], "narrow", 2), swap(proj_dealt[2], "wide", 1)
-        send, feed = fold_fourth(feed, feed_got, after(here, proj_dealt[1]), 0)
+        encoded = copied(encoded, after(here, grad_tokens), span)
+        send, feed = fold_fourth(feed, feed_got, after(here, encoded), 0)
         feed_got = swap(send, "wide", 4)
-        encoded = copied(encoded, after(here, feed), span)
         proj_dealt = fold_second(
-            proj_dealt[1], proj_a, proj_dealt[3], proj_b, after(here, encoded), pieces, 1
+            proj_dealt[1], proj_a, proj_dealt[3], proj_b, after(here, feed), pieces, 1
         )
         proj_a, proj_b = swap(proj_dealt[0], "wide", 1), swap(proj_dealt[2], "narrow", 2)
         (feed,) = fold_last(feed, feed_got, after(here, proj_dealt[1]), 0)

time: 229 us -> 220 us (0.961)
  starting transfers between devices: 39.8 us -> 28.1 us
  waiting for transfers between devices: 37 us -> 44.3 us
  Pallas kernels: 148 us -> 144 us
    ppermute x25, starting transfers between devices: 32.5 us -> 20.8 us  [swap(): lax.ppermute(item, axis, [(index, index ^ step) for index in range(count)])]
    ppermute x25, waiting for transfers between devices: 37 us -> 44.3 us  [swap(): lax.ppermute(item, axis, [(index, index ^ step) for index in range(count)])]
    pallas_call x12, Pallas kernels: 137 us -> 131 us  [call(): pl.pallas_call(kernel, grid_spec=pltpu.PrefetchScalarGridSpec(num_scalar_...]
  transfers between devices with their start and end apart: 26 -> 26, of which waited for: 12 -> 9; matrix products, arithmetic and copies ran while one was open for 0% -> 0% of each run, Pallas kernels for 38% -> 37%
where the time goes in v6:
time: 220 us; the launch traced here: 219 us
  Pallas kernels  144 us (65%)
  waiting for transfers between devices  44.3 us (20%)
  starting transfers between devices  28.1 us (13%)
    pallas_call x12, Pallas kernels, call(): pl.pallas_call(kernel, grid_spec=pltpu.PrefetchScalarGridSpec(num_scalar_...  131 us
    ppermute x25, waiting for transfers between devices, swap(): lax.ppermute(item, axis, [(index, index ^ step) for index in range(count)])  44.3 us
    ppermute x25, starting transfers between devices, swap(): lax.ppermute(item, axis, [(index, index ^ step) for index in range(count)])  20.8 us
    pallas_call x11, Pallas kernels, small_call(): pl.pallas_call(kernel, in_specs=[pl.BlockSpec(memory_space=pltpu.SMEM)] +...  12.2 us
    all_to_all x1, starting transfers between devices, regroup_rows(): got = lax.all_to_all(sent, 'wide', split_axis=0, concat_axis=0, tiled=True)  7.31 us
  transfers between devices with their start and end apart: 26, of which 9 were waited for; matrix products, arithmetic and copies ran while one was open for 0% of the time, Pallas kernels for 37%

profile of v6, /device:TPU:0, one launch (start us, length us, event | category | flops | bytes accessed | tf_op | source)
XLA Modules:
  0.0 218.9 jit_solution(10133701510535349087)
XLA Ops:
  0.7 0.9 vector_table.1.tab_ref
  1.6 16.5 %attn_fwd.1 = (bf16[1024,2304]{1,0:T(8,128)(2,1)}, bf16[8,6,256,128]{3,2,1,0:T(8,128)(2,1)}, bf16[1024,768]{1,0:T(8,128)(2,1)}, f32[1024,768]{1,0:T(8,128)}, f32...) custom-call(s32[8]{0:T(128)} %slots_s.1, s32[26]{0:T(128)} %lengths_s.1, bf16[1024,768]{1,0:T(8,128)(2,1)} %x_ref.5, ...), custom_call_target="tpu_custom_call" | custom-call | flops 483183808 | bytes 1500000 | tf_op jit(solution)/shard_map/attn_fwd/pallas_call | solution.py:72
  18.1 24.3 %ffn_fwd.1 = (bf16[1024,3072]{1,0:T(8,128)(2,1)}, bf16[1024,3072]{1,0:T(8,128)(2,1)}, bf16[768,1024]{1,0:T(8,128)(2,1)S(1)}, bf16[8,128,768]{2,1,0:T(8,128)(2,1)...) custom-call(s32[8]{0:T(128)} %slots_s.1, s32[1,26]{1,0:T(1,128)} %pairing_s.1, ...), custom_call_target="tpu_custom_call" | custom-call | flops 966367616 | bytes 2000000 | tf_op jit(solution)/shard_map/ffn_fwd/pallas_call | solution.py:72
  42.4 0.6 stack.35.here_s
  43.0 7.7 %down_give.1 = bf16[3072,384]{1,0:T(8,128)(2,1)} custom-call(s32[8]{0:T(128)} %stack.35.here_s, bf16[1024,3072]{1,0:T(8,128)(2,1)} %get-tuple-element.104.act_ref, bf16[1024,768]{1,0:T(8,128)(2,1)S(1)} %get-tuple-element.105.gs_ref), custom_call_target="tpu_custom_call" | custom-call | flops 120795952 | bytes 450000 | tf_op jit(solution)/shard_map/down_give/pallas_call | solution.py:72
  50.7 0.5 collective-permute-start
  51.2 9.3 %up_give.1 = (bf16[768,1536]{1,0:T(8,128)(2,1)}, bf16[1024,1536]{1,0:T(8,128)(2,1)}, f32[1,1536]{1,0:T(1,128)S(1)}) custom-call(s32[8]{0:T(128)} %stack.35.here_s, bf16[1024,768]{1,0:T(8,128)(2,1)S(1)} %get-tuple-element.105.gs_ref, bf16[1024,3072]{1,0:T(8,128)(2,1)} %get-tuple-element.107.dg_ref, bf16[768,1024]{1,0:T(8,128)(2,1)S(1)} %get-tuple-element.108.ht_ref, ...), custom_call_target="tpu_custom_call" | custom-call | flops 241591904 | bytes 800000 | tf_op jit(solution)/shard_map/up_give/pallas_call | solution.py:72
  60.5 0.0 collective-permute-start.1
  60.5 7.3 %all-to-all-start = ((bf16[8,128,768]{2,1,0:T(8,128)(2,1)}), bf16[8,128,768]{2,1,0:T(8,128)(2,1)}, u32[]{:S(2)}, u32[]{:S(2)}) async-start(bf16[8,128,768]{2,1,0:T(8,128)(2,1)} %get-tuple-element.131), calls=%async_computation | async-start | bytes 3145728 | tf_op jit(solution)/shard_map/all_to_all | solution.py:915
  67.8 0.0 collective-permute-done.got_ref
  67.8 8.0 %down_own.1 = (bf16[24,8,1536]{2,1,0:T(8,128)(2,1)S(1)}, bf16[24,8,1536]{2,1,0:T(8,128)(2,1)}, bf16[24,8,1536]{2,1,0:T(8,128)(2,1)S(1)}, bf16[24,8,1536]{2,1,0:T(8,128)(2,1)}) custom-call(s32[8]{0:T(128)} %stack.35.here_s, bf16[1024,3072]{1,0:T(8,128)(2,1)} %get-tuple-element.104.act_ref, bf16[1024,768]{1,0:T(8,128)(2,1)S(1)} %get-tuple-element.105.gs_ref, ...), custom_call_target="tpu_custom_call" | custom-call | flops 120795952 | bytes 550000 | tf_op jit(solution)/shard_map/down_own/pallas_call | solution.py:72
  75.8 1.5 collective-permute-start.2
  77.3 2.0 collective-permute-start.3
  79.3 5.7 %hidden_grad.1.gh_ref = f32[1024,768]{1,0:T(8,128)S(1)} custom-call(s32[8]{0:T(128)} %stack.35.here_s, bf16[1024,1536]{1,0:T(8,128)(2,1)} %get-tuple-element.113.gi_ref, bf16[768,3072]{1,0:T(8,128)(2,1)} %wu_ref.5), custom_call_target="tpu_custom_call" | custom-call | flops 120795952 | bytes 450000 | tf_op jit(solution)/shard_map/hidden_grad/pallas_call | solution.py:72
  85.0 0.0 copy-start.6
  85.1 0.0 collective-permute-done.1.refs_0_
  85.1 9.9 %up_own.1 = (bf16[24,8,1536]{2,1,0:T(8,128)(2,1)}, bf16[24,8,1536]{2,1,0:T(8,128)(2,1)}, bf16[24,8,1536]{2,1,0:T(8,128)(2,1)}, bf16[24,8,1536]{2,1,0:T(8,128)(2,...) custom-call(s32[8]{0:T(128)} %stack.35.here_s, bf16[1024,768]{1,0:T(8,128)(2,1)S(1)} %get-tuple-element.105.gs_ref, ...), custom_call_target="tpu_custom_call" | custom-call | flops 241591904 | bytes 800000 | tf_op jit(solution)/shard_map/up_own/pallas_call | solution.py:72
  95.0 0.5 collective-permute-start.4
  95.5 0.0 collective-permute-done.2.ga
  95.5 5.5 %collective-permute-done.3.gb = bf16[24,8,1536]{2,1,0:T(8,128)(2,1)S(1)} collective-permute-done((bf16[24,8,1536]{2,1,0:T(8,128)(2,1)S(1)}, bf16[24,8,1536]{2,1,0:T(8,128)(2,1)S(1)}, u32[]{:S(2)}, u32[]{:S(2)}) %collective-permute-start.3) | collective-permute-done | bytes 589856 | tf_op jit(solution)/shard_map/ppermute | solution.py:904
  101.0 1.6 fold_second.3
  102.6 18.7 %attn_bwd.1 = (f32[1024,768]{1,0:T(8,128)}, bf16[1024,768]{1,0:T(8,128)(2,1)S(1)}, bf16[1024,2304]{1,0:T(8,128)(2,1)}, f32[8,768]{1,0:T(8,128)S(1)}) custom-call(s32[8]{0:T(128)} %stack.35.here_s, f32[1024,768]{1,0:T(8,128)S(1)} %hidden_grad.1.gh_ref, f32[1024,768]{1,0:T(8,128)} %get-tuple-element.123.gres_ref, ...), custom_call_target="tpu_custom_call" | custom-call | flops 483183808 | bytes 2000000 | tf_op jit(solution)/shard_map/attn_bwd/pallas_call | solution.py:72
  121.3 0.0 all-to-all-done
  121.3 0.0 collective-permute-done.5.gb
  121.3 1.5 fold_second.4
  122.9 7.6 %proj_give.1 = bf16[776,1536]{1,0:T(8,128)(2,1)S(1)} custom-call(s32[8]{0:T(128)} %stack.35.here_s, bf16[1024,768]{1,0:T(8,128)(2,1)} %x_ref.5, bf16[1024,2304]{1,0:T(8,128)(2,1)} %get-tuple-element.152.gm_ref, bf16[1024,768]{1,0:T(8,128)(2,1)} %get-tuple-element.139.att_ref, bf16[1024,768]{1,0:T(8,128)(2,1)S(1)} %get-tuple-element.140.gb_ref, ...), custom_call_target="tpu_custom_call" | custom-call | flops 120795952 | bytes 450000 | tf_op jit(solution)/shard_map/proj_give/pallas_call | solution.py:72
  130.4 0.1 collective-permute-start.6
  130.5 0.1 collective-permute-start.7
  130.6 1.3 collective-permute-start.8
  131.9 1.9 collective-permute-start.9
  133.9 0.8 collective-permute-start.10
  134.6 0.4 collective-permute-done.6.got_ref
  135.1 8.5 %proj_own.1 = (bf16[25,8,1536]{2,1,0:T(8,128)(2,1)S(1)}, bf16[25,8,1536]{2,1,0:T(8,128)(2,1)S(1)}, bf16[24,8,1536]{2,1,0:T(8,128)(2,1)S(1)}, bf16[24,8,1536]{2,1,0:T(8,128)(2,1)S(1)}) custom-call(s32[8]{0:T(128)} %stack.35.here_s, bf16[1024,768]{1,0:T(8,128)(2,1)} %x_ref.5, bf16[1024,2304]{1,0:T(8,128)(2,1)} %get-tuple-element.152.gm_ref, ...), custom_call_target="tpu_custom_call" | custom-call | flops 120795952 | bytes 550000 | tf_op jit(solution)/shard_map/proj_own/pallas_call | solution.py:72
  143.6 2.6 %collective-permute-done.9.refs_5_ = bf16[12,8,1536]{2,1,0:T(8,128)(2,1)S(1)} collective-permute-done((bf16[12,8,1536]{2,1,0:T(8,128)(2,1)S(1)}, bf16[12,8,1536]{2,1,0:T(8,128)(2,1)S(1)}, u32[]{:S(2)}, u32[]{:S(2)}) %collective-permute-start.9) | collective-permute-done | bytes 294944 | tf_op jit(solution)/shard_map/ppermute | solution.py:904
  146.3 0.8 fold_third.2
  147.1 1.6 collective-permute-start.11
  148.7 1.5 collective-permute-start.12
  150.2 0.3 collective-permute-start.13
  150.5 8.9 %input_grad.1 = bf16[1024,768]{1,0:T(8,128)(2,1)} custom-call(bf16[1024,2304]{1,0:T(8,128)(2,1)} %get-tuple-element.152.gm_ref, bf16[768,2304]{1,0:T(8,128)(2,1)} %wq_ref.3, f32[1024,768]{1,0:T(8,128)} %get-tuple-element.153.gr_ref), custom_call_target="tpu_custom_call" | custom-call | flops 181193936 | bytes 650000 | tf_op jit(solution)/shard_map/input_grad/pallas_call | solution.py:72
  159.4 6.2 %copied.1 = bf16[1024,768]{1,0:T(8,128)(2,1)} custom-call(s32[8]{0:T(128)} %stack.35.here_s, bf16[1024,768]{1,0:T(8,128)(2,1)} %bitcast.8.in_ref), custom_call_target="tpu_custom_call" | custom-call | bytes 150000 | tf_op jit(solution)/shard_map/copied/pallas_call | solution.py:72
  165.6 0.0 collective-permute-done.11.got_ref
  165.6 0.7 fold_fourth.2
  166.3 6.4 %collective-permute-start.16 = (bf16[12,8,1536]{2,1,0:T(8,128)(2,1)S(1)}, bf16[12,8,1536]{2,1,0:T(8,128)(2,1)S(1)}, u32[]{:S(2)}, u32[]{:S(2)}) collective-permute-start(bf16[12,8,1536]{2,1,0:T(8,128)(2,1)S(1)} %get-tuple-element.169), channel_id=1, source_target_pairs={{0,16},{4,20},{8,24},{12,28},{16,0},{20,4},{24,8},{28,12},{1,17},{... | collective-permute-start | bytes 884744 | tf_op jit(solution)/shard_map/ppermute | solution.py:904
  172.7 0.8 fold_second.5
  173.5 0.4 collective-permute-start.14
  173.9 0.5 collective-permute-start.15
  174.4 10.0 %collective-permute-done.16.got_ref = bf16[12,8,1536]{2,1,0:T(8,128)(2,1)S(1)} collective-permute-done((bf16[12,8,1536]{2,1,0:T(8,128)(2,1)S(1)}, bf16[12,8,1536]{2,1,0:T(8,128)(2,1)S(1)}, u32[]{:S(2)}, u32[]{:S(2)}) %collective-permute-start.16) | collective-permute-done | bytes 294944 | tf_op jit(solution)/shard_map/ppermute | solution.py:904
  184.4 0.6 fold_last.2.me
  185.0 0.6 collective-permute-start.17
  185.6 0.7 fold_third.3
  186.3 0.1 collective-permute-start.20
  186.4 0.1 collective-permute-start.18
  186.5 7.5 %collective-permute-done.17.gx = bf16[12,8,1536]{2,1,0:T(8,128)(2,1)S(1)} collective-permute-done((bf16[12,8,1536]{2,1,0:T(8,128)(2,1)S(1)}, bf16[12,8,1536]{2,1,0:T(8,128)(2,1)S(1)}, u32[]{:S(2)}, u32[]{:S(2)}) %collective-permute-start.17) | collective-permute-done | bytes 294944 | tf_op jit(solution)/shard_map/ppermute | solution.py:904
  194.0 1.6 collective-permute-done.19.gd
  195.6 2.4 %feed_blocks.1 = (f32[384,768]{1,0:T(8,128)}, f32[96,3072]{1,0:T(8,128)}) custom-call(s32[8]{0:T(128)S(1)} %copy-done.9, bf16[12,8,1536]{2,1,0:T(8,128)(2,1)S(1)} %fold_last.2.me, bf16[12,8,1536]{2,1,0:T(8,128)(2,1)S(1)} %collective-permute-done.17.gx, bf16[12,8,1536]{2,1,0:T(8,128)(2,1)S(1)} %collective-permute-done.18.gc, ...), custom_call_target="tpu_custom_call" | custom-call | flops 50000 | bytes 200000 | tf_op jit(solution)/shard_map/feed_blocks/pallas_call | solution.py:732
  198.0 0.6 fold_fourth.3
  198.7 0.1 collective-permute-start.21
  198.7 9.9 %collective-permute-done.21.got_ref = bf16[7,8,1536]{2,1,0:T(8,128)(2,1)S(1)} collective-permute-done((bf16[7,8,1536]{2,1,0:T(8,128)(2,1)S(1)}, bf16[7,8,1536]{2,1,0:T(8,128)(2,1)S(1)}, u32[]{:S(2)}, u32[]{:S(2)}) %collective-permute-start.21) | collective-permute-done | bytes 172064 | tf_op jit(solution)/shard_map/ppermute | solution.py:904
  208.6 0.6 fold_last.3
  209.2 0.6 collective-permute-start.22
  209.8 5.3 %collective-permute-done.22.gx = bf16[6,8,1536]{2,1,0:T(8,128)(2,1)S(1)} collective-permute-done((bf16[6,8,1536]{2,1,0:T(8,128)(2,1)S(1)}, bf16[6,8,1536]{2,1,0:T(8,128)(2,1)S(1)}, u32[]{:S(2)}, u32[]{:S(2)}) %collective-permute-start.22) | collective-permute-done | bytes 147488 | tf_op jit(solution)/shard_map/ppermute | solution.py:904
  215.1 1.4 collective-permute-done.24.gd
  216.4 1.9 projection_blocks.1
  218.3 0.6 reduce
  (34 shorter events, 0.1 us)
Async XLA Ops:
  50.7 17.1 %collective-permute-start = (bf16[3072,384]{1,0:T(8,128)(2,1)}, bf16[3072,384]{1,0:T(8,128)(2,1)}, u32[]{:S(2)}, u32[]{:S(2)}) collective-permute-start(bf16[3072,384]{1,0:T(8,128)(2,1)} %down_give.1), channel_id=1, source_target_pairs={{0,1},{1,0},{2,3},{3,2},{4,5},{5,4},{6,7},{7,6},{8,9},{9,8},{10,11... | collective-permute-start | bytes 7077896 | tf_op jit(solution)/shard_map/ppermute | solution.py:904
  60.5 24.5 %collective-permute-start.1 = (bf16[768,1536]{1,0:T(8,128)(2,1)}, bf16[768,1536]{1,0:T(8,128)(2,1)}, u32[]{:S(2)}, u32[]{:S(2)}) collective-permute-start(bf16[768,1536]{1,0:T(8,128)(2,1)} %get-tuple-element.115), channel_id=1, source_target_pairs={{0,1},{1,0},{2,3},{3,2},{4,5},{5,4},{6,7},{7,6},{8,9},{9,8},{10,11... | collective-permute-start | bytes 7077896 | tf_op jit(solution)/shard_map/ppermute | solution.py:904
  60.5 60.7 %all-to-all-start = ((bf16[8,128,768]{2,1,0:T(8,128)(2,1)}), bf16[8,128,768]{2,1,0:T(8,128)(2,1)}, u32[]{:S(2)}, u32[]{:S(2)}) async-start(bf16[8,128,768]{2,1,0:T(8,128)(2,1)} %get-tuple-element.131), calls=%async_computation | async-start | bytes 3145728 | tf_op jit(solution)/shard_map/all_to_all | solution.py:915
  75.8 19.7 %collective-permute-start.2 = (bf16[24,8,1536]{2,1,0:T(8,128)(2,1)S(1)}, bf16[24,8,1536]{2,1,0:T(8,128)(2,1)S(1)}, u32[]{:S(2)}, u32[]{:S(2)}) collective-permute-start(bf16[24,8,1536]{2,1,0:T(8,128)(2,1)S(1)} %get-tuple-element.118), channel_id=1, source_target_pairs={{0,2},{1,3},{2,0},{3,1},{4,6},{5,7},{6,4},{7,5},{8,10},{9,11},{10,... | collective-permute-start | bytes 1769480 | tf_op jit(solution)/shard_map/ppermute | solution.py:904
  77.3 23.7 %collective-permute-start.3 = (bf16[24,8,1536]{2,1,0:T(8,128)(2,1)S(1)}, bf16[24,8,1536]{2,1,0:T(8,128)(2,1)S(1)}, u32[]{:S(2)}, u32[]{:S(2)}) collective-permute-start(bf16[24,8,1536]{2,1,0:T(8,128)(2,1)S(1)} %get-tuple-element.120), channel_id=1, source_target_pairs={{0,4},{4,0},{8,12},{12,8},{16,20},{20,16},{24,28},{28,24},{1,5},{5... | collective-permute-start | bytes 1769480 | tf_op jit(solution)/shard_map/ppermute | solution.py:904
  85.0 16.0 %copy-start.2 = (bf16[24,8,1536]{2,1,0:T(8,128)(2,1)S(1)}, bf16[24,8,1536]{2,1,0:T(8,128)(2,1)}, u32[]{:S(2)}) copy-start(bf16[24,8,1536]{2,1,0:T(8,128)(2,1)} %get-tuple-element.111.ka) | copy-start | bytes 1769476
  85.0 16.0 %copy-start.3 = (bf16[24,8,1536]{2,1,0:T(8,128)(2,1)S(1)}, bf16[24,8,1536]{2,1,0:T(8,128)(2,1)}, u32[]{:S(2)}) copy-start(bf16[24,8,1536]{2,1,0:T(8,128)(2,1)} %get-tuple-element.119.kb) | copy-start | bytes 1769476
  85.0 16.0 %copy-start.6 = (s32[8]{0:T(128)S(1)}, s32[8]{0:T(128)}, u32[]{:S(2)}) copy-start(s32[8]{0:T(128)} %stack.35.here_s) | copy-start | bytes 100
  95.0 26.3 %collective-permute-start.4 = (bf16[24,8,1536]{2,1,0:T(8,128)(2,1)}, bf16[24,8,1536]{2,1,0:T(8,128)(2,1)}, u32[]{:S(2)}, u32[]{:S(2)}) collective-permute-start(bf16[24,8,1536]{2,1,0:T(8,128)(2,1)} %get-tuple-element.134), channel_id=1, source_target_pairs={{0,2},{1,3},{2,0},{3,1},{4,6},{5,7},{6,4},{7,5},{8,10},{9,11},{10,... | collective-permute-start | bytes 1769480 | tf_op jit(solution)/shard_map/ppermute | solution.py:904
  95.5 25.8 %collective-permute-start.5 = (bf16[24,8,1536]{2,1,0:T(8,128)(2,1)}, bf16[24,8,1536]{2,1,0:T(8,128)(2,1)}, u32[]{:S(2)}, u32[]{:S(2)}) collective-permute-start(bf16[24,8,1536]{2,1,0:T(8,128)(2,1)} %get-tuple-element.136), channel_id=1, source_target_pairs={{0,4},{4,0},{8,12},{12,8},{16,20},{20,16},{24,28},{28,24},{1,5},{5... | collective-permute-start | bytes 1769480 | tf_op jit(solution)/shard_map/ppermute | solution.py:904
  102.6 18.7 %copy-start = (bf16[24,8,1536]{2,1,0:T(8,128)(2,1)S(1)}, bf16[24,8,1536]{2,1,0:T(8,128)(2,1)}, u32[]{:S(2)}) copy-start(bf16[24,8,1536]{2,1,0:T(8,128)(2,1)} %get-tuple-element.133.ka) | copy-start | bytes 1769476
  102.6 18.7 %copy-start.1 = (bf16[24,8,1536]{2,1,0:T(8,128)(2,1)S(1)}, bf16[24,8,1536]{2,1,0:T(8,128)(2,1)}, u32[]{:S(2)}) copy-start(bf16[24,8,1536]{2,1,0:T(8,128)(2,1)} %get-tuple-element.135.kb) | copy-start | bytes 1769476
  102.6 18.7 %copy-start.7 = (s32[8]{0:T(128)S(1)}, s32[8]{0:T(128)}, u32[]{:S(2)}) copy-start(s32[8]{0:T(128)} %stack.35.here_s) | copy-start | bytes 100
  130.4 4.6 %collective-permute-start.6 = (bf16[776,1536]{1,0:T(8,128)(2,1)S(1)}, bf16[776,1536]{1,0:T(8,128)(2,1)S(1)}, u32[]{:S(2)}, u32[]{:S(2)}) collective-permute-start(bf16[776,1536]{1,0:T(8,128)(2,1)S(1)} %proj_give.1), channel_id=1, source_target_pairs={{0,1},{1,0},{2,3},{3,2},{4,5},{5,4},{6,7},{7,6},{8,9},{9,8},{10,11... | collective-permute-start | bytes 7151624 | tf_op jit(solution)/shard_map/ppermute | solution.py:904
  130.5 13.1 %collective-permute-start.7 = (bf16[12,8,1536]{2,1,0:T(8,128)(2,1)S(1)}, bf16[12,8,1536]{2,1,0:T(8,128)(2,1)S(1)}, u32[]{:S(2)}, u32[]{:S(2)}) collective-permute-start(bf16[12,8,1536]{2,1,0:T(8,128)(2,1)S(1)} %get-tuple-element.145), channel_id=1, source_target_pairs={{0,4},{4,0},{8,12},{12,8},{16,20},{20,16},{24,28},{28,24},{1,5},{5... | collective-permute-start | bytes 884744 | tf_op jit(solution)/shard_map/ppermute | solution.py:904
  130.6 13.0 %collective-permute-start.8 = (bf16[12,8,1536]{2,1,0:T(8,128)(2,1)S(1)}, bf16[12,8,1536]{2,1,0:T(8,128)(2,1)S(1)}, u32[]{:S(2)}, u32[]{:S(2)}) collective-permute-start(bf16[12,8,1536]{2,1,0:T(8,128)(2,1)S(1)} %get-tuple-element.147), channel_id=1, source_target_pairs={{0,2},{1,3},{2,0},{3,1},{4,6},{5,7},{6,4},{7,5},{8,10},{9,11},{10,... | collective-permute-start | bytes 884744 | tf_op jit(solution)/shard_map/ppermute | solution.py:904
  131.9 14.3 %collective-permute-start.9 = (bf16[12,8,1536]{2,1,0:T(8,128)(2,1)S(1)}, bf16[12,8,1536]{2,1,0:T(8,128)(2,1)S(1)}, u32[]{:S(2)}, u32[]{:S(2)}) collective-permute-start(bf16[12,8,1536]{2,1,0:T(8,128)(2,1)S(1)} %get-tuple-element.148), channel_id=1, source_target_pairs={{0,4},{4,0},{8,12},{12,8},{16,20},{20,16},{24,28},{28,24},{1,5},{5... | collective-permute-start | bytes 884744 | tf_op jit(solution)/shard_map/ppermute | solution.py:904
  133.9 12.4 %copy-start.4 = (bf16[12,8,1536]{2,1,0:T(8,128)(2,1)S(1)}, bf16[12,8,1536]{2,1,0:T(8,128)(2,1)}, u32[]{:S(2)}) copy-start(bf16[12,8,1536]{2,1,0:T(8,128)(2,1)} %get-tuple-element.121.refs_0_) | copy-start | bytes 884740
  133.9 12.4 %copy-start.5 = (bf16[12,8,1536]{2,1,0:T(8,128)(2,1)S(1)}, bf16[12,8,1536]{2,1,0:T(8,128)(2,1)}, u32[]{:S(2)}) copy-start(bf16[12,8,1536]{2,1,0:T(8,128)(2,1)} %get-tuple-element.146.refs_2_) | copy-start | bytes 884740
  133.9 12.4 %copy-start.8 = (s32[8]{0:T(128)S(1)}, s32[8]{0:T(128)}, u32[]{:S(2)}) copy-start(s32[8]{0:T(128)} %stack.35.here_s) | copy-start | bytes 100
  133.9 12.4 %collective-permute-start.10 = (bf16[12,8,1536]{2,1,0:T(8,128)(2,1)S(1)}, bf16[12,8,1536]{2,1,0:T(8,128)(2,1)S(1)}, u32[]{:S(2)}, u32[]{:S(2)}) collective-permute-start(bf16[12,8,1536]{2,1,0:T(8,128)(2,1)S(1)} %get-tuple-element.150), channel_id=1, source_target_pairs={{0,2},{1,3},{2,0},{3,1},{4,6},{5,7},{6,4},{7,5},{8,10},{9,11},{10,... | collective-permute-start | bytes 884744 | tf_op jit(solution)/shard_map/ppermute | solution.py:904
  147.1 18.5 %collective-permute-start.11 = (bf16[24,8,1536]{2,1,0:T(8,128)(2,1)S(1)}, bf16[24,8,1536]{2,1,0:T(8,128)(2,1)S(1)}, u32[]{:S(2)}, u32[]{:S(2)}) collective-permute-start(bf16[24,8,1536]{2,1,0:T(8,128)(2,1)S(1)} %get-tuple-element.156), channel_id=1, source_target_pairs={{0,8},{4,12},{8,0},{12,4},{16,24},{20,28},{24,16},{28,20},{1,9},{5... | collective-permute-start | bytes 1769480 | tf_op jit(solution)/shard_map/ppermute | solution.py:904
  148.7 24.0 %collective-permute-start.12 = (bf16[25,8,1536]{2,1,0:T(8,128)(2,1)S(1)}, bf16[25,8,1536]{2,1,0:T(8,128)(2,1)S(1)}, u32[]{:S(2)}, u32[]{:S(2)}) collective-permute-start(bf16[25,8,1536]{2,1,0:T(8,128)(2,1)S(1)} %get-tuple-element.159), channel_id=1, source_target_pairs={{0,2},{1,3},{2,0},{3,1},{4,6},{5,7},{6,4},{7,5},{8,10},{9,11},{10,... | collective-permute-start | bytes 1843208 | tf_op jit(solution)/shard_map/ppermute | solution.py:904
  150.2 22.5 %collective-permute-start.13 = (bf16[24,8,1536]{2,1,0:T(8,128)(2,1)S(1)}, bf16[24,8,1536]{2,1,0:T(8,128)(2,1)S(1)}, u32[]{:S(2)}, u32[]{:S(2)}) collective-permute-start(bf16[24,8,1536]{2,1,0:T(8,128)(2,1)S(1)} %get-tuple-element.161), channel_id=1, source_target_pairs={{0,4},{4,0},{8,12},{12,8},{16,20},{20,16},{24,28},{28,24},{1,5},{5... | collective-permute-start | bytes 1769480 | tf_op jit(solution)/shard_map/ppermute | solution.py:904
  159.4 6.2 %copy-start.9 = (s32[8]{0:T(128)S(1)}, s32[8]{0:T(128)}, u32[]{:S(2)}) copy-start(s32[8]{0:T(128)} %stack.35.here_s) | copy-start | bytes 100
  166.3 18.1 %collective-permute-start.16 = (bf16[12,8,1536]{2,1,0:T(8,128)(2,1)S(1)}, bf16[12,8,1536]{2,1,0:T(8,128)(2,1)S(1)}, u32[]{:S(2)}, u32[]{:S(2)}) collective-permute-start(bf16[12,8,1536]{2,1,0:T(8,128)(2,1)S(1)} %get-tuple-element.169), channel_id=1, source_target_pairs={{0,16},{4,20},{8,24},{12,28},{16,0},{20,4},{24,8},{28,12},{1,17},{... | collective-permute-start | bytes 884744 | tf_op jit(solution)/shard_map/ppermute | solution.py:904
  173.5 12.1 %collective-permute-start.14 = (bf16[13,8,1536]{2,1,0:T(8,128)(2,1)S(1)}, bf16[13,8,1536]{2,1,0:T(8,128)(2,1)S(1)}, u32[]{:S(2)}, u32[]{:S(2)}) collective-permute-start(bf16[13,8,1536]{2,1,0:T(8,128)(2,1)S(1)} %get-tuple-element.163), channel_id=1, source_target_pairs={{0,4},{4,0},{8,12},{12,8},{16,20},{20,16},{24,28},{28,24},{1,5},{5... | collective-permute-start | bytes 958472 | tf_op jit(solution)/shard_map/ppermute | solution.py:904
  173.9 11.8 %collective-permute-start.15 = (bf16[12,8,1536]{2,1,0:T(8,128)(2,1)S(1)}, bf16[12,8,1536]{2,1,0:T(8,128)(2,1)S(1)}, u32[]{:S(2)}, u32[]{:S(2)}) collective-permute-start(bf16[12,8,1536]{2,1,0:T(8,128)(2,1)S(1)} %get-tuple-element.165), channel_id=1, source_target_pairs={{0,2},{1,3},{2,0},{3,1},{4,6},{5,7},{6,4},{7,5},{8,10},{9,11},{10,... | collective-permute-start | bytes 884744 | tf_op jit(solution)/shard_map/ppermute | solution.py:904
  185.0 9.0 %collective-permute-start.17 = (bf16[12,8,1536]{2,1,0:T(8,128)(2,1)S(1)}, bf16[12,8,1536]{2,1,0:T(8,128)(2,1)S(1)}, u32[]{:S(2)}, u32[]{:S(2)}) collective-permute-start(bf16[12,8,1536]{2,1,0:T(8,128)(2,1)S(1)} %fold_last.2.me), channel_id=1, source_target_pairs={{0,2},{1,3},{2,0},{3,1},{4,6},{5,7},{6,4},{7,5},{8,10},{9,11},{10,... | collective-permute-start | bytes 884744 | tf_op jit(solution)/shard_map/ppermute | solution.py:904
  186.3 11.7 %collective-permute-start.20 = (bf16[13,8,1536]{2,1,0:T(8,128)(2,1)S(1)}, bf16[13,8,1536]{2,1,0:T(8,128)(2,1)S(1)}, u32[]{:S(2)}, u32[]{:S(2)}) collective-permute-start(bf16[13,8,1536]{2,1,0:T(8,128)(2,1)S(1)} %get-tuple-element.172), channel_id=1, source_target_pairs={{0,8},{4,12},{8,0},{12,4},{16,24},{20,28},{24,16},{28,20},{1,9},{5... | collective-permute-start | bytes 958472 | tf_op jit(solution)/shard_map/ppermute | solution.py:904
  186.4 7.6 %collective-permute-start.18 = (bf16[12,8,1536]{2,1,0:T(8,128)(2,1)S(1)}, bf16[12,8,1536]{2,1,0:T(8,128)(2,1)S(1)}, u32[]{:S(2)}, u32[]{:S(2)}) collective-permute-start(bf16[12,8,1536]{2,1,0:T(8,128)(2,1)S(1)} %fold_last.2.me), channel_id=1, source_target_pairs={{0,1},{1,0},{2,3},{3,2},{4,5},{5,4},{6,7},{7,6},{8,9},{9,8},{10,11... | collective-permute-start | bytes 884744 | tf_op jit(solution)/shard_map/ppermute | solution.py:904
  194.0 1.6 collective-permute-start.19
  198.7 10.0 %collective-permute-start.21 = (bf16[7,8,1536]{2,1,0:T(8,128)(2,1)S(1)}, bf16[7,8,1536]{2,1,0:T(8,128)(2,1)S(1)}, u32[]{:S(2)}, u32[]{:S(2)}) collective-permute-start(bf16[7,8,1536]{2,1,0:T(8,128)(2,1)S(1)} %get-tuple-element.174), channel_id=1, source_target_pairs={{0,16},{4,20},{8,24},{12,28},{16,0},{20,4},{24,8},{28,12},{1,17},{... | collective-permute-start | bytes 516104 | tf_op jit(solution)/shard_map/ppermute | solution.py:904
  209.2 5.9 %collective-permute-start.22 = (bf16[6,8,1536]{2,1,0:T(8,128)(2,1)S(1)}, bf16[6,8,1536]{2,1,0:T(8,128)(2,1)S(1)}, u32[]{:S(2)}, u32[]{:S(2)}) collective-permute-start(bf16[6,8,1536]{2,1,0:T(8,128)(2,1)S(1)} %get-tuple-element.175.me), channel_id=1, source_target_pairs={{0,2},{1,3},{2,0},{3,1},{4,6},{5,7},{6,4},{7,5},{8,10},{9,11},{10,... | collective-permute-start | bytes 442376 | tf_op jit(solution)/shard_map/ppermute | solution.py:904
  209.8 5.3 %collective-permute-start.23 = (bf16[6,8,1536]{2,1,0:T(8,128)(2,1)S(1)}, bf16[6,8,1536]{2,1,0:T(8,128)(2,1)S(1)}, u32[]{:S(2)}, u32[]{:S(2)}) collective-permute-start(bf16[6,8,1536]{2,1,0:T(8,128)(2,1)S(1)} %get-tuple-element.175.me), channel_id=1, source_target_pairs={{0,1},{1,0},{2,3},{3,2},{4,5},{5,4},{6,7},{7,6},{8,9},{9,8},{10,11... | collective-permute-start | bytes 442376 | tf_op jit(solution)/shard_map/ppermute | solution.py:904
  215.1 1.4 collective-permute-start.24

commit v7 on v6

--- a/solution.py
+++ b/solution.py
@@ -745,59 +745,59 @@
     return (left.astype(F32) + right.astype(F32)).astype(BF16)
 
 
-def fold_second(keep_a, got_a, keep_b, got_b, here, pieces, extra, far=False):
-    cols = keep_a.shape[2]
-
-    def kernel(here_s, ka, ga, kb, gb, send_a, left_a, send_b, left_b):
-        x, y = here_s[2], here_s[3]
-        for z in range(4):
-            at = pl.ds(z * pieces, pieces)
-
-            def sum_of(keep, got, other):
-                rows = pl.ds(z * 2 * pieces + other * pieces, pieces)
-                return add(keep[rows], got[rows])
-
-            send_a[at] = sum_of(ka, ga, 1 - y)
-            left_a[at] = sum_of(ka, ga, y)
-            send_b[at] = sum_of(kb, gb, 1 - x)
-            left_b[at] = sum_of(kb, gb, x)
-        if extra:
-            total = add(ka[8 * pieces], ga[8 * pieces])
-            send_a[4 * pieces] = total
-            left_a[4 * pieces] = total
-
-    a_out = shaped((4 * pieces + extra, 8, cols), BF16)
-    b_out = shaped((4 * pieces, 8, cols), BF16)
-    a_left, b_left = a_out, b_out
-    if far:
-        a_left, b_left = pltpu.HBM(a_out.shape, BF16), pltpu.HBM(b_out.shape, BF16)
-    return small_call(
-        kernel, "fold_second", here, (keep_a, got_a, keep_b, got_b), [a_out, a_left, b_out, b_left]
-    )
-
-
-def fold_third(terms, here, pieces, extra):
+def fold_second(terms, here, pieces, extra):
     cols = terms[0][0].shape[2]
     count = len(terms)
+
+    def kernel(here_s, *refs):
+        send_a, left_a, send_b, left_b = refs[4 * count :]
+        x, y = here_s[2], here_s[3]
+        for term in range(count):
+            ka, ga, kb, gb = refs[4 * term : 4 * term + 4]
+            for z in range(4):
+                at = pl.ds((term * 4 + z) * pieces, pieces)
+
+                def sum_of(keep, got, other):
+                    rows = pl.ds(z * 2 * pieces + other * pieces, pieces)
+                    return add(keep[rows], got[rows])
+
+                send_a[at] = sum_of(ka, ga, 1 - y)
+                left_a[at] = sum_of(ka, ga, y)
+                send_b[at] = sum_of(kb, gb, 1 - x)
+                left_b[at] = sum_of(kb, gb, x)
+        if extra:
+            total = add(refs[0][8 * pieces], refs[1][8 * pieces])
+            send_a[4 * count * pieces] = total
+            left_a[4 * count * pieces] = total
+
+    a_out = shaped((4 * count * pieces + extra, 8, cols), BF16)
+    b_out = shaped((4 * count * pieces, 8, cols), BF16)
+    args = [item for term in terms for item in term]
+    return small_call(kernel, "fold_second", here, args, [a_out, a_out, b_out, b_out])
+
+
+def fold_third(pairs, here, pieces, extra):
+    cols = pairs[0].shape[2]
+    count = pairs[2].shape[0] // (4 * pieces)
 
     def kernel(here_s, *refs):
         ins, (send, left) = refs[:-2], refs[-2:]
         low = here_s[4]
         for high in range(2):
-            for number in range(2 * count):
-                keep, got = ins[2 * number : 2 * number + 2]
-                at = pl.ds((high * 2 * count + number) * pieces, pieces)
-                for out, pick in ((send, 1 - low), (left, low)):
-                    rows = pl.ds((high * 2 + pick) * pieces, pieces)
-                    out[at] = add(keep[rows], got[rows])
+            for term in range(count):
+                for ab in range(2):
+                    keep, got = ins[2 * ab : 2 * ab + 2]
+                    at = pl.ds(((high * count + term) * 2 + ab) * pieces, pieces)
+                    for out, pick in ((send, 1 - low), (left, low)):
+                        rows = pl.ds((term * 4 + high * 2 + pick) * pieces, pieces)
+                        out[at] = add(keep[rows], got[rows])
         if extra:
-            total = add(ins[0][4 * pieces], ins[1][4 * pieces])
+            total = add(ins[0][4 * count * pieces], ins[1][4 * count * pieces])
             send[4 * count * pieces] = total
             left[4 * count * pieces] = total
 
     out = shaped((4 * count * pieces + extra, 8, cols), BF16)
-    args = [item for term in terms for item in term]
-    return small_call(kernel, "fold_third", here, args, [out, out])
+    return small_call(kernel, "fold_third", here, pairs, [out, out])
 
 
 def fold_fourth(keep, got, here, extra):
@@ -980,46 +980,45 @@
             *ups, after(here, gh), 0, swap(up_sent, "narrow", 1)
         )
         up_a, up_b = swap(up_dealt[0], "narrow", 2), swap(up_dealt[2], "wide", 1)
-        down_dealt = fold_second(
-            down_dealt[1], down_a, down_dealt[3], down_b, after(here, bup_kept), pieces, 0, True
+        gr, gb, gm, vec_attn = attention_backward(
+            gh, gres, gi_kept, w_up, *heads, after(here, up_dealt[1]), 0, span, 2 * span
         )
-        down_a, down_b = swap(down_dealt[0], "wide", 1), swap(down_dealt[2], "narrow", 2)
-        gr, gb, gm, vec_attn = attention_backward(
-            gh, gres, gi_kept, w_up, *heads, after(here, down_dealt[1]), 0, span, 2 * span
+        feed = fold_second(
+            [
+                (down_dealt[1], down_a, down_dealt[3], down_b),
+                (up_dealt[1], up_a, up_dealt[3], up_b),
+            ],
+            after(here, vec_attn, encoded), pieces, 0,
         )
-        up_dealt = fold_second(
-            up_dealt[1], up_a, up_dealt[3], up_b, after(here, vec_attn, encoded), pieces, 0
-        )
-        up_a, up_b = swap(up_dealt[0], "wide", 1), swap(up_dealt[2], "narrow", 2)
+        feed_a, feed_b = swap(feed[0], "wide", 1), swap(feed[2], "narrow", 2)
         projections = (tokens, gm, attended, gb, (vec_ffn, vec_attn, bup_sent, bup_kept))
-        proj_sent = projection_terms(*projections, after(here, up_dealt[1]), 1)
+        proj_sent = projection_terms(*projections, after(here, feed[1]), 1)
         proj_dealt = projection_terms(
             *projections, after(here, proj_sent), 0, swap(proj_sent, "narrow", 1)
         )
         proj_a, proj_b = swap(proj_dealt[0], "narrow", 2), swap(proj_dealt[2], "wide", 1)
         send, feed = fold_third(
-            [(down_dealt[1], down_a, down_dealt[3], down_b), (up_dealt[1], up_a, up_dealt[3], up_b)],
-            after(here, proj_dealt[1]), pieces, 0,
+            [feed[1], feed_a, feed[3], feed_b], after(here, proj_dealt[1]), pieces, 0
         )
         feed_got = swap(send, "wide", 2)
         grad_tokens = input_gradient(after(gm, feed), w_qkv, gr, 2 * span)
-        encoded = copied(encoded, after(here, grad_tokens), span)
-        send, feed = fold_fourth(feed, feed_got, after(here, encoded), 0)
+        send, feed = fold_fourth(feed, feed_got, after(here, grad_tokens), 0)
         feed_got = swap(send, "wide", 4)
         proj_dealt = fold_second(
-            proj_dealt[1], proj_a, proj_dealt[3], proj_b, after(here, feed), pieces, 1
+            [(proj_dealt[1], proj_a, proj_dealt[3], proj_b)], after(here, feed), pieces, 1
         )
         proj_a, proj_b = swap(proj_dealt[0], "wide", 1), swap(proj_dealt[2], "narrow", 2)
-        (feed,) = fold_last(feed, feed_got, after(here, proj_dealt[1]), 0)
-        feed = quarters(feed)
+        encoded = copied(encoded, after(here, proj_dealt[1]), span)
         send, proj = fold_third(
-            [(proj_dealt[1], proj_a, proj_dealt[3], proj_b)], here, pieces, 1
+            [proj_dealt[1], proj_a, proj_dealt[3], proj_b], after(here, encoded), pieces, 1
         )
         proj_got = swap(send, "wide", 2)
+        (feed,) = fold_last(feed, feed_got, after(here, proj), 0)
+        feed = quarters(feed)
+        send, proj = fold_fourth(proj, proj_got, after(here, feed[0]), 1)
         grad_w_down, grad_w_up = feed_blocks(feed, after(here, proj), pieces, width)
-        send, proj = fold_fourth(proj, proj_got, after(here, grad_w_down), 1)
         proj_got = swap(send, "wide", 4)
-        proj, vectors = fold_last(proj, proj_got, here, 1)
+        proj, vectors = fold_last(proj, proj_got, after(here, grad_w_down), 1)
         proj = quarters(proj)
         grad_w_qkv, grad_w_out, *small = projection_blocks(proj, vectors, here, pieces)
         small = [item.reshape(-1) for item in small]

time: 220 us -> 210 us (0.955)
  waiting for transfers between devices: 44.3 us -> 35.6 us
    ppermute x25 -> x23, waiting for transfers between devices: 44.3 us -> 35.6 us  [swap(): lax.ppermute(item, axis, [(index, index ^ step) for index in range(count)])]
    ppermute x25 -> x23, starting transfers between devices: 20.8 us -> 19.4 us  [swap(): lax.ppermute(item, axis, [(index, index ^ step) for index in range(count)])]
    pallas_call x11 -> x10, Pallas kernels: 12.2 us -> 11.3 us  [small_call(): pl.pallas_call(kernel, in_specs=[pl.BlockSpec(memory_space=pltpu.SMEM)] +...]
  transfers between devices with their start and end apart: 26 -> 24, of which waited for: 9 -> 12; matrix products, arithmetic and copies ran while one was open for 0% -> 0% of each run, Pallas kernels for 37% -> 38%
where the time goes in v7:
time: 210 us
  Pallas kernels  143 us (68%)
  waiting for transfers between devices  35.6 us (17%)
  starting transfers between devices  26.7 us (13%)
  local copies, waits for them, and re-layouts  2.75 us (1%)
    pallas_call x12, Pallas kernels, call(): pl.pallas_call(kernel, grid_spec=pltpu.PrefetchScalarGridSpec(num_scalar_...  131 us
    ppermute x23, waiting for transfers between devices, swap(): lax.ppermute(item, axis, [(index, index ^ step) for index in range(count)])  35.6 us
    ppermute x23, starting transfers between devices, swap(): lax.ppermute(item, axis, [(index, index ^ step) for index in range(count)])  19.4 us
    pallas_call x10, Pallas kernels, small_call(): pl.pallas_call(kernel, in_specs=[pl.BlockSpec(memory_space=pltpu.SMEM)] +...  11.3 us
    all_to_all x1, starting transfers between devices, regroup_rows(): got = lax.all_to_all(sent, 'wide', split_axis=0, concat_axis=0, tiled=True)  7.31 us
  transfers between devices with their start and end apart: 24, of which 12 were waited for; matrix products, arithmetic and copies ran while one was open for 0% of the time, Pallas kernels for 38%

profile of v7, /device:TPU:0, one launch (start us, length us, event | category | flops | bytes accessed | tf_op | source)
XLA Modules:
  0.0 209.6 jit_solution(10195592031732802764)
XLA Ops:
  0.7 0.9 vector_table.1.tab_ref
  1.6 16.5 %attn_fwd.1 = (bf16[1024,2304]{1,0:T(8,128)(2,1)}, bf16[8,6,256,128]{3,2,1,0:T(8,128)(2,1)}, bf16[1024,768]{1,0:T(8,128)(2,1)}, f32[1024,768]{1,0:T(8,128)}, f32...) custom-call(s32[8]{0:T(128)} %slots_s.1, s32[26]{0:T(128)} %lengths_s.1, bf16[1024,768]{1,0:T(8,128)(2,1)} %x_ref.5, ...), custom_call_target="tpu_custom_call" | custom-call | flops 483183808 | bytes 1500000 | tf_op jit(solution)/shard_map/attn_fwd/pallas_call | solution.py:72
  18.1 24.2 %ffn_fwd.1 = (bf16[1024,3072]{1,0:T(8,128)(2,1)}, bf16[1024,3072]{1,0:T(8,128)(2,1)}, bf16[768,1024]{1,0:T(8,128)(2,1)S(1)}, bf16[8,128,768]{2,1,0:T(8,128)(2,1)...) custom-call(s32[8]{0:T(128)} %slots_s.1, s32[1,26]{1,0:T(1,128)} %pairing_s.1, ...), custom_call_target="tpu_custom_call" | custom-call | flops 966367616 | bytes 2000000 | tf_op jit(solution)/shard_map/ffn_fwd/pallas_call | solution.py:72
  42.4 0.6 stack.35.here_s
  43.0 7.7 %down_give.1 = bf16[3072,384]{1,0:T(8,128)(2,1)} custom-call(s32[8]{0:T(128)} %stack.35.here_s, bf16[1024,3072]{1,0:T(8,128)(2,1)} %get-tuple-element.101.act_ref, bf16[1024,768]{1,0:T(8,128)(2,1)S(1)} %get-tuple-element.102.gs_ref), custom_call_target="tpu_custom_call" | custom-call | flops 120795952 | bytes 450000 | tf_op jit(solution)/shard_map/down_give/pallas_call | solution.py:72
  50.7 0.5 collective-permute-start
  51.1 9.3 %up_give.1 = (bf16[768,1536]{1,0:T(8,128)(2,1)}, bf16[1024,1536]{1,0:T(8,128)(2,1)}, f32[1,1536]{1,0:T(1,128)S(1)}) custom-call(s32[8]{0:T(128)} %stack.35.here_s, bf16[1024,768]{1,0:T(8,128)(2,1)S(1)} %get-tuple-element.102.gs_ref, bf16[1024,3072]{1,0:T(8,128)(2,1)} %get-tuple-element.104.dg_ref, bf16[768,1024]{1,0:T(8,128)(2,1)S(1)} %get-tuple-element.105.ht_ref, ...), custom_call_target="tpu_custom_call" | custom-call | flops 241591904 | bytes 800000 | tf_op jit(solution)/shard_map/up_give/pallas_call | solution.py:72
  60.5 0.0 collective-permute-start.1
  60.5 7.3 %all-to-all-start = ((bf16[8,128,768]{2,1,0:T(8,128)(2,1)}), bf16[8,128,768]{2,1,0:T(8,128)(2,1)}, u32[]{:S(2)}, u32[]{:S(2)}) async-start(bf16[8,128,768]{2,1,0:T(8,128)(2,1)} %get-tuple-element.123), calls=%async_computation | async-start | bytes 3145728 | tf_op jit(solution)/shard_map/all_to_all | solution.py:915
  67.8 8.2 %down_own.1 = (bf16[24,8,1536]{2,1,0:T(8,128)(2,1)}, bf16[24,8,1536]{2,1,0:T(8,128)(2,1)}, bf16[24,8,1536]{2,1,0:T(8,128)(2,1)}, bf16[24,8,1536]{2,1,0:T(8,128)(2,1)}) custom-call(s32[8]{0:T(128)} %stack.35.here_s, bf16[1024,3072]{1,0:T(8,128)(2,1)} %get-tuple-element.101.act_ref, bf16[1024,768]{1,0:T(8,128)(2,1)S(1)} %get-tuple-element.102.gs_ref, ...), custom_call_target="tpu_custom_call" | custom-call | flops 120795952 | bytes 550000 | tf_op jit(solution)/shard_map/down_own/pallas_call | solution.py:72
  76.0 5.7 %hidden_grad.1.gh_ref = f32[1024,768]{1,0:T(8,128)S(1)} custom-call(s32[8]{0:T(128)} %stack.35.here_s, bf16[1024,1536]{1,0:T(8,128)(2,1)} %get-tuple-element.110.gi_ref, bf16[768,3072]{1,0:T(8,128)(2,1)} %wu_ref.5), custom_call_target="tpu_custom_call" | custom-call | flops 120795952 | bytes 450000 | tf_op jit(solution)/shard_map/hidden_grad/pallas_call | solution.py:72
  81.7 1.6 collective-permute-start.2
  83.2 2.0 collective-permute-start.3
  85.3 0.0 collective-permute-done.1.refs_0_
  85.3 9.7 %up_own.1 = (bf16[24,8,1536]{2,1,0:T(8,128)(2,1)}, bf16[24,8,1536]{2,1,0:T(8,128)(2,1)}, bf16[24,8,1536]{2,1,0:T(8,128)(2,1)}, bf16[24,8,1536]{2,1,0:T(8,128)(2,...) custom-call(s32[8]{0:T(128)} %stack.35.here_s, bf16[1024,768]{1,0:T(8,128)(2,1)S(1)} %get-tuple-element.102.gs_ref, ...), custom_call_target="tpu_custom_call" | custom-call | flops 241591904 | bytes 800000 | tf_op jit(solution)/shard_map/up_own/pallas_call | solution.py:72
  95.0 0.5 collective-permute-start.4
  95.5 0.0 collective-permute-start.5
  95.5 18.7 %attn_bwd.1 = (f32[1024,768]{1,0:T(8,128)}, bf16[1024,768]{1,0:T(8,128)(2,1)S(1)}, bf16[1024,2304]{1,0:T(8,128)(2,1)}, f32[8,768]{1,0:T(8,128)S(1)}) custom-call(s32[8]{0:T(128)} %stack.35.here_s, f32[1024,768]{1,0:T(8,128)S(1)} %hidden_grad.1.gh_ref, f32[1024,768]{1,0:T(8,128)} %get-tuple-element.115.gres_ref, ...), custom_call_target="tpu_custom_call" | custom-call | flops 483183808 | bytes 2000000 | tf_op jit(solution)/shard_map/attn_bwd/pallas_call | solution.py:72
  114.2 0.0 all-to-all-done
  114.3 0.0 collective-permute-done.4.refs_5_
  114.3 2.7 %collective-permute-done.5.refs_7_ = bf16[24,8,1536]{2,1,0:T(8,128)(2,1)} collective-permute-done((bf16[24,8,1536]{2,1,0:T(8,128)(2,1)}, bf16[24,8,1536]{2,1,0:T(8,128)(2,1)}, u32[]{:S(2)}, u32[]{:S(2)}) %collective-permute-start.5) | collective-permute-done | bytes 589856 | tf_op jit(solution)/shard_map/ppermute | solution.py:904
  117.0 0.0 copy-start.2
  117.0 1.1 copy-done.2
  118.0 1.1 copy-done.3
  119.1 2.1 %fold_second.2 = (bf16[24,8,1536]{2,1,0:T(8,128)(2,1)S(1)}, bf16[24,8,1536]{2,1,0:T(8,128)(2,1)S(1)}, bf16[24,8,1536]{2,1,0:T(8,128)(2,1)S(1)}, bf16[24,8,1536]{2,1,0:T(8,128)(2,1)S(1)}) custom-call(s32[8]{0:T(128)S(1)} %copy-done.4, bf16[24,8,1536]{2,1,0:T(8,128)(2,1)S(1)} %copy-done, bf16[24,8,1536]{2,1,0:T(8,128)(2,1)} %collective-permute-done.2.refs_1_, ...), custom_call_target="tpu_custom_call" | custom-call | flops 50000 | bytes 200000 | tf_op jit(solution)/shard_map/fold_second/pallas_call | solution.py:732
  121.3 7.6 %proj_give.1 = bf16[776,1536]{1,0:T(8,128)(2,1)S(1)} custom-call(s32[8]{0:T(128)} %stack.35.here_s, bf16[1024,768]{1,0:T(8,128)(2,1)} %x_ref.5, bf16[1024,2304]{1,0:T(8,128)(2,1)} %get-tuple-element.144.gm_ref, bf16[1024,768]{1,0:T(8,128)(2,1)} %get-tuple-element.133.att_ref, bf16[1024,768]{1,0:T(8,128)(2,1)S(1)} %get-tuple-element.134.gb_ref, ...), custom_call_target="tpu_custom_call" | custom-call | flops 120795952 | bytes 450000 | tf_op jit(solution)/shard_map/proj_give/pallas_call | solution.py:72
  128.8 0.1 collective-permute-start.6
  128.9 0.1 collective-permute-start.7
  129.0 0.0 copy-start.5
  129.0 1.0 collective-permute-start.8
  130.0 3.5 %collective-permute-done.6.got_ref = bf16[776,1536]{1,0:T(8,128)(2,1)S(1)} collective-permute-done((bf16[776,1536]{1,0:T(8,128)(2,1)S(1)}, bf16[776,1536]{1,0:T(8,128)(2,1)S(1)}, u32[]{:S(2)}, u32[]{:S(2)}) %collective-permute-start.6) | collective-permute-done | bytes 2383904 | tf_op jit(solution)/shard_map/ppermute | solution.py:904
  133.5 8.3 %proj_own.1 = (bf16[25,8,1536]{2,1,0:T(8,128)(2,1)S(1)}, bf16[25,8,1536]{2,1,0:T(8,128)(2,1)S(1)}, bf16[24,8,1536]{2,1,0:T(8,128)(2,1)S(1)}, bf16[24,8,1536]{2,1,0:T(8,128)(2,1)S(1)}) custom-call(s32[8]{0:T(128)} %stack.35.here_s, bf16[1024,768]{1,0:T(8,128)(2,1)} %x_ref.5, bf16[1024,2304]{1,0:T(8,128)(2,1)} %get-tuple-element.144.gm_ref, ...), custom_call_target="tpu_custom_call" | custom-call | flops 120795952 | bytes 550000 | tf_op jit(solution)/shard_map/proj_own/pallas_call | solution.py:72
  141.8 1.0 collective-permute-start.10
  142.8 1.9 collective-permute-done.7.refs_1_
  144.7 0.1 collective-permute-done.8.refs_3_
  144.8 0.8 fold_third.2
  145.6 4.1 %collective-permute-start.9 = (bf16[24,8,1536]{2,1,0:T(8,128)(2,1)S(1)}, bf16[24,8,1536]{2,1,0:T(8,128)(2,1)S(1)}, u32[]{:S(2)}, u32[]{:S(2)}) collective-permute-start(bf16[24,8,1536]{2,1,0:T(8,128)(2,1)S(1)} %get-tuple-element.147), channel_id=1, source_target_pairs={{0,8},{4,12},{8,0},{12,4},{16,24},{20,28},{24,16},{28,20},{1,9},{5... | collective-permute-start | bytes 1769480 | tf_op jit(solution)/shard_map/ppermute | solution.py:904
  149.7 2.5 %collective-permute-start.11 = (bf16[24,8,1536]{2,1,0:T(8,128)(2,1)S(1)}, bf16[24,8,1536]{2,1,0:T(8,128)(2,1)S(1)}, u32[]{:S(2)}, u32[]{:S(2)}) collective-permute-start(bf16[24,8,1536]{2,1,0:T(8,128)(2,1)S(1)} %get-tuple-element.152), channel_id=1, source_target_pairs={{0,4},{4,0},{8,12},{12,8},{16,20},{20,16},{24,28},{28,24},{1,5},{5... | collective-permute-start | bytes 1769480 | tf_op jit(solution)/shard_map/ppermute | solution.py:904
  152.2 8.9 %input_grad.1 = bf16[1024,768]{1,0:T(8,128)(2,1)} custom-call(bf16[1024,2304]{1,0:T(8,128)(2,1)} %get-tuple-element.144.gm_ref, bf16[768,2304]{1,0:T(8,128)(2,1)} %wq_ref.3, f32[1024,768]{1,0:T(8,128)} %get-tuple-element.145.gr_ref), custom_call_target="tpu_custom_call" | custom-call | flops 181193936 | bytes 650000 | tf_op jit(solution)/shard_map/input_grad/pallas_call | solution.py:72
  161.0 1.6 collective-permute-done.9.got_ref
  162.7 0.7 fold_fourth.2
  163.4 0.8 collective-permute-done.11.refs_3_
  164.2 0.8 fold_second.3
  165.0 1.5 collective-permute-start.12
  166.5 0.5 collective-permute-start.13
  167.0 0.9 collective-permute-start.14
  167.9 6.1 %copied.1 = bf16[1024,768]{1,0:T(8,128)(2,1)} custom-call(s32[8]{0:T(128)} %stack.35.here_s, bf16[1024,768]{1,0:T(8,128)(2,1)} %bitcast.8.in_ref), custom_call_target="tpu_custom_call" | custom-call | bytes 150000 | tf_op jit(solution)/shard_map/copied/pallas_call | solution.py:72
  174.0 0.0 collective-permute-done.13.refs_3_
  174.0 0.7 fold_third.3
  174.7 5.2 %collective-permute-done.14.got_ref = bf16[12,8,1536]{2,1,0:T(8,128)(2,1)S(1)} collective-permute-done((bf16[12,8,1536]{2,1,0:T(8,128)(2,1)S(1)}, bf16[12,8,1536]{2,1,0:T(8,128)(2,1)S(1)}, u32[]{:S(2)}, u32[]{:S(2)}) %collective-permute-start.14) | collective-permute-done | bytes 294944 | tf_op jit(solution)/shard_map/ppermute | solution.py:904
  179.9 0.6 fold_last.2.me
  180.6 1.6 collective-permute-start.16
  182.1 6.5 %collective-permute-done.16.gx = bf16[12,8,1536]{2,1,0:T(8,128)(2,1)S(1)} collective-permute-done((bf16[12,8,1536]{2,1,0:T(8,128)(2,1)S(1)}, bf16[12,8,1536]{2,1,0:T(8,128)(2,1)S(1)}, u32[]{:S(2)}, u32[]{:S(2)}) %collective-permute-start.16) | collective-permute-done | bytes 294944 | tf_op jit(solution)/shard_map/ppermute | solution.py:904
  188.6 1.7 collective-permute-done.15.got_ref
  190.4 0.6 fold_fourth.3
  191.0 0.3 collective-permute-start.19
  191.3 2.4 %feed_blocks.1 = (f32[384,768]{1,0:T(8,128)}, f32[96,3072]{1,0:T(8,128)}) custom-call(s32[8]{0:T(128)S(1)} %copy-done.6, bf16[12,8,1536]{2,1,0:T(8,128)(2,1)S(1)} %fold_last.2.me, bf16[12,8,1536]{2,1,0:T(8,128)(2,1)S(1)} %collective-permute-done.16.gx, bf16[12,8,1536]{2,1,0:T(8,128)(2,1)S(1)} %collective-permute-done.17.gc, ...), custom_call_target="tpu_custom_call" | custom-call | flops 50000 | bytes 200000 | tf_op jit(solution)/shard_map/feed_blocks/pallas_call | solution.py:732
  193.7 6.2 %collective-permute-done.19.got_ref = bf16[7,8,1536]{2,1,0:T(8,128)(2,1)S(1)} collective-permute-done((bf16[7,8,1536]{2,1,0:T(8,128)(2,1)S(1)}, bf16[7,8,1536]{2,1,0:T(8,128)(2,1)S(1)}, u32[]{:S(2)}, u32[]{:S(2)}) %collective-permute-start.19) | collective-permute-done | bytes 172064 | tf_op jit(solution)/shard_map/ppermute | solution.py:904
  199.9 0.6 fold_last.3
  200.5 1.2 collective-permute-start.20
  201.6 4.0 %collective-permute-done.20.gx = bf16[6,8,1536]{2,1,0:T(8,128)(2,1)S(1)} collective-permute-done((bf16[6,8,1536]{2,1,0:T(8,128)(2,1)S(1)}, bf16[6,8,1536]{2,1,0:T(8,128)(2,1)S(1)}, u32[]{:S(2)}, u32[]{:S(2)}) %collective-permute-start.20) | collective-permute-done | bytes 147488 | tf_op jit(solution)/shard_map/ppermute | solution.py:904
  205.7 1.4 collective-permute-done.22.gd
  207.1 1.9 projection_blocks.1
  209.0 0.6 reduce
  (23 shorter events, 0.1 us)
Async XLA Ops:
  50.7 17.2 %collective-permute-start = (bf16[3072,384]{1,0:T(8,128)(2,1)}, bf16[3072,384]{1,0:T(8,128)(2,1)}, u32[]{:S(2)}, u32[]{:S(2)}) collective-permute-start(bf16[3072,384]{1,0:T(8,128)(2,1)} %down_give.1), channel_id=1, source_target_pairs={{0,1},{1,0},{2,3},{3,2},{4,5},{5,4},{6,7},{7,6},{8,9},{9,8},{10,11... | collective-permute-start | bytes 7077896 | tf_op jit(solution)/shard_map/ppermute | solution.py:904
  60.5 24.8 %collective-permute-start.1 = (bf16[768,1536]{1,0:T(8,128)(2,1)}, bf16[768,1536]{1,0:T(8,128)(2,1)}, u32[]{:S(2)}, u32[]{:S(2)}) collective-permute-start(bf16[768,1536]{1,0:T(8,128)(2,1)} %get-tuple-element.112), channel_id=1, source_target_pairs={{0,1},{1,0},{2,3},{3,2},{4,5},{5,4},{6,7},{7,6},{8,9},{9,8},{10,11... | collective-permute-start | bytes 7077896 | tf_op jit(solution)/shard_map/ppermute | solution.py:904
  60.5 53.7 %all-to-all-start = ((bf16[8,128,768]{2,1,0:T(8,128)(2,1)}), bf16[8,128,768]{2,1,0:T(8,128)(2,1)}, u32[]{:S(2)}, u32[]{:S(2)}) async-start(bf16[8,128,768]{2,1,0:T(8,128)(2,1)} %get-tuple-element.123), calls=%async_computation | async-start | bytes 3145728 | tf_op jit(solution)/shard_map/all_to_all | solution.py:915
  81.7 32.6 %collective-permute-start.2 = (bf16[24,8,1536]{2,1,0:T(8,128)(2,1)}, bf16[24,8,1536]{2,1,0:T(8,128)(2,1)}, u32[]{:S(2)}, u32[]{:S(2)}) collective-permute-start(bf16[24,8,1536]{2,1,0:T(8,128)(2,1)} %get-tuple-element.125), channel_id=1, source_target_pairs={{0,2},{1,3},{2,0},{3,1},{4,6},{5,7},{6,4},{7,5},{8,10},{9,11},{10,... | collective-permute-start | bytes 1769480 | tf_op jit(solution)/shard_map/ppermute | solution.py:904
  83.2 31.0 %collective-permute-start.3 = (bf16[24,8,1536]{2,1,0:T(8,128)(2,1)}, bf16[24,8,1536]{2,1,0:T(8,128)(2,1)}, u32[]{:S(2)}, u32[]{:S(2)}) collective-permute-start(bf16[24,8,1536]{2,1,0:T(8,128)(2,1)} %get-tuple-element.127), channel_id=1, source_target_pairs={{0,4},{4,0},{8,12},{12,8},{16,20},{20,16},{24,28},{28,24},{1,5},{5... | collective-permute-start | bytes 1769480 | tf_op jit(solution)/shard_map/ppermute | solution.py:904
  95.0 19.2 %collective-permute-start.4 = (bf16[24,8,1536]{2,1,0:T(8,128)(2,1)}, bf16[24,8,1536]{2,1,0:T(8,128)(2,1)}, u32[]{:S(2)}, u32[]{:S(2)}) collective-permute-start(bf16[24,8,1536]{2,1,0:T(8,128)(2,1)} %get-tuple-element.128), channel_id=1, source_target_pairs={{0,2},{1,3},{2,0},{3,1},{4,6},{5,7},{6,4},{7,5},{8,10},{9,11},{10,... | collective-permute-start | bytes 1769480 | tf_op jit(solution)/shard_map/ppermute | solution.py:904
  95.5 21.4 %collective-permute-start.5 = (bf16[24,8,1536]{2,1,0:T(8,128)(2,1)}, bf16[24,8,1536]{2,1,0:T(8,128)(2,1)}, u32[]{:S(2)}, u32[]{:S(2)}) collective-permute-start(bf16[24,8,1536]{2,1,0:T(8,128)(2,1)} %get-tuple-element.130), channel_id=1, source_target_pairs={{0,4},{4,0},{8,12},{12,8},{16,20},{20,16},{24,28},{28,24},{1,5},{5... | collective-permute-start | bytes 1769480 | tf_op jit(solution)/shard_map/ppermute | solution.py:904
  95.5 21.4 %copy-start = (bf16[24,8,1536]{2,1,0:T(8,128)(2,1)S(1)}, bf16[24,8,1536]{2,1,0:T(8,128)(2,1)}, u32[]{:S(2)}) copy-start(bf16[24,8,1536]{2,1,0:T(8,128)(2,1)} %get-tuple-element.108.refs_0_) | copy-start | bytes 1769476
  95.5 21.4 %copy-start.1 = (bf16[24,8,1536]{2,1,0:T(8,128)(2,1)S(1)}, bf16[24,8,1536]{2,1,0:T(8,128)(2,1)}, u32[]{:S(2)}) copy-start(bf16[24,8,1536]{2,1,0:T(8,128)(2,1)} %get-tuple-element.126.refs_2_) | copy-start | bytes 1769476
  95.5 21.4 %copy-start.4 = (s32[8]{0:T(128)S(1)}, s32[8]{0:T(128)}, u32[]{:S(2)}) copy-start(s32[8]{0:T(128)} %stack.35.here_s) | copy-start | bytes 100
  117.0 1.1 copy-start.2
  118.0 1.1 copy-start.3
  128.8 4.6 %collective-permute-start.6 = (bf16[776,1536]{1,0:T(8,128)(2,1)S(1)}, bf16[776,1536]{1,0:T(8,128)(2,1)S(1)}, u32[]{:S(2)}, u32[]{:S(2)}) collective-permute-start(bf16[776,1536]{1,0:T(8,128)(2,1)S(1)} %proj_give.1), channel_id=1, source_target_pairs={{0,1},{1,0},{2,3},{3,2},{4,5},{5,4},{6,7},{7,6},{8,9},{9,8},{10,11... | collective-permute-start | bytes 7151624 | tf_op jit(solution)/shard_map/ppermute | solution.py:904
  128.9 15.7 %collective-permute-start.7 = (bf16[24,8,1536]{2,1,0:T(8,128)(2,1)S(1)}, bf16[24,8,1536]{2,1,0:T(8,128)(2,1)S(1)}, u32[]{:S(2)}, u32[]{:S(2)}) collective-permute-start(bf16[24,8,1536]{2,1,0:T(8,128)(2,1)S(1)} %get-tuple-element.140), channel_id=1, source_target_pairs={{0,4},{4,0},{8,12},{12,8},{16,20},{20,16},{24,28},{28,24},{1,5},{5... | collective-permute-start | bytes 1769480 | tf_op jit(solution)/shard_map/ppermute | solution.py:904
  129.0 15.8 %copy-start.5 = (s32[8]{0:T(128)S(1)}, s32[8]{0:T(128)}, u32[]{:S(2)}) copy-start(s32[8]{0:T(128)} %stack.35.here_s) | copy-start | bytes 100
  129.0 15.7 %collective-permute-start.8 = (bf16[24,8,1536]{2,1,0:T(8,128)(2,1)S(1)}, bf16[24,8,1536]{2,1,0:T(8,128)(2,1)S(1)}, u32[]{:S(2)}, u32[]{:S(2)}) collective-permute-start(bf16[24,8,1536]{2,1,0:T(8,128)(2,1)S(1)} %get-tuple-element.142), channel_id=1, source_target_pairs={{0,2},{1,3},{2,0},{3,1},{4,6},{5,7},{6,4},{7,5},{8,10},{9,11},{10,... | collective-permute-start | bytes 1769480 | tf_op jit(solution)/shard_map/ppermute | solution.py:904
  141.8 22.4 %collective-permute-start.10 = (bf16[25,8,1536]{2,1,0:T(8,128)(2,1)S(1)}, bf16[25,8,1536]{2,1,0:T(8,128)(2,1)S(1)}, u32[]{:S(2)}, u32[]{:S(2)}) collective-permute-start(bf16[25,8,1536]{2,1,0:T(8,128)(2,1)S(1)} %get-tuple-element.150), channel_id=1, source_target_pairs={{0,2},{1,3},{2,0},{3,1},{4,6},{5,7},{6,4},{7,5},{8,10},{9,11},{10,... | collective-permute-start | bytes 1843208 | tf_op jit(solution)/shard_map/ppermute | solution.py:904
  145.6 17.1 %collective-permute-start.9 = (bf16[24,8,1536]{2,1,0:T(8,128)(2,1)S(1)}, bf16[24,8,1536]{2,1,0:T(8,128)(2,1)S(1)}, u32[]{:S(2)}, u32[]{:S(2)}) collective-permute-start(bf16[24,8,1536]{2,1,0:T(8,128)(2,1)S(1)} %get-tuple-element.147), channel_id=1, source_target_pairs={{0,8},{4,12},{8,0},{12,4},{16,24},{20,28},{24,16},{28,20},{1,9},{5... | collective-permute-start | bytes 1769480 | tf_op jit(solution)/shard_map/ppermute | solution.py:904
  149.7 14.4 %collective-permute-start.11 = (bf16[24,8,1536]{2,1,0:T(8,128)(2,1)S(1)}, bf16[24,8,1536]{2,1,0:T(8,128)(2,1)S(1)}, u32[]{:S(2)}, u32[]{:S(2)}) collective-permute-start(bf16[24,8,1536]{2,1,0:T(8,128)(2,1)S(1)} %get-tuple-element.152), channel_id=1, source_target_pairs={{0,4},{4,0},{8,12},{12,8},{16,20},{20,16},{24,28},{28,24},{1,5},{5... | collective-permute-start | bytes 1769480 | tf_op jit(solution)/shard_map/ppermute | solution.py:904
  164.2 9.9 %copy-start.6 = (s32[8]{0:T(128)S(1)}, s32[8]{0:T(128)}, u32[]{:S(2)}) copy-start(s32[8]{0:T(128)} %stack.35.here_s) | copy-start | bytes 100
  165.0 9.0 %collective-permute-start.12 = (bf16[13,8,1536]{2,1,0:T(8,128)(2,1)S(1)}, bf16[13,8,1536]{2,1,0:T(8,128)(2,1)S(1)}, u32[]{:S(2)}, u32[]{:S(2)}) collective-permute-start(bf16[13,8,1536]{2,1,0:T(8,128)(2,1)S(1)} %get-tuple-element.156), channel_id=1, source_target_pairs={{0,4},{4,0},{8,12},{12,8},{16,20},{20,16},{24,28},{28,24},{1,5},{5... | collective-permute-start | bytes 958472 | tf_op jit(solution)/shard_map/ppermute | solution.py:904
  166.5 7.5 %collective-permute-start.13 = (bf16[12,8,1536]{2,1,0:T(8,128)(2,1)S(1)}, bf16[12,8,1536]{2,1,0:T(8,128)(2,1)S(1)}, u32[]{:S(2)}, u32[]{:S(2)}) collective-permute-start(bf16[12,8,1536]{2,1,0:T(8,128)(2,1)S(1)} %get-tuple-element.158), channel_id=1, source_target_pairs={{0,2},{1,3},{2,0},{3,1},{4,6},{5,7},{6,4},{7,5},{8,10},{9,11},{10,... | collective-permute-start | bytes 884744 | tf_op jit(solution)/shard_map/ppermute | solution.py:904
  167.0 12.9 %collective-permute-start.14 = (bf16[12,8,1536]{2,1,0:T(8,128)(2,1)S(1)}, bf16[12,8,1536]{2,1,0:T(8,128)(2,1)S(1)}, u32[]{:S(2)}, u32[]{:S(2)}) collective-permute-start(bf16[12,8,1536]{2,1,0:T(8,128)(2,1)S(1)} %get-tuple-element.161), channel_id=1, source_target_pairs={{0,16},{4,20},{8,24},{12,28},{16,0},{20,4},{24,8},{28,12},{1,17},{... | collective-permute-start | bytes 884744 | tf_op jit(solution)/shard_map/ppermute | solution.py:904
  180.6 8.1 %collective-permute-start.16 = (bf16[12,8,1536]{2,1,0:T(8,128)(2,1)S(1)}, bf16[12,8,1536]{2,1,0:T(8,128)(2,1)S(1)}, u32[]{:S(2)}, u32[]{:S(2)}) collective-permute-start(bf16[12,8,1536]{2,1,0:T(8,128)(2,1)S(1)} %fold_last.2.me), channel_id=1, source_target_pairs={{0,2},{1,3},{2,0},{3,1},{4,6},{5,7},{6,4},{7,5},{8,10},{9,11},{10,... | collective-permute-start | bytes 884744 | tf_op jit(solution)/shard_map/ppermute | solution.py:904
  182.1 8.2 %collective-permute-start.15 = (bf16[13,8,1536]{2,1,0:T(8,128)(2,1)S(1)}, bf16[13,8,1536]{2,1,0:T(8,128)(2,1)S(1)}, u32[]{:S(2)}, u32[]{:S(2)}) collective-permute-start(bf16[13,8,1536]{2,1,0:T(8,128)(2,1)S(1)} %get-tuple-element.163), channel_id=1, source_target_pairs={{0,8},{4,12},{8,0},{12,4},{16,24},{20,28},{24,16},{28,20},{1,9},{5... | collective-permute-start | bytes 958472 | tf_op jit(solution)/shard_map/ppermute | solution.py:904
  182.1 9.2 %collective-permute-start.17 = (bf16[12,8,1536]{2,1,0:T(8,128)(2,1)S(1)}, bf16[12,8,1536]{2,1,0:T(8,128)(2,1)S(1)}, u32[]{:S(2)}, u32[]{:S(2)}) collective-permute-start(bf16[12,8,1536]{2,1,0:T(8,128)(2,1)S(1)} %fold_last.2.me), channel_id=1, source_target_pairs={{0,1},{1,0},{2,3},{3,2},{4,5},{5,4},{6,7},{7,6},{8,9},{9,8},{10,11... | collective-permute-start | bytes 884744 | tf_op jit(solution)/shard_map/ppermute | solution.py:904
  188.6 2.7 %collective-permute-start.18 = (bf16[12,8,1536]{2,1,0:T(8,128)(2,1)S(1)}, bf16[12,8,1536]{2,1,0:T(8,128)(2,1)S(1)}, u32[]{:S(2)}, u32[]{:S(2)}) collective-permute-start(bf16[12,8,1536]{2,1,0:T(8,128)(2,1)S(1)} %collective-permute-done.16.gx), channel_id=1, source_target_pairs={{0,1},{1,0},{2,3},{3,2},{4,5},{5,4},{6,7},{7,6},{8,9},{9,8},{10,11... | collective-permute-start | bytes 884744 | tf_op jit(solution)/shard_map/ppermute | solution.py:904
  191.0 8.9 %collective-permute-start.19 = (bf16[7,8,1536]{2,1,0:T(8,128)(2,1)S(1)}, bf16[7,8,1536]{2,1,0:T(8,128)(2,1)S(1)}, u32[]{:S(2)}, u32[]{:S(2)}) collective-permute-start(bf16[7,8,1536]{2,1,0:T(8,128)(2,1)S(1)} %get-tuple-element.168), channel_id=1, source_target_pairs={{0,16},{4,20},{8,24},{12,28},{16,0},{20,4},{24,8},{28,12},{1,17},{... | collective-permute-start | bytes 516104 | tf_op jit(solution)/shard_map/ppermute | solution.py:904
  200.5 5.2 %collective-permute-start.20 = (bf16[6,8,1536]{2,1,0:T(8,128)(2,1)S(1)}, bf16[6,8,1536]{2,1,0:T(8,128)(2,1)S(1)}, u32[]{:S(2)}, u32[]{:S(2)}) collective-permute-start(bf16[6,8,1536]{2,1,0:T(8,128)(2,1)S(1)} %get-tuple-element.169.me), channel_id=1, source_target_pairs={{0,2},{1,3},{2,0},{3,1},{4,6},{5,7},{6,4},{7,5},{8,10},{9,11},{10,... | collective-permute-start | bytes 442376 | tf_op jit(solution)/shard_map/ppermute | solution.py:904
  201.6 4.0 %collective-permute-start.21 = (bf16[6,8,1536]{2,1,0:T(8,128)(2,1)S(1)}, bf16[6,8,1536]{2,1,0:T(8,128)(2,1)S(1)}, u32[]{:S(2)}, u32[]{:S(2)}) collective-permute-start(bf16[6,8,1536]{2,1,0:T(8,128)(2,1)S(1)} %get-tuple-element.169.me), channel_id=1, source_target_pairs={{0,1},{1,0},{2,3},{3,2},{4,5},{5,4},{6,7},{7,6},{8,9},{9,8},{10,11... | collective-permute-start | bytes 442376 | tf_op jit(solution)/shard_map/ppermute | solution.py:904
  205.7 1.4 collective-permute-start.22

commit v8 on v7

--- a/solution.py
+++ b/solution.py
@@ -1014,13 +1014,13 @@
         )
         proj_got = swap(send, "wide", 2)
         (feed,) = fold_last(feed, feed_got, after(here, proj), 0)
-        feed = quarters(feed)
-        send, proj = fold_fourth(proj, proj_got, after(here, feed[0]), 1)
-        grad_w_down, grad_w_up = feed_blocks(feed, after(here, proj), pieces, width)
+        send, proj = fold_fourth(proj, proj_got, after(here, feed), 1)
         proj_got = swap(send, "wide", 4)
-        proj, vectors = fold_last(proj, proj_got, after(here, grad_w_down), 1)
+        feed = quarters(after(feed, proj))
+        proj, vectors = fold_last(proj, proj_got, here, 1)
         proj = quarters(proj)
-        grad_w_qkv, grad_w_out, *small = projection_blocks(proj, vectors, here, pieces)
+        grad_w_down, grad_w_up = feed_blocks(feed, after(here, proj[0]), pieces, width)
+        grad_w_qkv, grad_w_out, *small = projection_blocks(proj, vectors, after(here, grad_w_down), pieces)
         small = [item.reshape(-1) for item in small]
     else:
         encoded = regroup_rows(sent, bucket, wide_count, batches)

time: 210 us -> 210 us (level)
  transfers between devices with their start and end apart: 24 -> 24, of which waited for: 12 -> 11; matrix products, arithmetic and copies ran while one was open for 0% -> 0% of each run, Pallas kernels for 38% -> 38%
where the time goes in v8:
time: 210 us; the launch traced here: 209 us
  Pallas kernels  143 us (68%)
  waiting for transfers between devices  34.7 us (17%)
  starting transfers between devices  26.9 us (13%)
  local copies, waits for them, and re-layouts  2.75 us (1%)
    pallas_call x12, Pallas kernels, call(): pl.pallas_call(kernel, grid_spec=pltpu.PrefetchScalarGridSpec(num_scalar_...  131 us
    ppermute x23, waiting for transfers between devices, swap(): lax.ppermute(item, axis, [(index, index ^ step) for index in range(count)])  34.7 us
    ppermute x23, starting transfers between devices, swap(): lax.ppermute(item, axis, [(index, index ^ step) for index in range(count)])  19.6 us
    pallas_call x10, Pallas kernels, small_call(): pl.pallas_call(kernel, in_specs=[pl.BlockSpec(memory_space=pltpu.SMEM)] +...  11.3 us
    all_to_all x1, starting transfers between devices, regroup_rows(): got = lax.all_to_all(sent, 'wide', split_axis=0, concat_axis=0, tiled=True)  7.31 us
  transfers between devices with their start and end apart: 24, of which 11 were waited for; matrix products, arithmetic and copies ran while one was open for 0% of the time, Pallas kernels for 38%

profile of v8, /device:TPU:0, one launch (start us, length us, event | category | flops | bytes accessed | tf_op | source)
XLA Modules:
  0.0 208.9 jit_solution(3912858773801235073)
XLA Ops:
  0.7 0.9 vector_table.1.tab_ref
  1.6 16.5 %attn_fwd.1 = (bf16[1024,2304]{1,0:T(8,128)(2,1)}, bf16[8,6,256,128]{3,2,1,0:T(8,128)(2,1)}, bf16[1024,768]{1,0:T(8,128)(2,1)}, f32[1024,768]{1,0:T(8,128)}, f32...) custom-call(s32[8]{0:T(128)} %slots_s.1, s32[26]{0:T(128)} %lengths_s.1, bf16[1024,768]{1,0:T(8,128)(2,1)} %x_ref.5, ...), custom_call_target="tpu_custom_call" | custom-call | flops 483183808 | bytes 1500000 | tf_op jit(solution)/shard_map/attn_fwd/pallas_call | solution.py:72
  18.1 24.2 %ffn_fwd.1 = (bf16[1024,3072]{1,0:T(8,128)(2,1)}, bf16[1024,3072]{1,0:T(8,128)(2,1)}, bf16[768,1024]{1,0:T(8,128)(2,1)S(1)}, bf16[8,128,768]{2,1,0:T(8,128)(2,1)...) custom-call(s32[8]{0:T(128)} %slots_s.1, s32[1,26]{1,0:T(1,128)} %pairing_s.1, ...), custom_call_target="tpu_custom_call" | custom-call | flops 966367616 | bytes 2000000 | tf_op jit(solution)/shard_map/ffn_fwd/pallas_call | solution.py:72
  42.4 0.6 stack.35.here_s
  43.0 7.7 %down_give.1 = bf16[3072,384]{1,0:T(8,128)(2,1)} custom-call(s32[8]{0:T(128)} %stack.35.here_s, bf16[1024,3072]{1,0:T(8,128)(2,1)} %get-tuple-element.102.act_ref, bf16[1024,768]{1,0:T(8,128)(2,1)S(1)} %get-tuple-element.103.gs_ref), custom_call_target="tpu_custom_call" | custom-call | flops 120795952 | bytes 450000 | tf_op jit(solution)/shard_map/down_give/pallas_call | solution.py:72
  50.7 0.5 collective-permute-start
  51.1 9.3 %up_give.1 = (bf16[768,1536]{1,0:T(8,128)(2,1)}, bf16[1024,1536]{1,0:T(8,128)(2,1)}, f32[1,1536]{1,0:T(1,128)S(1)}) custom-call(s32[8]{0:T(128)} %stack.35.here_s, bf16[1024,768]{1,0:T(8,128)(2,1)S(1)} %get-tuple-element.103.gs_ref, bf16[1024,3072]{1,0:T(8,128)(2,1)} %get-tuple-element.105.dg_ref, bf16[768,1024]{1,0:T(8,128)(2,1)S(1)} %get-tuple-element.106.ht_ref, ...), custom_call_target="tpu_custom_call" | custom-call | flops 241591904 | bytes 800000 | tf_op jit(solution)/shard_map/up_give/pallas_call | solution.py:72
  60.5 0.0 collective-permute-start.1
  60.5 7.3 %all-to-all-start = ((bf16[8,128,768]{2,1,0:T(8,128)(2,1)}), bf16[8,128,768]{2,1,0:T(8,128)(2,1)}, u32[]{:S(2)}, u32[]{:S(2)}) async-start(bf16[8,128,768]{2,1,0:T(8,128)(2,1)} %get-tuple-element.124), calls=%async_computation | async-start | bytes 3145728 | tf_op jit(solution)/shard_map/all_to_all | solution.py:915
  67.8 0.0 collective-permute-done.got_ref
  67.8 8.2 %down_own.1 = (bf16[24,8,1536]{2,1,0:T(8,128)(2,1)}, bf16[24,8,1536]{2,1,0:T(8,128)(2,1)}, bf16[24,8,1536]{2,1,0:T(8,128)(2,1)}, bf16[24,8,1536]{2,1,0:T(8,128)(2,1)}) custom-call(s32[8]{0:T(128)} %stack.35.here_s, bf16[1024,3072]{1,0:T(8,128)(2,1)} %get-tuple-element.102.act_ref, bf16[1024,768]{1,0:T(8,128)(2,1)S(1)} %get-tuple-element.103.gs_ref, ...), custom_call_target="tpu_custom_call" | custom-call | flops 120795952 | bytes 550000 | tf_op jit(solution)/shard_map/down_own/pallas_call | solution.py:72
  76.0 5.7 %hidden_grad.1.gh_ref = f32[1024,768]{1,0:T(8,128)S(1)} custom-call(s32[8]{0:T(128)} %stack.35.here_s, bf16[1024,1536]{1,0:T(8,128)(2,1)} %get-tuple-element.111.gi_ref, bf16[768,3072]{1,0:T(8,128)(2,1)} %wu_ref.5), custom_call_target="tpu_custom_call" | custom-call | flops 120795952 | bytes 450000 | tf_op jit(solution)/shard_map/hidden_grad/pallas_call | solution.py:72
  81.7 1.6 collective-permute-start.2
  83.2 2.0 collective-permute-start.3
  85.3 0.0 collective-permute-done.1.refs_0_
  85.3 9.7 %up_own.1 = (bf16[24,8,1536]{2,1,0:T(8,128)(2,1)}, bf16[24,8,1536]{2,1,0:T(8,128)(2,1)}, bf16[24,8,1536]{2,1,0:T(8,128)(2,1)}, bf16[24,8,1536]{2,1,0:T(8,128)(2,...) custom-call(s32[8]{0:T(128)} %stack.35.here_s, bf16[1024,768]{1,0:T(8,128)(2,1)S(1)} %get-tuple-element.103.gs_ref, ...), custom_call_target="tpu_custom_call" | custom-call | flops 241591904 | bytes 800000 | tf_op jit(solution)/shard_map/up_own/pallas_call | solution.py:72
  95.0 0.5 collective-permute-start.4
  95.5 0.0 collective-permute-start.5
  95.5 18.7 %attn_bwd.1 = (f32[1024,768]{1,0:T(8,128)}, bf16[1024,768]{1,0:T(8,128)(2,1)S(1)}, bf16[1024,2304]{1,0:T(8,128)(2,1)}, f32[8,768]{1,0:T(8,128)S(1)}) custom-call(s32[8]{0:T(128)} %stack.35.here_s, f32[1024,768]{1,0:T(8,128)S(1)} %hidden_grad.1.gh_ref, f32[1024,768]{1,0:T(8,128)} %get-tuple-element.116.gres_ref, ...), custom_call_target="tpu_custom_call" | custom-call | flops 483183808 | bytes 2000000 | tf_op jit(solution)/shard_map/attn_bwd/pallas_call | solution.py:72
  114.2 0.0 all-to-all-done
  114.2 0.0 collective-permute-done.3.refs_3_
  114.3 2.7 %collective-permute-done.5.refs_7_ = bf16[24,8,1536]{2,1,0:T(8,128)(2,1)} collective-permute-done((bf16[24,8,1536]{2,1,0:T(8,128)(2,1)}, bf16[24,8,1536]{2,1,0:T(8,128)(2,1)}, u32[]{:S(2)}, u32[]{:S(2)}) %collective-permute-start.5) | collective-permute-done | bytes 589856 | tf_op jit(solution)/shard_map/ppermute | solution.py:904
  117.0 0.0 copy-start.2
  117.0 1.1 copy-done.2
  118.0 1.1 copy-done.3
  119.1 2.1 %fold_second.2 = (bf16[24,8,1536]{2,1,0:T(8,128)(2,1)S(1)}, bf16[24,8,1536]{2,1,0:T(8,128)(2,1)S(1)}, bf16[24,8,1536]{2,1,0:T(8,128)(2,1)S(1)}, bf16[24,8,1536]{2,1,0:T(8,128)(2,1)S(1)}) custom-call(s32[8]{0:T(128)S(1)} %copy-done.4, bf16[24,8,1536]{2,1,0:T(8,128)(2,1)S(1)} %copy-done, bf16[24,8,1536]{2,1,0:T(8,128)(2,1)} %collective-permute-done.2.refs_1_, ...), custom_call_target="tpu_custom_call" | custom-call | flops 50000 | bytes 200000 | tf_op jit(solution)/shard_map/fold_second/pallas_call | solution.py:732
  121.3 7.6 %proj_give.1 = bf16[776,1536]{1,0:T(8,128)(2,1)S(1)} custom-call(s32[8]{0:T(128)} %stack.35.here_s, bf16[1024,768]{1,0:T(8,128)(2,1)} %x_ref.5, bf16[1024,2304]{1,0:T(8,128)(2,1)} %get-tuple-element.145.gm_ref, bf16[1024,768]{1,0:T(8,128)(2,1)} %get-tuple-element.134.att_ref, bf16[1024,768]{1,0:T(8,128)(2,1)S(1)} %get-tuple-element.135.gb_ref, ...), custom_call_target="tpu_custom_call" | custom-call | flops 120795952 | bytes 450000 | tf_op jit(solution)/shard_map/proj_give/pallas_call | solution.py:72
  128.8 0.1 collective-permute-start.6
  128.9 0.1 collective-permute-start.7
  129.0 0.0 copy-start.5
  129.0 1.0 collective-permute-start.8
  130.0 3.5 %collective-permute-done.6.got_ref = bf16[776,1536]{1,0:T(8,128)(2,1)S(1)} collective-permute-done((bf16[776,1536]{1,0:T(8,128)(2,1)S(1)}, bf16[776,1536]{1,0:T(8,128)(2,1)S(1)}, u32[]{:S(2)}, u32[]{:S(2)}) %collective-permute-start.6) | collective-permute-done | bytes 2383904 | tf_op jit(solution)/shard_map/ppermute | solution.py:904
  133.5 8.3 %proj_own.1 = (bf16[25,8,1536]{2,1,0:T(8,128)(2,1)S(1)}, bf16[25,8,1536]{2,1,0:T(8,128)(2,1)S(1)}, bf16[24,8,1536]{2,1,0:T(8,128)(2,1)S(1)}, bf16[24,8,1536]{2,1,0:T(8,128)(2,1)S(1)}) custom-call(s32[8]{0:T(128)} %stack.35.here_s, bf16[1024,768]{1,0:T(8,128)(2,1)} %x_ref.5, bf16[1024,2304]{1,0:T(8,128)(2,1)} %get-tuple-element.145.gm_ref, ...), custom_call_target="tpu_custom_call" | custom-call | flops 120795952 | bytes 550000 | tf_op jit(solution)/shard_map/proj_own/pallas_call | solution.py:72
  141.8 1.0 collective-permute-start.10
  142.8 1.9 collective-permute-done.7.refs_1_
  144.7 0.1 collective-permute-done.8.refs_3_
  144.8 0.8 fold_third.2
  145.6 4.1 %collective-permute-start.9 = (bf16[24,8,1536]{2,1,0:T(8,128)(2,1)S(1)}, bf16[24,8,1536]{2,1,0:T(8,128)(2,1)S(1)}, u32[]{:S(2)}, u32[]{:S(2)}) collective-permute-start(bf16[24,8,1536]{2,1,0:T(8,128)(2,1)S(1)} %get-tuple-element.148), channel_id=1, source_target_pairs={{0,8},{4,12},{8,0},{12,4},{16,24},{20,28},{24,16},{28,20},{1,9},{5... | collective-permute-start | bytes 1769480 | tf_op jit(solution)/shard_map/ppermute | solution.py:904
  149.7 2.5 %collective-permute-start.11 = (bf16[24,8,1536]{2,1,0:T(8,128)(2,1)S(1)}, bf16[24,8,1536]{2,1,0:T(8,128)(2,1)S(1)}, u32[]{:S(2)}, u32[]{:S(2)}) collective-permute-start(bf16[24,8,1536]{2,1,0:T(8,128)(2,1)S(1)} %get-tuple-element.153), channel_id=1, source_target_pairs={{0,4},{4,0},{8,12},{12,8},{16,20},{20,16},{24,28},{28,24},{1,5},{5... | collective-permute-start | bytes 1769480 | tf_op jit(solution)/shard_map/ppermute | solution.py:904
  152.2 8.9 %input_grad.1 = bf16[1024,768]{1,0:T(8,128)(2,1)} custom-call(bf16[1024,2304]{1,0:T(8,128)(2,1)} %get-tuple-element.145.gm_ref, bf16[768,2304]{1,0:T(8,128)(2,1)} %wq_ref.3, f32[1024,768]{1,0:T(8,128)} %get-tuple-element.146.gr_ref), custom_call_target="tpu_custom_call" | custom-call | flops 181193936 | bytes 650000 | tf_op jit(solution)/shard_map/input_grad/pallas_call | solution.py:72
  161.0 1.6 collective-permute-done.9.got_ref
  162.7 0.7 fold_fourth.2
  163.4 0.8 collective-permute-done.11.refs_3_
  164.2 0.8 fold_second.3
  165.0 1.5 collective-permute-start.12
  166.5 0.5 collective-permute-start.13
  167.0 6.1 %copied.1 = bf16[1024,768]{1,0:T(8,128)(2,1)} custom-call(s32[8]{0:T(128)} %stack.35.here_s, bf16[1024,768]{1,0:T(8,128)(2,1)} %bitcast.8.in_ref), custom_call_target="tpu_custom_call" | custom-call | bytes 150000 | tf_op jit(solution)/shard_map/copied/pallas_call | solution.py:72
  173.1 0.1 collective-permute-done.13.refs_3_
  173.2 0.7 fold_third.3
  173.9 1.1 collective-permute-start.15
  175.0 0.8 collective-permute-start.14
  175.8 13.2 %collective-permute-done.14.got_ref = bf16[12,8,1536]{2,1,0:T(8,128)(2,1)S(1)} collective-permute-done((bf16[12,8,1536]{2,1,0:T(8,128)(2,1)S(1)}, bf16[12,8,1536]{2,1,0:T(8,128)(2,1)S(1)}, u32[]{:S(2)}, u32[]{:S(2)}) %collective-permute-start.14) | collective-permute-done | bytes 294944 | tf_op jit(solution)/shard_map/ppermute | solution.py:904
  189.0 0.6 fold_last.2.me
  189.6 0.6 fold_fourth.3
  190.2 0.4 collective-permute-start.17
  190.7 0.8 collective-permute-start.16
  191.5 5.5 %collective-permute-done.17.gx = bf16[12,8,1536]{2,1,0:T(8,128)(2,1)S(1)} collective-permute-done((bf16[12,8,1536]{2,1,0:T(8,128)(2,1)S(1)}, bf16[12,8,1536]{2,1,0:T(8,128)(2,1)S(1)}, u32[]{:S(2)}, u32[]{:S(2)}) %collective-permute-start.17) | collective-permute-done | bytes 294944 | tf_op jit(solution)/shard_map/ppermute | solution.py:904
  197.0 0.7 collective-permute-done.16.got_ref
  197.7 0.6 fold_last.3
  198.3 1.0 collective-permute-start.20
  199.3 4.6 %collective-permute-done.20.gx = bf16[6,8,1536]{2,1,0:T(8,128)(2,1)S(1)} collective-permute-done((bf16[6,8,1536]{2,1,0:T(8,128)(2,1)S(1)}, bf16[6,8,1536]{2,1,0:T(8,128)(2,1)S(1)}, u32[]{:S(2)}, u32[]{:S(2)}) %collective-permute-start.20) | collective-permute-done | bytes 147488 | tf_op jit(solution)/shard_map/ppermute | solution.py:904
  203.9 2.4 %feed_blocks.1 = (f32[384,768]{1,0:T(8,128)}, f32[96,3072]{1,0:T(8,128)}) custom-call(s32[8]{0:T(128)S(1)} %copy-done.6, bf16[12,8,1536]{2,1,0:T(8,128)(2,1)S(1)} %fold_last.2.me, bf16[12,8,1536]{2,1,0:T(8,128)(2,1)S(1)} %collective-permute-done.17.gx, bf16[12,8,1536]{2,1,0:T(8,128)(2,1)S(1)} %collective-permute-done.18.gc, ...), custom_call_target="tpu_custom_call" | custom-call | flops 50000 | bytes 200000 | tf_op jit(solution)/shard_map/feed_blocks/pallas_call | solution.py:732
  206.4 1.9 projection_blocks.1
  208.3 0.6 reduce
  (23 shorter events, 0.1 us)
Async XLA Ops:
  50.7 17.2 %collective-permute-start = (bf16[3072,384]{1,0:T(8,128)(2,1)}, bf16[3072,384]{1,0:T(8,128)(2,1)}, u32[]{:S(2)}, u32[]{:S(2)}) collective-permute-start(bf16[3072,384]{1,0:T(8,128)(2,1)} %down_give.1), channel_id=1, source_target_pairs={{0,1},{1,0},{2,3},{3,2},{4,5},{5,4},{6,7},{7,6},{8,9},{9,8},{10,11... | collective-permute-start | bytes 7077896 | tf_op jit(solution)/shard_map/ppermute | solution.py:904
  60.5 24.8 %collective-permute-start.1 = (bf16[768,1536]{1,0:T(8,128)(2,1)}, bf16[768,1536]{1,0:T(8,128)(2,1)}, u32[]{:S(2)}, u32[]{:S(2)}) collective-permute-start(bf16[768,1536]{1,0:T(8,128)(2,1)} %get-tuple-element.113), channel_id=1, source_target_pairs={{0,1},{1,0},{2,3},{3,2},{4,5},{5,4},{6,7},{7,6},{8,9},{9,8},{10,11... | collective-permute-start | bytes 7077896 | tf_op jit(solution)/shard_map/ppermute | solution.py:904
  60.5 53.7 %all-to-all-start = ((bf16[8,128,768]{2,1,0:T(8,128)(2,1)}), bf16[8,128,768]{2,1,0:T(8,128)(2,1)}, u32[]{:S(2)}, u32[]{:S(2)}) async-start(bf16[8,128,768]{2,1,0:T(8,128)(2,1)} %get-tuple-element.124), calls=%async_computation | async-start | bytes 3145728 | tf_op jit(solution)/shard_map/all_to_all | solution.py:915
  81.7 32.6 %collective-permute-start.2 = (bf16[24,8,1536]{2,1,0:T(8,128)(2,1)}, bf16[24,8,1536]{2,1,0:T(8,128)(2,1)}, u32[]{:S(2)}, u32[]{:S(2)}) collective-permute-start(bf16[24,8,1536]{2,1,0:T(8,128)(2,1)} %get-tuple-element.126), channel_id=1, source_target_pairs={{0,2},{1,3},{2,0},{3,1},{4,6},{5,7},{6,4},{7,5},{8,10},{9,11},{10,... | collective-permute-start | bytes 1769480 | tf_op jit(solution)/shard_map/ppermute | solution.py:904
  83.2 31.0 %collective-permute-start.3 = (bf16[24,8,1536]{2,1,0:T(8,128)(2,1)}, bf16[24,8,1536]{2,1,0:T(8,128)(2,1)}, u32[]{:S(2)}, u32[]{:S(2)}) collective-permute-start(bf16[24,8,1536]{2,1,0:T(8,128)(2,1)} %get-tuple-element.128), channel_id=1, source_target_pairs={{0,4},{4,0},{8,12},{12,8},{16,20},{20,16},{24,28},{28,24},{1,5},{5... | collective-permute-start | bytes 1769480 | tf_op jit(solution)/shard_map/ppermute | solution.py:904
  95.0 19.2 %collective-permute-start.4 = (bf16[24,8,1536]{2,1,0:T(8,128)(2,1)}, bf16[24,8,1536]{2,1,0:T(8,128)(2,1)}, u32[]{:S(2)}, u32[]{:S(2)}) collective-permute-start(bf16[24,8,1536]{2,1,0:T(8,128)(2,1)} %get-tuple-element.129), channel_id=1, source_target_pairs={{0,2},{1,3},{2,0},{3,1},{4,6},{5,7},{6,4},{7,5},{8,10},{9,11},{10,... | collective-permute-start | bytes 1769480 | tf_op jit(solution)/shard_map/ppermute | solution.py:904
  95.5 21.4 %collective-permute-start.5 = (bf16[24,8,1536]{2,1,0:T(8,128)(2,1)}, bf16[24,8,1536]{2,1,0:T(8,128)(2,1)}, u32[]{:S(2)}, u32[]{:S(2)}) collective-permute-start(bf16[24,8,1536]{2,1,0:T(8,128)(2,1)} %get-tuple-element.131), channel_id=1, source_target_pairs={{0,4},{4,0},{8,12},{12,8},{16,20},{20,16},{24,28},{28,24},{1,5},{5... | collective-permute-start | bytes 1769480 | tf_op jit(solution)/shard_map/ppermute | solution.py:904
  95.5 21.4 %copy-start = (bf16[24,8,1536]{2,1,0:T(8,128)(2,1)S(1)}, bf16[24,8,1536]{2,1,0:T(8,128)(2,1)}, u32[]{:S(2)}) copy-start(bf16[24,8,1536]{2,1,0:T(8,128)(2,1)} %get-tuple-element.109.refs_0_) | copy-start | bytes 1769476
  95.5 21.4 %copy-start.1 = (bf16[24,8,1536]{2,1,0:T(8,128)(2,1)S(1)}, bf16[24,8,1536]{2,1,0:T(8,128)(2,1)}, u32[]{:S(2)}) copy-start(bf16[24,8,1536]{2,1,0:T(8,128)(2,1)} %get-tuple-element.127.refs_2_) | copy-start | bytes 1769476
  95.5 21.4 %copy-start.4 = (s32[8]{0:T(128)S(1)}, s32[8]{0:T(128)}, u32[]{:S(2)}) copy-start(s32[8]{0:T(128)} %stack.35.here_s) | copy-start | bytes 100
  117.0 1.1 copy-start.2
  118.0 1.1 copy-start.3
  128.8 4.6 %collective-permute-start.6 = (bf16[776,1536]{1,0:T(8,128)(2,1)S(1)}, bf16[776,1536]{1,0:T(8,128)(2,1)S(1)}, u32[]{:S(2)}, u32[]{:S(2)}) collective-permute-start(bf16[776,1536]{1,0:T(8,128)(2,1)S(1)} %proj_give.1), channel_id=1, source_target_pairs={{0,1},{1,0},{2,3},{3,2},{4,5},{5,4},{6,7},{7,6},{8,9},{9,8},{10,11... | collective-permute-start | bytes 7151624 | tf_op jit(solution)/shard_map/ppermute | solution.py:904
  128.9 15.7 %collective-permute-start.7 = (bf16[24,8,1536]{2,1,0:T(8,128)(2,1)S(1)}, bf16[24,8,1536]{2,1,0:T(8,128)(2,1)S(1)}, u32[]{:S(2)}, u32[]{:S(2)}) collective-permute-start(bf16[24,8,1536]{2,1,0:T(8,128)(2,1)S(1)} %get-tuple-element.141), channel_id=1, source_target_pairs={{0,4},{4,0},{8,12},{12,8},{16,20},{20,16},{24,28},{28,24},{1,5},{5... | collective-permute-start | bytes 1769480 | tf_op jit(solution)/shard_map/ppermute | solution.py:904
  129.0 15.8 %copy-start.5 = (s32[8]{0:T(128)S(1)}, s32[8]{0:T(128)}, u32[]{:S(2)}) copy-start(s32[8]{0:T(128)} %stack.35.here_s) | copy-start | bytes 100
  129.0 15.7 %collective-permute-start.8 = (bf16[24,8,1536]{2,1,0:T(8,128)(2,1)S(1)}, bf16[24,8,1536]{2,1,0:T(8,128)(2,1)S(1)}, u32[]{:S(2)}, u32[]{:S(2)}) collective-permute-start(bf16[24,8,1536]{2,1,0:T(8,128)(2,1)S(1)} %get-tuple-element.143), channel_id=1, source_target_pairs={{0,2},{1,3},{2,0},{3,1},{4,6},{5,7},{6,4},{7,5},{8,10},{9,11},{10,... | collective-permute-start | bytes 1769480 | tf_op jit(solution)/shard_map/ppermute | solution.py:904
  141.8 22.4 %collective-permute-start.10 = (bf16[25,8,1536]{2,1,0:T(8,128)(2,1)S(1)}, bf16[25,8,1536]{2,1,0:T(8,128)(2,1)S(1)}, u32[]{:S(2)}, u32[]{:S(2)}) collective-permute-start(bf16[25,8,1536]{2,1,0:T(8,128)(2,1)S(1)} %get-tuple-element.151), channel_id=1, source_target_pairs={{0,2},{1,3},{2,0},{3,1},{4,6},{5,7},{6,4},{7,5},{8,10},{9,11},{10,... | collective-permute-start | bytes 1843208 | tf_op jit(solution)/shard_map/ppermute | solution.py:904
  145.6 17.1 %collective-permute-start.9 = (bf16[24,8,1536]{2,1,0:T(8,128)(2,1)S(1)}, bf16[24,8,1536]{2,1,0:T(8,128)(2,1)S(1)}, u32[]{:S(2)}, u32[]{:S(2)}) collective-permute-start(bf16[24,8,1536]{2,1,0:T(8,128)(2,1)S(1)} %get-tuple-element.148), channel_id=1, source_target_pairs={{0,8},{4,12},{8,0},{12,4},{16,24},{20,28},{24,16},{28,20},{1,9},{5... | collective-permute-start | bytes 1769480 | tf_op jit(solution)/shard_map/ppermute | solution.py:904
  149.7 14.4 %collective-permute-start.11 = (bf16[24,8,1536]{2,1,0:T(8,128)(2,1)S(1)}, bf16[24,8,1536]{2,1,0:T(8,128)(2,1)S(1)}, u32[]{:S(2)}, u32[]{:S(2)}) collective-permute-start(bf16[24,8,1536]{2,1,0:T(8,128)(2,1)S(1)} %get-tuple-element.153), channel_id=1, source_target_pairs={{0,4},{4,0},{8,12},{12,8},{16,20},{20,16},{24,28},{28,24},{1,5},{5... | collective-permute-start | bytes 1769480 | tf_op jit(solution)/shard_map/ppermute | solution.py:904
  164.2 9.1 %copy-start.6 = (s32[8]{0:T(128)S(1)}, s32[8]{0:T(128)}, u32[]{:S(2)}) copy-start(s32[8]{0:T(128)} %stack.35.here_s) | copy-start | bytes 100
  165.0 8.3 %collective-permute-start.12 = (bf16[13,8,1536]{2,1,0:T(8,128)(2,1)S(1)}, bf16[13,8,1536]{2,1,0:T(8,128)(2,1)S(1)}, u32[]{:S(2)}, u32[]{:S(2)}) collective-permute-start(bf16[13,8,1536]{2,1,0:T(8,128)(2,1)S(1)} %get-tuple-element.157), channel_id=1, source_target_pairs={{0,4},{4,0},{8,12},{12,8},{16,20},{20,16},{24,28},{28,24},{1,5},{5... | collective-permute-start | bytes 958472 | tf_op jit(solution)/shard_map/ppermute | solution.py:904
  166.5 6.7 %collective-permute-start.13 = (bf16[12,8,1536]{2,1,0:T(8,128)(2,1)S(1)}, bf16[12,8,1536]{2,1,0:T(8,128)(2,1)S(1)}, u32[]{:S(2)}, u32[]{:S(2)}) collective-permute-start(bf16[12,8,1536]{2,1,0:T(8,128)(2,1)S(1)} %get-tuple-element.159), channel_id=1, source_target_pairs={{0,2},{1,3},{2,0},{3,1},{4,6},{5,7},{6,4},{7,5},{8,10},{9,11},{10,... | collective-permute-start | bytes 884744 | tf_op jit(solution)/shard_map/ppermute | solution.py:904
  173.9 15.6 %collective-permute-start.15 = (bf16[13,8,1536]{2,1,0:T(8,128)(2,1)S(1)}, bf16[13,8,1536]{2,1,0:T(8,128)(2,1)S(1)}, u32[]{:S(2)}, u32[]{:S(2)}) collective-permute-start(bf16[13,8,1536]{2,1,0:T(8,128)(2,1)S(1)} %get-tuple-element.164), channel_id=1, source_target_pairs={{0,8},{4,12},{8,0},{12,4},{16,24},{20,28},{24,16},{28,20},{1,9},{5... | collective-permute-start | bytes 958472 | tf_op jit(solution)/shard_map/ppermute | solution.py:904
  175.0 14.0 %collective-permute-start.14 = (bf16[12,8,1536]{2,1,0:T(8,128)(2,1)S(1)}, bf16[12,8,1536]{2,1,0:T(8,128)(2,1)S(1)}, u32[]{:S(2)}, u32[]{:S(2)}) collective-permute-start(bf16[12,8,1536]{2,1,0:T(8,128)(2,1)S(1)} %get-tuple-element.162), channel_id=1, source_target_pairs={{0,16},{4,20},{8,24},{12,28},{16,0},{20,4},{24,8},{28,12},{1,17},{... | collective-permute-start | bytes 884744 | tf_op jit(solution)/shard_map/ppermute | solution.py:904
  190.2 6.8 %collective-permute-start.17 = (bf16[12,8,1536]{2,1,0:T(8,128)(2,1)S(1)}, bf16[12,8,1536]{2,1,0:T(8,128)(2,1)S(1)}, u32[]{:S(2)}, u32[]{:S(2)}) collective-permute-start(bf16[12,8,1536]{2,1,0:T(8,128)(2,1)S(1)} %fold_last.2.me), channel_id=1, source_target_pairs={{0,2},{1,3},{2,0},{3,1},{4,6},{5,7},{6,4},{7,5},{8,10},{9,11},{10,... | collective-permute-start | bytes 884744 | tf_op jit(solution)/shard_map/ppermute | solution.py:904
  190.7 7.0 %collective-permute-start.16 = (bf16[7,8,1536]{2,1,0:T(8,128)(2,1)S(1)}, bf16[7,8,1536]{2,1,0:T(8,128)(2,1)S(1)}, u32[]{:S(2)}, u32[]{:S(2)}) collective-permute-start(bf16[7,8,1536]{2,1,0:T(8,128)(2,1)S(1)} %get-tuple-element.166), channel_id=1, source_target_pairs={{0,16},{4,20},{8,24},{12,28},{16,0},{20,4},{24,8},{28,12},{1,17},{... | collective-permute-start | bytes 516104 | tf_op jit(solution)/shard_map/ppermute | solution.py:904
  191.5 12.5 %collective-permute-start.18 = (bf16[12,8,1536]{2,1,0:T(8,128)(2,1)S(1)}, bf16[12,8,1536]{2,1,0:T(8,128)(2,1)S(1)}, u32[]{:S(2)}, u32[]{:S(2)}) collective-permute-start(bf16[12,8,1536]{2,1,0:T(8,128)(2,1)S(1)} %fold_last.2.me), channel_id=1, source_target_pairs={{0,1},{1,0},{2,3},{3,2},{4,5},{5,4},{6,7},{7,6},{8,9},{9,8},{10,11... | collective-permute-start | bytes 884744 | tf_op jit(solution)/shard_map/ppermute | solution.py:904
  197.0 6.9 %collective-permute-start.19 = (bf16[12,8,1536]{2,1,0:T(8,128)(2,1)S(1)}, bf16[12,8,1536]{2,1,0:T(8,128)(2,1)S(1)}, u32[]{:S(2)}, u32[]{:S(2)}) collective-permute-start(bf16[12,8,1536]{2,1,0:T(8,128)(2,1)S(1)} %collective-permute-done.17.gx), channel_id=1, source_target_pairs={{0,1},{1,0},{2,3},{3,2},{4,5},{5,4},{6,7},{7,6},{8,9},{9,8},{10,11... | collective-permute-start | bytes 884744 | tf_op jit(solution)/shard_map/ppermute | solution.py:904
  198.3 5.6 %collective-permute-start.20 = (bf16[6,8,1536]{2,1,0:T(8,128)(2,1)S(1)}, bf16[6,8,1536]{2,1,0:T(8,128)(2,1)S(1)}, u32[]{:S(2)}, u32[]{:S(2)}) collective-permute-start(bf16[6,8,1536]{2,1,0:T(8,128)(2,1)S(1)} %get-tuple-element.167.me), channel_id=1, source_target_pairs={{0,2},{1,3},{2,0},{3,1},{4,6},{5,7},{6,4},{7,5},{8,10},{9,11},{10,... | collective-permute-start | bytes 442376 | tf_op jit(solution)/shard_map/ppermute | solution.py:904
  199.3 7.1 %collective-permute-start.21 = (bf16[6,8,1536]{2,1,0:T(8,128)(2,1)S(1)}, bf16[6,8,1536]{2,1,0:T(8,128)(2,1)S(1)}, u32[]{:S(2)}, u32[]{:S(2)}) collective-permute-start(bf16[6,8,1536]{2,1,0:T(8,128)(2,1)S(1)} %get-tuple-element.167.me), channel_id=1, source_target_pairs={{0,1},{1,0},{2,3},{3,2},{4,5},{5,4},{6,7},{7,6},{8,9},{9,8},{10,11... | collective-permute-start | bytes 442376 | tf_op jit(solution)/shard_map/ppermute | solution.py:904
  203.9 2.4 %collective-permute-start.22 = (bf16[6,8,1536]{2,1,0:T(8,128)(2,1)S(1)}, bf16[6,8,1536]{2,1,0:T(8,128)(2,1)S(1)}, u32[]{:S(2)}, u32[]{:S(2)}) collective-permute-start(bf16[6,8,1536]{2,1,0:T(8,128)(2,1)S(1)} %collective-permute-done.20.gx), channel_id=1, source_target_pairs={{0,1},{1,0},{2,3},{3,2},{4,5},{5,4},{6,7},{7,6},{8,9},{9,8},{10,11... | collective-permute-start | bytes 442376 | tf_op jit(solution)/shard_map/ppermute | solution.py:904

commit v9 on v8

--- a/solution.py
+++ b/solution.py
@@ -253,6 +253,7 @@
     side = -(-pair_count // 8) * 8
     chunk = width
     steps = ff // chunk
+    tall = 2 * block
     blocks = rows // block
     per_block = block // span
 
@@ -271,8 +272,8 @@
             ht_ref[...] = hidden.T
             acc_scr[...] = jnp.zeros_like(acc_scr)
 
-        for number in range(blocks):
-            base = slice(number * block, (number + 1) * block)
+        for number in range(rows // tall):
+            base = slice(number * tall, (number + 1) * tall)
             inner = dot(low_scr[base, :], wu_ref[...]) + tab_ref[pl.ds(ROW_BU + step, 1), :]
             active, slope = gelu_pair(inner)
             active = active.astype(BF16)
@@ -457,7 +458,7 @@
     half = ff // 2
     chunk = width
     steps = half // chunk
-    block = rows // 4
+    block = rows // 2
     pieces = width // 32 // 8
 
     def kernel(here_s, gs_ref, dg_ref, ht_ref, wd_ref, *refs):
@@ -516,32 +517,13 @@
     )
 
 
-def hidden_gradient(grad_inner, w_up, here, which):
-    rows, half = grad_inner.shape
-    width = w_up.shape[0]
-    block = rows // 2
-
-    def kernel(here_s, gi_ref, wu_ref, out_ref):
-        out_ref[...] = dot_t(gi_ref[...], wu_ref[...])
-
-    return call(
-        kernel, "hidden_grad", (rows // block,), (here,),
-        [
-            pl.BlockSpec((block, half), lambda i, h: (i, 0)),
-            pl.BlockSpec((width, half), lambda i, h: (0, h[which]), pipeline_mode=pl.Buffered(1)),
-        ],
-        pl.BlockSpec((block, width), lambda i, h: (i, 0)),
-        shaped((rows, width), F32), [], 2 * rows * width * half, 9e6, (grad_inner, w_up), 16, 0, (0,),
-    )
-
-
-def attention_backward(gh, gres, grad_inner, w_up, n_attn, spread, table, w_out, qkv, probs, here, which, span, rows_step):
-    rows, width = gh.shape
-    half = grad_inner.shape[1]
+def attention_backward(grads_inner, gres, w_up, n_attn, spread, table, w_out, qkv, probs, here, span, rows_step):
+    rows, width = gres.shape
+    half = grads_inner[0].shape[1]
     pairs = width // LANES
     per_step = rows_step // span
 
-    def kernel(here_s, gh_ref, gres_ref, gi_ref, wu_ref, n_ref, s_ref, tab_ref, wo_ref, qkv_ref, p_ref, gr_ref, gb_ref, gm_ref, vec_ref, ga_scr):
+    def kernel(here_s, gi_ref, other_ref, gres_ref, wu_ref, wu_other_ref, n_ref, s_ref, tab_ref, wo_ref, qkv_ref, p_ref, gr_ref, gb_ref, gm_ref, vec_ref, ga_scr):
         step = pl.program_id(0)
         low_b, high_b, low_m = head_masks()
 
@@ -550,7 +532,9 @@
             vec_ref[...] = jnp.zeros_like(vec_ref)
 
         normed = n_ref[...]
-        grad_hidden = dot_t(gi_ref[...], wu_ref[...]) + gh_ref[...] + gres_ref[...]
+        grad_hidden = (
+            dot_t(gi_ref[...], wu_ref[...]) + dot_t(other_ref[...], wu_other_ref[...]) + gres_ref[...]
+        )
         resid = norm_backward(grad_hidden, normed, s_ref[:, :1], tab_ref[ROW_GA : ROW_GA + 1, :])
         gr_ref[...] = resid
         low = resid.astype(BF16)
@@ -592,8 +576,9 @@
         (rows // rows_step,),
         (here,),
         [
-            rows_of(width), rows_of(width), rows_of(half),
-            pl.BlockSpec((width, half), lambda i, h: (0, h[which]), pipeline_mode=pl.Buffered(1)),
+            rows_of(half), rows_of(half), rows_of(width),
+            pl.BlockSpec((width, half), lambda i, h: (0, h[0]), pipeline_mode=pl.Buffered(1)),
+            pl.BlockSpec((width, half), lambda i, h: (0, h[1]), pipeline_mode=pl.Buffered(1)),
             rows_of(width), rows_of(LANES),
             once(table.shape), once((width, width)), rows_of(3 * width),
             pl.BlockSpec((per_step, pairs, 2 * span, span), lambda i, h: (i, 0, 0, 0)),
@@ -606,8 +591,8 @@
         [pltpu.VMEM((rows_step, width), BF16)],
         8 * rows * width * width * 2,
         40e6,
-        (gh, gres, grad_inner, w_up, n_attn, spread, table, w_out, qkv, probs),
-        24, 0, (1,), (0, 2),
+        (*grads_inner, gres, w_up, w_up, n_attn, spread, table, w_out, qkv, probs),
+        40, 0, (1,), (0, 1),
     )
 
 
@@ -962,7 +947,7 @@
     pieces = width // 32 // 8
 
     qkv, probs, attended, n_attn, spread, sid = attention_forward(
-        tokens, w_qkv, w_out, table, bucket, lengths, wide_count // batches, span, 2 * span
+        tokens, w_qkv, w_out, table, bucket, lengths, wide_count // batches, span, 4 * span
     )
     active, slope, hidden_t, sent, gres, grad_second, vec_ffn = feed_forward(
         n_attn, w_up, w_down, table, sid, slots, pairing, targets, batches, 2 * span
@@ -975,13 +960,12 @@
         up_sent, gi_sent, bup_sent = up_terms(*ups, after(here, down_sent), 1)
         down_dealt = down_terms(active, grad_second, after(here, bup_sent), 0, swap(down_sent, "narrow", 1))
         down_a, down_b = swap(down_dealt[0], "narrow", 2), swap(down_dealt[2], "wide", 1)
-        gh = hidden_gradient(gi_sent, w_up, after(here, down_dealt[1]), 1)
         *up_dealt, gi_kept, bup_kept = up_terms(
-            *ups, after(here, gh), 0, swap(up_sent, "narrow", 1)
+            *ups, after(here, down_dealt[1]), 0, swap(up_sent, "narrow", 1)
         )
         up_a, up_b = swap(up_dealt[0], "narrow", 2), swap(up_dealt[2], "wide", 1)
         gr, gb, gm, vec_attn = attention_backward(
-            gh, gres, gi_kept, w_up, *heads, after(here, up_dealt[1]), 0, span, 2 * span
+            (gi_kept, gi_sent), gres, w_up, *heads, after(here, up_dealt[1]), span, 4 * span
         )
         feed = fold_second(
             [
@@ -1001,7 +985,7 @@
             [feed[1], feed_a, feed[3], feed_b], after(here, proj_dealt[1]), pieces, 0
         )
         feed_got = swap(send, "wide", 2)
-        grad_tokens = input_gradient(after(gm, feed), w_qkv, gr, 2 * span)
+        grad_tokens = input_gradient(after(gm, feed), w_qkv, gr, 4 * span)
         send, feed = fold_fourth(feed, feed_got, after(here, grad_tokens), 0)
         feed_got = swap(send, "wide", 4)
         proj_dealt = fold_second(
@@ -1027,9 +1011,8 @@
         down_kept = down_terms(active, grad_second, here, 0)
         up_sent, gi_sent, bup_sent = up_terms(*ups, here, 1)
         up_kept, gi_kept, bup_kept = up_terms(*ups, here, 0)
-        gh = hidden_gradient(gi_sent, w_up, here, 1)
         gr, gb, gm, vec_attn = attention_backward(
-            gh, gres, gi_kept, w_up, *heads, here, 0, span, 2 * span
+            (gi_kept, gi_sent), gres, w_up, *heads, here, span, 2 * span
         )
         projections = (tokens, gm, attended, gb, (vec_ffn, vec_attn, bup_sent, bup_kept), here)
         grad_tokens = input_gradient(gm, w_qkv, gr, 2 * span)

time: 210 us -> 207 us (0.986); the launches traced: 209 us -> 203 us
  waiting for transfers between devices: 34.7 us -> 25.6 us
  starting transfers between devices: 26.9 us -> 30.2 us
    ppermute x23, waiting for transfers between devices: 34.7 us -> 25.6 us  [swap(): lax.ppermute(item, axis, [(index, index ^ step) for index in range(count)])]
    ppermute x23, starting transfers between devices: 19.6 us -> 22.9 us  [swap(): lax.ppermute(item, axis, [(index, index ^ step) for index in range(count)])]
    pallas_call x12 -> x11, Pallas kernels: 131 us -> 131 us  [call(): pl.pallas_call(kernel, grid_spec=pltpu.PrefetchScalarGridSpec(num_scalar_...]
  transfers between devices with their start and end apart: 24 -> 24, of which waited for: 11 -> 10; matrix products, arithmetic and copies ran while one was open for 0% -> 0% of each run, Pallas kernels for 38% -> 39%
where the time goes in v9:
time: 207 us; the launch traced here: 203 us
  Pallas kernels  143 us (69%)
  starting transfers between devices  30.2 us (15%)
  waiting for transfers between devices  25.6 us (12%)
  local copies, waits for them, and re-layouts  2.75 us (1%)
    pallas_call x11, Pallas kernels, call(): pl.pallas_call(kernel, grid_spec=pltpu.PrefetchScalarGridSpec(num_scalar_...  131 us
    ppermute x23, waiting for transfers between devices, swap(): lax.ppermute(item, axis, [(index, index ^ step) for index in range(count)])  25.6 us
    ppermute x23, starting transfers between devices, swap(): lax.ppermute(item, axis, [(index, index ^ step) for index in range(count)])  22.9 us
    pallas_call x10, Pallas kernels, small_call(): pl.pallas_call(kernel, in_specs=[pl.BlockSpec(memory_space=pltpu.SMEM)] +...  11.3 us
    all_to_all x1, starting transfers between devices, regroup_rows(): got = lax.all_to_all(sent, 'wide', split_axis=0, concat_axis=0, tiled=True)  7.31 us
  transfers between devices with their start and end apart: 24, of which 10 were waited for; matrix products, arithmetic and copies ran while one was open for 0% of the time, Pallas kernels for 39%

profile of v9, /device:TPU:0, one launch (start us, length us, event | category | flops | bytes accessed | tf_op | source)
XLA Modules:
  0.0 203.2 jit_solution(11242255808438295335)
XLA Ops:
  0.7 0.9 vector_table.1.tab_ref
  1.6 17.1 %attn_fwd.1 = (bf16[1024,2304]{1,0:T(8,128)(2,1)}, bf16[8,6,256,128]{3,2,1,0:T(8,128)(2,1)}, bf16[1024,768]{1,0:T(8,128)(2,1)}, f32[1024,768]{1,0:T(8,128)}, f32...) custom-call(s32[8]{0:T(128)} %slots_s.1, s32[26]{0:T(128)} %lengths_s.1, bf16[1024,768]{1,0:T(8,128)(2,1)} %x_ref.5, ...), custom_call_target="tpu_custom_call" | custom-call | flops 483183808 | bytes 1500000 | tf_op jit(solution)/shard_map/attn_fwd/pallas_call | solution.py:72
  18.7 24.5 %ffn_fwd.1 = (bf16[1024,3072]{1,0:T(8,128)(2,1)}, bf16[1024,3072]{1,0:T(8,128)(2,1)}, bf16[768,1024]{1,0:T(8,128)(2,1)S(1)}, bf16[8,128,768]{2,1,0:T(8,128)(2,1)...) custom-call(s32[8]{0:T(128)} %slots_s.1, s32[1,26]{1,0:T(1,128)} %pairing_s.1, ...), custom_call_target="tpu_custom_call" | custom-call | flops 966367616 | bytes 2000000 | tf_op jit(solution)/shard_map/ffn_fwd/pallas_call | solution.py:72
  43.2 0.6 stack.35.here_s
  43.8 7.7 %down_give.1 = bf16[3072,384]{1,0:T(8,128)(2,1)} custom-call(s32[8]{0:T(128)} %stack.35.here_s, bf16[1024,3072]{1,0:T(8,128)(2,1)} %get-tuple-element.101.act_ref, bf16[1024,768]{1,0:T(8,128)(2,1)S(1)} %get-tuple-element.102.gs_ref), custom_call_target="tpu_custom_call" | custom-call | flops 120795952 | bytes 450000 | tf_op jit(solution)/shard_map/down_give/pallas_call | solution.py:72
  51.5 0.5 collective-permute-start
  52.0 9.1 %up_give.1 = (bf16[768,1536]{1,0:T(8,128)(2,1)}, bf16[1024,1536]{1,0:T(8,128)(2,1)}, f32[1,1536]{1,0:T(1,128)S(1)}) custom-call(s32[8]{0:T(128)} %stack.35.here_s, bf16[1024,768]{1,0:T(8,128)(2,1)S(1)} %get-tuple-element.102.gs_ref, bf16[1024,3072]{1,0:T(8,128)(2,1)} %get-tuple-element.104.dg_ref, bf16[768,1024]{1,0:T(8,128)(2,1)S(1)} %get-tuple-element.105.ht_ref, ...), custom_call_target="tpu_custom_call" | custom-call | flops 241591904 | bytes 800000 | tf_op jit(solution)/shard_map/up_give/pallas_call | solution.py:72
  61.2 0.0 collective-permute-start.1
  61.2 7.3 %all-to-all-start = ((bf16[8,128,768]{2,1,0:T(8,128)(2,1)}), bf16[8,128,768]{2,1,0:T(8,128)(2,1)}, u32[]{:S(2)}, u32[]{:S(2)}) async-start(bf16[8,128,768]{2,1,0:T(8,128)(2,1)} %get-tuple-element.122), calls=%async_computation | async-start | bytes 3145728 | tf_op jit(solution)/shard_map/all_to_all | solution.py:900
  68.5 0.0 collective-permute-done.got_ref
  68.5 8.1 %down_own.1 = (bf16[24,8,1536]{2,1,0:T(8,128)(2,1)}, bf16[24,8,1536]{2,1,0:T(8,128)(2,1)}, bf16[24,8,1536]{2,1,0:T(8,128)(2,1)}, bf16[24,8,1536]{2,1,0:T(8,128)(2,1)}) custom-call(s32[8]{0:T(128)} %stack.35.here_s, bf16[1024,3072]{1,0:T(8,128)(2,1)} %get-tuple-element.101.act_ref, bf16[1024,768]{1,0:T(8,128)(2,1)S(1)} %get-tuple-element.102.gs_ref, ...), custom_call_target="tpu_custom_call" | custom-call | flops 120795952 | bytes 550000 | tf_op jit(solution)/shard_map/down_own/pallas_call | solution.py:72
  76.6 1.5 collective-permute-start.2
  78.1 2.0 collective-permute-start.3
  80.2 0.0 collective-permute-done.1.refs_0_
  80.2 9.6 %up_own.1 = (bf16[24,8,1536]{2,1,0:T(8,128)(2,1)}, bf16[24,8,1536]{2,1,0:T(8,128)(2,1)}, bf16[24,8,1536]{2,1,0:T(8,128)(2,1)}, bf16[24,8,1536]{2,1,0:T(8,128)(2,...) custom-call(s32[8]{0:T(128)} %stack.35.here_s, bf16[1024,768]{1,0:T(8,128)(2,1)S(1)} %get-tuple-element.102.gs_ref, ...), custom_call_target="tpu_custom_call" | custom-call | flops 241591904 | bytes 800000 | tf_op jit(solution)/shard_map/up_own/pallas_call | solution.py:72
  89.8 0.5 collective-permute-start.4
  90.3 0.3 collective-permute-start.5
  90.6 24.3 %attn_bwd.1 = (f32[1024,768]{1,0:T(8,128)}, bf16[1024,768]{1,0:T(8,128)(2,1)S(1)}, bf16[1024,2304]{1,0:T(8,128)(2,1)}, f32[8,768]{1,0:T(8,128)S(1)}) custom-call(s32[8]{0:T(128)} %stack.35.here_s, bf16[1024,1536]{1,0:T(8,128)(2,1)S(1)} %get-tuple-element.113.gi_ref, bf16[1024,1536]{1,0:T(8,128)(2,1)S(1)} %copy-done, ...), custom_call_target="tpu_custom_call" | custom-call | flops 483183808 | bytes 2000000 | tf_op jit(solution)/shard_map/attn_bwd/pallas_call | solution.py:72
  114.9 0.0 all-to-all-done
  114.9 0.0 collective-permute-done.3.refs_3_
  114.9 0.0 collective-permute-done.4.refs_5_
  115.0 0.0 copy-start.3
  115.0 1.1 copy-done.3
  116.1 1.1 copy-done.4
  117.1 2.1 %fold_second.2 = (bf16[24,8,1536]{2,1,0:T(8,128)(2,1)S(1)}, bf16[24,8,1536]{2,1,0:T(8,128)(2,1)S(1)}, bf16[24,8,1536]{2,1,0:T(8,128)(2,1)S(1)}, bf16[24,8,1536]{2,1,0:T(8,128)(2,1)S(1)}) custom-call(s32[8]{0:T(128)S(1)} %copy-done.5, bf16[24,8,1536]{2,1,0:T(8,128)(2,1)S(1)} %copy-done.1, bf16[24,8,1536]{2,1,0:T(8,128)(2,1)} %collective-permute-done.2.refs_1_, ...), custom_call_target="tpu_custom_call" | custom-call | flops 50000 | bytes 200000 | tf_op jit(solution)/shard_map/fold_second/pallas_call | solution.py:717
  119.3 7.8 %proj_give.1 = bf16[776,1536]{1,0:T(8,128)(2,1)S(1)} custom-call(s32[8]{0:T(128)} %stack.35.here_s, bf16[1024,768]{1,0:T(8,128)(2,1)} %x_ref.5, bf16[1024,2304]{1,0:T(8,128)(2,1)} %get-tuple-element.143.gm_ref, bf16[1024,768]{1,0:T(8,128)(2,1)} %get-tuple-element.132.att_ref, bf16[1024,768]{1,0:T(8,128)(2,1)S(1)} %get-tuple-element.133.gb_ref, ...), custom_call_target="tpu_custom_call" | custom-call | flops 120795952 | bytes 450000 | tf_op jit(solution)/shard_map/proj_give/pallas_call | solution.py:72
  127.1 0.1 collective-permute-start.6
  127.2 1.8 collective-permute-start.7
  129.0 1.5 collective-permute-start.8
  130.5 1.2 collective-permute-done.6.got_ref
  131.8 8.3 %proj_own.1 = (bf16[25,8,1536]{2,1,0:T(8,128)(2,1)S(1)}, bf16[25,8,1536]{2,1,0:T(8,128)(2,1)S(1)}, bf16[24,8,1536]{2,1,0:T(8,128)(2,1)S(1)}, bf16[24,8,1536]{2,1,0:T(8,128)(2,1)S(1)}) custom-call(s32[8]{0:T(128)} %stack.35.here_s, bf16[1024,768]{1,0:T(8,128)(2,1)} %x_ref.5, bf16[1024,2304]{1,0:T(8,128)(2,1)} %get-tuple-element.143.gm_ref, ...), custom_call_target="tpu_custom_call" | custom-call | flops 120795952 | bytes 550000 | tf_op jit(solution)/shard_map/proj_own/pallas_call | solution.py:72
  140.0 1.5 collective-permute-start.10
  141.6 1.4 collective-permute-done.7.refs_1_
  143.0 2.3 %collective-permute-done.8.refs_3_ = bf16[24,8,1536]{2,1,0:T(8,128)(2,1)S(1)} collective-permute-done((bf16[24,8,1536]{2,1,0:T(8,128)(2,1)S(1)}, bf16[24,8,1536]{2,1,0:T(8,128)(2,1)S(1)}, u32[]{:S(2)}, u32[]{:S(2)}) %collective-permute-start.8) | collective-permute-done | bytes 589856 | tf_op jit(solution)/shard_map/ppermute | solution.py:889
  145.2 0.8 fold_third.2
  146.1 1.5 collective-permute-start.9
  147.6 0.4 collective-permute-start.11
  148.0 8.2 %input_grad.1 = bf16[1024,768]{1,0:T(8,128)(2,1)} custom-call(bf16[1024,2304]{1,0:T(8,128)(2,1)} %get-tuple-element.143.gm_ref, bf16[768,2304]{1,0:T(8,128)(2,1)} %wq_ref.3, f32[1024,768]{1,0:T(8,128)} %get-tuple-element.144.gr_ref), custom_call_target="tpu_custom_call" | custom-call | flops 181193936 | bytes 650000 | tf_op jit(solution)/shard_map/input_grad/pallas_call | solution.py:72
  156.1 3.7 %collective-permute-done.9.got_ref = bf16[24,8,1536]{2,1,0:T(8,128)(2,1)S(1)} collective-permute-done((bf16[24,8,1536]{2,1,0:T(8,128)(2,1)S(1)}, bf16[24,8,1536]{2,1,0:T(8,128)(2,1)S(1)}, u32[]{:S(2)}, u32[]{:S(2)}) %collective-permute-start.9) | collective-permute-done | bytes 589856 | tf_op jit(solution)/shard_map/ppermute | solution.py:889
  159.8 0.7 fold_fourth.2
  160.5 0.5 collective-permute-done.11.refs_3_
  161.0 0.8 fold_second.3
  161.8 0.8 collective-permute-start.12
  162.6 1.5 collective-permute-start.13
  164.1 6.1 %copied.1 = bf16[1024,768]{1,0:T(8,128)(2,1)} custom-call(s32[8]{0:T(128)} %stack.35.here_s, bf16[1024,768]{1,0:T(8,128)(2,1)} %bitcast.8.in_ref), custom_call_target="tpu_custom_call" | custom-call | bytes 150000 | tf_op jit(solution)/shard_map/copied/pallas_call | solution.py:72
  170.2 0.0 collective-permute-done.13.refs_3_
  170.2 0.0 collective-permute-done.12.refs_1_
  170.2 0.7 fold_third.3
  170.9 1.1 collective-permute-start.15
  171.9 3.4 %collective-permute-start.14 = (bf16[12,8,1536]{2,1,0:T(8,128)(2,1)S(1)}, bf16[12,8,1536]{2,1,0:T(8,128)(2,1)S(1)}, u32[]{:S(2)}, u32[]{:S(2)}) collective-permute-start(bf16[12,8,1536]{2,1,0:T(8,128)(2,1)S(1)} %get-tuple-element.160), channel_id=1, source_target_pairs={{0,16},{4,20},{8,24},{12,28},{16,0},{20,4},{24,8},{28,12},{1,17},{... | collective-permute-start | bytes 884744 | tf_op jit(solution)/shard_map/ppermute | solution.py:889
  175.3 7.7 %collective-permute-done.14.got_ref = bf16[12,8,1536]{2,1,0:T(8,128)(2,1)S(1)} collective-permute-done((bf16[12,8,1536]{2,1,0:T(8,128)(2,1)S(1)}, bf16[12,8,1536]{2,1,0:T(8,128)(2,1)S(1)}, u32[]{:S(2)}, u32[]{:S(2)}) %collective-permute-start.14) | collective-permute-done | bytes 294944 | tf_op jit(solution)/shard_map/ppermute | solution.py:889
  183.0 0.6 fold_last.2.me
  183.6 0.3 collective-permute-done.15.got_ref
  183.9 0.6 fold_fourth.3
  184.5 0.8 collective-permute-start.17
  185.3 2.6 %collective-permute-start.16 = (bf16[7,8,1536]{2,1,0:T(8,128)(2,1)S(1)}, bf16[7,8,1536]{2,1,0:T(8,128)(2,1)S(1)}, u32[]{:S(2)}, u32[]{:S(2)}) collective-permute-start(bf16[7,8,1536]{2,1,0:T(8,128)(2,1)S(1)} %get-tuple-element.164), channel_id=1, source_target_pairs={{0,16},{4,20},{8,24},{12,28},{16,0},{20,4},{24,8},{28,12},{1,17},{... | collective-permute-start | bytes 516104 | tf_op jit(solution)/shard_map/ppermute | solution.py:889
  187.9 3.4 %collective-permute-done.17.gx = bf16[12,8,1536]{2,1,0:T(8,128)(2,1)S(1)} collective-permute-done((bf16[12,8,1536]{2,1,0:T(8,128)(2,1)S(1)}, bf16[12,8,1536]{2,1,0:T(8,128)(2,1)S(1)}, u32[]{:S(2)}, u32[]{:S(2)}) %collective-permute-start.17) | collective-permute-done | bytes 294944 | tf_op jit(solution)/shard_map/ppermute | solution.py:889
  191.3 0.5 collective-permute-done.16.got_ref
  191.8 0.6 fold_last.3
  192.4 1.2 collective-permute-start.20
  193.6 4.7 %collective-permute-done.20.gx = bf16[6,8,1536]{2,1,0:T(8,128)(2,1)S(1)} collective-permute-done((bf16[6,8,1536]{2,1,0:T(8,128)(2,1)S(1)}, bf16[6,8,1536]{2,1,0:T(8,128)(2,1)S(1)}, u32[]{:S(2)}, u32[]{:S(2)}) %collective-permute-start.20) | collective-permute-done | bytes 147488 | tf_op jit(solution)/shard_map/ppermute | solution.py:889
  198.3 2.4 %feed_blocks.1 = (f32[384,768]{1,0:T(8,128)}, f32[96,3072]{1,0:T(8,128)}) custom-call(s32[8]{0:T(128)S(1)} %copy-done.7, bf16[12,8,1536]{2,1,0:T(8,128)(2,1)S(1)} %fold_last.2.me, bf16[12,8,1536]{2,1,0:T(8,128)(2,1)S(1)} %collective-permute-done.17.gx, bf16[12,8,1536]{2,1,0:T(8,128)(2,1)S(1)} %collective-permute-done.18.gc, ...), custom_call_target="tpu_custom_call" | custom-call | flops 50000 | bytes 200000 | tf_op jit(solution)/shard_map/feed_blocks/pallas_call | solution.py:717
  200.7 1.9 projection_blocks.1
  202.6 0.6 reduce
  (24 shorter events, 0.1 us)
Async XLA Ops:
  51.5 17.0 %collective-permute-start = (bf16[3072,384]{1,0:T(8,128)(2,1)}, bf16[3072,384]{1,0:T(8,128)(2,1)}, u32[]{:S(2)}, u32[]{:S(2)}) collective-permute-start(bf16[3072,384]{1,0:T(8,128)(2,1)} %down_give.1), channel_id=1, source_target_pairs={{0,1},{1,0},{2,3},{3,2},{4,5},{5,4},{6,7},{7,6},{8,9},{9,8},{10,11... | collective-permute-start | bytes 7077896 | tf_op jit(solution)/shard_map/ppermute | solution.py:889
  61.2 19.0 %collective-permute-start.1 = (bf16[768,1536]{1,0:T(8,128)(2,1)}, bf16[768,1536]{1,0:T(8,128)(2,1)}, u32[]{:S(2)}, u32[]{:S(2)}) collective-permute-start(bf16[768,1536]{1,0:T(8,128)(2,1)} %get-tuple-element.110), channel_id=1, source_target_pairs={{0,1},{1,0},{2,3},{3,2},{4,5},{5,4},{6,7},{7,6},{8,9},{9,8},{10,11... | collective-permute-start | bytes 7077896 | tf_op jit(solution)/shard_map/ppermute | solution.py:889
  61.2 53.7 %all-to-all-start = ((bf16[8,128,768]{2,1,0:T(8,128)(2,1)}), bf16[8,128,768]{2,1,0:T(8,128)(2,1)}, u32[]{:S(2)}, u32[]{:S(2)}) async-start(bf16[8,128,768]{2,1,0:T(8,128)(2,1)} %get-tuple-element.122), calls=%async_computation | async-start | bytes 3145728 | tf_op jit(solution)/shard_map/all_to_all | solution.py:900
  76.6 38.3 %collective-permute-start.2 = (bf16[24,8,1536]{2,1,0:T(8,128)(2,1)}, bf16[24,8,1536]{2,1,0:T(8,128)(2,1)}, u32[]{:S(2)}, u32[]{:S(2)}) collective-permute-start(bf16[24,8,1536]{2,1,0:T(8,128)(2,1)} %get-tuple-element.124), channel_id=1, source_target_pairs={{0,2},{1,3},{2,0},{3,1},{4,6},{5,7},{6,4},{7,5},{8,10},{9,11},{10,... | collective-permute-start | bytes 1769480 | tf_op jit(solution)/shard_map/ppermute | solution.py:889
  78.1 12.5 %copy-start = (bf16[1024,1536]{1,0:T(8,128)(2,1)S(1)}, bf16[1024,1536]{1,0:T(8,128)(2,1)}, u32[]{:S(2)}) copy-start(bf16[1024,1536]{1,0:T(8,128)(2,1)} %get-tuple-element.114.other_ref) | copy-start | bytes 9437188
  78.1 36.8 %collective-permute-start.3 = (bf16[24,8,1536]{2,1,0:T(8,128)(2,1)}, bf16[24,8,1536]{2,1,0:T(8,128)(2,1)}, u32[]{:S(2)}, u32[]{:S(2)}) collective-permute-start(bf16[24,8,1536]{2,1,0:T(8,128)(2,1)} %get-tuple-element.126), channel_id=1, source_target_pairs={{0,4},{4,0},{8,12},{12,8},{16,20},{20,16},{24,28},{28,24},{1,5},{5... | collective-permute-start | bytes 1769480 | tf_op jit(solution)/shard_map/ppermute | solution.py:889
  89.8 25.2 %collective-permute-start.4 = (bf16[24,8,1536]{2,1,0:T(8,128)(2,1)}, bf16[24,8,1536]{2,1,0:T(8,128)(2,1)}, u32[]{:S(2)}, u32[]{:S(2)}) collective-permute-start(bf16[24,8,1536]{2,1,0:T(8,128)(2,1)} %get-tuple-element.127), channel_id=1, source_target_pairs={{0,2},{1,3},{2,0},{3,1},{4,6},{5,7},{6,4},{7,5},{8,10},{9,11},{10,... | collective-permute-start | bytes 1769480 | tf_op jit(solution)/shard_map/ppermute | solution.py:889
  90.3 24.6 %collective-permute-start.5 = (bf16[24,8,1536]{2,1,0:T(8,128)(2,1)}, bf16[24,8,1536]{2,1,0:T(8,128)(2,1)}, u32[]{:S(2)}, u32[]{:S(2)}) collective-permute-start(bf16[24,8,1536]{2,1,0:T(8,128)(2,1)} %get-tuple-element.129), channel_id=1, source_target_pairs={{0,4},{4,0},{8,12},{12,8},{16,20},{20,16},{24,28},{28,24},{1,5},{5... | collective-permute-start | bytes 1769480 | tf_op jit(solution)/shard_map/ppermute | solution.py:889
  90.6 24.4 %copy-start.1 = (bf16[24,8,1536]{2,1,0:T(8,128)(2,1)S(1)}, bf16[24,8,1536]{2,1,0:T(8,128)(2,1)}, u32[]{:S(2)}) copy-start(bf16[24,8,1536]{2,1,0:T(8,128)(2,1)} %get-tuple-element.108.refs_0_) | copy-start | bytes 1769476
  90.6 24.4 %copy-start.2 = (bf16[24,8,1536]{2,1,0:T(8,128)(2,1)S(1)}, bf16[24,8,1536]{2,1,0:T(8,128)(2,1)}, u32[]{:S(2)}) copy-start(bf16[24,8,1536]{2,1,0:T(8,128)(2,1)} %get-tuple-element.125.refs_2_) | copy-start | bytes 1769476
  90.6 24.4 %copy-start.5 = (s32[8]{0:T(128)S(1)}, s32[8]{0:T(128)}, u32[]{:S(2)}) copy-start(s32[8]{0:T(128)} %stack.35.here_s) | copy-start | bytes 100
  115.0 1.1 copy-start.3
  116.1 1.1 copy-start.4
  127.1 4.6 %collective-permute-start.6 = (bf16[776,1536]{1,0:T(8,128)(2,1)S(1)}, bf16[776,1536]{1,0:T(8,128)(2,1)S(1)}, u32[]{:S(2)}, u32[]{:S(2)}) collective-permute-start(bf16[776,1536]{1,0:T(8,128)(2,1)S(1)} %proj_give.1), channel_id=1, source_target_pairs={{0,1},{1,0},{2,3},{3,2},{4,5},{5,4},{6,7},{7,6},{8,9},{9,8},{10,11... | collective-permute-start | bytes 7151624 | tf_op jit(solution)/shard_map/ppermute | solution.py:889
  127.2 15.8 %collective-permute-start.7 = (bf16[24,8,1536]{2,1,0:T(8,128)(2,1)S(1)}, bf16[24,8,1536]{2,1,0:T(8,128)(2,1)S(1)}, u32[]{:S(2)}, u32[]{:S(2)}) collective-permute-start(bf16[24,8,1536]{2,1,0:T(8,128)(2,1)S(1)} %get-tuple-element.139), channel_id=1, source_target_pairs={{0,4},{4,0},{8,12},{12,8},{16,20},{20,16},{24,28},{28,24},{1,5},{5... | collective-permute-start | bytes 1769480 | tf_op jit(solution)/shard_map/ppermute | solution.py:889
  129.0 16.2 %copy-start.6 = (s32[8]{0:T(128)S(1)}, s32[8]{0:T(128)}, u32[]{:S(2)}) copy-start(s32[8]{0:T(128)} %stack.35.here_s) | copy-start | bytes 100
  129.0 16.2 %collective-permute-start.8 = (bf16[24,8,1536]{2,1,0:T(8,128)(2,1)S(1)}, bf16[24,8,1536]{2,1,0:T(8,128)(2,1)S(1)}, u32[]{:S(2)}, u32[]{:S(2)}) collective-permute-start(bf16[24,8,1536]{2,1,0:T(8,128)(2,1)S(1)} %get-tuple-element.141), channel_id=1, source_target_pairs={{0,2},{1,3},{2,0},{3,1},{4,6},{5,7},{6,4},{7,5},{8,10},{9,11},{10,... | collective-permute-start | bytes 1769480 | tf_op jit(solution)/shard_map/ppermute | solution.py:889
  140.0 21.0 %collective-permute-start.10 = (bf16[25,8,1536]{2,1,0:T(8,128)(2,1)S(1)}, bf16[25,8,1536]{2,1,0:T(8,128)(2,1)S(1)}, u32[]{:S(2)}, u32[]{:S(2)}) collective-permute-start(bf16[25,8,1536]{2,1,0:T(8,128)(2,1)S(1)} %get-tuple-element.149), channel_id=1, source_target_pairs={{0,2},{1,3},{2,0},{3,1},{4,6},{5,7},{6,4},{7,5},{8,10},{9,11},{10,... | collective-permute-start | bytes 1843208 | tf_op jit(solution)/shard_map/ppermute | solution.py:889
  146.1 13.8 %collective-permute-start.9 = (bf16[24,8,1536]{2,1,0:T(8,128)(2,1)S(1)}, bf16[24,8,1536]{2,1,0:T(8,128)(2,1)S(1)}, u32[]{:S(2)}, u32[]{:S(2)}) collective-permute-start(bf16[24,8,1536]{2,1,0:T(8,128)(2,1)S(1)} %get-tuple-element.146), channel_id=1, source_target_pairs={{0,8},{4,12},{8,0},{12,4},{16,24},{20,28},{24,16},{28,20},{1,9},{5... | collective-permute-start | bytes 1769480 | tf_op jit(solution)/shard_map/ppermute | solution.py:889
  147.6 13.4 %collective-permute-start.11 = (bf16[24,8,1536]{2,1,0:T(8,128)(2,1)S(1)}, bf16[24,8,1536]{2,1,0:T(8,128)(2,1)S(1)}, u32[]{:S(2)}, u32[]{:S(2)}) collective-permute-start(bf16[24,8,1536]{2,1,0:T(8,128)(2,1)S(1)} %get-tuple-element.151), channel_id=1, source_target_pairs={{0,4},{4,0},{8,12},{12,8},{16,20},{20,16},{24,28},{28,24},{1,5},{5... | collective-permute-start | bytes 1769480 | tf_op jit(solution)/shard_map/ppermute | solution.py:889
  161.0 9.2 %copy-start.7 = (s32[8]{0:T(128)S(1)}, s32[8]{0:T(128)}, u32[]{:S(2)}) copy-start(s32[8]{0:T(128)} %stack.35.here_s) | copy-start | bytes 100
  161.8 8.3 %collective-permute-start.12 = (bf16[13,8,1536]{2,1,0:T(8,128)(2,1)S(1)}, bf16[13,8,1536]{2,1,0:T(8,128)(2,1)S(1)}, u32[]{:S(2)}, u32[]{:S(2)}) collective-permute-start(bf16[13,8,1536]{2,1,0:T(8,128)(2,1)S(1)} %get-tuple-element.155), channel_id=1, source_target_pairs={{0,4},{4,0},{8,12},{12,8},{16,20},{20,16},{24,28},{28,24},{1,5},{5... | collective-permute-start | bytes 958472 | tf_op jit(solution)/shard_map/ppermute | solution.py:889
  162.6 7.6 %collective-permute-start.13 = (bf16[12,8,1536]{2,1,0:T(8,128)(2,1)S(1)}, bf16[12,8,1536]{2,1,0:T(8,128)(2,1)S(1)}, u32[]{:S(2)}, u32[]{:S(2)}) collective-permute-start(bf16[12,8,1536]{2,1,0:T(8,128)(2,1)S(1)} %get-tuple-element.157), channel_id=1, source_target_pairs={{0,2},{1,3},{2,0},{3,1},{4,6},{5,7},{6,4},{7,5},{8,10},{9,11},{10,... | collective-permute-start | bytes 884744 | tf_op jit(solution)/shard_map/ppermute | solution.py:889
  170.9 13.0 %collective-permute-start.15 = (bf16[13,8,1536]{2,1,0:T(8,128)(2,1)S(1)}, bf16[13,8,1536]{2,1,0:T(8,128)(2,1)S(1)}, u32[]{:S(2)}, u32[]{:S(2)}) collective-permute-start(bf16[13,8,1536]{2,1,0:T(8,128)(2,1)S(1)} %get-tuple-element.162), channel_id=1, source_target_pairs={{0,8},{4,12},{8,0},{12,4},{16,24},{20,28},{24,16},{28,20},{1,9},{5... | collective-permute-start | bytes 958472 | tf_op jit(solution)/shard_map/ppermute | solution.py:889
  171.9 11.0 %collective-permute-start.14 = (bf16[12,8,1536]{2,1,0:T(8,128)(2,1)S(1)}, bf16[12,8,1536]{2,1,0:T(8,128)(2,1)S(1)}, u32[]{:S(2)}, u32[]{:S(2)}) collective-permute-start(bf16[12,8,1536]{2,1,0:T(8,128)(2,1)S(1)} %get-tuple-element.160), channel_id=1, source_target_pairs={{0,16},{4,20},{8,24},{12,28},{16,0},{20,4},{24,8},{28,12},{1,17},{... | collective-permute-start | bytes 884744 | tf_op jit(solution)/shard_map/ppermute | solution.py:889
  184.5 6.8 %collective-permute-start.17 = (bf16[12,8,1536]{2,1,0:T(8,128)(2,1)S(1)}, bf16[12,8,1536]{2,1,0:T(8,128)(2,1)S(1)}, u32[]{:S(2)}, u32[]{:S(2)}) collective-permute-start(bf16[12,8,1536]{2,1,0:T(8,128)(2,1)S(1)} %fold_last.2.me), channel_id=1, source_target_pairs={{0,2},{1,3},{2,0},{3,1},{4,6},{5,7},{6,4},{7,5},{8,10},{9,11},{10,... | collective-permute-start | bytes 884744 | tf_op jit(solution)/shard_map/ppermute | solution.py:889
  185.3 6.5 %collective-permute-start.16 = (bf16[7,8,1536]{2,1,0:T(8,128)(2,1)S(1)}, bf16[7,8,1536]{2,1,0:T(8,128)(2,1)S(1)}, u32[]{:S(2)}, u32[]{:S(2)}) collective-permute-start(bf16[7,8,1536]{2,1,0:T(8,128)(2,1)S(1)} %get-tuple-element.164), channel_id=1, source_target_pairs={{0,16},{4,20},{8,24},{12,28},{16,0},{20,4},{24,8},{28,12},{1,17},{... | collective-permute-start | bytes 516104 | tf_op jit(solution)/shard_map/ppermute | solution.py:889
  187.9 10.3 %collective-permute-start.18 = (bf16[12,8,1536]{2,1,0:T(8,128)(2,1)S(1)}, bf16[12,8,1536]{2,1,0:T(8,128)(2,1)S(1)}, u32[]{:S(2)}, u32[]{:S(2)}) collective-permute-start(bf16[12,8,1536]{2,1,0:T(8,128)(2,1)S(1)} %fold_last.2.me), channel_id=1, source_target_pairs={{0,1},{1,0},{2,3},{3,2},{4,5},{5,4},{6,7},{7,6},{8,9},{9,8},{10,11... | collective-permute-start | bytes 884744 | tf_op jit(solution)/shard_map/ppermute | solution.py:889
  191.3 6.9 %collective-permute-start.19 = (bf16[12,8,1536]{2,1,0:T(8,128)(2,1)S(1)}, bf16[12,8,1536]{2,1,0:T(8,128)(2,1)S(1)}, u32[]{:S(2)}, u32[]{:S(2)}) collective-permute-start(bf16[12,8,1536]{2,1,0:T(8,128)(2,1)S(1)} %collective-permute-done.17.gx), channel_id=1, source_target_pairs={{0,1},{1,0},{2,3},{3,2},{4,5},{5,4},{6,7},{7,6},{8,9},{9,8},{10,11... | collective-permute-start | bytes 884744 | tf_op jit(solution)/shard_map/ppermute | solution.py:889
  192.4 5.8 %collective-permute-start.20 = (bf16[6,8,1536]{2,1,0:T(8,128)(2,1)S(1)}, bf16[6,8,1536]{2,1,0:T(8,128)(2,1)S(1)}, u32[]{:S(2)}, u32[]{:S(2)}) collective-permute-start(bf16[6,8,1536]{2,1,0:T(8,128)(2,1)S(1)} %get-tuple-element.165.me), channel_id=1, source_target_pairs={{0,2},{1,3},{2,0},{3,1},{4,6},{5,7},{6,4},{7,5},{8,10},{9,11},{10,... | collective-permute-start | bytes 442376 | tf_op jit(solution)/shard_map/ppermute | solution.py:889
  193.6 7.1 %collective-permute-start.21 = (bf16[6,8,1536]{2,1,0:T(8,128)(2,1)S(1)}, bf16[6,8,1536]{2,1,0:T(8,128)(2,1)S(1)}, u32[]{:S(2)}, u32[]{:S(2)}) collective-permute-start(bf16[6,8,1536]{2,1,0:T(8,128)(2,1)S(1)} %get-tuple-element.165.me), channel_id=1, source_target_pairs={{0,1},{1,0},{2,3},{3,2},{4,5},{5,4},{6,7},{7,6},{8,9},{9,8},{10,11... | collective-permute-start | bytes 442376 | tf_op jit(solution)/shard_map/ppermute | solution.py:889
  198.2 2.4 %collective-permute-start.22 = (bf16[6,8,1536]{2,1,0:T(8,128)(2,1)S(1)}, bf16[6,8,1536]{2,1,0:T(8,128)(2,1)S(1)}, u32[]{:S(2)}, u32[]{:S(2)}) collective-permute-start(bf16[6,8,1536]{2,1,0:T(8,128)(2,1)S(1)} %collective-permute-done.20.gx), channel_id=1, source_target_pairs={{0,1},{1,0},{2,3},{3,2},{4,5},{5,4},{6,7},{7,6},{8,9},{9,8},{10,11... | collective-permute-start | bytes 442376 | tf_op jit(solution)/shard_map/ppermute | solution.py:889

commit v10 on v9

--- a/solution.py
+++ b/solution.py
@@ -592,7 +592,7 @@
         8 * rows * width * width * 2,
         40e6,
         (*grads_inner, gres, w_up, w_up, n_attn, spread, table, w_out, qkv, probs),
-        40, 0, (1,), (0, 1),
+        40, 0, (1,), (0, 1, 3, 4, 8),
     )
 
 
@@ -666,7 +666,7 @@
             give, "proj_give", (4,), (here,), in_specs,
             pl.BlockSpec((width + 8, part), lambda i, *_: (0, i)),
             shaped((width + 8, 4 * part), BF16),
-            [pltpu.VMEM((width, part), F32)], flops, 9e6, args, 20, 0, (0,), (3,),
+            [pltpu.VMEM((width, part), F32)], flops, 9e6, args, 20, 0, (0,), (0, 2, 3),
         )
     return call(
         own, "proj_own", (4,), (here,),
@@ -677,7 +677,7 @@
         ],
         [shaped((8 * pieces + extra, 8, 4 * part), BF16) for extra in (1, 1, 0, 0)],
         [pltpu.VMEM((width, part), F32), pltpu.VMEM((4, 2, 2, 2, pieces, 8, part), F32)],
-        flops, 11e6, args + [got], 24, 1, (0, 1, 2, 3), (3,),
+        flops, 11e6, args + [got], 24, 1, (0, 1, 2, 3), (0, 2, 3),
     )
 
 
@@ -696,7 +696,7 @@
         ],
         pl.BlockSpec((rows_step, width), lambda i: (i, 0)),
         shaped((rows, width), BF16), [], 6 * rows * width * width, 13e6,
-        (grad_mixed, w_qkv, grad_resid), 20,
+        (grad_mixed, w_qkv, grad_resid), 20, 0, (), (1,),
     )
 
 
@@ -947,7 +947,7 @@
     pieces = width // 32 // 8
 
     qkv, probs, attended, n_attn, spread, sid = attention_forward(
-        tokens, w_qkv, w_out, table, bucket, lengths, wide_count // batches, span, 4 * span
+        tokens, w_qkv, w_out, table, bucket, lengths, wide_count // batches, span, 2 * span
     )
     active, slope, hidden_t, sent, gres, grad_second, vec_ffn = feed_forward(
         n_attn, w_up, w_down, table, sid, slots, pairing, targets, batches, 2 * span

time: 207 us -> 204 us (0.986)
  Pallas kernels: 143 us -> 137 us
  waiting for transfers between devices: 25.6 us -> 28.3 us
    pallas_call x11, Pallas kernels: 131 us -> 125 us  [call(): pl.pallas_call(kernel, grid_spec=pltpu.PrefetchScalarGridSpec(num_scalar_...]
    ppermute x23, waiting for transfers between devices: 25.6 us -> 28.3 us  [swap(): lax.ppermute(item, axis, [(index, index ^ step) for index in range(count)])]
  transfers between devices with their start and end apart: 24 -> 24, of which waited for: 10 -> 10; matrix products, arithmetic and copies ran while one was open for 0% -> 0% of each run, Pallas kernels for 39% -> 37%
where the time goes in v10:
time: 204 us; the launch traced here: 202 us
  Pallas kernels  137 us (67%)
  starting transfers between devices  32.1 us (16%)
  waiting for transfers between devices  28.3 us (14%)
  local copies, waits for them, and re-layouts  3.05 us (1%)
    pallas_call x11, Pallas kernels, call(): pl.pallas_call(kernel, grid_spec=pltpu.PrefetchScalarGridSpec(num_scalar_...  125 us
    ppermute x23, waiting for transfers between devices, swap(): lax.ppermute(item, axis, [(index, index ^ step) for index in range(count)])  28.3 us
    ppermute x23, starting transfers between devices, swap(): lax.ppermute(item, axis, [(index, index ^ step) for index in range(count)])  24.8 us
    pallas_call x10, Pallas kernels, small_call(): pl.pallas_call(kernel, in_specs=[pl.BlockSpec(memory_space=pltpu.SMEM)] +...  11.4 us
    all_to_all x1, starting transfers between devices, regroup_rows(): got = lax.all_to_all(sent, 'wide', split_axis=0, concat_axis=0, tiled=True)  7.31 us
  transfers between devices with their start and end apart: 24, of which 10 were waited for; matrix products, arithmetic and copies ran while one was open for 0% of the time, Pallas kernels for 37%

profile of v10, /device:TPU:0, one launch (start us, length us, event | category | flops | bytes accessed | tf_op | source)
XLA Modules:
  0.0 202.0 jit_solution(7145830902781050841)
XLA Ops:
  0.7 0.9 vector_table.1.tab_ref
  1.6 16.6 %attn_fwd.1 = (bf16[1024,2304]{1,0:T(8,128)(2,1)}, bf16[8,6,256,128]{3,2,1,0:T(8,128)(2,1)}, bf16[1024,768]{1,0:T(8,128)(2,1)}, f32[1024,768]{1,0:T(8,128)}, f32...) custom-call(s32[8]{0:T(128)} %slots_s.1, s32[26]{0:T(128)} %lengths_s.1, bf16[1024,768]{1,0:T(8,128)(2,1)} %x_ref.5, ...), custom_call_target="tpu_custom_call" | custom-call | flops 483183808 | bytes 1500000 | tf_op jit(solution)/shard_map/attn_fwd/pallas_call | solution.py:72
  18.1 24.4 %ffn_fwd.1 = (bf16[1024,3072]{1,0:T(8,128)(2,1)}, bf16[1024,3072]{1,0:T(8,128)(2,1)}, bf16[768,1024]{1,0:T(8,128)(2,1)S(1)}, bf16[8,128,768]{2,1,0:T(8,128)(2,1)...) custom-call(s32[8]{0:T(128)} %slots_s.1, s32[1,26]{1,0:T(1,128)} %pairing_s.1, ...), custom_call_target="tpu_custom_call" | custom-call | flops 966367616 | bytes 2000000 | tf_op jit(solution)/shard_map/ffn_fwd/pallas_call | solution.py:72
  42.5 0.6 stack.35.here_s
  43.1 7.7 %down_give.1 = bf16[3072,384]{1,0:T(8,128)(2,1)} custom-call(s32[8]{0:T(128)} %stack.35.here_s, bf16[1024,3072]{1,0:T(8,128)(2,1)} %get-tuple-element.101.act_ref, bf16[1024,768]{1,0:T(8,128)(2,1)S(1)} %get-tuple-element.102.gs_ref), custom_call_target="tpu_custom_call" | custom-call | flops 120795952 | bytes 450000 | tf_op jit(solution)/shard_map/down_give/pallas_call | solution.py:72
  50.8 0.5 collective-permute-start
  51.3 9.2 %up_give.1 = (bf16[768,1536]{1,0:T(8,128)(2,1)}, bf16[1024,1536]{1,0:T(8,128)(2,1)}, f32[1,1536]{1,0:T(1,128)S(1)}) custom-call(s32[8]{0:T(128)} %stack.35.here_s, bf16[1024,768]{1,0:T(8,128)(2,1)S(1)} %get-tuple-element.102.gs_ref, bf16[1024,3072]{1,0:T(8,128)(2,1)} %get-tuple-element.104.dg_ref, bf16[768,1024]{1,0:T(8,128)(2,1)S(1)} %get-tuple-element.105.ht_ref, ...), custom_call_target="tpu_custom_call" | custom-call | flops 241591904 | bytes 800000 | tf_op jit(solution)/shard_map/up_give/pallas_call | solution.py:72
  60.5 0.0 collective-permute-start.1
  60.5 7.3 %all-to-all-start = ((bf16[8,128,768]{2,1,0:T(8,128)(2,1)}), bf16[8,128,768]{2,1,0:T(8,128)(2,1)}, u32[]{:S(2)}, u32[]{:S(2)}) async-start(bf16[8,128,768]{2,1,0:T(8,128)(2,1)} %get-tuple-element.122), calls=%async_computation | async-start | bytes 3145728 | tf_op jit(solution)/shard_map/all_to_all | solution.py:900
  67.8 0.0 collective-permute-done.got_ref
  67.8 8.2 %down_own.1 = (bf16[24,8,1536]{2,1,0:T(8,128)(2,1)}, bf16[24,8,1536]{2,1,0:T(8,128)(2,1)}, bf16[24,8,1536]{2,1,0:T(8,128)(2,1)}, bf16[24,8,1536]{2,1,0:T(8,128)(2,1)}) custom-call(s32[8]{0:T(128)} %stack.35.here_s, bf16[1024,3072]{1,0:T(8,128)(2,1)} %get-tuple-element.101.act_ref, bf16[1024,768]{1,0:T(8,128)(2,1)S(1)} %get-tuple-element.102.gs_ref, ...), custom_call_target="tpu_custom_call" | custom-call | flops 120795952 | bytes 550000 | tf_op jit(solution)/shard_map/down_own/pallas_call | solution.py:72
  76.0 1.5 collective-permute-start.2
  77.5 2.1 %collective-permute-start.3 = (bf16[24,8,1536]{2,1,0:T(8,128)(2,1)}, bf16[24,8,1536]{2,1,0:T(8,128)(2,1)}, u32[]{:S(2)}, u32[]{:S(2)}) collective-permute-start(bf16[24,8,1536]{2,1,0:T(8,128)(2,1)} %get-tuple-element.126), channel_id=1, source_target_pairs={{0,4},{4,0},{8,12},{12,8},{16,20},{20,16},{24,28},{28,24},{1,5},{5... | collective-permute-start | bytes 1769480 | tf_op jit(solution)/shard_map/ppermute | solution.py:889
  79.6 9.8 %up_own.1 = (bf16[24,8,1536]{2,1,0:T(8,128)(2,1)}, bf16[24,8,1536]{2,1,0:T(8,128)(2,1)}, bf16[24,8,1536]{2,1,0:T(8,128)(2,1)}, bf16[24,8,1536]{2,1,0:T(8,128)(2,...) custom-call(s32[8]{0:T(128)} %stack.35.here_s, bf16[1024,768]{1,0:T(8,128)(2,1)S(1)} %get-tuple-element.102.gs_ref, ...), custom_call_target="tpu_custom_call" | custom-call | flops 241591904 | bytes 800000 | tf_op jit(solution)/shard_map/up_own/pallas_call | solution.py:72
  89.4 0.5 collective-permute-start.4
  89.9 0.5 collective-permute-start.5
  90.4 0.0 copy-start.9
  90.4 21.5 %attn_bwd.1 = (f32[1024,768]{1,0:T(8,128)}, bf16[1024,768]{1,0:T(8,128)(2,1)S(1)}, bf16[1024,2304]{1,0:T(8,128)(2,1)}, f32[8,768]{1,0:T(8,128)S(1)}) custom-call(s32[8]{0:T(128)} %stack.35.here_s, bf16[1024,1536]{1,0:T(8,128)(2,1)S(1)} %get-tuple-element.113.gi_ref, bf16[1024,1536]{1,0:T(8,128)(2,1)S(1)} %copy-done.4, ...), custom_call_target="tpu_custom_call" | custom-call | flops 483183808 | bytes 2000000 | tf_op jit(solution)/shard_map/attn_bwd/pallas_call | solution.py:72
  112.0 0.0 all-to-all-done
  112.0 0.0 collective-permute-done.3.refs_3_
  112.0 1.5 collective-permute-done.5.refs_7_
  113.5 0.0 copy-start.7
  113.5 1.1 copy-done.7
  114.6 1.1 copy-done.8
  115.7 2.3 %fold_second.2 = (bf16[24,8,1536]{2,1,0:T(8,128)(2,1)S(1)}, bf16[24,8,1536]{2,1,0:T(8,128)(2,1)S(1)}, bf16[24,8,1536]{2,1,0:T(8,128)(2,1)S(1)}, bf16[24,8,1536]{2,1,0:T(8,128)(2,1)S(1)}) custom-call(s32[8]{0:T(128)S(1)} %copy-done.9, bf16[24,8,1536]{2,1,0:T(8,128)(2,1)S(1)} %copy-done.5, bf16[24,8,1536]{2,1,0:T(8,128)(2,1)} %collective-permute-done.2.refs_1_, ...), custom_call_target="tpu_custom_call" | custom-call | flops 50000 | bytes 200000 | tf_op jit(solution)/shard_map/fold_second/pallas_call | solution.py:717
  118.0 0.3 copy-done.2
  118.2 6.8 %proj_give.1 = bf16[776,1536]{1,0:T(8,128)(2,1)S(1)} custom-call(s32[8]{0:T(128)} %stack.35.here_s, bf16[1024,768]{1,0:T(8,128)(2,1)S(1)} %copy-done.1, bf16[1024,2304]{1,0:T(8,128)(2,1)} %get-tuple-element.143.gm_ref, bf16[1024,768]{1,0:T(8,128)(2,1)S(1)} %copy-done.2, bf16[1024,768]{1,0:T(8,128)(2,1)S(1)} %get-tuple-element.133.gb_ref, ...), custom_call_target="tpu_custom_call" | custom-call | flops 120795952 | bytes 450000 | tf_op jit(solution)/shard_map/proj_give/pallas_call | solution.py:72
  125.0 0.1 collective-permute-start.6
  125.1 0.1 collective-permute-start.7
  125.2 1.5 collective-permute-start.8
  126.7 2.9 %collective-permute-done.6.got_ref = bf16[776,1536]{1,0:T(8,128)(2,1)S(1)} collective-permute-done((bf16[776,1536]{1,0:T(8,128)(2,1)S(1)}, bf16[776,1536]{1,0:T(8,128)(2,1)S(1)}, u32[]{:S(2)}, u32[]{:S(2)}) %collective-permute-start.6) | collective-permute-done | bytes 2383904 | tf_op jit(solution)/shard_map/ppermute | solution.py:889
  129.6 7.6 %proj_own.1 = (bf16[25,8,1536]{2,1,0:T(8,128)(2,1)S(1)}, bf16[25,8,1536]{2,1,0:T(8,128)(2,1)S(1)}, bf16[24,8,1536]{2,1,0:T(8,128)(2,1)S(1)}, bf16[24,8,1536]{2,1,0:T(8,128)(2,1)S(1)}) custom-call(s32[8]{0:T(128)} %stack.35.here_s, bf16[1024,768]{1,0:T(8,128)(2,1)S(1)} %copy-done.1, bf16[1024,2304]{1,0:T(8,128)(2,1)} %get-tuple-element.143.gm_ref, ...), custom_call_target="tpu_custom_call" | custom-call | flops 120795952 | bytes 550000 | tf_op jit(solution)/shard_map/proj_own/pallas_call | solution.py:72
  137.3 1.6 collective-permute-start.10
  138.8 2.0 collective-permute-done.7.refs_1_
  140.8 0.6 collective-permute-done.8.refs_3_
  141.4 0.8 fold_third.2
  142.3 2.0 collective-permute-start.9
  144.2 1.9 collective-permute-start.11
  146.2 7.1 %input_grad.1 = bf16[1024,768]{1,0:T(8,128)(2,1)} custom-call(bf16[1024,2304]{1,0:T(8,128)(2,1)} %get-tuple-element.143.gm_ref, bf16[768,2304]{1,0:T(8,128)(2,1)S(1)} %copy-done, f32[1024,768]{1,0:T(8,128)} %get-tuple-element.144.gr_ref), custom_call_target="tpu_custom_call" | custom-call | flops 181193936 | bytes 650000 | tf_op jit(solution)/shard_map/input_grad/pallas_call | solution.py:72
  153.2 3.4 %collective-permute-done.9.got_ref = bf16[24,8,1536]{2,1,0:T(8,128)(2,1)S(1)} collective-permute-done((bf16[24,8,1536]{2,1,0:T(8,128)(2,1)S(1)}, bf16[24,8,1536]{2,1,0:T(8,128)(2,1)S(1)}, u32[]{:S(2)}, u32[]{:S(2)}) %collective-permute-start.9) | collective-permute-done | bytes 589856 | tf_op jit(solution)/shard_map/ppermute | solution.py:889
  156.7 0.7 fold_fourth.2
  157.4 0.8 collective-permute-done.11.refs_3_
  158.1 0.0 collective-permute-done.10.refs_1_
  158.1 0.8 fold_second.3
  159.0 1.5 collective-permute-start.12
  160.5 0.6 collective-permute-start.13
  161.1 6.1 %copied.1 = bf16[1024,768]{1,0:T(8,128)(2,1)} custom-call(s32[8]{0:T(128)} %stack.35.here_s, bf16[1024,768]{1,0:T(8,128)(2,1)} %bitcast.8.in_ref), custom_call_target="tpu_custom_call" | custom-call | bytes 150000 | tf_op jit(solution)/shard_map/copied/pallas_call | solution.py:72
  167.2 0.0 collective-permute-done.13.refs_3_
  167.2 0.7 fold_third.3
  167.9 1.1 collective-permute-start.15
  169.0 5.1 %collective-permute-start.14 = (bf16[12,8,1536]{2,1,0:T(8,128)(2,1)S(1)}, bf16[12,8,1536]{2,1,0:T(8,128)(2,1)S(1)}, u32[]{:S(2)}, u32[]{:S(2)}) collective-permute-start(bf16[12,8,1536]{2,1,0:T(8,128)(2,1)S(1)} %get-tuple-element.160), channel_id=1, source_target_pairs={{0,16},{4,20},{8,24},{12,28},{16,0},{20,4},{24,8},{28,12},{1,17},{... | collective-permute-start | bytes 884744 | tf_op jit(solution)/shard_map/ppermute | solution.py:889
  174.1 7.6 %collective-permute-done.14.got_ref = bf16[12,8,1536]{2,1,0:T(8,128)(2,1)S(1)} collective-permute-done((bf16[12,8,1536]{2,1,0:T(8,128)(2,1)S(1)}, bf16[12,8,1536]{2,1,0:T(8,128)(2,1)S(1)}, u32[]{:S(2)}, u32[]{:S(2)}) %collective-permute-start.14) | collective-permute-done | bytes 294944 | tf_op jit(solution)/shard_map/ppermute | solution.py:889
  181.6 0.6 fold_last.2.me
  182.3 0.6 fold_fourth.3
  182.9 1.1 collective-permute-start.17
  184.0 2.0 %collective-permute-start.16 = (bf16[7,8,1536]{2,1,0:T(8,128)(2,1)S(1)}, bf16[7,8,1536]{2,1,0:T(8,128)(2,1)S(1)}, u32[]{:S(2)}, u32[]{:S(2)}) collective-permute-start(bf16[7,8,1536]{2,1,0:T(8,128)(2,1)S(1)} %get-tuple-element.164), channel_id=1, source_target_pairs={{0,16},{4,20},{8,24},{12,28},{16,0},{20,4},{24,8},{28,12},{1,17},{... | collective-permute-start | bytes 516104 | tf_op jit(solution)/shard_map/ppermute | solution.py:889
  186.0 3.7 %collective-permute-done.17.gx = bf16[12,8,1536]{2,1,0:T(8,128)(2,1)S(1)} collective-permute-done((bf16[12,8,1536]{2,1,0:T(8,128)(2,1)S(1)}, bf16[12,8,1536]{2,1,0:T(8,128)(2,1)S(1)}, u32[]{:S(2)}, u32[]{:S(2)}) %collective-permute-start.17) | collective-permute-done | bytes 294944 | tf_op jit(solution)/shard_map/ppermute | solution.py:889
  189.7 1.6 collective-permute-done.16.got_ref
  191.3 0.6 fold_last.3
  191.9 1.1 collective-permute-start.20
  193.0 4.1 %collective-permute-done.20.gx = bf16[6,8,1536]{2,1,0:T(8,128)(2,1)S(1)} collective-permute-done((bf16[6,8,1536]{2,1,0:T(8,128)(2,1)S(1)}, bf16[6,8,1536]{2,1,0:T(8,128)(2,1)S(1)}, u32[]{:S(2)}, u32[]{:S(2)}) %collective-permute-start.20) | collective-permute-done | bytes 147488 | tf_op jit(solution)/shard_map/ppermute | solution.py:889
  197.1 2.4 %feed_blocks.1 = (f32[384,768]{1,0:T(8,128)}, f32[96,3072]{1,0:T(8,128)}) custom-call(s32[8]{0:T(128)S(1)} %copy-done.11, bf16[12,8,1536]{2,1,0:T(8,128)(2,1)S(1)} %fold_last.2.me, bf16[12,8,1536]{2,1,0:T(8,128)(2,1)S(1)} %collective-permute-done.17.gx, bf16[12,8,1536]{2,1,0:T(8,128)(2,1)S(1)} %collective-permute-done.18.gc, ...), custom_call_target="tpu_custom_call" | custom-call | flops 50000 | bytes 200000 | tf_op jit(solution)/shard_map/feed_blocks/pallas_call | solution.py:717
  199.5 1.9 projection_blocks.1
  201.4 0.6 reduce
  (37 shorter events, 0.1 us)
Async XLA Ops:
  50.8 17.0 %collective-permute-start = (bf16[3072,384]{1,0:T(8,128)(2,1)}, bf16[3072,384]{1,0:T(8,128)(2,1)}, u32[]{:S(2)}, u32[]{:S(2)}) collective-permute-start(bf16[3072,384]{1,0:T(8,128)(2,1)} %down_give.1), channel_id=1, source_target_pairs={{0,1},{1,0},{2,3},{3,2},{4,5},{5,4},{6,7},{7,6},{8,9},{9,8},{10,11... | collective-permute-start | bytes 7077896 | tf_op jit(solution)/shard_map/ppermute | solution.py:889
  60.5 19.1 %collective-permute-start.1 = (bf16[768,1536]{1,0:T(8,128)(2,1)}, bf16[768,1536]{1,0:T(8,128)(2,1)}, u32[]{:S(2)}, u32[]{:S(2)}) collective-permute-start(bf16[768,1536]{1,0:T(8,128)(2,1)} %get-tuple-element.110), channel_id=1, source_target_pairs={{0,1},{1,0},{2,3},{3,2},{4,5},{5,4},{6,7},{7,6},{8,9},{9,8},{10,11... | collective-permute-start | bytes 7077896 | tf_op jit(solution)/shard_map/ppermute | solution.py:889
  60.5 51.4 %all-to-all-start = ((bf16[8,128,768]{2,1,0:T(8,128)(2,1)}), bf16[8,128,768]{2,1,0:T(8,128)(2,1)}, u32[]{:S(2)}, u32[]{:S(2)}) async-start(bf16[8,128,768]{2,1,0:T(8,128)(2,1)} %get-tuple-element.122), calls=%async_computation | async-start | bytes 3145728 | tf_op jit(solution)/shard_map/all_to_all | solution.py:900
  76.0 36.0 %collective-permute-start.2 = (bf16[24,8,1536]{2,1,0:T(8,128)(2,1)}, bf16[24,8,1536]{2,1,0:T(8,128)(2,1)}, u32[]{:S(2)}, u32[]{:S(2)}) collective-permute-start(bf16[24,8,1536]{2,1,0:T(8,128)(2,1)} %get-tuple-element.124), channel_id=1, source_target_pairs={{0,2},{1,3},{2,0},{3,1},{4,6},{5,7},{6,4},{7,5},{8,10},{9,11},{10,... | collective-permute-start | bytes 1769480 | tf_op jit(solution)/shard_map/ppermute | solution.py:889
  77.5 12.9 %slice-start = ((s8[4718592]{0:T(1024)(128)(4,1)}), s8[4194304]{0:T(1024)(128)(4,1)S(1)}, s32[]{:S(2)}) async-start(s8[4718592]{0:T(1024)(128)(4,1)} %bitcast.17), calls=%async_computation.1 | async-start | bytes 8388608
  77.5 12.9 %slice-start.1 = ((s8[4718592]{0:T(1024)(128)(4,1)}), s8[524288]{0:T(1024)(128)(4,1)S(1)}, s32[]{:S(2)}) async-start(s8[4718592]{0:T(1024)(128)(4,1)} %bitcast.17), calls=%async_computation.2 | async-start | bytes 1048576
  77.5 12.9 %copy-start.3 = (bf16[768,768]{1,0:T(8,128)(2,1)S(1)}, bf16[768,768]{1,0:T(8,128)(2,1)}, u32[]{:S(2)}) copy-start(bf16[768,768]{1,0:T(8,128)(2,1)} %wo_ref.3) | copy-start | bytes 3538948
  77.5 12.9 %copy-start.4 = (bf16[1024,1536]{1,0:T(8,128)(2,1)S(1)}, bf16[1024,1536]{1,0:T(8,128)(2,1)}, u32[]{:S(2)}) copy-start(bf16[1024,1536]{1,0:T(8,128)(2,1)} %get-tuple-element.114.other_ref) | copy-start | bytes 9437188
  77.5 34.5 %collective-permute-start.3 = (bf16[24,8,1536]{2,1,0:T(8,128)(2,1)}, bf16[24,8,1536]{2,1,0:T(8,128)(2,1)}, u32[]{:S(2)}, u32[]{:S(2)}) collective-permute-start(bf16[24,8,1536]{2,1,0:T(8,128)(2,1)} %get-tuple-element.126), channel_id=1, source_target_pairs={{0,4},{4,0},{8,12},{12,8},{16,20},{20,16},{24,28},{28,24},{1,5},{5... | collective-permute-start | bytes 1769480 | tf_op jit(solution)/shard_map/ppermute | solution.py:889
  89.4 22.6 %collective-permute-start.4 = (bf16[24,8,1536]{2,1,0:T(8,128)(2,1)}, bf16[24,8,1536]{2,1,0:T(8,128)(2,1)}, u32[]{:S(2)}, u32[]{:S(2)}) collective-permute-start(bf16[24,8,1536]{2,1,0:T(8,128)(2,1)} %get-tuple-element.127), channel_id=1, source_target_pairs={{0,2},{1,3},{2,0},{3,1},{4,6},{5,7},{6,4},{7,5},{8,10},{9,11},{10,... | collective-permute-start | bytes 1769480 | tf_op jit(solution)/shard_map/ppermute | solution.py:889
  89.9 23.6 %collective-permute-start.5 = (bf16[24,8,1536]{2,1,0:T(8,128)(2,1)}, bf16[24,8,1536]{2,1,0:T(8,128)(2,1)}, u32[]{:S(2)}, u32[]{:S(2)}) collective-permute-start(bf16[24,8,1536]{2,1,0:T(8,128)(2,1)} %get-tuple-element.129), channel_id=1, source_target_pairs={{0,4},{4,0},{8,12},{12,8},{16,20},{20,16},{24,28},{28,24},{1,5},{5... | collective-permute-start | bytes 1769480 | tf_op jit(solution)/shard_map/ppermute | solution.py:889
  90.4 23.1 %copy-start.5 = (bf16[24,8,1536]{2,1,0:T(8,128)(2,1)S(1)}, bf16[24,8,1536]{2,1,0:T(8,128)(2,1)}, u32[]{:S(2)}) copy-start(bf16[24,8,1536]{2,1,0:T(8,128)(2,1)} %get-tuple-element.108.refs_0_) | copy-start | bytes 1769476
  90.4 23.1 %copy-start.6 = (bf16[24,8,1536]{2,1,0:T(8,128)(2,1)S(1)}, bf16[24,8,1536]{2,1,0:T(8,128)(2,1)}, u32[]{:S(2)}) copy-start(bf16[24,8,1536]{2,1,0:T(8,128)(2,1)} %get-tuple-element.125.refs_2_) | copy-start | bytes 1769476
  90.4 23.1 %copy-start.9 = (s32[8]{0:T(128)S(1)}, s32[8]{0:T(128)}, u32[]{:S(2)}) copy-start(s32[8]{0:T(128)} %stack.35.here_s) | copy-start | bytes 100
  113.5 1.1 copy-start.7
  114.6 1.1 copy-start.8
  115.7 2.3 %copy-start.1 = (bf16[1024,768]{1,0:T(8,128)(2,1)S(1)}, bf16[1024,768]{1,0:T(8,128)(2,1)}, u32[]{:S(2)}) copy-start(bf16[1024,768]{1,0:T(8,128)(2,1)} %x_ref.5) | copy-start | bytes 4718596
  115.7 2.6 %copy-start.2 = (bf16[1024,768]{1,0:T(8,128)(2,1)S(1)}, bf16[1024,768]{1,0:T(8,128)(2,1)}, u32[]{:S(2)}) copy-start(bf16[1024,768]{1,0:T(8,128)(2,1)} %get-tuple-element.132.att_ref) | copy-start | bytes 4718596
  125.0 4.6 %collective-permute-start.6 = (bf16[776,1536]{1,0:T(8,128)(2,1)S(1)}, bf16[776,1536]{1,0:T(8,128)(2,1)S(1)}, u32[]{:S(2)}, u32[]{:S(2)}) collective-permute-start(bf16[776,1536]{1,0:T(8,128)(2,1)S(1)} %proj_give.1), channel_id=1, source_target_pairs={{0,1},{1,0},{2,3},{3,2},{4,5},{5,4},{6,7},{7,6},{8,9},{9,8},{10,11... | collective-permute-start | bytes 7151624 | tf_op jit(solution)/shard_map/ppermute | solution.py:889
  125.1 15.7 %collective-permute-start.7 = (bf16[24,8,1536]{2,1,0:T(8,128)(2,1)S(1)}, bf16[24,8,1536]{2,1,0:T(8,128)(2,1)S(1)}, u32[]{:S(2)}, u32[]{:S(2)}) collective-permute-start(bf16[24,8,1536]{2,1,0:T(8,128)(2,1)S(1)} %get-tuple-element.139), channel_id=1, source_target_pairs={{0,4},{4,0},{8,12},{12,8},{16,20},{20,16},{24,28},{28,24},{1,5},{5... | collective-permute-start | bytes 1769480 | tf_op jit(solution)/shard_map/ppermute | solution.py:889
  125.2 16.2 %copy-start.10 = (s32[8]{0:T(128)S(1)}, s32[8]{0:T(128)}, u32[]{:S(2)}) copy-start(s32[8]{0:T(128)} %stack.35.here_s) | copy-start | bytes 100
  125.2 16.2 %collective-permute-start.8 = (bf16[24,8,1536]{2,1,0:T(8,128)(2,1)S(1)}, bf16[24,8,1536]{2,1,0:T(8,128)(2,1)S(1)}, u32[]{:S(2)}, u32[]{:S(2)}) collective-permute-start(bf16[24,8,1536]{2,1,0:T(8,128)(2,1)S(1)} %get-tuple-element.141), channel_id=1, source_target_pairs={{0,2},{1,3},{2,0},{3,1},{4,6},{5,7},{6,4},{7,5},{8,10},{9,11},{10,... | collective-permute-start | bytes 1769480 | tf_op jit(solution)/shard_map/ppermute | solution.py:889
  129.6 16.5 %copy-start = (bf16[768,2304]{1,0:T(8,128)(2,1)S(1)}, bf16[768,2304]{1,0:T(8,128)(2,1)}, u32[]{:S(2)}) copy-start(bf16[768,2304]{1,0:T(8,128)(2,1)} %wq_ref.3) | copy-start | bytes 10616836
  137.3 20.9 %collective-permute-start.10 = (bf16[25,8,1536]{2,1,0:T(8,128)(2,1)S(1)}, bf16[25,8,1536]{2,1,0:T(8,128)(2,1)S(1)}, u32[]{:S(2)}, u32[]{:S(2)}) collective-permute-start(bf16[25,8,1536]{2,1,0:T(8,128)(2,1)S(1)} %get-tuple-element.149), channel_id=1, source_target_pairs={{0,2},{1,3},{2,0},{3,1},{4,6},{5,7},{6,4},{7,5},{8,10},{9,11},{10,... | collective-permute-start | bytes 1843208 | tf_op jit(solution)/shard_map/ppermute | solution.py:889
  142.3 14.4 %collective-permute-start.9 = (bf16[24,8,1536]{2,1,0:T(8,128)(2,1)S(1)}, bf16[24,8,1536]{2,1,0:T(8,128)(2,1)S(1)}, u32[]{:S(2)}, u32[]{:S(2)}) collective-permute-start(bf16[24,8,1536]{2,1,0:T(8,128)(2,1)S(1)} %get-tuple-element.146), channel_id=1, source_target_pairs={{0,8},{4,12},{8,0},{12,4},{16,24},{20,28},{24,16},{28,20},{1,9},{5... | collective-permute-start | bytes 1769480 | tf_op jit(solution)/shard_map/ppermute | solution.py:889
  144.2 13.9 %collective-permute-start.11 = (bf16[24,8,1536]{2,1,0:T(8,128)(2,1)S(1)}, bf16[24,8,1536]{2,1,0:T(8,128)(2,1)S(1)}, u32[]{:S(2)}, u32[]{:S(2)}) collective-permute-start(bf16[24,8,1536]{2,1,0:T(8,128)(2,1)S(1)} %get-tuple-element.151), channel_id=1, source_target_pairs={{0,4},{4,0},{8,12},{12,8},{16,20},{20,16},{24,28},{28,24},{1,5},{5... | collective-permute-start | bytes 1769480 | tf_op jit(solution)/shard_map/ppermute | solution.py:889
  158.1 9.1 %copy-start.11 = (s32[8]{0:T(128)S(1)}, s32[8]{0:T(128)}, u32[]{:S(2)}) copy-start(s32[8]{0:T(128)} %stack.35.here_s) | copy-start | bytes 100
  159.0 8.3 %collective-permute-start.12 = (bf16[13,8,1536]{2,1,0:T(8,128)(2,1)S(1)}, bf16[13,8,1536]{2,1,0:T(8,128)(2,1)S(1)}, u32[]{:S(2)}, u32[]{:S(2)}) collective-permute-start(bf16[13,8,1536]{2,1,0:T(8,128)(2,1)S(1)} %get-tuple-element.155), channel_id=1, source_target_pairs={{0,4},{4,0},{8,12},{12,8},{16,20},{20,16},{24,28},{28,24},{1,5},{5... | collective-permute-start | bytes 958472 | tf_op jit(solution)/shard_map/ppermute | solution.py:889
  160.5 6.7 %collective-permute-start.13 = (bf16[12,8,1536]{2,1,0:T(8,128)(2,1)S(1)}, bf16[12,8,1536]{2,1,0:T(8,128)(2,1)S(1)}, u32[]{:S(2)}, u32[]{:S(2)}) collective-permute-start(bf16[12,8,1536]{2,1,0:T(8,128)(2,1)S(1)} %get-tuple-element.157), channel_id=1, source_target_pairs={{0,2},{1,3},{2,0},{3,1},{4,6},{5,7},{6,4},{7,5},{8,10},{9,11},{10,... | collective-permute-start | bytes 884744 | tf_op jit(solution)/shard_map/ppermute | solution.py:889
  167.9 14.3 %collective-permute-start.15 = (bf16[13,8,1536]{2,1,0:T(8,128)(2,1)S(1)}, bf16[13,8,1536]{2,1,0:T(8,128)(2,1)S(1)}, u32[]{:S(2)}, u32[]{:S(2)}) collective-permute-start(bf16[13,8,1536]{2,1,0:T(8,128)(2,1)S(1)} %get-tuple-element.162), channel_id=1, source_target_pairs={{0,8},{4,12},{8,0},{12,4},{16,24},{20,28},{24,16},{28,20},{1,9},{5... | collective-permute-start | bytes 958472 | tf_op jit(solution)/shard_map/ppermute | solution.py:889
  169.0 12.6 %collective-permute-start.14 = (bf16[12,8,1536]{2,1,0:T(8,128)(2,1)S(1)}, bf16[12,8,1536]{2,1,0:T(8,128)(2,1)S(1)}, u32[]{:S(2)}, u32[]{:S(2)}) collective-permute-start(bf16[12,8,1536]{2,1,0:T(8,128)(2,1)S(1)} %get-tuple-element.160), channel_id=1, source_target_pairs={{0,16},{4,20},{8,24},{12,28},{16,0},{20,4},{24,8},{28,12},{1,17},{... | collective-permute-start | bytes 884744 | tf_op jit(solution)/shard_map/ppermute | solution.py:889
  182.9 6.8 %collective-permute-start.17 = (bf16[12,8,1536]{2,1,0:T(8,128)(2,1)S(1)}, bf16[12,8,1536]{2,1,0:T(8,128)(2,1)S(1)}, u32[]{:S(2)}, u32[]{:S(2)}) collective-permute-start(bf16[12,8,1536]{2,1,0:T(8,128)(2,1)S(1)} %fold_last.2.me), channel_id=1, source_target_pairs={{0,2},{1,3},{2,0},{3,1},{4,6},{5,7},{6,4},{7,5},{8,10},{9,11},{10,... | collective-permute-start | bytes 884744 | tf_op jit(solution)/shard_map/ppermute | solution.py:889
  184.0 7.3 %collective-permute-start.16 = (bf16[7,8,1536]{2,1,0:T(8,128)(2,1)S(1)}, bf16[7,8,1536]{2,1,0:T(8,128)(2,1)S(1)}, u32[]{:S(2)}, u32[]{:S(2)}) collective-permute-start(bf16[7,8,1536]{2,1,0:T(8,128)(2,1)S(1)} %get-tuple-element.164), channel_id=1, source_target_pairs={{0,16},{4,20},{8,24},{12,28},{16,0},{20,4},{24,8},{28,12},{1,17},{... | collective-permute-start | bytes 516104 | tf_op jit(solution)/shard_map/ppermute | solution.py:889
  186.0 11.1 %collective-permute-start.18 = (bf16[12,8,1536]{2,1,0:T(8,128)(2,1)S(1)}, bf16[12,8,1536]{2,1,0:T(8,128)(2,1)S(1)}, u32[]{:S(2)}, u32[]{:S(2)}) collective-permute-start(bf16[12,8,1536]{2,1,0:T(8,128)(2,1)S(1)} %fold_last.2.me), channel_id=1, source_target_pairs={{0,1},{1,0},{2,3},{3,2},{4,5},{5,4},{6,7},{7,6},{8,9},{9,8},{10,11... | collective-permute-start | bytes 884744 | tf_op jit(solution)/shard_map/ppermute | solution.py:889
  189.7 7.4 %collective-permute-start.19 = (bf16[12,8,1536]{2,1,0:T(8,128)(2,1)S(1)}, bf16[12,8,1536]{2,1,0:T(8,128)(2,1)S(1)}, u32[]{:S(2)}, u32[]{:S(2)}) collective-permute-start(bf16[12,8,1536]{2,1,0:T(8,128)(2,1)S(1)} %collective-permute-done.17.gx), channel_id=1, source_target_pairs={{0,1},{1,0},{2,3},{3,2},{4,5},{5,4},{6,7},{7,6},{8,9},{9,8},{10,11... | collective-permute-start | bytes 884744 | tf_op jit(solution)/shard_map/ppermute | solution.py:889
  191.9 5.2 %collective-permute-start.20 = (bf16[6,8,1536]{2,1,0:T(8,128)(2,1)S(1)}, bf16[6,8,1536]{2,1,0:T(8,128)(2,1)S(1)}, u32[]{:S(2)}, u32[]{:S(2)}) collective-permute-start(bf16[6,8,1536]{2,1,0:T(8,128)(2,1)S(1)} %get-tuple-element.165.me), channel_id=1, source_target_pairs={{0,2},{1,3},{2,0},{3,1},{4,6},{5,7},{6,4},{7,5},{8,10},{9,11},{10,... | collective-permute-start | bytes 442376 | tf_op jit(solution)/shard_map/ppermute | solution.py:889
  192.9 6.6 %collective-permute-start.21 = (bf16[6,8,1536]{2,1,0:T(8,128)(2,1)S(1)}, bf16[6,8,1536]{2,1,0:T(8,128)(2,1)S(1)}, u32[]{:S(2)}, u32[]{:S(2)}) collective-permute-start(bf16[6,8,1536]{2,1,0:T(8,128)(2,1)S(1)} %get-tuple-element.165.me), channel_id=1, source_target_pairs={{0,1},{1,0},{2,3},{3,2},{4,5},{5,4},{6,7},{7,6},{8,9},{9,8},{10,11... | collective-permute-start | bytes 442376 | tf_op jit(solution)/shard_map/ppermute | solution.py:889
  197.1 2.4 %collective-permute-start.22 = (bf16[6,8,1536]{2,1,0:T(8,128)(2,1)S(1)}, bf16[6,8,1536]{2,1,0:T(8,128)(2,1)S(1)}, u32[]{:S(2)}, u32[]{:S(2)}) collective-permute-start(bf16[6,8,1536]{2,1,0:T(8,128)(2,1)S(1)} %collective-permute-done.20.gx), channel_id=1, source_target_pairs={{0,1},{1,0},{2,3},{3,2},{4,5},{5,4},{6,7},{7,6},{8,9},{9,8},{10,11... | collective-permute-start | bytes 442376 | tf_op jit(solution)/shard_map/ppermute | solution.py:889

commit v11 on v10

--- a/solution.py
+++ b/solution.py
@@ -392,7 +392,7 @@
         8 * rows * width * ff,
         40e6,
         (n_attn, w_up, w_down, table, sid),
-        38, 0, (2, 5),
+        38, 0, (2, 5), (2,),
     )
 
 
@@ -513,7 +513,7 @@
             pl.BlockSpec((1, chunk), lambda i, *_: (0, i)),
         ],
         out_shape + [shaped((rows, half), BF16), shaped((1, half), F32)],
-        scratch, 4 * rows * width * half, 16e6, args, 26, 0 if got is None else 1, (0,) if got is None else (0, 2, 4), (0, 2),
+        scratch, 4 * rows * width * half, 16e6, args, 26, 0 if got is None else 1, (0,) if got is None else (0, 2, 4), (0, 2, 3),
     )
 
 

time: 204 us -> 206 us (level)
  transfers between devices with their start and end apart: 24 -> 24, of which waited for: 10 -> 11; matrix products, arithmetic and copies ran while one was open for 0% -> 0% of each run, Pallas kernels for 37% -> 37%
where the time goes in v11:
time: 206 us; the launch traced here: 203 us
  Pallas kernels  138 us (67%)
  starting transfers between devices  33.1 us (16%)
  waiting for transfers between devices  26.7 us (13%)
  local copies, waits for them, and re-layouts  3.07 us (1%)
    pallas_call x11, Pallas kernels, call(): pl.pallas_call(kernel, grid_spec=pltpu.PrefetchScalarGridSpec(num_scalar_...  126 us
    ppermute x23, waiting for transfers between devices, swap(): lax.ppermute(item, axis, [(index, index ^ step) for index in range(count)])  26.7 us
    ppermute x23, starting transfers between devices, swap(): lax.ppermute(item, axis, [(index, index ^ step) for index in range(count)])  25.8 us
    pallas_call x10, Pallas kernels, small_call(): pl.pallas_call(kernel, in_specs=[pl.BlockSpec(memory_space=pltpu.SMEM)] +...  11.4 us
    all_to_all x1, starting transfers between devices, regroup_rows(): got = lax.all_to_all(sent, 'wide', split_axis=0, concat_axis=0, tiled=True)  7.31 us
  transfers between devices with their start and end apart: 24, of which 11 were waited for; matrix products, arithmetic and copies ran while one was open for 0% of the time, Pallas kernels for 37%

profile of v11, /device:TPU:0, one launch (start us, length us, event | category | flops | bytes accessed | tf_op | source)
XLA Modules:
  0.0 202.6 jit_solution(10080702673174033708)
XLA Ops:
  0.7 0.9 vector_table.1.tab_ref
  1.6 0.0 copy-start
  1.6 17.1 %attn_fwd.1 = (bf16[1024,2304]{1,0:T(8,128)(2,1)}, bf16[8,6,256,128]{3,2,1,0:T(8,128)(2,1)}, bf16[1024,768]{1,0:T(8,128)(2,1)}, f32[1024,768]{1,0:T(8,128)}, f32...) custom-call(s32[8]{0:T(128)} %slots_s.1, s32[26]{0:T(128)} %lengths_s.1, bf16[1024,768]{1,0:T(8,128)(2,1)} %x_ref.5, ...), custom_call_target="tpu_custom_call" | custom-call | flops 483183808 | bytes 1500000 | tf_op jit(solution)/shard_map/attn_fwd/pallas_call | solution.py:72
  18.7 24.4 %ffn_fwd.1 = (bf16[1024,3072]{1,0:T(8,128)(2,1)}, bf16[1024,3072]{1,0:T(8,128)(2,1)}, bf16[768,1024]{1,0:T(8,128)(2,1)S(1)}, bf16[8,128,768]{2,1,0:T(8,128)(2,1)...) custom-call(s32[8]{0:T(128)} %slots_s.1, s32[1,26]{1,0:T(1,128)} %pairing_s.1, ...), custom_call_target="tpu_custom_call" | custom-call | flops 966367616 | bytes 2000000 | tf_op jit(solution)/shard_map/ffn_fwd/pallas_call | solution.py:72
  43.0 0.6 stack.35.here_s
  43.6 8.2 %down_give.1 = bf16[3072,384]{1,0:T(8,128)(2,1)} custom-call(s32[8]{0:T(128)} %stack.35.here_s, bf16[1024,3072]{1,0:T(8,128)(2,1)} %get-tuple-element.101.act_ref, bf16[1024,768]{1,0:T(8,128)(2,1)S(1)} %get-tuple-element.102.gs_ref), custom_call_target="tpu_custom_call" | custom-call | flops 120795952 | bytes 450000 | tf_op jit(solution)/shard_map/down_give/pallas_call | solution.py:72
  51.9 0.5 collective-permute-start
  52.4 8.9 %up_give.1 = (bf16[768,1536]{1,0:T(8,128)(2,1)}, bf16[1024,1536]{1,0:T(8,128)(2,1)}, f32[1,1536]{1,0:T(1,128)S(1)}) custom-call(s32[8]{0:T(128)} %stack.35.here_s, bf16[1024,768]{1,0:T(8,128)(2,1)S(1)} %get-tuple-element.102.gs_ref, bf16[1024,3072]{1,0:T(8,128)(2,1)} %get-tuple-element.104.dg_ref, bf16[768,1024]{1,0:T(8,128)(2,1)S(1)} %get-tuple-element.105.ht_ref, ...), custom_call_target="tpu_custom_call" | custom-call | flops 241591904 | bytes 800000 | tf_op jit(solution)/shard_map/up_give/pallas_call | solution.py:72
  61.3 0.0 collective-permute-start.1
  61.3 7.3 %all-to-all-start = ((bf16[8,128,768]{2,1,0:T(8,128)(2,1)}), bf16[8,128,768]{2,1,0:T(8,128)(2,1)}, u32[]{:S(2)}, u32[]{:S(2)}) async-start(bf16[8,128,768]{2,1,0:T(8,128)(2,1)} %get-tuple-element.122), calls=%async_computation | async-start | bytes 3145728 | tf_op jit(solution)/shard_map/all_to_all | solution.py:900
  68.6 0.0 slice-start.3
  68.6 0.0 collective-permute-done.got_ref
  68.6 8.7 %down_own.1 = (bf16[24,8,1536]{2,1,0:T(8,128)(2,1)}, bf16[24,8,1536]{2,1,0:T(8,128)(2,1)}, bf16[24,8,1536]{2,1,0:T(8,128)(2,1)}, bf16[24,8,1536]{2,1,0:T(8,128)(2,1)}) custom-call(s32[8]{0:T(128)} %stack.35.here_s, bf16[1024,3072]{1,0:T(8,128)(2,1)} %get-tuple-element.101.act_ref, bf16[1024,768]{1,0:T(8,128)(2,1)S(1)} %get-tuple-element.102.gs_ref, ...), custom_call_target="tpu_custom_call" | custom-call | flops 120795952 | bytes 550000 | tf_op jit(solution)/shard_map/down_own/pallas_call | solution.py:72
  77.3 1.5 collective-permute-start.2
  78.8 2.1 %collective-permute-start.3 = (bf16[24,8,1536]{2,1,0:T(8,128)(2,1)}, bf16[24,8,1536]{2,1,0:T(8,128)(2,1)}, u32[]{:S(2)}, u32[]{:S(2)}) collective-permute-start(bf16[24,8,1536]{2,1,0:T(8,128)(2,1)} %get-tuple-element.126), channel_id=1, source_target_pairs={{0,4},{4,0},{8,12},{12,8},{16,20},{20,16},{24,28},{28,24},{1,5},{5... | collective-permute-start | bytes 1769480 | tf_op jit(solution)/shard_map/ppermute | solution.py:889
  80.9 0.0 collective-permute-done.1.refs_0_
  80.9 9.4 %up_own.1 = (bf16[24,8,1536]{2,1,0:T(8,128)(2,1)}, bf16[24,8,1536]{2,1,0:T(8,128)(2,1)}, bf16[24,8,1536]{2,1,0:T(8,128)(2,1)}, bf16[24,8,1536]{2,1,0:T(8,128)(2,...) custom-call(s32[8]{0:T(128)} %stack.35.here_s, bf16[1024,768]{1,0:T(8,128)(2,1)S(1)} %get-tuple-element.102.gs_ref, ...), custom_call_target="tpu_custom_call" | custom-call | flops 241591904 | bytes 800000 | tf_op jit(solution)/shard_map/up_own/pallas_call | solution.py:72
  90.3 0.5 collective-permute-start.4
  90.9 0.5 collective-permute-start.5
  91.4 0.0 copy-start.10
  91.4 21.5 %attn_bwd.1 = (f32[1024,768]{1,0:T(8,128)}, bf16[1024,768]{1,0:T(8,128)(2,1)S(1)}, bf16[1024,2304]{1,0:T(8,128)(2,1)}, f32[8,768]{1,0:T(8,128)S(1)}) custom-call(s32[8]{0:T(128)} %stack.35.here_s, bf16[1024,1536]{1,0:T(8,128)(2,1)S(1)} %get-tuple-element.113.gi_ref, bf16[1024,1536]{1,0:T(8,128)(2,1)S(1)} %copy-done.5, ...), custom_call_target="tpu_custom_call" | custom-call | flops 483183808 | bytes 2000000 | tf_op jit(solution)/shard_map/attn_bwd/pallas_call | solution.py:72
  113.0 1.3 collective-permute-done.5.refs_7_
  114.3 0.0 copy-start.8
  114.3 1.1 copy-done.8
  115.4 1.1 copy-done.9
  116.4 2.3 %fold_second.2 = (bf16[24,8,1536]{2,1,0:T(8,128)(2,1)S(1)}, bf16[24,8,1536]{2,1,0:T(8,128)(2,1)S(1)}, bf16[24,8,1536]{2,1,0:T(8,128)(2,1)S(1)}, bf16[24,8,1536]{2,1,0:T(8,128)(2,1)S(1)}) custom-call(s32[8]{0:T(128)S(1)} %copy-done.10, bf16[24,8,1536]{2,1,0:T(8,128)(2,1)S(1)} %copy-done.6, bf16[24,8,1536]{2,1,0:T(8,128)(2,1)} %collective-permute-done.2.refs_1_, ...), custom_call_target="tpu_custom_call" | custom-call | flops 50000 | bytes 200000 | tf_op jit(solution)/shard_map/fold_second/pallas_call | solution.py:717
  118.7 0.3 copy-done.3
  119.0 6.8 %proj_give.1 = bf16[776,1536]{1,0:T(8,128)(2,1)S(1)} custom-call(s32[8]{0:T(128)} %stack.35.here_s, bf16[1024,768]{1,0:T(8,128)(2,1)S(1)} %copy-done.2, bf16[1024,2304]{1,0:T(8,128)(2,1)} %get-tuple-element.143.gm_ref, bf16[1024,768]{1,0:T(8,128)(2,1)S(1)} %copy-done.3, bf16[1024,768]{1,0:T(8,128)(2,1)S(1)} %get-tuple-element.133.gb_ref, ...), custom_call_target="tpu_custom_call" | custom-call | flops 120795952 | bytes 450000 | tf_op jit(solution)/shard_map/proj_give/pallas_call | solution.py:72
  125.8 0.1 collective-permute-start.6
  125.9 0.3 collective-permute-start.7
  126.2 1.5 collective-permute-start.8
  127.7 2.7 %collective-permute-done.6.got_ref = bf16[776,1536]{1,0:T(8,128)(2,1)S(1)} collective-permute-done((bf16[776,1536]{1,0:T(8,128)(2,1)S(1)}, bf16[776,1536]{1,0:T(8,128)(2,1)S(1)}, u32[]{:S(2)}, u32[]{:S(2)}) %collective-permute-start.6) | collective-permute-done | bytes 2383904 | tf_op jit(solution)/shard_map/ppermute | solution.py:889
  130.4 7.6 %proj_own.1 = (bf16[25,8,1536]{2,1,0:T(8,128)(2,1)S(1)}, bf16[25,8,1536]{2,1,0:T(8,128)(2,1)S(1)}, bf16[24,8,1536]{2,1,0:T(8,128)(2,1)S(1)}, bf16[24,8,1536]{2,1,0:T(8,128)(2,1)S(1)}) custom-call(s32[8]{0:T(128)} %stack.35.here_s, bf16[1024,768]{1,0:T(8,128)(2,1)S(1)} %copy-done.2, bf16[1024,2304]{1,0:T(8,128)(2,1)} %get-tuple-element.143.gm_ref, ...), custom_call_target="tpu_custom_call" | custom-call | flops 120795952 | bytes 550000 | tf_op jit(solution)/shard_map/proj_own/pallas_call | solution.py:72
  138.1 1.5 collective-permute-start.10
  139.6 2.0 collective-permute-done.7.refs_1_
  141.6 0.8 collective-permute-done.8.refs_3_
  142.4 0.8 fold_third.2
  143.2 2.3 %collective-permute-start.9 = (bf16[24,8,1536]{2,1,0:T(8,128)(2,1)S(1)}, bf16[24,8,1536]{2,1,0:T(8,128)(2,1)S(1)}, u32[]{:S(2)}, u32[]{:S(2)}) collective-permute-start(bf16[24,8,1536]{2,1,0:T(8,128)(2,1)S(1)} %get-tuple-element.146), channel_id=1, source_target_pairs={{0,8},{4,12},{8,0},{12,4},{16,24},{20,28},{24,16},{28,20},{1,9},{5... | collective-permute-start | bytes 1769480 | tf_op jit(solution)/shard_map/ppermute | solution.py:889
  145.5 1.9 collective-permute-start.11
  147.5 7.1 %input_grad.1 = bf16[1024,768]{1,0:T(8,128)(2,1)} custom-call(bf16[1024,2304]{1,0:T(8,128)(2,1)} %get-tuple-element.143.gm_ref, bf16[768,2304]{1,0:T(8,128)(2,1)S(1)} %copy-done.1, f32[1024,768]{1,0:T(8,128)} %get-tuple-element.144.gr_ref), custom_call_target="tpu_custom_call" | custom-call | flops 181193936 | bytes 650000 | tf_op jit(solution)/shard_map/input_grad/pallas_call | solution.py:72
  154.5 3.4 %collective-permute-done.9.got_ref = bf16[24,8,1536]{2,1,0:T(8,128)(2,1)S(1)} collective-permute-done((bf16[24,8,1536]{2,1,0:T(8,128)(2,1)S(1)}, bf16[24,8,1536]{2,1,0:T(8,128)(2,1)S(1)}, u32[]{:S(2)}, u32[]{:S(2)}) %collective-permute-start.9) | collective-permute-done | bytes 589856 | tf_op jit(solution)/shard_map/ppermute | solution.py:889
  158.0 0.7 fold_fourth.2
  158.6 0.8 collective-permute-done.11.refs_3_
  159.4 0.8 fold_second.3
  160.3 1.5 collective-permute-start.12
  161.8 0.5 collective-permute-start.13
  162.3 6.1 %copied.1 = bf16[1024,768]{1,0:T(8,128)(2,1)} custom-call(s32[8]{0:T(128)} %stack.35.here_s, bf16[1024,768]{1,0:T(8,128)(2,1)} %bitcast.8.in_ref), custom_call_target="tpu_custom_call" | custom-call | bytes 150000 | tf_op jit(solution)/shard_map/copied/pallas_call | solution.py:72
  168.4 0.1 collective-permute-done.13.refs_3_
  168.5 0.7 fold_third.3
  169.2 1.1 collective-permute-start.15
  170.3 4.8 %collective-permute-start.14 = (bf16[12,8,1536]{2,1,0:T(8,128)(2,1)S(1)}, bf16[12,8,1536]{2,1,0:T(8,128)(2,1)S(1)}, u32[]{:S(2)}, u32[]{:S(2)}) collective-permute-start(bf16[12,8,1536]{2,1,0:T(8,128)(2,1)S(1)} %get-tuple-element.160), channel_id=1, source_target_pairs={{0,16},{4,20},{8,24},{12,28},{16,0},{20,4},{24,8},{28,12},{1,17},{... | collective-permute-start | bytes 884744 | tf_op jit(solution)/shard_map/ppermute | solution.py:889
  175.1 7.6 %collective-permute-done.14.got_ref = bf16[12,8,1536]{2,1,0:T(8,128)(2,1)S(1)} collective-permute-done((bf16[12,8,1536]{2,1,0:T(8,128)(2,1)S(1)}, bf16[12,8,1536]{2,1,0:T(8,128)(2,1)S(1)}, u32[]{:S(2)}, u32[]{:S(2)}) %collective-permute-start.14) | collective-permute-done | bytes 294944 | tf_op jit(solution)/shard_map/ppermute | solution.py:889
  182.7 0.6 fold_last.2.me
  183.3 0.6 fold_fourth.3
  183.9 0.8 collective-permute-start.17
  184.7 2.5 %collective-permute-start.16 = (bf16[7,8,1536]{2,1,0:T(8,128)(2,1)S(1)}, bf16[7,8,1536]{2,1,0:T(8,128)(2,1)S(1)}, u32[]{:S(2)}, u32[]{:S(2)}) collective-permute-start(bf16[7,8,1536]{2,1,0:T(8,128)(2,1)S(1)} %get-tuple-element.164), channel_id=1, source_target_pairs={{0,16},{4,20},{8,24},{12,28},{16,0},{20,4},{24,8},{28,12},{1,17},{... | collective-permute-start | bytes 516104 | tf_op jit(solution)/shard_map/ppermute | solution.py:889
  187.3 3.4 %collective-permute-done.17.gx = bf16[12,8,1536]{2,1,0:T(8,128)(2,1)S(1)} collective-permute-done((bf16[12,8,1536]{2,1,0:T(8,128)(2,1)S(1)}, bf16[12,8,1536]{2,1,0:T(8,128)(2,1)S(1)}, u32[]{:S(2)}, u32[]{:S(2)}) %collective-permute-start.17) | collective-permute-done | bytes 294944 | tf_op jit(solution)/shard_map/ppermute | solution.py:889
  190.7 1.0 collective-permute-done.16.got_ref
  191.7 0.6 fold_last.3
  192.3 1.7 collective-permute-start.20
  194.0 3.6 %collective-permute-done.20.gx = bf16[6,8,1536]{2,1,0:T(8,128)(2,1)S(1)} collective-permute-done((bf16[6,8,1536]{2,1,0:T(8,128)(2,1)S(1)}, bf16[6,8,1536]{2,1,0:T(8,128)(2,1)S(1)}, u32[]{:S(2)}, u32[]{:S(2)}) %collective-permute-start.20) | collective-permute-done | bytes 147488 | tf_op jit(solution)/shard_map/ppermute | solution.py:889
  197.6 2.4 %feed_blocks.1 = (f32[384,768]{1,0:T(8,128)}, f32[96,3072]{1,0:T(8,128)}) custom-call(s32[8]{0:T(128)S(1)} %copy-done.12, bf16[12,8,1536]{2,1,0:T(8,128)(2,1)S(1)} %fold_last.2.me, bf16[12,8,1536]{2,1,0:T(8,128)(2,1)S(1)} %collective-permute-done.17.gx, bf16[12,8,1536]{2,1,0:T(8,128)(2,1)S(1)} %collective-permute-done.18.gc, ...), custom_call_target="tpu_custom_call" | custom-call | flops 50000 | bytes 200000 | tf_op jit(solution)/shard_map/feed_blocks/pallas_call | solution.py:717
  200.1 1.9 projection_blocks.1
  202.0 0.6 reduce
  (49 shorter events, 0.1 us)
Async XLA Ops:
  1.6 17.1 %copy-start = (bf16[3072,768]{1,0:T(8,128)(2,1)S(1)}, bf16[3072,768]{1,0:T(8,128)(2,1)}, u32[]{:S(2)}) copy-start(bf16[3072,768]{1,0:T(8,128)(2,1)} %wd_ref.5) | copy-start | bytes 14155780
  43.6 8.7 %slice-start = ((s8[4718592]{0:T(1024)(128)(4,1)}), s8[4194304]{0:T(1024)(128)(4,1)S(1)}, s32[]{:S(2)}) async-start(s8[4718592]{0:T(1024)(128)(4,1)} %bitcast.17), calls=%async_computation.1 | async-start | bytes 8388608
  43.6 8.7 %slice-start.1 = ((s8[4718592]{0:T(1024)(128)(4,1)}), s8[524288]{0:T(1024)(128)(4,1)S(1)}, s32[]{:S(2)}) async-start(s8[4718592]{0:T(1024)(128)(4,1)} %bitcast.17), calls=%async_computation.2 | async-start | bytes 1048576
  51.9 16.7 %collective-permute-start = (bf16[3072,384]{1,0:T(8,128)(2,1)}, bf16[3072,384]{1,0:T(8,128)(2,1)}, u32[]{:S(2)}, u32[]{:S(2)}) collective-permute-start(bf16[3072,384]{1,0:T(8,128)(2,1)} %down_give.1), channel_id=1, source_target_pairs={{0,1},{1,0},{2,3},{3,2},{4,5},{5,4},{6,7},{7,6},{8,9},{9,8},{10,11... | collective-permute-start | bytes 7077896 | tf_op jit(solution)/shard_map/ppermute | solution.py:889
  61.3 19.6 %collective-permute-start.1 = (bf16[768,1536]{1,0:T(8,128)(2,1)}, bf16[768,1536]{1,0:T(8,128)(2,1)}, u32[]{:S(2)}, u32[]{:S(2)}) collective-permute-start(bf16[768,1536]{1,0:T(8,128)(2,1)} %get-tuple-element.110), channel_id=1, source_target_pairs={{0,1},{1,0},{2,3},{3,2},{4,5},{5,4},{6,7},{7,6},{8,9},{9,8},{10,11... | collective-permute-start | bytes 7077896 | tf_op jit(solution)/shard_map/ppermute | solution.py:889
  61.3 51.7 %all-to-all-start = ((bf16[8,128,768]{2,1,0:T(8,128)(2,1)}), bf16[8,128,768]{2,1,0:T(8,128)(2,1)}, u32[]{:S(2)}, u32[]{:S(2)}) async-start(bf16[8,128,768]{2,1,0:T(8,128)(2,1)} %get-tuple-element.122), calls=%async_computation | async-start | bytes 3145728 | tf_op jit(solution)/shard_map/all_to_all | solution.py:900
  68.6 12.3 %slice-start.2 = ((s8[4718592]{0:T(1024)(128)(4,1)}), s8[4194304]{0:T(1024)(128)(4,1)S(1)}, s32[]{:S(2)}) async-start(s8[4718592]{0:T(1024)(128)(4,1)} %bitcast.19), calls=%async_computation.3 | async-start | bytes 8388608
  68.6 12.3 %slice-start.3 = ((s8[4718592]{0:T(1024)(128)(4,1)}), s8[524288]{0:T(1024)(128)(4,1)S(1)}, s32[]{:S(2)}) async-start(s8[4718592]{0:T(1024)(128)(4,1)} %bitcast.19), calls=%async_computation.4 | async-start | bytes 1048576
  77.3 35.6 %collective-permute-start.2 = (bf16[24,8,1536]{2,1,0:T(8,128)(2,1)}, bf16[24,8,1536]{2,1,0:T(8,128)(2,1)}, u32[]{:S(2)}, u32[]{:S(2)}) collective-permute-start(bf16[24,8,1536]{2,1,0:T(8,128)(2,1)} %get-tuple-element.124), channel_id=1, source_target_pairs={{0,2},{1,3},{2,0},{3,1},{4,6},{5,7},{6,4},{7,5},{8,10},{9,11},{10,... | collective-permute-start | bytes 1769480 | tf_op jit(solution)/shard_map/ppermute | solution.py:889
  78.8 12.5 %slice-start.4 = ((s8[4718592]{0:T(1024)(128)(4,1)}), s8[4194304]{0:T(1024)(128)(4,1)S(1)}, s32[]{:S(2)}) async-start(s8[4718592]{0:T(1024)(128)(4,1)} %bitcast.21), calls=%async_computation.5 | async-start | bytes 8388608
  78.8 12.5 %slice-start.5 = ((s8[4718592]{0:T(1024)(128)(4,1)}), s8[524288]{0:T(1024)(128)(4,1)S(1)}, s32[]{:S(2)}) async-start(s8[4718592]{0:T(1024)(128)(4,1)} %bitcast.21), calls=%async_computation.6 | async-start | bytes 1048576
  78.8 12.5 %copy-start.4 = (bf16[768,768]{1,0:T(8,128)(2,1)S(1)}, bf16[768,768]{1,0:T(8,128)(2,1)}, u32[]{:S(2)}) copy-start(bf16[768,768]{1,0:T(8,128)(2,1)} %wo_ref.3) | copy-start | bytes 3538948
  78.8 12.5 %copy-start.5 = (bf16[1024,1536]{1,0:T(8,128)(2,1)S(1)}, bf16[1024,1536]{1,0:T(8,128)(2,1)}, u32[]{:S(2)}) copy-start(bf16[1024,1536]{1,0:T(8,128)(2,1)} %get-tuple-element.114.other_ref) | copy-start | bytes 9437188
  78.8 34.1 %collective-permute-start.3 = (bf16[24,8,1536]{2,1,0:T(8,128)(2,1)}, bf16[24,8,1536]{2,1,0:T(8,128)(2,1)}, u32[]{:S(2)}, u32[]{:S(2)}) collective-permute-start(bf16[24,8,1536]{2,1,0:T(8,128)(2,1)} %get-tuple-element.126), channel_id=1, source_target_pairs={{0,4},{4,0},{8,12},{12,8},{16,20},{20,16},{24,28},{28,24},{1,5},{5... | collective-permute-start | bytes 1769480 | tf_op jit(solution)/shard_map/ppermute | solution.py:889
  90.3 22.6 %collective-permute-start.4 = (bf16[24,8,1536]{2,1,0:T(8,128)(2,1)}, bf16[24,8,1536]{2,1,0:T(8,128)(2,1)}, u32[]{:S(2)}, u32[]{:S(2)}) collective-permute-start(bf16[24,8,1536]{2,1,0:T(8,128)(2,1)} %get-tuple-element.127), channel_id=1, source_target_pairs={{0,2},{1,3},{2,0},{3,1},{4,6},{5,7},{6,4},{7,5},{8,10},{9,11},{10,... | collective-permute-start | bytes 1769480 | tf_op jit(solution)/shard_map/ppermute | solution.py:889
  90.9 23.4 %collective-permute-start.5 = (bf16[24,8,1536]{2,1,0:T(8,128)(2,1)}, bf16[24,8,1536]{2,1,0:T(8,128)(2,1)}, u32[]{:S(2)}, u32[]{:S(2)}) collective-permute-start(bf16[24,8,1536]{2,1,0:T(8,128)(2,1)} %get-tuple-element.129), channel_id=1, source_target_pairs={{0,4},{4,0},{8,12},{12,8},{16,20},{20,16},{24,28},{28,24},{1,5},{5... | collective-permute-start | bytes 1769480 | tf_op jit(solution)/shard_map/ppermute | solution.py:889
  91.4 22.9 %copy-start.6 = (bf16[24,8,1536]{2,1,0:T(8,128)(2,1)S(1)}, bf16[24,8,1536]{2,1,0:T(8,128)(2,1)}, u32[]{:S(2)}) copy-start(bf16[24,8,1536]{2,1,0:T(8,128)(2,1)} %get-tuple-element.108.refs_0_) | copy-start | bytes 1769476
  91.4 22.9 %copy-start.7 = (bf16[24,8,1536]{2,1,0:T(8,128)(2,1)S(1)}, bf16[24,8,1536]{2,1,0:T(8,128)(2,1)}, u32[]{:S(2)}) copy-start(bf16[24,8,1536]{2,1,0:T(8,128)(2,1)} %get-tuple-element.125.refs_2_) | copy-start | bytes 1769476
  91.4 22.9 %copy-start.10 = (s32[8]{0:T(128)S(1)}, s32[8]{0:T(128)}, u32[]{:S(2)}) copy-start(s32[8]{0:T(128)} %stack.35.here_s) | copy-start | bytes 100
  114.3 1.1 copy-start.8
  115.4 1.1 copy-start.9
  116.4 2.3 %copy-start.2 = (bf16[1024,768]{1,0:T(8,128)(2,1)S(1)}, bf16[1024,768]{1,0:T(8,128)(2,1)}, u32[]{:S(2)}) copy-start(bf16[1024,768]{1,0:T(8,128)(2,1)} %x_ref.5) | copy-start | bytes 4718596
  116.4 2.6 %copy-start.3 = (bf16[1024,768]{1,0:T(8,128)(2,1)S(1)}, bf16[1024,768]{1,0:T(8,128)(2,1)}, u32[]{:S(2)}) copy-start(bf16[1024,768]{1,0:T(8,128)(2,1)} %get-tuple-element.132.att_ref) | copy-start | bytes 4718596
  125.8 4.6 %collective-permute-start.6 = (bf16[776,1536]{1,0:T(8,128)(2,1)S(1)}, bf16[776,1536]{1,0:T(8,128)(2,1)S(1)}, u32[]{:S(2)}, u32[]{:S(2)}) collective-permute-start(bf16[776,1536]{1,0:T(8,128)(2,1)S(1)} %proj_give.1), channel_id=1, source_target_pairs={{0,1},{1,0},{2,3},{3,2},{4,5},{5,4},{6,7},{7,6},{8,9},{9,8},{10,11... | collective-permute-start | bytes 7151624 | tf_op jit(solution)/shard_map/ppermute | solution.py:889
  125.9 15.7 %collective-permute-start.7 = (bf16[24,8,1536]{2,1,0:T(8,128)(2,1)S(1)}, bf16[24,8,1536]{2,1,0:T(8,128)(2,1)S(1)}, u32[]{:S(2)}, u32[]{:S(2)}) collective-permute-start(bf16[24,8,1536]{2,1,0:T(8,128)(2,1)S(1)} %get-tuple-element.139), channel_id=1, source_target_pairs={{0,4},{4,0},{8,12},{12,8},{16,20},{20,16},{24,28},{28,24},{1,5},{5... | collective-permute-start | bytes 1769480 | tf_op jit(solution)/shard_map/ppermute | solution.py:889
  126.2 16.2 %copy-start.11 = (s32[8]{0:T(128)S(1)}, s32[8]{0:T(128)}, u32[]{:S(2)}) copy-start(s32[8]{0:T(128)} %stack.35.here_s) | copy-start | bytes 100
  126.2 16.1 %collective-permute-start.8 = (bf16[24,8,1536]{2,1,0:T(8,128)(2,1)S(1)}, bf16[24,8,1536]{2,1,0:T(8,128)(2,1)S(1)}, u32[]{:S(2)}, u32[]{:S(2)}) collective-permute-start(bf16[24,8,1536]{2,1,0:T(8,128)(2,1)S(1)} %get-tuple-element.141), channel_id=1, source_target_pairs={{0,2},{1,3},{2,0},{3,1},{4,6},{5,7},{6,4},{7,5},{8,10},{9,11},{10,... | collective-permute-start | bytes 1769480 | tf_op jit(solution)/shard_map/ppermute | solution.py:889
  130.4 17.0 %copy-start.1 = (bf16[768,2304]{1,0:T(8,128)(2,1)S(1)}, bf16[768,2304]{1,0:T(8,128)(2,1)}, u32[]{:S(2)}) copy-start(bf16[768,2304]{1,0:T(8,128)(2,1)} %wq_ref.3) | copy-start | bytes 10616836
  138.1 21.4 %collective-permute-start.10 = (bf16[25,8,1536]{2,1,0:T(8,128)(2,1)S(1)}, bf16[25,8,1536]{2,1,0:T(8,128)(2,1)S(1)}, u32[]{:S(2)}, u32[]{:S(2)}) collective-permute-start(bf16[25,8,1536]{2,1,0:T(8,128)(2,1)S(1)} %get-tuple-element.149), channel_id=1, source_target_pairs={{0,2},{1,3},{2,0},{3,1},{4,6},{5,7},{6,4},{7,5},{8,10},{9,11},{10,... | collective-permute-start | bytes 1843208 | tf_op jit(solution)/shard_map/ppermute | solution.py:889
  143.2 14.8 %collective-permute-start.9 = (bf16[24,8,1536]{2,1,0:T(8,128)(2,1)S(1)}, bf16[24,8,1536]{2,1,0:T(8,128)(2,1)S(1)}, u32[]{:S(2)}, u32[]{:S(2)}) collective-permute-start(bf16[24,8,1536]{2,1,0:T(8,128)(2,1)S(1)} %get-tuple-element.146), channel_id=1, source_target_pairs={{0,8},{4,12},{8,0},{12,4},{16,24},{20,28},{24,16},{28,20},{1,9},{5... | collective-permute-start | bytes 1769480 | tf_op jit(solution)/shard_map/ppermute | solution.py:889
  145.5 13.9 %collective-permute-start.11 = (bf16[24,8,1536]{2,1,0:T(8,128)(2,1)S(1)}, bf16[24,8,1536]{2,1,0:T(8,128)(2,1)S(1)}, u32[]{:S(2)}, u32[]{:S(2)}) collective-permute-start(bf16[24,8,1536]{2,1,0:T(8,128)(2,1)S(1)} %get-tuple-element.151), channel_id=1, source_target_pairs={{0,4},{4,0},{8,12},{12,8},{16,20},{20,16},{24,28},{28,24},{1,5},{5... | collective-permute-start | bytes 1769480 | tf_op jit(solution)/shard_map/ppermute | solution.py:889
  159.4 9.1 %copy-start.12 = (s32[8]{0:T(128)S(1)}, s32[8]{0:T(128)}, u32[]{:S(2)}) copy-start(s32[8]{0:T(128)} %stack.35.here_s) | copy-start | bytes 100
  160.3 8.3 %collective-permute-start.12 = (bf16[13,8,1536]{2,1,0:T(8,128)(2,1)S(1)}, bf16[13,8,1536]{2,1,0:T(8,128)(2,1)S(1)}, u32[]{:S(2)}, u32[]{:S(2)}) collective-permute-start(bf16[13,8,1536]{2,1,0:T(8,128)(2,1)S(1)} %get-tuple-element.155), channel_id=1, source_target_pairs={{0,4},{4,0},{8,12},{12,8},{16,20},{20,16},{24,28},{28,24},{1,5},{5... | collective-permute-start | bytes 958472 | tf_op jit(solution)/shard_map/ppermute | solution.py:889
  161.8 6.7 %collective-permute-start.13 = (bf16[12,8,1536]{2,1,0:T(8,128)(2,1)S(1)}, bf16[12,8,1536]{2,1,0:T(8,128)(2,1)S(1)}, u32[]{:S(2)}, u32[]{:S(2)}) collective-permute-start(bf16[12,8,1536]{2,1,0:T(8,128)(2,1)S(1)} %get-tuple-element.157), channel_id=1, source_target_pairs={{0,2},{1,3},{2,0},{3,1},{4,6},{5,7},{6,4},{7,5},{8,10},{9,11},{10,... | collective-permute-start | bytes 884744 | tf_op jit(solution)/shard_map/ppermute | solution.py:889
  169.2 14.1 %collective-permute-start.15 = (bf16[13,8,1536]{2,1,0:T(8,128)(2,1)S(1)}, bf16[13,8,1536]{2,1,0:T(8,128)(2,1)S(1)}, u32[]{:S(2)}, u32[]{:S(2)}) collective-permute-start(bf16[13,8,1536]{2,1,0:T(8,128)(2,1)S(1)} %get-tuple-element.162), channel_id=1, source_target_pairs={{0,8},{4,12},{8,0},{12,4},{16,24},{20,28},{24,16},{28,20},{1,9},{5... | collective-permute-start | bytes 958472 | tf_op jit(solution)/shard_map/ppermute | solution.py:889
  170.3 12.4 %collective-permute-start.14 = (bf16[12,8,1536]{2,1,0:T(8,128)(2,1)S(1)}, bf16[12,8,1536]{2,1,0:T(8,128)(2,1)S(1)}, u32[]{:S(2)}, u32[]{:S(2)}) collective-permute-start(bf16[12,8,1536]{2,1,0:T(8,128)(2,1)S(1)} %get-tuple-element.160), channel_id=1, source_target_pairs={{0,16},{4,20},{8,24},{12,28},{16,0},{20,4},{24,8},{28,12},{1,17},{... | collective-permute-start | bytes 884744 | tf_op jit(solution)/shard_map/ppermute | solution.py:889
  183.9 6.8 %collective-permute-start.17 = (bf16[12,8,1536]{2,1,0:T(8,128)(2,1)S(1)}, bf16[12,8,1536]{2,1,0:T(8,128)(2,1)S(1)}, u32[]{:S(2)}, u32[]{:S(2)}) collective-permute-start(bf16[12,8,1536]{2,1,0:T(8,128)(2,1)S(1)} %fold_last.2.me), channel_id=1, source_target_pairs={{0,2},{1,3},{2,0},{3,1},{4,6},{5,7},{6,4},{7,5},{8,10},{9,11},{10,... | collective-permute-start | bytes 884744 | tf_op jit(solution)/shard_map/ppermute | solution.py:889
  184.7 6.9 %collective-permute-start.16 = (bf16[7,8,1536]{2,1,0:T(8,128)(2,1)S(1)}, bf16[7,8,1536]{2,1,0:T(8,128)(2,1)S(1)}, u32[]{:S(2)}, u32[]{:S(2)}) collective-permute-start(bf16[7,8,1536]{2,1,0:T(8,128)(2,1)S(1)} %get-tuple-element.164), channel_id=1, source_target_pairs={{0,16},{4,20},{8,24},{12,28},{16,0},{20,4},{24,8},{28,12},{1,17},{... | collective-permute-start | bytes 516104 | tf_op jit(solution)/shard_map/ppermute | solution.py:889
  187.3 10.4 %collective-permute-start.18 = (bf16[12,8,1536]{2,1,0:T(8,128)(2,1)S(1)}, bf16[12,8,1536]{2,1,0:T(8,128)(2,1)S(1)}, u32[]{:S(2)}, u32[]{:S(2)}) collective-permute-start(bf16[12,8,1536]{2,1,0:T(8,128)(2,1)S(1)} %fold_last.2.me), channel_id=1, source_target_pairs={{0,1},{1,0},{2,3},{3,2},{4,5},{5,4},{6,7},{7,6},{8,9},{9,8},{10,11... | collective-permute-start | bytes 884744 | tf_op jit(solution)/shard_map/ppermute | solution.py:889
  190.7 6.9 %collective-permute-start.19 = (bf16[12,8,1536]{2,1,0:T(8,128)(2,1)S(1)}, bf16[12,8,1536]{2,1,0:T(8,128)(2,1)S(1)}, u32[]{:S(2)}, u32[]{:S(2)}) collective-permute-start(bf16[12,8,1536]{2,1,0:T(8,128)(2,1)S(1)} %collective-permute-done.17.gx), channel_id=1, source_target_pairs={{0,1},{1,0},{2,3},{3,2},{4,5},{5,4},{6,7},{7,6},{8,9},{9,8},{10,11... | collective-permute-start | bytes 884744 | tf_op jit(solution)/shard_map/ppermute | solution.py:889
  192.3 5.4 %collective-permute-start.20 = (bf16[6,8,1536]{2,1,0:T(8,128)(2,1)S(1)}, bf16[6,8,1536]{2,1,0:T(8,128)(2,1)S(1)}, u32[]{:S(2)}, u32[]{:S(2)}) collective-permute-start(bf16[6,8,1536]{2,1,0:T(8,128)(2,1)S(1)} %get-tuple-element.165.me), channel_id=1, source_target_pairs={{0,2},{1,3},{2,0},{3,1},{4,6},{5,7},{6,4},{7,5},{8,10},{9,11},{10,... | collective-permute-start | bytes 442376 | tf_op jit(solution)/shard_map/ppermute | solution.py:889
  194.0 6.1 %collective-permute-start.21 = (bf16[6,8,1536]{2,1,0:T(8,128)(2,1)S(1)}, bf16[6,8,1536]{2,1,0:T(8,128)(2,1)S(1)}, u32[]{:S(2)}, u32[]{:S(2)}) collective-permute-start(bf16[6,8,1536]{2,1,0:T(8,128)(2,1)S(1)} %get-tuple-element.165.me), channel_id=1, source_target_pairs={{0,1},{1,0},{2,3},{3,2},{4,5},{5,4},{6,7},{7,6},{8,9},{9,8},{10,11... | collective-permute-start | bytes 442376 | tf_op jit(solution)/shard_map/ppermute | solution.py:889
  197.6 2.4 %collective-permute-start.22 = (bf16[6,8,1536]{2,1,0:T(8,128)(2,1)S(1)}, bf16[6,8,1536]{2,1,0:T(8,128)(2,1)S(1)}, u32[]{:S(2)}, u32[]{:S(2)}) collective-permute-start(bf16[6,8,1536]{2,1,0:T(8,128)(2,1)S(1)} %collective-permute-done.20.gx), channel_id=1, source_target_pairs={{0,1},{1,0},{2,3},{3,2},{4,5},{5,4},{6,7},{7,6},{8,9},{9,8},{10,11... | collective-permute-start | bytes 442376 | tf_op jit(solution)/shard_map/ppermute | solution.py:889
